TPU v7x, 32 devices: a whole 2x2x4 slice. The times are simulated.
32 devices in a mesh: ep: 4 (over x, core), rep: 8 (over z, y).
Axes of the slice: x: 2, y: 2, z: 4, core: 2. Of those that a mesh axis runs over, the one named last changes fastest.
Arguments:
- tokens: float32 [4, 2048, 1024], P('ep', 'rep'), may hold values from -6 to 6
- segments: int32 [4, 2048], P('ep', 'rep'), may hold values from 0 to 2, never falling along the last dimension, each value on 1 to 1536 neighbouring positions
- routes: int32 [4, 2048, 8], P('ep', 'rep'), may hold values from 0 to 31, all different within a row
- attn_gain: float32 [1024], replicated, may hold values from 0.5 to 1.5
- w_query: bfloat16 [1024, 1024], P(('ep', 'rep')), may hold values from -0.75 to 0.75
- w_key: bfloat16 [1024, 512], P(('ep', 'rep')), may hold values from -0.75 to 0.75
- w_value: bfloat16 [1024, 512], P(('ep', 'rep')), may hold values from -0.1875 to 0.1875
- w_out: bfloat16 [1024, 1024], P(('ep', 'rep')), may hold values from -3 to 3
- mlp_gain: float32 [1024], replicated, may hold values from 0.5 to 1.5
- w_router: bfloat16 [1024, 32], P(('ep', 'rep')), may hold values from -0.09375 to 0.09375
- w_gate_up: bfloat16 [32, 1024, 1024], P('ep'), may hold values from -0.1875 to 0.1875
- w_down: bfloat16 [32, 512, 1024], P('ep'), may hold values from -3 to 3
- cotangent: float32 [4, 2048, 1024], P('ep', 'rep'), may hold values from -6 to 6
Outputs:
- output: float32 [4, 2048, 1024], P('ep', 'rep')
- grad_tokens: float32 [4, 2048, 1024], P('ep', 'rep')
- grad_attn_gain: float32 [1024], P(('ep', 'rep'))
- grad_w_query: float32 [1024, 1024], P(('ep', 'rep'))
- grad_w_key: float32 [1024, 512], P(('ep', 'rep'))
- grad_w_value: float32 [1024, 512], P(('ep', 'rep'))
- grad_w_out: float32 [1024, 1024], P(('ep', 'rep'))
- grad_mlp_gain: float32 [1024], P(('ep', 'rep'))
- grad_w_router: float32 [1024, 32], P(('ep', 'rep'))
- grad_w_gate_up: float32 [32, 1024, 1024], P('ep', 'rep')
- grad_w_down: float32 [32, 512, 1024], P('ep', None, 'rep')
Inputs may be any that keep to these rules, and one draw needn't show every extreme that they name: `segments`: segment numbers never fall along a pack; each of the 3 documents of a pack has 1 to 1536 tokens, one of them exactly 1536. `routes`: each token names 8 different experts.
All inputs are finite; a program needn't handle non-finite values.
Results may differ from a plain program's by a relative error of at most 0.015.
The roundings to bfloat16 on the way count: a program that leaves them out, or rounds other values in their place, can miss the bound.
Values may be sent and summed in bfloat16 or wider, within the bound.
A program may use at most 256 MiB of HBM per device.

v0:
```python
import math

import jax
import jax.numpy as jnp
from jax import lax
from jax.sharding import PartitionSpec as P

HEADS = 16
KV_HEADS = 8
HEAD_DIM = 64
CAP = 80


epsilon = 1e-06
score_scale = 0.015625
branch_scale = 0.22
far_below = -1e30


def product(left, right):
    return jnp.dot(left, right, preferred_element_type=jnp.float32)


def rms_norm(values, gain):
    factor = lax.rsqrt(jnp.mean(values * values, -1, keepdims=True) + epsilon)
    return (values * factor * gain, factor)


def norm_back(grad_normed, values, factor, gain):
    scaled = grad_normed * gain
    gain_part = jnp.sum(grad_normed * values * factor, 0)
    inner_sum = jnp.mean(scaled * values, -1, keepdims=True)
    return (factor * scaled - values * (factor * factor * factor) * inner_sum, gain_part)


def rotate(values, cosine, sine_table):
    half_dim = values.shape[-1] // 2
    lower = values[..., :half_dim]
    upper = values[..., half_dim:]
    return jnp.concatenate(
        [lower * cosine - upper * sine_table, upper * cosine + lower * sine_table], -1
    )


def unrotate(grads, cosine, sine_table):
    half_dim = grads.shape[-1] // 2
    lower = grads[..., :half_dim]
    upper = grads[..., half_dim:]
    return jnp.concatenate(
        [lower * cosine + upper * sine_table, upper * cosine - lower * sine_table], -1
    )


def by_head(rows):
    count = rows.shape[0]
    group_size = HEADS // KV_HEADS
    return (
        rows.reshape(count, KV_HEADS, group_size, HEAD_DIM)
        .transpose(1, 2, 0, 3)
        .reshape(KV_HEADS, group_size * count, HEAD_DIM)
    )


def from_head(blocks, count):
    group_size = HEADS // KV_HEADS
    return (
        blocks.reshape(KV_HEADS, group_size, count, HEAD_DIM)
        .transpose(2, 0, 1, 3)
        .reshape(count, HEADS * HEAD_DIM)
    )


def stats_rows(stats, count):
    group_size = HEADS // KV_HEADS
    return stats.reshape(KV_HEADS, group_size, count).transpose(2, 0, 1).reshape(count, HEADS)


def stats_heads(rows):
    count = rows.shape[0]
    group_size = HEADS // KV_HEADS
    return (
        rows.reshape(count, KV_HEADS, group_size)
        .transpose(1, 2, 0)
        .reshape(KV_HEADS, group_size * count)
    )


def key_heads(rows):
    return rows.reshape(rows.shape[0], KV_HEADS, HEAD_DIM).transpose(1, 0, 2)


def key_rows_of(blocks):
    return blocks.transpose(1, 0, 2).reshape(blocks.shape[1], KV_HEADS * HEAD_DIM)


def on_device(
    tokens,
    segments,
    routes,
    attn_gain,
    w_query,
    w_key,
    w_value,
    w_out,
    mlp_gain,
    w_router,
    w_gate_up,
    w_down,
    cotangent,
):
    inputs = tokens[0]
    own_ids = segments[0]
    own_routes = routes[0]
    grad_output = cotangent[0]
    rows_dev, model_width = inputs.shape
    top_count = own_routes.shape[1]
    group_size = HEADS // KV_HEADS
    pack_ids = lax.all_gather(own_ids, "rep", axis=0, tiled=True)
    length = pack_ids.shape[0]
    offset = lax.axis_index("rep") * rows_dev
    places = jnp.arange(length, dtype=jnp.int32)
    query_at = offset + jnp.arange(rows_dev, dtype=jnp.int32)
    doc_start = jnp.sum((pack_ids[None, :] < own_ids[:, None]).astype(jnp.int32), 1)
    position = (query_at - doc_start).astype(jnp.float32)
    half_dim = HEAD_DIM // 2
    angles = (
        position[:, None]
        * jnp.exp(jnp.arange(half_dim, dtype=jnp.float32) * (-math.log(10000.0) / half_dim))[
            None, :
        ]
    )
    cosine = jnp.cos(angles)[:, None, :]
    sine_table = jnp.sin(angles)[:, None, :]
    allowed = (own_ids[:, None] == pack_ids[None, :]) & (places[None, :] <= query_at[:, None])
    allowed_rows = jnp.tile(allowed, (group_size, 1))
    full_query, full_key, full_value, full_out, full_router = (
        lax.all_gather(w_query, ("ep", "rep"), axis=0, tiled=True),
        lax.all_gather(w_key, ("ep", "rep"), axis=0, tiled=True),
        lax.all_gather(w_value, ("ep", "rep"), axis=0, tiled=True),
        lax.all_gather(w_out, ("ep", "rep"), axis=0, tiled=True),
        lax.all_gather(w_router, ("ep", "rep"), axis=0, tiled=True),
    )
    normed, factor_one = rms_norm(inputs, attn_gain)
    normed_b = normed.astype(jnp.bfloat16)
    query_rows = rotate(
        product(normed_b, full_query).reshape(rows_dev, HEADS, HEAD_DIM), cosine, sine_table
    )
    query_rows = query_rows.astype(jnp.bfloat16).reshape(rows_dev, HEADS * HEAD_DIM)
    key_rows = rotate(
        product(normed_b, full_key).reshape(rows_dev, KV_HEADS, HEAD_DIM), cosine, sine_table
    )
    key_rows = key_rows.astype(jnp.bfloat16).reshape(rows_dev, KV_HEADS * HEAD_DIM)
    value_rows = product(normed_b, full_value).astype(jnp.bfloat16)
    pack_keys, pack_values = (
        lax.all_gather(key_rows, "rep", axis=0, tiled=True),
        lax.all_gather(value_rows, "rep", axis=0, tiled=True),
    )
    query_heads = by_head(query_rows)

    def head_forward(operands):
        query_part, key_part, value_part = operands
        scores = product(query_part, key_part.T) * score_scale
        scores = jnp.where(allowed_rows, scores, far_below)
        row_peak = jnp.max(scores, -1, keepdims=True)
        raised = jnp.exp(scores - row_peak)
        row_total = jnp.sum(raised, -1, keepdims=True)
        weights_b = (raised / row_total).astype(jnp.bfloat16)
        return (product(weights_b, value_part), (row_peak + jnp.log(row_total))[:, 0])

    mixed_heads, log_totals = lax.map(
        head_forward, (query_heads, key_heads(pack_keys), key_heads(pack_values))
    )
    mixed_rows = from_head(mixed_heads, rows_dev).astype(jnp.bfloat16)
    hidden = inputs + branch_scale * product(mixed_rows, full_out)
    normed_two, factor_two = rms_norm(hidden, mlp_gain)
    normed_two_b = normed_two.astype(jnp.bfloat16)
    normed_two_f = normed_two_b.astype(jnp.float32)
    router_f = full_router.astype(jnp.float32)
    logits = product(normed_two_b, full_router)
    experts_all = full_router.shape[1]
    numbers = jnp.arange(experts_all, dtype=jnp.int32)
    pick_table = (own_routes[:, :, None] == numbers).astype(jnp.int32)
    pick_float = pick_table.astype(jnp.float32)
    chosen = jnp.sum(pick_float * logits[:, None, :], -1)
    gate_probs = jax.nn.softmax(chosen, -1)
    onehot = jnp.sum(pick_table, 1)
    before = jnp.cumsum(onehot, 0) - onehot
    slot_rank = jnp.sum(pick_table * before[:, None, :], -1)
    kept_mask = slot_rank < CAP
    kept_float = kept_mask.astype(jnp.float32)
    slots_all = experts_all * CAP
    slot_index = jnp.where(kept_mask, own_routes * CAP + slot_rank, slots_all).reshape(-1)
    safe_index = jnp.minimum(slot_index, slots_all - 1)
    weights_kept = gate_probs * kept_float
    copies = jnp.broadcast_to(normed_two_b[:, None, :], (rows_dev, top_count, model_width)).reshape(
        -1, model_width
    )
    outgoing = (
        jnp.zeros((slots_all, model_width), jnp.bfloat16).at[slot_index].set(copies, mode="drop")
    )
    arrived = lax.all_to_all(
        outgoing.reshape(experts_all, CAP, model_width),
        "ep",
        split_axis=0,
        concat_axis=1,
        tiled=True,
    )
    hidden_units = w_down.shape[1]
    gate_up_out = jnp.einsum("erd,edf->erf", arrived, w_gate_up, preferred_element_type=jnp.float32)
    gate_part = gate_up_out[..., :hidden_units]
    up_part = gate_up_out[..., hidden_units:]
    sigmoid_gate = jax.nn.sigmoid(gate_part)
    active = (gate_part * sigmoid_gate * up_part).astype(jnp.bfloat16)
    produced = jnp.einsum(
        "erf,efd->erd", active, w_down, preferred_element_type=jnp.float32
    ).astype(jnp.bfloat16)
    returned = lax.all_to_all(produced, "ep", split_axis=1, concat_axis=0, tiled=True).reshape(
        slots_all, model_width
    )
    picked = returned[safe_index].reshape(rows_dev, top_count, model_width).astype(jnp.float32)
    output = hidden + branch_scale * jnp.sum(weights_kept[..., None] * picked, 1)
    grad_mix = branch_scale * grad_output
    grad_gate_probs = jnp.sum(grad_mix[:, None, :] * picked, -1) * kept_float
    sending = (
        (weights_kept[..., None] * grad_mix[:, None, :])
        .astype(jnp.bfloat16)
        .reshape(-1, model_width)
    )
    grad_outgoing = (
        jnp.zeros((slots_all, model_width), jnp.bfloat16).at[slot_index].set(sending, mode="drop")
    )
    grad_arrived = lax.all_to_all(
        grad_outgoing.reshape(experts_all, CAP, model_width),
        "ep",
        split_axis=0,
        concat_axis=1,
        tiled=True,
    )
    grad_active = jnp.einsum(
        "erd,efd->erf", grad_arrived, w_down, preferred_element_type=jnp.float32
    )
    grad_down = jnp.einsum("erf,erd->efd", active, grad_arrived, preferred_element_type=jnp.float32)
    grad_gate = grad_active * up_part * sigmoid_gate * (1.0 + gate_part * (1.0 - sigmoid_gate))
    grad_up = grad_active * gate_part * sigmoid_gate
    grad_both = jnp.concatenate([grad_gate, grad_up], -1).astype(jnp.bfloat16)
    grad_gate_up = jnp.einsum(
        "erd,erf->edf", arrived, grad_both, preferred_element_type=jnp.float32
    )
    grad_expert_in = jnp.einsum(
        "erf,edf->erd", grad_both, w_gate_up, preferred_element_type=jnp.float32
    ).astype(jnp.bfloat16)
    grad_back = lax.all_to_all(
        grad_expert_in, "ep", split_axis=1, concat_axis=0, tiled=True
    ).reshape(slots_all, model_width)
    grad_picked = (
        grad_back[safe_index].reshape(rows_dev, top_count, model_width).astype(jnp.float32)
    )
    grad_normed_two = jnp.sum(grad_picked * kept_float[..., None], 1)
    grad_chosen = gate_probs * (
        grad_gate_probs - jnp.sum(grad_gate_probs * gate_probs, -1, keepdims=True)
    )
    grad_logits = jnp.sum(pick_float * grad_chosen[..., None], 1)
    grad_router = jnp.dot(normed_two_f.T, grad_logits, precision=lax.Precision.HIGHEST)
    grad_normed_two = grad_normed_two + jnp.dot(
        grad_logits, router_f.T, precision=lax.Precision.HIGHEST
    )
    grad_hidden_norm, grad_mlp_gain = norm_back(grad_normed_two, hidden, factor_two, mlp_gain)
    grad_hidden = grad_output + grad_hidden_norm
    grad_attn = (branch_scale * grad_hidden).astype(jnp.bfloat16)
    grad_out_w = jnp.einsum("tf,td->fd", mixed_rows, grad_attn, preferred_element_type=jnp.float32)
    grad_mixed = jnp.einsum(
        "td,fd->tf", grad_attn, full_out, preferred_element_type=jnp.float32
    ).astype(jnp.bfloat16)
    back_keys, back_values = (pack_keys, pack_values)

    def score_grads(query_part, key_part, value_part, grad_part, log_total):
        scores = product(query_part, key_part.T) * score_scale
        scores = jnp.where(allowed_rows, scores, far_below)
        prob_rows = jnp.exp(scores - log_total[:, None])
        grad_weights = product(grad_part, value_part.T)
        inner_sum = jnp.sum(prob_rows * grad_weights, -1, keepdims=True)
        grad_scores = (prob_rows * (grad_weights - inner_sum) * score_scale).astype(jnp.bfloat16)
        return (prob_rows, inner_sum, grad_scores)

    def head_query_side(operands):
        query_part, key_part, value_part, grad_part, log_total = operands
        prob_rows, inner_sum, grad_scores = score_grads(
            query_part, key_part, value_part, grad_part, log_total
        )
        return (product(grad_scores, key_part), inner_sum[:, 0])

    grad_mixed_heads = by_head(grad_mixed)
    head_inputs = (
        query_heads,
        key_heads(back_keys),
        key_heads(back_values),
        grad_mixed_heads,
        log_totals,
    )
    grad_query_heads, inner_sums = lax.map(head_query_side, head_inputs)
    pack_logs, pack_inner = (
        lax.all_gather(stats_rows(log_totals, rows_dev), "rep", axis=0, tiled=True),
        lax.all_gather(stats_rows(inner_sums, rows_dev), "rep", axis=0, tiled=True),
    )
    own_key_heads = key_heads(key_rows)
    own_value_heads = key_heads(value_rows)
    empty_heads = jnp.zeros((KV_HEADS, rows_dev, HEAD_DIM), jnp.float32)
    query_piece = lax.all_gather(query_rows, "rep", axis=0, tiled=True)
    grad_piece = lax.all_gather(grad_mixed, "rep", axis=0, tiled=True)
    count = query_piece.shape[0]
    block = 512
    steps_count = count // block

    def one_block(inner_carry, index):
        local_start = index * block
        query_block = by_head(lax.dynamic_slice_in_dim(query_piece, local_start, block, 0))
        grad_block = by_head(lax.dynamic_slice_in_dim(grad_piece, local_start, block, 0))
        log_block = stats_heads(lax.dynamic_slice_in_dim(pack_logs, local_start, block, 0))
        inner_block = stats_heads(lax.dynamic_slice_in_dim(pack_inner, local_start, block, 0))
        id_block = lax.dynamic_slice_in_dim(pack_ids, local_start, block, 0)
        query_place = local_start + jnp.arange(block, dtype=jnp.int32)
        mask_block = (id_block[:, None] == own_ids[None, :]) & (
            query_at[None, :] <= query_place[:, None]
        )
        mask_block = jnp.tile(mask_block, (group_size, 1))
        scores = (
            jnp.einsum(
                "kqd,kud->kqu", query_block, own_key_heads, preferred_element_type=jnp.float32
            )
            * score_scale
        )
        scores = jnp.where(mask_block[None], scores, far_below)
        prob_rows = jnp.exp(scores - log_block[..., None])
        grad_weights = jnp.einsum(
            "kqd,kud->kqu", grad_block, own_value_heads, preferred_element_type=jnp.float32
        )
        grad_scores = (prob_rows * (grad_weights - inner_block[..., None]) * score_scale).astype(
            jnp.bfloat16
        )
        key_sum = inner_carry[0] + jnp.einsum(
            "kqu,kqd->kud", grad_scores, query_block, preferred_element_type=jnp.float32
        )
        value_sum = inner_carry[1] + jnp.einsum(
            "kqu,kqd->kud",
            prob_rows.astype(jnp.bfloat16),
            grad_block,
            preferred_element_type=jnp.float32,
        )
        return ((key_sum, value_sum), None)

    result, unused = lax.scan(
        one_block, (empty_heads, empty_heads), jnp.arange(steps_count, dtype=jnp.int32)
    )
    key_sum, value_sum = result
    own_grad_key = key_rows_of(key_sum)
    own_grad_value = key_rows_of(value_sum)
    grad_query_rows = unrotate(
        from_head(grad_query_heads, rows_dev).reshape(rows_dev, HEADS, HEAD_DIM), cosine, sine_table
    )
    grad_query_rows = grad_query_rows.reshape(rows_dev, HEADS * HEAD_DIM).astype(jnp.bfloat16)
    grad_key_rows = unrotate(own_grad_key.reshape(rows_dev, KV_HEADS, HEAD_DIM), cosine, sine_table)
    grad_key_rows = grad_key_rows.reshape(rows_dev, KV_HEADS * HEAD_DIM).astype(jnp.bfloat16)
    grad_value_rows = own_grad_value.astype(jnp.bfloat16)
    grad_wq = jnp.einsum("td,tf->df", normed_b, grad_query_rows, preferred_element_type=jnp.float32)
    grad_wk = jnp.einsum("td,tf->df", normed_b, grad_key_rows, preferred_element_type=jnp.float32)
    grad_wv = jnp.einsum("td,tf->df", normed_b, grad_value_rows, preferred_element_type=jnp.float32)
    grad_normed = jnp.einsum(
        "tf,df->td", grad_query_rows, full_query, preferred_element_type=jnp.float32
    )
    grad_normed = grad_normed + jnp.einsum(
        "tf,df->td", grad_key_rows, full_key, preferred_element_type=jnp.float32
    )
    grad_normed = grad_normed + jnp.einsum(
        "tf,df->td", grad_value_rows, full_value, preferred_element_type=jnp.float32
    )
    grad_inputs_norm, grad_attn_gain = norm_back(grad_normed, inputs, factor_one, attn_gain)
    grad_inputs = grad_hidden + grad_inputs_norm
    summed = (
        lax.psum_scatter(grad_wq, ("ep", "rep"), scatter_dimension=0, tiled=True),
        lax.psum_scatter(grad_wk, ("ep", "rep"), scatter_dimension=0, tiled=True),
        lax.psum_scatter(grad_wv, ("ep", "rep"), scatter_dimension=0, tiled=True),
        lax.psum_scatter(grad_out_w, ("ep", "rep"), scatter_dimension=0, tiled=True),
        lax.psum_scatter(grad_router, ("ep", "rep"), scatter_dimension=0, tiled=True),
        lax.psum_scatter(grad_attn_gain, ("ep", "rep"), scatter_dimension=0, tiled=True),
        lax.psum_scatter(grad_mlp_gain, ("ep", "rep"), scatter_dimension=0, tiled=True),
    )
    expert_up, expert_down = (
        lax.psum_scatter(grad_gate_up, "rep", scatter_dimension=1, tiled=True),
        lax.psum_scatter(grad_down, "rep", scatter_dimension=2, tiled=True),
    )
    return (
        output[None],
        grad_inputs[None],
        summed[5],
        summed[0],
        summed[1],
        summed[2],
        summed[3],
        summed[6],
        summed[4],
        expert_up,
        expert_down,
    )


def solution(mesh):
    placed = (
        P("ep", "rep", None),
        P("ep", "rep"),
        P("ep", "rep", None),
        P(),
        P(("ep", "rep"), None),
        P(("ep", "rep"), None),
        P(("ep", "rep"), None),
        P(("ep", "rep"), None),
        P(),
        P(("ep", "rep"), None),
        P("ep", None, None),
        P("ep", None, None),
        P("ep", "rep", None),
    )
    return jax.shard_map(
        on_device,
        mesh=mesh,
        in_specs=placed,
        out_specs=(
            P("ep", "rep", None),
            P("ep", "rep", None),
            P(("ep", "rep")),
            P(("ep", "rep"), None),
            P(("ep", "rep"), None),
            P(("ep", "rep"), None),
            P(("ep", "rep"), None),
            P(("ep", "rep")),
            P(("ep", "rep"), None),
            P("ep", "rep", None),
            P("ep", None, "rep"),
        ),
        check_vma=False,
    )
```

profile of v0, /device:TPU:26, one launch (start us, length us, event | category | flops | bytes accessed | tf_op | source)
XLA Modules:
  0.0 2354.5 jit_solution(6181888090366712159)
XLA Ops:
  9.4 16.3 all-gather
  30.4 34.1 %all-gather.12.cloned.1.call-done = bf16[1024,512]{1,0:T(8,128)(2,1)} async-done(((bf16[32,512]{1,0:T(8,128)(2,1)}), bf16[1024,512]{1,0:T(8,128)(2,1)}) %all-gather.12.cloned.1.call-update) | async-done | bytes 1048592 | tf_op jit(solution)/shard_map/all_gather | solution.py:138
  68.1 52.3 %all-gather.16.cloned.1.call-done = bf16[1024,512]{1,0:T(8,128)(2,1)} async-done(((bf16[32,512]{1,0:T(8,128)(2,1)}), bf16[1024,512]{1,0:T(8,128)(2,1)}) %all-gather.16.cloned.1.call-update) | async-done | bytes 1048592 | tf_op jit(solution)/shard_map/all_gather | solution.py:139
  127.4 51.4 %all-gather.10.cloned.1.call-done = bf16[1024,1024]{1,0:T(8,128)(2,1)} async-done(((bf16[32,1024]{1,0:T(8,128)(2,1)}), bf16[1024,1024]{1,0:T(8,128)(2,1)}) %all-gather.10.cloned.1.call-update) | async-done | bytes 2097168 | tf_op jit(solution)/shard_map/all_gather | solution.py:137
  186.6 43.2 %all-gather.14.cloned.1.call-done = bf16[2048,512]{0,1:T(8,128)(2,1)} async-done(((bf16[256,512]{0,1:T(8,128)(2,1)}), bf16[2048,512]{0,1:T(8,128)(2,1)}) %all-gather.14.cloned.1.call-update) | async-done | bytes 2097168 | tf_op jit(solution)/shard_map/all_gather | solution.py:155
  234.6 44.9 %all-gather.18.cloned.1.call-done = bf16[2048,512]{1,0:T(8,128)(2,1)} async-done(((bf16[256,512]{1,0:T(8,128)(2,1)}), bf16[2048,512]{1,0:T(8,128)(2,1)}) %all-gather.18.cloned.1.call-update) | async-done | bytes 2097168 | tf_op jit(solution)/shard_map/all_gather | solution.py:156
  288.2 52.5 %while.42 = (s32[]{:T(128)}, bf16[8,512,64]{1,2,0:T(8,128)(2,1)S(1)}, f32[8,512]{1,0:T(8,128)S(1)}, bf16[8,512,64]{2,1,0:T(8,128)(2,1)S(1)}, bf16[8,2048,64]{2,1...) while((s32[]{:T(128)}, ...), condition=%wide.region_5.6_spmd.clone.clone, body=%wide.region_2.5_spmd.clone.sunk.clone | while | flops 281017856 | bytes 19683416 | solution.py:170
  346.7 13.3 scatter_custom_fusion
  365.8 60.4 %all_gather.43 = bf16[1024,32]{1,0:T(8,128)(2,1)S(1)} all-gather(bf16[32,32]{1,0:T(8,128)(2,1)S(1)} %copy-done.67), channel_id=1, replica_groups=mesh['ep'=4,'rep'=8] {'ep','rep'}, dimensions={0}, use_global_device_ids=true | all-gather | bytes 67584 | tf_op jit(solution)/shard_map/all_gather | solution.py:141
  428.2 13.8 scatter_custom_fusion.1
  454.8 51.6 %all-to-all-done.2 = bf16[32,80,1024]{2,1,0:T(8,128)(2,1)} async-done(((bf16[32,80,1024]{2,1,0:T(8,128)(2,1)}), bf16[32,80,1024]{2,1,0:T(8,128)(2,1)}, u32[]{:S(2)}, u32[]{:S(2)}) %all-to-all-start.2) | async-done | bytes 5242912 | tf_op jit(solution)/shard_map/all_to_all | solution.py:232
  512.3 14.1 fusion.109
  526.3 12.2 multiply_convert_fusion.11
  538.5 12.8 fusion.64
  580.3 44.2 %all-to-all-done.3 = bf16[8,320,1024]{2,0,1:T(8,128)(2,1)} async-done(((bf16[8,320,1024]{2,0,1:T(8,128)(2,1)}), bf16[8,320,1024]{2,0,1:T(8,128)(2,1)}, u32[]{:S(2)}, u32[]{:S(2)}) %all-to-all-start.3) | async-done | bytes 5242912 | tf_op jit(solution)/shard_map/all_to_all | solution.py:252
  639.3 49.7 %all-to-all-done.1 = bf16[8,320,1024]{2,0,1:T(8,128)(2,1)} async-done(((bf16[8,320,1024]{2,0,1:T(8,128)(2,1)}), bf16[8,320,1024]{2,0,1:T(8,128)(2,1)}, u32[]{:S(2)}, u32[]{:S(2)}) %all-to-all-start.1) | async-done | bytes 5242912 | tf_op jit(solution)/shard_map/all_to_all | solution.py:217
  696.7 14.4 gather_fusion.1
  711.1 14.3 gather_fusion
  743.1 59.0 %while.43 = (s32[]{:T(128)}, f32[8,512,64]{1,2,0:T(8,128)}, f32[8,512]{1,0:T(8,128)S(1)}, bf16[8,512,64]{2,1,0:T(8,128)(2,1)}, bf16[8,2048,64]{2,1,0:T(8,128)(2,...) while((s32[]{:T(128)}, f32[8,512,64]{1,2,0:T(8,128)}, ...), condition=%wide.region_24.25_spmd.clone.clone, body=%wide.region_22.24_spmd.clone.sunk.clone | while | flops 412089856 | bytes 23479404 | solution.py:300
  809.3 38.0 %all_gather.45 = f32[2048,16]{0,1:T(8,128)} all-gather(f32[256,16]{0,1:T(8,128)S(1)} %reshape.670), channel_id=1, replica_groups=mesh['ep'=4,'rep'=8] {'rep'}, dimensions={0}, use_global_device_ids=true | all-gather | bytes 147456 | tf_op jit(solution)/shard_map/all_gather | solution.py:302
  847.3 32.6 %all_gather.47 = f32[2048,16]{0,1:T(8,128)} all-gather(f32[256,16]{0,1:T(8,128)S(1)} %reshape.673), channel_id=1, replica_groups=mesh['ep'=4,'rep'=8] {'rep'}, dimensions={0}, use_global_device_ids=true | all-gather | bytes 147456 | tf_op jit(solution)/shard_map/all_gather | solution.py:303
  882.9 104.6 %while.44 = (s32[]{:T(128)}, f32[8,256,64]{1,2,0:T(8,128)}, f32[8,256,64]{1,2,0:T(8,128)}, s32[4]{0:T(128)S(1)}, s32[2048]{0:T(1024)}, /*index=5*/s32[1,256]{1,0...) while((s32[]{:T(128)}, f32[8,256,64]{1,2,0:T(8,128)}, ...), condition=%wide.region_26.27_spmd.clone.clone, body=%wide.region_25.26_spmd.clone.sunk.clone | while | flops 1097728768 | bytes 49263932 | solution.py:351
  973.2 8.2 fusion.211
  995.5 10.7 fusion.112
  1007.9 18.1 fusion.62
  1031.9 42.2 %all-reduce.2 = (f32[1024]{0:T(1024)S(1)}, f32[1024]{0:T(1024)S(1)}) all-reduce(f32[1024]{0:T(1024)S(1)} %get-tuple-element.403, f32[1024]{0:T(1024)S(1)} %copy-done.62), channel_id=3, replica_groups=mesh['ep'=4,'rep'=8] {'ep','rep'}, use_global_device_ids=true, to_apply=%region_29.30.clone | all-reduce | flops 2048 | bytes 16384
  1076.5 16.5 reduce-scatter.8.cloned.1.call-done
  1093.0 147.2 %reduce-scatter.14.cloned.1.call-done = f32[32,1024]{1,0:T(8,128)} async-done(((f32[1024,1024]{1,0:T(8,128)}), f32[32,1024]{1,0:T(8,128)}) %reduce-scatter.14.cloned.1.call-update) | async-done | bytes 131088 | tf_op jit(solution)/shard_map/reduce_scatter | solution.py:382
  1240.2 138.2 %reduce-scatter.10.cloned.1.call-done = f32[32,512]{1,0:T(8,128)} async-done(((f32[1024,512]{1,0:T(8,128)}), f32[32,512]{1,0:T(8,128)}) %reduce-scatter.10.cloned.1.call-update) | async-done | bytes 65552 | tf_op jit(solution)/shard_map/reduce_scatter | solution.py:380
  1378.5 139.6 %reduce-scatter.12.cloned.1.call-done = f32[32,512]{1,0:T(8,128)} async-done(((f32[1024,512]{1,0:T(8,128)}), f32[32,512]{1,0:T(8,128)}) %reduce-scatter.12.cloned.1.call-update) | async-done | bytes 65552 | tf_op jit(solution)/shard_map/reduce_scatter | solution.py:381
  1518.1 287.9 %reduce-scatter.20.cloned.1.call-done = f32[8,512,128]{2,1,0:T(8,128)} async-done(((f32[8,512,1024]{2,1,0:T(8,128)}), f32[8,512,128]{2,1,0:T(8,128)}) %reduce-scatter.20.cloned.1.call-update) | async-done | bytes 2097168 | tf_op jit(solution)/shard_map/reduce_scatter | solution.py:389
  1806.0 541.8 %reduce-scatter.18.cloned.1.call-done = f32[8,128,1024]{2,1,0:T(8,128)} async-done(((f32[8,1024,1024]{2,1,0:T(8,128)}), f32[8,128,1024]{2,1,0:T(8,128)}) %reduce-scatter.18.cloned.1.call-update) | async-done | bytes 4194320 | tf_op jit(solution)/shard_map/reduce_scatter | solution.py:388
  (466 shorter events, 371.1 us)
Async XLA Ops:
  7.2 57.4 %all-gather.12.cloned.1.call-start = ((), (), s32[]{:S(2)}) async-start(), calls=%async_computation.12 | async-start | bytes 1081344 | tf_op jit(solution)/shard_map/all_gather | solution.py:138
  7.9 112.5 %all-gather.16.cloned.1.call-start = ((), (), s32[]{:S(2)}) async-start(), calls=%async_computation.14 | async-start | bytes 1081344 | tf_op jit(solution)/shard_map/all_gather | solution.py:139
  8.7 170.2 %all-gather.10.cloned.1.call-start = ((), (), s32[]{:S(2)}) async-start(), calls=%async_computation.11 | async-start | bytes 2162688 | tf_op jit(solution)/shard_map/all_gather | solution.py:137
  9.4 220.4 %all-gather.14.cloned.1.call-start = ((), (), s32[]{:S(2)}) async-start(), calls=%async_computation.13 | async-start | bytes 2359296 | tf_op jit(solution)/shard_map/all_gather | solution.py:155
  25.7 98.6 %copy-start.45 = (s32[1,2048]{1,0:T(1,128)}, s32[1,2048]{1,0:T(1,128)S(1)}, u32[]{:S(2)}) copy-start(s32[1,2048]{1,0:T(1,128)S(1)} %all-gather) | copy-start | bytes 24580
  28.7 91.7 %copy-start.60 = (f32[256]{0:T(256)}, f32[256]{0:T(256)S(1)}, u32[]{:S(2)}) copy-start(f32[256]{0:T(256)S(1)} %get-tuple-element.491) | copy-start | bytes 3076
  28.9 156.2 %copy-start.38 = (f32[256,32]{0,1:T(8,128)}, f32[256,32]{0,1:T(8,128)S(1)}, u32[]{:S(2)}) copy-start(f32[256,32]{0,1:T(8,128)S(1)} %get-tuple-element.488) | copy-start | bytes 98308
  28.9 156.2 %copy-start.40 = (f32[256,32]{0,1:T(8,128)}, f32[256,32]{0,1:T(8,128)S(1)}, u32[]{:S(2)}) copy-start(f32[256,32]{0,1:T(8,128)S(1)} %get-tuple-element.489) | copy-start | bytes 98308
  28.9 91.5 %copy-start = (f32[1,256,1024]{2,1,0:T(8,128)S(1)}, f32[1,256,1024]{2,1,0:T(8,128)}, u32[]{:S(2)}) copy-start(f32[1,256,1024]{2,1,0:T(8,128)} %param.19) | copy-start | bytes 3145732
  28.9 91.5 %copy-start.50 = (f32[1024]{0:T(1024)S(1)}, f32[1024]{0:T(1024)}, u32[]{:S(2)}) copy-start(f32[1024]{0:T(1024)} %param.22) | copy-start | bytes 12292
  30.4 152.3 %copy-start.5 = (bf16[1,256,1024]{2,1,0:T(8,128)(2,1)}, bf16[1,256,1024]{2,1,0:T(8,128)(2,1)S(1)}, u32[]{:S(2)}) copy-start(bf16[1,256,1024]{2,1,0:T(8,128)(2,1)S(1)} %multiply_convert_fusion.15) | copy-start | bytes 1572868
  68.1 211.5 %all-gather.18.cloned.1.call-start = ((), (), s32[]{:S(2)}) async-start(), calls=%async_computation.15 | async-start | bytes 2359296 | tf_op jit(solution)/shard_map/all_gather | solution.py:156
  122.9 220.1 %all-gather.20.cloned.1.call-start = ((), (), s32[]{:S(2)}) async-start(), calls=%async_computation.16 | async-start | bytes 2162688 | tf_op jit(solution)/shard_map/all_gather | solution.py:140
  127.4 219.3 %copy-start.68 = (s32[2048,1]{0,1:T(1,128)}, s32[2048,1]{0,1:T(1,128)S(1)}, u32[]{:S(2)}) copy-start(s32[2048,1]{0,1:T(1,128)S(1)} %compare_select_fusion.1) | copy-start | bytes 24580
  346.7 80.2 %copy-start.16 = (bf16[256,1024]{1,0:T(8,128)(2,1)}, bf16[256,1024]{1,0:T(8,128)(2,1)S(1)}, u32[]{:S(2)}) copy-start(bf16[256,1024]{1,0:T(8,128)(2,1)S(1)} %multiply_convert_fusion.14) | copy-start | bytes 1572868
  360.0 66.7 %copy-start.25 = (f32[1,256,1024]{2,1,0:T(8,128)S(1)}, f32[1,256,1024]{2,1,0:T(8,128)}, u32[]{:S(2)}) copy-start(f32[1,256,1024]{2,1,0:T(8,128)} %param.31) | copy-start | bytes 3145732
  360.0 82.0 %all-to-all-start = ((bf16[32,80,1024]{2,1,0:T(8,128)(2,1)}), bf16[32,80,1024]{2,1,0:T(8,128)(2,1)}, u32[]{:S(2)}, u32[]{:S(2)}) async-start(bf16[32,80,1024]{2,1,0:T(8,128)(2,1)} %bitcast.387), calls=%async_computation | async-start | bytes 10485760 | tf_op jit(solution)/shard_map/all_to_all | solution.py:201
  442.0 64.4 %all-to-all-start.2 = ((bf16[32,80,1024]{2,1,0:T(8,128)(2,1)}), bf16[32,80,1024]{2,1,0:T(8,128)(2,1)}, u32[]{:S(2)}, u32[]{:S(2)}) async-start(bf16[32,80,1024]{2,1,0:T(8,128)(2,1)} %bitcast.388), calls=%async_computation.2 | async-start | bytes 10485760 | tf_op jit(solution)/shard_map/all_to_all | solution.py:232
  559.1 65.4 %all-to-all-start.3 = ((bf16[8,320,1024]{2,0,1:T(8,128)(2,1)}), bf16[8,320,1024]{2,0,1:T(8,128)(2,1)}, u32[]{:S(2)}, u32[]{:S(2)}) async-start(bf16[8,320,1024]{2,0,1:T(8,128)(2,1)} %copy.176), calls=%async_computation.3 | async-start | bytes 10485760 | tf_op jit(solution)/shard_map/all_to_all | solution.py:252
  566.6 316.2 %all-gather.22.cloned.1.call-start = ((), (), s32[]{:S(2)}) async-start(), calls=%async_computation.17 | async-start | bytes 4718592 | tf_op jit(solution)/shard_map/all_gather | solution.py:308
  624.5 64.5 %all-to-all-start.1 = ((bf16[8,320,1024]{2,0,1:T(8,128)(2,1)}), bf16[8,320,1024]{2,0,1:T(8,128)(2,1)}, u32[]{:S(2)}, u32[]{:S(2)}) async-start(bf16[8,320,1024]{2,0,1:T(8,128)(2,1)} %copy.172), calls=%async_computation.1 | async-start | bytes 10485760 | tf_op jit(solution)/shard_map/all_to_all | solution.py:217
  631.1 251.7 %all-gather.24.cloned.1.call-start = ((), (), s32[]{:S(2)}) async-start(), calls=%async_computation.18 | async-start | bytes 4718592 | tf_op jit(solution)/shard_map/all_gather | solution.py:309
  739.6 140.3 %copy-start.10 = (f32[256,1024]{1,0:T(8,128)}, f32[256,1024]{1,0:T(8,128)S(1)}, u32[]{:S(2)}) copy-start(f32[256,1024]{1,0:T(8,128)S(1)} %get-tuple-element.482) | copy-start | bytes 3145732
  741.3 335.2 %reduce-scatter.16.cloned.1.call-start = ((), (), s32[]{:S(2)}) async-start(), calls=%async_computation.23 | async-start | bytes 540672 | tf_op jit(solution)/shard_map/reduce_scatter | solution.py:383
  743.1 60.5 %copy-start.39 = (f32[256,32]{0,1:T(8,128)S(1)}, f32[256,32]{0,1:T(8,128)}, u32[]{:S(2)}) copy-start(f32[256,32]{0,1:T(8,128)} %copy-done.38) | copy-start | bytes 98308
  805.4 287.6 %reduce-scatter.8.cloned.1.call-start = ((), (), s32[]{:S(2)}) async-start(), calls=%async_computation.19 | async-start | bytes 4325376 | tf_op jit(solution)/shard_map/reduce_scatter | solution.py:379
  805.5 74.4 %copy-start.22 = (bf16[256,8,2,64]{0,3,2,1:T(8,128)(2,1)S(1)}, bf16[256,8,2,64]{0,3,2,1:T(8,128)(2,1)}, u32[]{:S(2)}) copy-start(bf16[256,8,2,64]{0,3,2,1:T(8,128)(2,1)} %copy-done.21) | copy-start | bytes 1572868
  808.3 431.9 %reduce-scatter.14.cloned.1.call-start = ((), (), s32[]{:S(2)}) async-start(), calls=%async_computation.22 | async-start | bytes 4325376 | tf_op jit(solution)/shard_map/reduce_scatter | solution.py:382
  882.8 495.7 %reduce-scatter.10.cloned.1.call-start = ((), (), s32[]{:S(2)}) async-start(), calls=%async_computation.20 | async-start | bytes 2162688 | tf_op jit(solution)/shard_map/reduce_scatter | solution.py:380
  992.3 525.8 %reduce-scatter.12.cloned.1.call-start = ((), (), s32[]{:S(2)}) async-start(), calls=%async_computation.21 | async-start | bytes 2162688 | tf_op jit(solution)/shard_map/reduce_scatter | solution.py:381
  995.4 810.6 %reduce-scatter.20.cloned.1.call-start = ((), (), s32[]{:S(2)}) async-start(), calls=%async_computation.25 | async-start | bytes 18874368 | tf_op jit(solution)/shard_map/reduce_scatter | solution.py:389
  1006.2 1341.6 %reduce-scatter.18.cloned.1.call-start = ((), (), s32[]{:S(2)}) async-start(), calls=%async_computation.24 | async-start | bytes 37748736 | tf_op jit(solution)/shard_map/reduce_scatter | solution.py:388
  (67 other events, 689.1 us)
Sparse Core Ops, SparseCore 0:
  11.1 53.4 all-gather.11
  67.7 52.7 all-gather.15
  123.4 55.3 all-gather.9
  181.3 48.4 all-gather.13
  231.8 47.6 all-gather.17
  282.3 55.1 all-gather.19
  569.5 78.1 all-gather.21
  741.4 76.7 all-gather.23
  821.0 126.9 reduce-scatter.15
  950.8 142.1 reduce-scatter.7
  1095.9 144.3 reduce-scatter.13
  1242.9 135.4 reduce-scatter.9
  1381.3 136.7 reduce-scatter.11
  1522.3 283.6 reduce-scatter.19
  1810.2 537.5 reduce-scatter.17
where the time goes:
time: 2370 us; the launch traced here: 2350 us
  waiting for transfers between devices  1650 us (70%)
  matrix products  263 us (11%)
  blocking collectives  189 us (8%)
  local copies, waits for them, and re-layouts  146 us (6%)
  other arithmetic  63.8 us (3%)
  starting transfers between devices  27.7 us (1%)
    reduce_scatter x1, waiting for transfers between devices, on_device(): lax.psum_scatter(grad_gate_up, 'rep', scatter_dimension=1, tiled=True)  542 us
    reduce_scatter x1, waiting for transfers between devices, on_device(): lax.psum_scatter(grad_down, 'rep', scatter_dimension=2, tiled=True)  288 us
    reduce_scatter x1, waiting for transfers between devices, on_device(): lax.psum_scatter(grad_out_w, ('ep', 'rep'), scatter_dimension=0, tiled=True)  147 us
    reduce_scatter x1, waiting for transfers between devices, on_device(): lax.psum_scatter(grad_wv, ('ep', 'rep'), scatter_dimension=0, tiled=True)  140 us
    reduce_scatter x1, waiting for transfers between devices, on_device(): lax.psum_scatter(grad_wk, ('ep', 'rep'), scatter_dimension=0, tiled=True)  138 us
    dot_general x45, matrix products, product(): return jnp.dot(left, right, preferred_element_type=jnp.float32)  97.3 us
    all_gather x1, blocking collectives, on_device(): lax.all_gather(w_router, ('ep', 'rep'), axis=0, tiled=True)  60.4 us
    all_gather x1, waiting for transfers between devices, on_device(): lax.all_gather(w_value, ('ep', 'rep'), axis=0, tiled=True)  52.3 us
  transfers between devices with their start and end apart: 19, of which 14 were waited for; matrix products, arithmetic and copies ran while one was open for 17% of the time, Pallas kernels for 0%

commit v1 on v0

v1 whole, which is shorter than its diff:
```python
import functools
import math

import jax
import jax.numpy as jnp
from jax import lax
from jax.experimental import pallas as pl
from jax.experimental.pallas import tpu as pltpu
from jax.sharding import PartitionSpec as P

HEADS = 16
KV_HEADS = 8
HEAD_DIM = 64
CAP = 80
BLOCK = 256

epsilon = 1e-06
score_scale = 0.015625
branch_scale = 0.22
far_below = -1e30

NT = (((1,), (1,)), ((), ()))
TN = (((0,), (0,)), ((), ()))


def product(left, right):
    return jnp.dot(left, right, preferred_element_type=jnp.float32)


def dot_nt(left, right):
    return lax.dot_general(left, right, NT, preferred_element_type=jnp.float32)


def dot_tn(left, right):
    return lax.dot_general(left, right, TN, preferred_element_type=jnp.float32)


def rms_norm(values, gain):
    factor = lax.rsqrt(jnp.mean(values * values, -1, keepdims=True) + epsilon)
    return (values * factor * gain, factor)


def norm_back(grad_normed, values, factor, gain):
    scaled = grad_normed * gain
    gain_part = jnp.sum(grad_normed * values * factor, 0)
    inner_sum = jnp.mean(scaled * values, -1, keepdims=True)
    return (factor * scaled - values * (factor * factor * factor) * inner_sum, gain_part)


def swap_halves(values):
    count, width = values.shape
    half_dim = HEAD_DIM // 2
    lane = lax.broadcasted_iota(jnp.int32, values.shape, 1)
    return jnp.where(
        lane % HEAD_DIM < half_dim,
        jnp.roll(values, -half_dim, 1),
        jnp.roll(values, half_dim, 1),
    )


def attend_forward_kernel(
    low_ref, rows_ref, start_ref, mixed_ref, out_ref, total_ref, key_s, value_s, *, heads
):
    step = pl.program_id(0)
    width = heads * HEAD_DIM

    @pl.when(step == 0)
    def _():
        key_s[...] = rows_ref[:, width : width + HEAD_DIM]
        value_s[...] = rows_ref[:, width + HEAD_DIM : width + 2 * HEAD_DIM]

    block_rows = rows_ref[pl.ds(pl.multiple_of(step * BLOCK, BLOCK), BLOCK), :]
    queries = [
        block_rows[:, h * HEAD_DIM : (h + 1) * HEAD_DIM] * jnp.bfloat16(score_scale)
        for h in range(heads)
    ]
    starts = start_ref[0]
    at = step * BLOCK + lax.broadcasted_iota(jnp.int32, (1, BLOCK), 1)

    def one(j, carry):
        rows = pl.ds(pl.multiple_of(j * BLOCK, BLOCK), BLOCK)
        key_block = key_s[rows, :]
        value_block = value_s[rows, :]
        place = j * BLOCK + lax.broadcasted_iota(jnp.int32, (BLOCK, BLOCK), 0)
        allowed = (place >= starts) & (place <= at)
        result = []
        for h in range(heads):
            peak, total, mixed = carry[h]
            scores = jnp.where(allowed, dot_nt(key_block, queries[h]), far_below)
            new_peak = jnp.maximum(peak, jnp.max(scores, 0, keepdims=True))
            fade = jnp.exp(peak - new_peak)
            raised = jnp.exp(scores - new_peak)
            total = fade * total + jnp.sum(raised, 0, keepdims=True)
            mixed = fade * mixed + dot_tn(value_block, raised.astype(jnp.bfloat16))
            result.append((new_peak, total, mixed))
        return tuple(result)

    first = tuple(
        (
            jnp.full((1, BLOCK), far_below, jnp.float32),
            jnp.zeros((1, BLOCK), jnp.float32),
            jnp.zeros((HEAD_DIM, BLOCK), jnp.float32),
        )
        for _ in range(heads)
    )
    done = lax.fori_loop(low_ref[step], step + 1, one, first)
    for h in range(heads):
        peak, total, mixed = done[h]
        mixed = mixed / total
        out_ref[h * HEAD_DIM : (h + 1) * HEAD_DIM, :] = mixed
        total_ref[0, h : h + 1, :] = peak + jnp.log(total)
        mixed_ref[:, h * HEAD_DIM : (h + 1) * HEAD_DIM] = mixed.T.astype(jnp.bfloat16)


def attend_forward(rows, starts, lows, heads):
    length, width = rows.shape
    blocks = length // BLOCK
    whole = lambda i, low: (0, 0)
    return pl.pallas_call(
        functools.partial(attend_forward_kernel, heads=heads),
        out_shape=(
            jax.ShapeDtypeStruct((length, heads * HEAD_DIM), jnp.bfloat16),
            jax.ShapeDtypeStruct((heads * HEAD_DIM, length), jnp.float32),
            jax.ShapeDtypeStruct((blocks, heads, BLOCK), jnp.float32),
        ),
        grid_spec=pltpu.PrefetchScalarGridSpec(
            num_scalar_prefetch=1,
            grid=(blocks,),
            in_specs=[
                pl.BlockSpec((length, width), whole),
                pl.BlockSpec((1, 1, BLOCK), lambda i, low: (i, 0, 0)),
            ],
            out_specs=[
                pl.BlockSpec((BLOCK, heads * HEAD_DIM), lambda i, low: (i, 0)),
                pl.BlockSpec((heads * HEAD_DIM, BLOCK), lambda i, low: (0, i)),
                pl.BlockSpec((1, heads, BLOCK), lambda i, low: (i, 0, 0)),
            ],
            scratch_shapes=[
                pltpu.VMEM((length, HEAD_DIM), jnp.bfloat16),
                pltpu.VMEM((length, HEAD_DIM), jnp.bfloat16),
            ],
        ),
        name="attend_forward",
    )(lows, rows, starts)


def attend_backward_kernel(
    low_ref,
    rows_ref,
    grad_ref,
    out_ref,
    total_ref,
    start_ref,
    grad_query_ref,
    grad_key_ref,
    grad_value_ref,
    key_s,
    value_s,
    *,
    heads,
):
    step = pl.program_id(0)
    width = heads * HEAD_DIM

    @pl.when(step == 0)
    def _():
        key_s[...] = rows_ref[:, width : width + HEAD_DIM]
        value_s[...] = rows_ref[:, width + HEAD_DIM : width + 2 * HEAD_DIM]
        grad_key_ref[...] = jnp.zeros_like(grad_key_ref)
        grad_value_ref[...] = jnp.zeros_like(grad_value_ref)

    own = pl.ds(pl.multiple_of(step * BLOCK, BLOCK), BLOCK)
    block_rows = rows_ref[own, :]
    grads_all = grad_ref[...]
    starts = start_ref[0]
    at = step * BLOCK + lax.broadcasted_iota(jnp.int32, (1, BLOCK), 1)
    queries, scaled, grads, inners, totals = [], [], [], [], []
    for h in range(heads):
        span = slice(h * HEAD_DIM, (h + 1) * HEAD_DIM)
        queries.append(block_rows[:, span])
        scaled.append(block_rows[:, span] * jnp.bfloat16(score_scale))
        grads.append(grads_all[:, span])
        turned = grads_all[:, span].astype(jnp.float32).T
        inners.append(jnp.sum(turned * out_ref[span, :], 0, keepdims=True))
        totals.append(total_ref[0, h : h + 1, :])

    def one(j, carry):
        rows = pl.ds(pl.multiple_of(j * BLOCK, BLOCK), BLOCK)
        key_block = key_s[rows, :]
        value_block = value_s[rows, :]
        place = j * BLOCK + lax.broadcasted_iota(jnp.int32, (BLOCK, BLOCK), 0)
        allowed = (place >= starts) & (place <= at)
        result = []
        key_sum = grad_key_ref[rows, :]
        value_sum = grad_value_ref[rows, :]
        for h in range(heads):
            scores = jnp.where(allowed, dot_nt(key_block, scaled[h]), far_below)
            prob = jnp.exp(scores - totals[h])
            grad_prob = dot_nt(value_block, grads[h])
            grad_scores = (prob * (grad_prob - inners[h]) * score_scale).astype(jnp.bfloat16)
            value_sum = value_sum + product(prob.astype(jnp.bfloat16), grads[h])
            key_sum = key_sum + product(grad_scores, queries[h])
            result.append(carry[h] + dot_tn(grad_scores, key_block))
        grad_key_ref[rows, :] = key_sum
        grad_value_ref[rows, :] = value_sum
        return tuple(result)

    first = tuple(jnp.zeros((BLOCK, HEAD_DIM), jnp.float32) for _ in range(heads))
    done = lax.fori_loop(low_ref[step], step + 1, one, first)
    for h in range(heads):
        grad_query_ref[:, h * HEAD_DIM : (h + 1) * HEAD_DIM] = done[h]


def attend_backward(rows, grads, outs, totals, starts, lows, heads):
    length, width = rows.shape
    blocks = length // BLOCK
    whole = lambda i, low: (0, 0)
    return pl.pallas_call(
        functools.partial(attend_backward_kernel, heads=heads),
        out_shape=(
            jax.ShapeDtypeStruct((length, heads * HEAD_DIM), jnp.float32),
            jax.ShapeDtypeStruct((length, HEAD_DIM), jnp.float32),
            jax.ShapeDtypeStruct((length, HEAD_DIM), jnp.float32),
        ),
        grid_spec=pltpu.PrefetchScalarGridSpec(
            num_scalar_prefetch=1,
            grid=(blocks,),
            in_specs=[
                pl.BlockSpec((length, width), whole),
                pl.BlockSpec((BLOCK, heads * HEAD_DIM), lambda i, low: (i, 0)),
                pl.BlockSpec((heads * HEAD_DIM, BLOCK), lambda i, low: (0, i)),
                pl.BlockSpec((1, heads, BLOCK), lambda i, low: (i, 0, 0)),
                pl.BlockSpec((1, 1, BLOCK), lambda i, low: (i, 0, 0)),
            ],
            out_specs=[
                pl.BlockSpec((BLOCK, heads * HEAD_DIM), lambda i, low: (i, 0)),
                pl.BlockSpec((length, HEAD_DIM), whole),
                pl.BlockSpec((length, HEAD_DIM), whole),
            ],
            scratch_shapes=[
                pltpu.VMEM((length, HEAD_DIM), jnp.bfloat16),
                pltpu.VMEM((length, HEAD_DIM), jnp.bfloat16),
            ],
        ),
        name="attend_backward",
    )(lows, rows, grads, outs, totals, starts)


def experts_kernel(
    rows_ref,
    cot_ref,
    rank_ref,
    prob_ref,
    gate_up_ref,
    down_ref,
    out_ref,
    grad_ref,
    inner_ref,
    grad_gate_up_ref,
    grad_down_ref,
    picks_s,
    out_s,
    grad_s,
    *,
    sources,
    rows_dev,
    count,
):
    step = pl.program_id(0)
    slots = pl.ds(pl.multiple_of(step * CAP, 16), CAP)
    numbers = lax.broadcasted_iota(jnp.int32, (CAP, rows_dev), 0).astype(jnp.float32)
    rows_in, cots, weights, picks = [], [], [], []
    for s in range(sources):
        rank = rank_ref[s, pl.ds(step, 1), :]
        pick = jnp.where(rank == numbers, 1.0, 0.0)
        weights.append(jnp.sum(pick * prob_ref[s, pl.ds(step, 1), :], 1, keepdims=True))
        pick_b = pick.astype(jnp.bfloat16)
        picks.append(pick)
        picks_s[s, slots, :] = pick_b
        own = slice(s * rows_dev, (s + 1) * rows_dev)
        rows_in.append(product(pick_b, rows_ref[own, :]).astype(jnp.bfloat16))
        cots.append(product(pick_b, cot_ref[own, :]))
    arrived = jnp.concatenate(rows_in, 0)
    weight = jnp.concatenate(weights, 0)
    grad_mix = branch_scale * jnp.concatenate(cots, 0)
    gate_up = gate_up_ref[0]
    down = down_ref[0]
    hidden_units = down.shape[0]
    both = product(arrived, gate_up)
    gate_part = both[:, :hidden_units]
    up_part = both[:, hidden_units:]
    sigmoid_gate = jax.nn.sigmoid(gate_part)
    active = (gate_part * sigmoid_gate * up_part).astype(jnp.bfloat16)
    produced = product(active, down).astype(jnp.bfloat16).astype(jnp.float32)
    inner = jnp.sum(grad_mix * produced, 1, keepdims=True)
    sent_out = (weight * produced).astype(jnp.bfloat16)
    grad_out = (weight * grad_mix).astype(jnp.bfloat16)
    grad_active = dot_nt(grad_out, down)
    grad_down_ref[0] = dot_tn(active, grad_out).astype(grad_down_ref.dtype)
    grad_gate = grad_active * up_part * sigmoid_gate * (1.0 + gate_part * (1.0 - sigmoid_gate))
    grad_up = grad_active * gate_part * sigmoid_gate
    grad_both = jnp.concatenate([grad_gate, grad_up], 1).astype(jnp.bfloat16)
    grad_gate_up_ref[0] = dot_tn(arrived, grad_both).astype(grad_gate_up_ref.dtype)
    grad_in = dot_nt(grad_both, gate_up).astype(jnp.bfloat16)
    for s in range(sources):
        part = slice(s * CAP, (s + 1) * CAP)
        out_s[s, slots, :] = sent_out[part]
        grad_s[s, slots, :] = grad_in[part]
        inner_ref[s, pl.ds(step, 1), :] = jnp.sum(picks[s] * inner[part], 0, keepdims=True)

    @pl.when(step == count - 1)
    def _():
        for s in range(sources):
            own = slice(s * rows_dev, (s + 1) * rows_dev)
            table = picks_s[s]
            out_ref[own, :] = dot_tn(table, out_s[s]).astype(jnp.bfloat16)
            grad_ref[own, :] = dot_tn(table, grad_s[s]).astype(jnp.bfloat16)


def experts(rows, cots, ranks, probs, w_gate_up, w_down):
    sources, count, rows_dev = ranks.shape
    total, model_width = rows.shape
    hidden_units = w_down.shape[1]
    flat = lambda i: (0, 0)
    cube = lambda i: (0, 0, 0)
    once = pl.Buffered(1)
    return pl.pallas_call(
        functools.partial(experts_kernel, sources=sources, rows_dev=rows_dev, count=count),
        out_shape=(
            jax.ShapeDtypeStruct((total, model_width), jnp.bfloat16),
            jax.ShapeDtypeStruct((total, model_width), jnp.bfloat16),
            jax.ShapeDtypeStruct((sources, count, rows_dev), jnp.float32),
            jax.ShapeDtypeStruct(w_gate_up.shape, jnp.bfloat16),
            jax.ShapeDtypeStruct(w_down.shape, jnp.bfloat16),
        ),
        grid=(count,),
        in_specs=[
            pl.BlockSpec((total, model_width), flat, pipeline_mode=once),
            pl.BlockSpec((total, model_width), flat, pipeline_mode=once),
            pl.BlockSpec((sources, count, rows_dev), cube, pipeline_mode=once),
            pl.BlockSpec((sources, count, rows_dev), cube, pipeline_mode=once),
            pl.BlockSpec((1, model_width, 2 * hidden_units), lambda i: (i, 0, 0)),
            pl.BlockSpec((1, hidden_units, model_width), lambda i: (i, 0, 0)),
        ],
        out_specs=[
            pl.BlockSpec((total, model_width), flat),
            pl.BlockSpec((total, model_width), flat),
            pl.BlockSpec((sources, count, rows_dev), cube),
            pl.BlockSpec((1, model_width, 2 * hidden_units), lambda i: (i, 0, 0)),
            pl.BlockSpec((1, hidden_units, model_width), lambda i: (i, 0, 0)),
        ],
        scratch_shapes=[
            pltpu.VMEM((sources, count * CAP, rows_dev), jnp.bfloat16),
            pltpu.VMEM((sources, count * CAP, model_width), jnp.bfloat16),
            pltpu.VMEM((sources, count * CAP, model_width), jnp.bfloat16),
        ],
        compiler_params=pltpu.CompilerParams(vmem_limit_bytes=64 * 1000 * 1000),
        name="experts",
    )(rows, cots, ranks, probs, w_gate_up, w_down)


def on_device(
    tokens,
    segments,
    routes,
    attn_gain,
    w_query,
    w_key,
    w_value,
    w_out,
    mlp_gain,
    w_router,
    w_gate_up,
    w_down,
    cotangent,
    *,
    n_ep,
    n_rep,
):
    inputs = tokens[0]
    own_routes = routes[0]
    grad_output = cotangent[0]
    rows_dev, model_width = inputs.shape
    everyone = ("ep", "rep")
    heads = HEADS // n_rep
    head_width = heads * HEAD_DIM
    shared = max(1, n_rep // KV_HEADS)
    query_width = w_query.shape[1]
    key_width = w_key.shape[1]
    experts_all = w_router.shape[1]
    half_dim = HEAD_DIM // 2

    pack_ids = lax.all_gather(segments[0], "rep", axis=0, tiled=True)
    length = pack_ids.shape[0]
    blocks = length // BLOCK
    offset = lax.axis_index("rep") * rows_dev
    doc_start = jnp.sum((pack_ids[None, :] < pack_ids[:, None]).astype(jnp.int32), 1)
    position = (jnp.arange(length, dtype=jnp.int32) - doc_start).astype(jnp.float32)
    angles = (
        position[:, None]
        * jnp.exp(jnp.arange(half_dim, dtype=jnp.float32) * (-math.log(10000.0) / half_dim))[
            None, :
        ]
    )
    cosine = jnp.cos(angles)
    sine = jnp.sin(angles)
    cosine = jnp.concatenate([cosine, cosine], 1)
    sine = jnp.concatenate([-sine, sine], 1)
    own_cosine = lax.dynamic_slice_in_dim(cosine, offset, rows_dev, 0)
    own_sine = lax.dynamic_slice_in_dim(sine, offset, rows_dev, 0)
    starts = doc_start.reshape(blocks, 1, BLOCK)
    lows = doc_start[::BLOCK] // BLOCK

    joined = jnp.concatenate([w_query, w_key, w_value, w_out, w_router], 1)
    full = lax.all_gather(joined, everyone, axis=0, tiled=True)
    rotated_width = query_width + key_width
    input_width = rotated_width + key_width
    full_in = full[:, :input_width]
    full_out = full[:, input_width : input_width + model_width]
    full_router = full[:, input_width + model_width :]

    normed, factor_one = rms_norm(inputs, attn_gain)
    normed_b = normed.astype(jnp.bfloat16)
    mixed_in = product(normed_b, full_in)
    turn = mixed_in[:, :rotated_width]
    times = rotated_width // HEAD_DIM
    turned = turn * jnp.tile(own_cosine, (1, times)) + swap_halves(turn) * jnp.tile(
        own_sine, (1, times)
    )
    turned_b = turned.astype(jnp.bfloat16)
    value_b = mixed_in[:, rotated_width:].astype(jnp.bfloat16)
    query_part = turned_b[:, :query_width].reshape(rows_dev, n_rep, head_width)
    key_part = turned_b[:, query_width:].reshape(rows_dev, KV_HEADS, HEAD_DIM)
    value_part = value_b.reshape(rows_dev, KV_HEADS, HEAD_DIM)
    if shared > 1:
        key_part = jnp.repeat(key_part, shared, 1)
        value_part = jnp.repeat(value_part, shared, 1)
    sending = jnp.concatenate([query_part, key_part, value_part], 2).transpose(1, 0, 2)
    head_rows = lax.all_to_all(sending, "rep", split_axis=0, concat_axis=0, tiled=True)
    head_rows = head_rows.reshape(length, head_width + 2 * HEAD_DIM)
    mixed, mixed_out, totals = attend_forward(head_rows, starts, lows, heads)
    mixed_rows = lax.all_to_all(
        mixed.reshape(n_rep, rows_dev, head_width), "rep", split_axis=0, concat_axis=0, tiled=True
    )
    mixed_rows = mixed_rows.transpose(1, 0, 2).reshape(rows_dev, query_width)
    hidden = inputs + branch_scale * product(mixed_rows, full_out)

    normed_two, factor_two = rms_norm(hidden, mlp_gain)
    normed_two_b = normed_two.astype(jnp.bfloat16)
    router_f = full_router.astype(jnp.float32)
    logits = product(normed_two_b, full_router)
    numbers = jnp.arange(experts_all, dtype=jnp.int32)
    onehot = jnp.sum((own_routes[:, :, None] == numbers).astype(jnp.float32), 1)
    chosen = onehot > 0.5
    peak = jnp.max(jnp.where(chosen, logits, far_below), 1, keepdims=True)
    raised = jnp.where(chosen, jnp.exp(jnp.minimum(logits - peak, 0.0)), 0.0)
    probs = raised / jnp.sum(raised, 1, keepdims=True)
    before = (
        lax.broadcasted_iota(jnp.int32, (rows_dev, rows_dev), 0)
        > lax.broadcasted_iota(jnp.int32, (rows_dev, rows_dev), 1)
    ).astype(jnp.bfloat16)
    rank = product(before, onehot.astype(jnp.bfloat16))
    kept = chosen & (rank < CAP)
    rank_sent = jnp.where(kept, rank, -1.0).T
    probs_sent = probs.T
    ranks = lax.all_to_all(
        rank_sent.reshape(n_ep, -1, rows_dev), "ep", split_axis=0, concat_axis=0, tiled=True
    )
    prob_all = lax.all_to_all(
        probs_sent.reshape(n_ep, -1, rows_dev), "ep", split_axis=0, concat_axis=0, tiled=True
    )
    expert_rows = lax.all_gather(normed_two_b, "ep", axis=0, tiled=True)
    expert_cots = lax.all_gather(grad_output.astype(jnp.bfloat16), "ep", axis=0, tiled=True)
    out_sum, grad_sum, inner, grad_gate_up, grad_down = experts(
        expert_rows, expert_cots, ranks, prob_all, w_gate_up, w_down
    )
    expert_up = lax.psum_scatter(grad_gate_up, "rep", scatter_dimension=1, tiled=True)
    expert_down = lax.psum_scatter(grad_down, "rep", scatter_dimension=2, tiled=True)
    out_back = lax.all_to_all(
        out_sum.reshape(n_ep, rows_dev, model_width), "ep", split_axis=0, concat_axis=0, tiled=True
    )
    grad_back = lax.all_to_all(
        grad_sum.reshape(n_ep, rows_dev, model_width), "ep", split_axis=0, concat_axis=0, tiled=True
    )
    inner_back = lax.all_to_all(inner, "ep", split_axis=0, concat_axis=0, tiled=True)
    output = hidden + branch_scale * jnp.sum(out_back.astype(jnp.float32), 0)
    grad_probs = inner_back.reshape(experts_all, rows_dev).T
    grad_logits = probs * (grad_probs - jnp.sum(grad_probs * probs, -1, keepdims=True))
    normed_two_f = normed_two_b.astype(jnp.float32)
    grad_router = jnp.dot(normed_two_f.T, grad_logits, precision=lax.Precision.HIGHEST)
    grad_normed_two = jnp.sum(grad_back.astype(jnp.float32), 0) + jnp.dot(
        grad_logits, router_f.T, precision=lax.Precision.HIGHEST
    )
    grad_hidden_norm, grad_mlp_gain = norm_back(grad_normed_two, hidden, factor_two, mlp_gain)
    grad_hidden = grad_output + grad_hidden_norm
    grad_attn = (branch_scale * grad_hidden).astype(jnp.bfloat16)
    grad_out_w = dot_tn(mixed_rows, grad_attn)
    grad_mixed = dot_nt(grad_attn, full_out).astype(jnp.bfloat16)
    grad_heads = lax.all_to_all(
        grad_mixed.reshape(rows_dev, n_rep, head_width).transpose(1, 0, 2),
        "rep",
        split_axis=0,
        concat_axis=0,
        tiled=True,
    ).reshape(length, head_width)
    grad_query, grad_key, grad_value = attend_backward(
        head_rows, grad_heads, mixed_out, totals, starts, lows, heads
    )
    turn_back = jnp.concatenate([grad_query, grad_key], 1)
    turn_back = turn_back * jnp.tile(cosine, (1, heads + 1)) - swap_halves(turn_back) * jnp.tile(
        sine, (1, heads + 1)
    )
    returning = jnp.concatenate([turn_back, grad_value], 1).astype(jnp.bfloat16)
    returned = lax.all_to_all(
        returning.reshape(n_rep, rows_dev, head_width + 2 * HEAD_DIM),
        "rep",
        split_axis=0,
        concat_axis=0,
        tiled=True,
    ).transpose(1, 0, 2)
    grad_query_rows = returned[:, :, :head_width].reshape(rows_dev, query_width)
    key_back = returned[:, :, head_width : head_width + HEAD_DIM]
    value_back = returned[:, :, head_width + HEAD_DIM :]
    if shared > 1:
        key_back = jnp.sum(
            key_back.reshape(rows_dev, KV_HEADS, shared, HEAD_DIM).astype(jnp.float32), 2
        ).astype(jnp.bfloat16)
        value_back = jnp.sum(
            value_back.reshape(rows_dev, KV_HEADS, shared, HEAD_DIM).astype(jnp.float32), 2
        ).astype(jnp.bfloat16)
    grad_in_rows = jnp.concatenate(
        [
            grad_query_rows,
            key_back.reshape(rows_dev, key_width),
            value_back.reshape(rows_dev, key_width),
        ],
        1,
    )
    grad_w_in = dot_tn(normed_b, grad_in_rows)
    grad_normed = dot_nt(grad_in_rows, full_in)
    grad_inputs_norm, grad_attn_gain = norm_back(grad_normed, inputs, factor_one, attn_gain)
    grad_inputs = grad_hidden + grad_inputs_norm
    weight_grads = jnp.concatenate([grad_w_in, grad_out_w, grad_router], 1).astype(jnp.bfloat16)
    summed = lax.psum_scatter(weight_grads, everyone, scatter_dimension=0, tiled=True)
    summed = summed.astype(jnp.float32)
    gains = lax.psum_scatter(
        jnp.stack([grad_attn_gain, grad_mlp_gain], 1), everyone, scatter_dimension=0, tiled=True
    )
    return (
        output[None],
        grad_inputs[None],
        gains[:, 0],
        summed[:, :query_width],
        summed[:, query_width:rotated_width],
        summed[:, rotated_width:input_width],
        summed[:, input_width : input_width + model_width],
        gains[:, 1],
        summed[:, input_width + model_width :],
        expert_up.astype(jnp.float32),
        expert_down.astype(jnp.float32),
    )


def solution(mesh):
    placed = (
        P("ep", "rep", None),
        P("ep", "rep"),
        P("ep", "rep", None),
        P(),
        P(("ep", "rep"), None),
        P(("ep", "rep"), None),
        P(("ep", "rep"), None),
        P(("ep", "rep"), None),
        P(),
        P(("ep", "rep"), None),
        P("ep", None, None),
        P("ep", None, None),
        P("ep", "rep", None),
    )
    return jax.shard_map(
        functools.partial(on_device, n_ep=mesh.shape["ep"], n_rep=mesh.shape["rep"]),
        mesh=mesh,
        in_specs=placed,
        out_specs=(
            P("ep", "rep", None),
            P("ep", "rep", None),
            P(("ep", "rep")),
            P(("ep", "rep"), None),
            P(("ep", "rep"), None),
            P(("ep", "rep"), None),
            P(("ep", "rep"), None),
            P(("ep", "rep")),
            P(("ep", "rep"), None),
            P("ep", "rep", None),
            P("ep", None, "rep"),
        ),
        check_vma=False,
    )
```

time: 2370 us -> 1170 us (0.49)
  waiting for transfers between devices: 1650 us -> 778 us
  matrix products: 263 us -> 21.7 us
  Pallas kernels: 0 us -> 97.8 us
  blocking collectives: 189 us -> 99.8 us
  local copies, waits for them, and re-layouts: 146 us -> 79.9 us
  other arithmetic: 63.8 us -> 32.5 us
    reduce_scatter x6 -> x1, waiting for transfers between devices: 729 us -> 147 us  [on_device(): lax.psum_scatter(weight_grads, everyone, scatter_dimension=0, tiled=True)]
    reduce_scatter x1, waiting for transfers between devices: 542 us -> 281 us  [on_device(): lax.psum_scatter(grad_gate_up, 'rep', scatter_dimension=1, tiled=True)]
    unnamed x15 -> x9, waiting for transfers between devices: 2.76 us -> 246 us
    all_gather x8 -> x3, waiting for transfers between devices: 226 us -> 48.9 us  [the longest x1 42.2 us: on_device(): full = lax.all_gather(joined, everyone, axis=0, tiled=True)]
    dot_general x26 -> x4, matrix products: 162 us -> 10.2 us  [the longest x2 8.11 us: dot_nt(): return lax.dot_general(left, right, NT, preferred_element_type=jnp.float32)]
    all_gather x4 -> x1, blocking collectives: 147 us -> 16.3 us  [on_device(): pack_ids = lax.all_gather(segments[0], 'rep', axis=0, tiled=True)]
    pallas_call x0 -> x3, Pallas kernels: none -> 97.8 us  [the longest x1 49.4 us: experts(): pl.pallas_call(functools.partial(experts_kernel, sources=sources, rows_de...]
    all_to_all x4 -> x5, waiting for transfers between devices: 145 us -> 53.7 us  [the longest x1 23.3 us: on_device(): lax.all_to_all(sending, 'rep', split_axis=0, concat_axis=0, tiled=True)]
  transfers between devices with their start and end apart: 19 -> 12, of which waited for: 14 -> 11; matrix products, arithmetic and copies ran while one was open for 17% -> 6% of each run, Pallas kernels for 0% -> 2%
where the time goes in v1:
time: 1170 us; the launch traced here: 1150 us
  waiting for transfers between devices  778 us (66%)
  blocking collectives  99.8 us (9%)
  Pallas kernels  97.8 us (8%)
  local copies, waits for them, and re-layouts  79.9 us (7%)
  other arithmetic  32.5 us (3%)
  starting transfers between devices  28 us (2%)
  matrix products  21.7 us (2%)
  between operations  16.3 us (1%)
    reduce_scatter x1, waiting for transfers between devices, on_device(): lax.psum_scatter(grad_gate_up, 'rep', scatter_dimension=1, tiled=True)  281 us
    unnamed x9, waiting for transfers between devices  246 us
    reduce_scatter x1, waiting for transfers between devices, on_device(): lax.psum_scatter(weight_grads, everyone, scatter_dimension=0, tiled=True)  147 us
    pallas_call x1, Pallas kernels, experts(): pl.pallas_call(functools.partial(experts_kernel, sources=sources, rows_de...  49.4 us
    unnamed x96, local copies, waits for them, and re-layouts  43.3 us
    all_gather x1, waiting for transfers between devices, on_device(): full = lax.all_gather(joined, everyone, axis=0, tiled=True)  42.2 us
    all_to_all x1, blocking collectives, on_device(): lax.all_to_all(grad_sum.reshape(n_ep, rows_dev, model_width), 'ep', split...  30.5 us
    all_to_all x1, blocking collectives, on_device(): lax.all_to_all(returning.reshape(n_rep, rows_dev, head_width + 2 * HEAD_D...  29.3 us
  transfers between devices with their start and end apart: 12, of which 11 were waited for; matrix products, arithmetic and copies ran while one was open for 6% of the time, Pallas kernels for 2%

profile of v1, /device:TPU:26, one launch (start us, length us, event | category | flops | bytes accessed | tf_op | source)
XLA Modules:
  0.0 1153.6 jit_solution(9777550264476552825)
XLA Ops:
  12.7 16.3 %all-gather = s32[1,2048]{1,0:T(1,128)S(1)} all-gather(s32[1,256]{1,0:T(1,128)} %param.14), channel_id=2, replica_groups=mesh['ep'=4,'rep'=8] {'rep'}, dimensions={1}, use_global_device_ids=true | all-gather | bytes 9216 | tf_op jit(solution)/shard_map/all_gather | solution.py:393
  36.4 3.0 copy.93
  40.2 42.2 %all-gather.5.cloned.1.call-done = bf16[1024,3104]{1,0:T(8,128)(2,1)} async-done(((bf16[32,3104]{1,0:T(8,128)(2,1)}), bf16[1024,3104]{1,0:T(8,128)(2,1)}) %all-gather.5.cloned.1.call-update) | async-done | bytes 6357008 | tf_op jit(solution)/shard_map/all_gather | solution.py:415
  82.4 3.5 fusion.2
  92.5 5.5 all-to-all-start
  99.5 23.3 %all-to-all-done = bf16[8,256,256]{2,1,0:T(8,128)(2,1)S(1)} async-done(((bf16[8,256,256]{2,1,0:T(8,128)(2,1)}), bf16[8,256,256]{2,1,0:T(8,128)(2,1)S(1)}, u32[]{:S(2)}, u32[]{:S(2)}) %all-to-all-start) | async-done | bytes 1048608 | tf_op jit(solution)/shard_map/all_to_all | solution.py:439
  123.8 21.7 %attend_forward.1 = (bf16[2048,128]{1,0:T(8,128)(2,1)}, f32[128,2048]{1,0:T(8,128)}, f32[8,2,256]{2,1,0:T(2,128)}) custom-call(s32[8]{0:T(128)} %and_select_fusion.low_ref, bf16[2048,256]{1,0:T(8,128)(2,1)} %bitcast.144, s32[8,1,256]{2,1,0:T(1,128)} %bitcast.173), custom_call_target="tpu_custom_call" | custom-call | tf_op jit(solution)/shard_map/attend_forward/pallas_call | solution.py:119
  146.7 17.1 %all_to_all.45 = bf16[8,256,128]{1,2,0:T(8,128)(2,1)S(1)} all-to-all(bf16[8,256,128]{1,2,0:T(8,128)(2,1)S(1)} %copy.99), channel_id=1, replica_groups=mesh['ep'=4,'rep'=8] {'rep'}, dimensions={0} | all-to-all | bytes 1048576 | tf_op jit(solution)/shard_map/all_to_all | solution.py:442
  169.7 4.4 all-to-all-start.2
  176.0 5.4 all-to-all-start.3
  183.8 6.7 all-gather.7.cloned.1.call-done.rows_ref
  190.6 49.4 %experts.1 = (bf16[1024,1024]{1,0:T(8,128)(2,1)}, bf16[1024,1024]{1,0:T(8,128)(2,1)}, f32[4,8,256]{2,1,0:T(8,128)}, bf16[8,1024,1024]{2,1,0:T(8,128)(2,1)}, bf16[8,512,1024]{2,1,0:T(8,128)(2,1)}) custom-call(bf16[1024,1024]{1,0:T(8,128)(2,1)} %all-gather.7.cloned.1.call-done.rows_ref, bf16[1024,1024]{1,0:T(8,128)(2,1)} %all-gather.9.cloned.1.call-done.cot_ref, ...), custom_call_target="tpu_custom_call" | custom-call | tf_op jit(solution)/shard_map/experts/pallas_call | solution.py:327
  240.0 6.6 all_to_all.46
  246.6 30.5 %all_to_all.47 = bf16[4,256,1024]{2,1,0:T(8,128)(2,1)} all-to-all(bf16[4,256,1024]{2,1,0:T(8,128)(2,1)} %bitcast.163), channel_id=1, replica_groups=mesh['ep'=4,'rep'=8] {'ep'}, dimensions={0} | all-to-all | bytes 4194304 | tf_op jit(solution)/shard_map/all_to_all | solution.py:482
  277.1 6.0 all-to-all-start.4
  285.3 2.8 multiply_reduce_fusion
  288.2 19.1 %all-to-all-done.4 = bf16[4,256,1024]{2,1,0:T(8,128)(2,1)} async-done(((bf16[4,256,1024]{2,1,0:T(8,128)(2,1)}), bf16[4,256,1024]{2,1,0:T(8,128)(2,1)}, u32[]{:S(2)}, u32[]{:S(2)}) %all-to-all-start.4) | async-done | bytes 2097184 | tf_op jit(solution)/shard_map/all_to_all | solution.py:479
  315.7 6.0 all-to-all-start.7
  326.0 7.6 all-to-all-done.7
  334.5 26.7 %attend_backward.1 = (f32[2048,128]{1,0:T(8,128)}, f32[2048,64]{1,0:T(8,128)}, f32[2048,64]{1,0:T(8,128)}) custom-call(s32[8]{0:T(128)} %and_select_fusion.low_ref, bf16[2048,256]{1,0:T(8,128)(2,1)} %bitcast.145, bf16[2048,128]{1,0:T(8,128)(2,1)} %bitcast.164, f32[128,2048]{1,0:T(8,128)} %get-tuple-element.26.out_ref, ...), custom_call_target="tpu_custom_call" | custom-call | tf_op jit(solution)/shard_map/attend_backward/pallas_call | solution.py:218
  375.4 2.9 copy.103
  381.7 4.3 fusion.9
  386.4 29.3 %all_to_all.48 = bf16[8,256,256]{1,2,0:T(8,128)(2,1)S(1)} all-to-all(bf16[8,256,256]{1,2,0:T(8,128)(2,1)S(1)} %copy.108), channel_id=1, replica_groups=mesh['ep'=4,'rep'=8] {'rep'}, dimensions={0} | all-to-all | bytes 2097152 | tf_op jit(solution)/shard_map/all_to_all | solution.py:514
  415.8 5.4 fusion.34
  422.6 12.6 %copy.114 = bf16[8,512,1024]{1,0,2:T(8,128)(2,1)} copy(bf16[8,512,1024]{2,1,0:T(8,128)(2,1)} %get-tuple-element.32) | data formatting | bytes 16777216
  435.2 12.3 %copy.122 = bf16[128,8,8,512]{3,1,2,0:T(8,128)(2,1)} copy(bf16[128,8,8,512]{3,2,1,0:T(8,128)(2,1)} %bitcast.141) | data formatting | bytes 16777216
  451.6 3.1 pad_maximum_fusion
  457.3 93.0 %reduce-scatter.13.cloned.1.call-done = f32[32,2]{1,0:T(8,128)} async-done(((f32[1024,2]{1,0:T(8,128)}), f32[32,2]{1,0:T(8,128)}) %reduce-scatter.13.cloned.1.call-update) | async-done | bytes 272
  552.3 152.7 %reduce-scatter.15.cloned.1.call-done = bf16[128,4096]{1,0:T(8,128)(2,1)} async-done(((bf16[1024,4096]{1,0:T(8,128)(2,1)}), bf16[128,4096]{1,0:T(8,128)(2,1)}) %reduce-scatter.15.cloned.1.call-update) | async-done | bytes 1048592
  709.1 147.2 %reduce-scatter.9.cloned.1.call-done = bf16[32,3104]{1,0:T(8,128)(2,1)} async-done(((bf16[1024,3104]{1,0:T(8,128)(2,1)}), bf16[32,3104]{1,0:T(8,128)(2,1)}) %reduce-scatter.9.cloned.1.call-update) | async-done | bytes 198672 | tf_op jit(solution)/shard_map/reduce_scatter | solution.py:544
  860.6 281.4 %reduce-scatter.11.cloned.1.call-done = bf16[8,128,1024]{2,1,0:T(8,128)(2,1)} async-done(((bf16[8,1024,1024]{2,1,0:T(8,128)(2,1)}), bf16[8,128,1024]{2,1,0:T(8,128)(2,1)}) %reduce-scatter.11.cloned.1.call-update) | async-done | bytes 2097168 | tf_op jit(solution)/shard_map/reduce_scatter | solution.py:477
  1142.0 4.1 convert_element_type.69
  (185 shorter events, 85.1 us)
Async XLA Ops:
  8.0 74.4 %all-gather.5.cloned.1.call-start = ((), (), s32[]{:S(2)}) async-start(), calls=%async_computation.13 | async-start | bytes 6758400 | tf_op jit(solution)/shard_map/all_gather | solution.py:415
  30.8 68.1 %copy-start.30 = (s32[2048]{0:T(1024)}, s32[2048]{0:T(1024)S(1)}, u32[]{:S(2)}) copy-start(s32[2048]{0:T(1024)S(1)} %convert_reduce_fusion) | copy-start | bytes 24580
  31.8 3.2 copy-start.13
  31.8 3.2 copy-start.15
  35.1 4.4 copy-start
  36.4 46.0 %copy-start.29 = (f32[1024]{0:T(1024)S(1)}, f32[1024]{0:T(1024)}, u32[]{:S(2)}) copy-start(f32[1024]{0:T(1024)} %param.16) | copy-start | bytes 12292
  40.2 375.6 %copy-start.34 = (f32[256]{0:T(256)}, f32[256]{0:T(256)S(1)}, u32[]{:S(2)}) copy-start(f32[256]{0:T(256)S(1)} %get-tuple-element.59) | copy-start | bytes 3076
  90.0 7.9 copy-start.12
  92.5 30.3 %all-to-all-start = ((bf16[8,256,256]{2,1,0:T(8,128)(2,1)}), bf16[8,256,256]{2,1,0:T(8,128)(2,1)S(1)}, u32[]{:S(2)}, u32[]{:S(2)}) async-start(bf16[8,256,256]{2,1,0:T(8,128)(2,1)} %maximum_bitcast_fusion), calls=%async_computation | async-start | bytes 2097152 | tf_op jit(solution)/shard_map/all_to_all | solution.py:439
  98.0 83.5 %all-gather.9.cloned.1.call-start = ((), (), s32[]{:S(2)}) async-start(), calls=%async_computation.15 | async-start | bytes 2621440 | tf_op jit(solution)/shard_map/all_gather | solution.py:473
  98.9 91.7 %all-gather.7.cloned.1.call-start = ((), (), s32[]{:S(2)}) async-start(), calls=%async_computation.14 | async-start | bytes 2621440 | tf_op jit(solution)/shard_map/all_gather | solution.py:472
  163.8 2.6 copy-start.31
  169.7 6.3 all-to-all-start.2
  174.1 111.3 %copy-start.32 = (f32[256]{0:T(256)}, f32[256]{0:T(256)S(1)}, u32[]{:S(2)}) copy-start(f32[256]{0:T(256)S(1)} %fusion.48) | copy-start | bytes 3076
  176.0 14.6 %copy-start.27 = (f32[4,8,256]{2,1,0:T(8,128)}, f32[4,8,256]{2,1,0:T(8,128)S(1)}, u32[]{:S(2)}) copy-start(f32[4,8,256]{2,1,0:T(8,128)S(1)} %all-to-all-done.2.rank_ref) | copy-start | bytes 98308
  176.0 7.8 all-to-all-start.3
  183.8 6.7 copy-start.28
  277.1 30.2 %all-to-all-start.4 = ((bf16[4,256,1024]{2,1,0:T(8,128)(2,1)}), bf16[4,256,1024]{2,1,0:T(8,128)(2,1)}, u32[]{:S(2)}, u32[]{:S(2)}) async-start(bf16[4,256,1024]{2,1,0:T(8,128)(2,1)} %bitcast.162), calls=%async_computation.4 | async-start | bytes 4194304 | tf_op jit(solution)/shard_map/all_to_all | solution.py:479
  283.2 5.0 copy-start.36
  312.0 3.7 copy-start.1
  312.0 9.9 copy-start.14
  312.0 9.9 copy-start.16
  315.7 17.9 %all-to-all-start.7 = ((bf16[8,256,128]{2,1,0:T(8,128)(2,1)}), bf16[8,256,128]{2,1,0:T(8,128)(2,1)S(1)}, u32[]{:S(2)}, u32[]{:S(2)}) async-start(bf16[8,256,128]{2,1,0:T(8,128)(2,1)} %bitcast.138), calls=%async_computation.7 | async-start | bytes 1048576 | tf_op jit(solution)/shard_map/all_to_all | solution.py:499
  321.7 228.6 %reduce-scatter.13.cloned.1.call-start = ((), (), s32[]{:S(2)}) async-start(), calls=%async_computation.18 | async-start | bytes 540672
  375.4 2.9 copy-start.6
  381.7 4.3 copy-start.25
  415.8 5.4 copy-start.21
  415.8 5.4 copy-start.23
  415.8 5.4 copy-start.17
  422.3 282.7 %reduce-scatter.15.cloned.1.call-start = ((), (), s32[]{:S(2)}) async-start(), calls=%async_computation.19 | async-start | bytes 9437184
  447.6 408.7 %reduce-scatter.9.cloned.1.call-start = ((), (), s32[]{:S(2)}) async-start(), calls=%async_computation.16 | async-start | bytes 6758400 | tf_op jit(solution)/shard_map/reduce_scatter | solution.py:544
  454.7 687.3 %reduce-scatter.11.cloned.1.call-start = ((), (), s32[]{:S(2)}) async-start(), calls=%async_computation.17 | async-start | bytes 18874368 | tf_op jit(solution)/shard_map/reduce_scatter | solution.py:477
  (21 other events, 27.4 us)
Sparse Core Ops, SparseCore 0:
  12.8 69.5 all-gather.4
  422.4 127.8 reduce-scatter.12
  553.9 151.0 reduce-scatter.14
  707.2 149.0 reduce-scatter.8
  859.9 282.1 reduce-scatter.10
Sparse Core Ops, SparseCore 1:
  100.6 22.4 all-gather.8
  167.5 23.0 all-gather.6

commit v2 on v1

--- a/solution.py
+++ b/solution.py
@@ -256,8 +256,7 @@
     out_ref,
     grad_ref,
     inner_ref,
-    grad_gate_up_ref,
-    grad_down_ref,
+    grad_w_ref,
     picks_s,
     out_s,
     grad_s,
@@ -265,6 +264,7 @@
     sources,
     rows_dev,
     count,
+    copies,
 ):
     step = pl.program_id(0)
     slots = pl.ds(pl.multiple_of(step * CAP, 16), CAP)
@@ -296,11 +296,20 @@
     sent_out = (weight * produced).astype(jnp.bfloat16)
     grad_out = (weight * grad_mix).astype(jnp.bfloat16)
     grad_active = dot_nt(grad_out, down)
-    grad_down_ref[0] = dot_tn(active, grad_out).astype(grad_down_ref.dtype)
+    grad_down = dot_tn(active, grad_out).astype(grad_w_ref.dtype)
+    share = grad_down.shape[1] // copies
+    tall = hidden_units // copies
+    for r in range(copies):
+        for k in range(copies):
+            grad_w_ref[0, r, 0, share : share + tall, k * share : (k + 1) * share] = grad_down[
+                k * tall : (k + 1) * tall, r * share : (r + 1) * share
+            ]
     grad_gate = grad_active * up_part * sigmoid_gate * (1.0 + gate_part * (1.0 - sigmoid_gate))
     grad_up = grad_active * gate_part * sigmoid_gate
     grad_both = jnp.concatenate([grad_gate, grad_up], 1).astype(jnp.bfloat16)
-    grad_gate_up_ref[0] = dot_tn(arrived, grad_both).astype(grad_gate_up_ref.dtype)
+    grad_gate_up = dot_tn(arrived, grad_both).astype(grad_w_ref.dtype)
+    for r in range(copies):
+        grad_w_ref[0, r, 0, :share, :] = grad_gate_up[r * share : (r + 1) * share]
     grad_in = dot_nt(grad_both, gate_up).astype(jnp.bfloat16)
     for s in range(sources):
         part = slice(s * CAP, (s + 1) * CAP)
@@ -317,21 +326,24 @@
             grad_ref[own, :] = dot_tn(table, grad_s[s]).astype(jnp.bfloat16)
 
 
-def experts(rows, cots, ranks, probs, w_gate_up, w_down):
+def experts(rows, cots, ranks, probs, w_gate_up, w_down, copies, chunks):
     sources, count, rows_dev = ranks.shape
     total, model_width = rows.shape
     hidden_units = w_down.shape[1]
+    per = count // chunks
+    tall = model_width // copies + hidden_units // copies
     flat = lambda i: (0, 0)
     cube = lambda i: (0, 0, 0)
     once = pl.Buffered(1)
     return pl.pallas_call(
-        functools.partial(experts_kernel, sources=sources, rows_dev=rows_dev, count=count),
+        functools.partial(
+            experts_kernel, sources=sources, rows_dev=rows_dev, count=count, copies=copies
+        ),
         out_shape=(
             jax.ShapeDtypeStruct((total, model_width), jnp.bfloat16),
             jax.ShapeDtypeStruct((total, model_width), jnp.bfloat16),
             jax.ShapeDtypeStruct((sources, count, rows_dev), jnp.float32),
-            jax.ShapeDtypeStruct(w_gate_up.shape, jnp.bfloat16),
-            jax.ShapeDtypeStruct(w_down.shape, jnp.bfloat16),
+            jax.ShapeDtypeStruct((chunks, copies, per, tall, model_width), jnp.bfloat16),
         ),
         grid=(count,),
         in_specs=[
@@ -346,8 +358,9 @@
             pl.BlockSpec((total, model_width), flat),
             pl.BlockSpec((total, model_width), flat),
             pl.BlockSpec((sources, count, rows_dev), cube),
-            pl.BlockSpec((1, model_width, 2 * hidden_units), lambda i: (i, 0, 0)),
-            pl.BlockSpec((1, hidden_units, model_width), lambda i: (i, 0, 0)),
+            pl.BlockSpec(
+                (1, copies, 1, tall, model_width), lambda i: (i // per, 0, i % per, 0, 0)
+            ),
         ],
         scratch_shapes=[
             pltpu.VMEM((sources, count * CAP, rows_dev), jnp.bfloat16),
@@ -357,6 +370,25 @@
         compiler_params=pltpu.CompilerParams(vmem_limit_bytes=64 * 1000 * 1000),
         name="experts",
     )(rows, cots, ranks, probs, w_gate_up, w_down)
+
+
+def bits_of(size):
+    return max(size.bit_length() - 1, 0)
+
+
+def halving(block, labels, order, last=jnp.bfloat16):
+    labels = list(labels)
+    for number, (axis, bit) in enumerate(order):
+        dim = labels.index((axis, bit))
+        mine = (lax.axis_index(axis) >> bit) & 1
+        sent = lax.dynamic_index_in_dim(block, 1 - mine, dim, keepdims=False)
+        kept = lax.dynamic_index_in_dim(block, mine, dim, keepdims=False)
+        size = lax.axis_size(axis)
+        came = lax.ppermute(sent, axis, [(i, i ^ (1 << bit)) for i in range(size)])
+        total = kept.astype(jnp.float32) + came.astype(jnp.float32)
+        block = total.astype(last if number == len(order) - 1 else jnp.bfloat16)
+        labels.pop(dim)
+    return block
 
 
 def on_device(
@@ -463,19 +495,39 @@
     kept = chosen & (rank < CAP)
     rank_sent = jnp.where(kept, rank, -1.0).T
     probs_sent = probs.T
-    ranks = lax.all_to_all(
-        rank_sent.reshape(n_ep, -1, rows_dev), "ep", split_axis=0, concat_axis=0, tiled=True
-    )
-    prob_all = lax.all_to_all(
-        probs_sent.reshape(n_ep, -1, rows_dev), "ep", split_axis=0, concat_axis=0, tiled=True
-    )
+    both_sent = jnp.concatenate(
+        [rank_sent.reshape(n_ep, -1, rows_dev), probs_sent.reshape(n_ep, -1, rows_dev)], 1
+    )
+    both_all = lax.all_to_all(both_sent, "ep", split_axis=0, concat_axis=0, tiled=True)
+    ranks = both_all[:, : experts_all // n_ep]
+    prob_all = both_all[:, experts_all // n_ep :]
     expert_rows = lax.all_gather(normed_two_b, "ep", axis=0, tiled=True)
     expert_cots = lax.all_gather(grad_output.astype(jnp.bfloat16), "ep", axis=0, tiled=True)
-    out_sum, grad_sum, inner, grad_gate_up, grad_down = experts(
-        expert_rows, expert_cots, ranks, prob_all, w_gate_up, w_down
-    )
-    expert_up = lax.psum_scatter(grad_gate_up, "rep", scatter_dimension=1, tiled=True)
-    expert_down = lax.psum_scatter(grad_down, "rep", scatter_dimension=2, tiled=True)
+    chunks = 4
+    out_sum, grad_sum, inner, grad_experts = experts(
+        expert_rows, expert_cots, ranks, prob_all, w_gate_up, w_down, n_rep, chunks
+    )
+    rep_bits = [("rep", b) for b in reversed(range(bits_of(n_rep)))]
+    ep_bits = [("ep", b) for b in reversed(range(bits_of(n_ep)))]
+    near_first = rep_bits[::-1]
+    far_first = near_first[-2:-1] + near_first[:-2] + near_first[-1:]
+    share = model_width // n_rep
+    tall = w_down.shape[1] // n_rep
+    pieces = []
+    for c in range(chunks):
+        block = grad_experts[c].reshape(
+            (2,) * len(rep_bits) + grad_experts.shape[2:]
+        )
+        order = far_first if c == chunks - 1 else near_first
+        pieces.append(halving(block, rep_bits, order, jnp.float32))
+    grad_experts = jnp.concatenate(pieces, 0)
+    expert_up = grad_experts[:, :share, :]
+    expert_down = (
+        grad_experts[:, share:, :]
+        .reshape(-1, tall, n_rep, share)
+        .transpose(0, 2, 1, 3)
+        .reshape(-1, tall * n_rep, share)
+    )
     out_back = lax.all_to_all(
         out_sum.reshape(n_ep, rows_dev, model_width), "ep", split_axis=0, concat_axis=0, tiled=True
     )
@@ -536,28 +588,46 @@
         ],
         1,
     )
-    grad_w_in = dot_tn(normed_b, grad_in_rows)
+    grad_w_query = dot_tn(normed_b, grad_in_rows[:, :query_width])
+    grad_w_rest = dot_tn(normed_b, grad_in_rows[:, query_width:])
     grad_normed = dot_nt(grad_in_rows, full_in)
     grad_inputs_norm, grad_attn_gain = norm_back(grad_normed, inputs, factor_one, attn_gain)
     grad_inputs = grad_hidden + grad_inputs_norm
-    weight_grads = jnp.concatenate([grad_w_in, grad_out_w, grad_router], 1).astype(jnp.bfloat16)
-    summed = lax.psum_scatter(weight_grads, everyone, scatter_dimension=0, tiled=True)
-    summed = summed.astype(jnp.float32)
-    gains = lax.psum_scatter(
-        jnp.stack([grad_attn_gain, grad_mlp_gain], 1), everyone, scatter_dimension=0, tiled=True
-    )
+    shape = (2,) * (len(ep_bits) + len(rep_bits)) + (-1,)
+    near = ep_bits[::-1] + near_first
+    other = ep_bits[::-1][:1] + near_first + ep_bits[::-1][1:]
+    first = jnp.concatenate([grad_out_w, grad_router], 1).astype(jnp.bfloat16)
+    first = halving(
+        first.reshape(shape + first.shape[1:]), ep_bits + rep_bits, near, jnp.float32
+    )
+    query_grad = grad_w_query.astype(jnp.bfloat16)
+    query_grad = halving(
+        query_grad.reshape(shape + query_grad.shape[1:]), ep_bits + rep_bits, near, jnp.float32
+    )
+    rest_grad = grad_w_rest.astype(jnp.bfloat16)
+    rest_grad = halving(
+        rest_grad.reshape(shape + rest_grad.shape[1:]), ep_bits + rep_bits, other, jnp.float32
+    )
+    everything = n_ep * n_rep
+    gains = jnp.concatenate(
+        [grad_attn_gain.reshape(everything, -1), grad_mlp_gain.reshape(everything, -1)], 1
+    )
+    gains = jnp.sum(
+        lax.all_to_all(gains, everyone, split_axis=0, concat_axis=0, tiled=True), 0
+    )
+    part = model_width // everything
     return (
         output[None],
         grad_inputs[None],
-        gains[:, 0],
-        summed[:, :query_width],
-        summed[:, query_width:rotated_width],
-        summed[:, rotated_width:input_width],
-        summed[:, input_width : input_width + model_width],
-        gains[:, 1],
-        summed[:, input_width + model_width :],
-        expert_up.astype(jnp.float32),
-        expert_down.astype(jnp.float32),
+        gains[:part],
+        query_grad,
+        rest_grad[:, :key_width],
+        rest_grad[:, key_width:],
+        first[:, :model_width],
+        gains[part:],
+        first[:, model_width:],
+        expert_up,
+        expert_down,
     )
 
 

time: 1170 us -> 831 us (0.71)
  waiting for transfers between devices: 778 us -> 399 us
  blocking collectives: 99.8 us -> 46.1 us
  local copies, waits for them, and re-layouts: 79.9 us -> 116 us
  starting transfers between devices: 28 us -> 61.7 us
  other arithmetic: 32.5 us -> 56.4 us
    reduce_scatter x2 -> x0, waiting for transfers between devices: 429 us -> none  [the longest x1 281 us: on_device(): lax.psum_scatter(grad_gate_up, 'rep', scatter_dimension=1, tiled=True)]
    ppermute x0 -> x27, waiting for transfers between devices: none -> 271 us  [halving(): came = lax.ppermute(sent, axis, [(i, i ^ 1 << bit) for i in range(size)])]
    unnamed x9 -> x3, waiting for transfers between devices: 246 us -> 0.05 us
    all_to_all x2 -> x1, blocking collectives: 59.8 us -> 6.15 us  [on_device(): lax.all_to_all(both_sent, 'ep', split_axis=0, concat_axis=0, tiled=True)]
    dynamic_slice x0 -> x12, local copies, waits for them, and re-layouts: none -> 30.9 us  [the longest x6 20.3 us: halving(): kept = lax.dynamic_index_in_dim(block, mine, dim, keepdims=False)]
    all_to_all x1, waiting for transfers between devices: 7.65 us -> 37 us  [on_device(): lax.all_to_all(grad_mixed.reshape(rows_dev, n_rep, head_width).transpose(...]
    unnamed x96 -> x83, local copies, waits for them, and re-layouts: 43.3 us -> 15 us
    ppermute x0 -> x27, starting transfers between devices: none -> 25.3 us  [halving(): came = lax.ppermute(sent, axis, [(i, i ^ 1 << bit) for i in range(size)])]
  transfers between devices with their start and end apart: 12 -> 36, of which waited for: 11 -> 19; matrix products, arithmetic and copies ran while one was open for 6% -> 21% of each run, Pallas kernels for 2% -> 6%
where the time goes in v2:
time: 831 us; the launch traced here: 815 us
  waiting for transfers between devices  399 us (48%)
  local copies, waits for them, and re-layouts  116 us (14%)
  Pallas kernels  98.3 us (12%)
  starting transfers between devices  61.7 us (7%)
  other arithmetic  56.4 us (7%)
  blocking collectives  46.1 us (6%)
  matrix products  20.3 us (2%)
  between operations  17 us (2%)
    ppermute x27, waiting for transfers between devices, halving(): came = lax.ppermute(sent, axis, [(i, i ^ 1 << bit) for i in range(size)])  271 us
    pallas_call x1, Pallas kernels, experts(): pl.pallas_call(functools.partial(experts_kernel, sources=sources, rows_de...  49.9 us
    all_gather x1, waiting for transfers between devices, on_device(): full = lax.all_gather(joined, everyone, axis=0, tiled=True)  42 us
    all_to_all x1, waiting for transfers between devices, on_device(): lax.all_to_all(grad_mixed.reshape(rows_dev, n_rep, head_width).transpose(...  37 us
    convert_element_type x20, other arithmetic, halving(): block = total.astype(last if number == len(order) - 1 else jnp.bfloat16)  27.3 us
    pallas_call x1, Pallas kernels, attend_backward(): pl.pallas_call(functools.partial(attend_backward_kernel, heads=heads), ou...  26.7 us
    ppermute x27, starting transfers between devices, halving(): came = lax.ppermute(sent, axis, [(i, i ^ 1 << bit) for i in range(size)])  25.3 us
    all_to_all x1, waiting for transfers between devices, on_device(): lax.all_to_all(sending, 'rep', split_axis=0, concat_axis=0, tiled=True)  22 us
  transfers between devices with their start and end apart: 36, of which 19 were waited for; matrix products, arithmetic and copies ran while one was open for 21% of the time, Pallas kernels for 6%

profile of v2, /device:TPU:26, one launch (start us, length us, event | category | flops | bytes accessed | tf_op | source)
XLA Modules:
  0.0 814.8 jit_solution(11612231634377221232)
XLA Ops:
  12.7 16.3 %all-gather = s32[1,2048]{1,0:T(1,128)S(1)} all-gather(s32[1,256]{1,0:T(1,128)} %param.14), channel_id=2, replica_groups=mesh['ep'=4,'rep'=8] {'rep'}, dimensions={1}, use_global_device_ids=true | all-gather | bytes 9216 | tf_op jit(solution)/shard_map/all_gather | solution.py:425
  40.4 42.0 %all-gather.5.cloned.1.call-done = bf16[1024,3104]{1,0:T(8,128)(2,1)} async-done(((bf16[32,3104]{1,0:T(8,128)(2,1)}), bf16[1024,3104]{1,0:T(8,128)(2,1)}) %all-gather.5.cloned.1.call-update) | async-done | bytes 6357008 | tf_op jit(solution)/shard_map/all_gather | solution.py:447
  92.4 5.5 all-to-all-start
  100.7 22.0 %all-to-all-done = bf16[8,256,256]{2,1,0:T(8,128)(2,1)S(1)} async-done(((bf16[8,256,256]{2,1,0:T(8,128)(2,1)}), bf16[8,256,256]{2,1,0:T(8,128)(2,1)S(1)}, u32[]{:S(2)}, u32[]{:S(2)}) %all-to-all-start) | async-done | bytes 1048608 | tf_op jit(solution)/shard_map/all_to_all | solution.py:471
  123.7 21.7 %attend_forward.1 = (bf16[2048,128]{1,0:T(8,128)(2,1)}, f32[128,2048]{1,0:T(8,128)}, f32[8,2,256]{2,1,0:T(2,128)}) custom-call(s32[8]{0:T(128)} %and_select_fusion.low_ref, bf16[2048,256]{1,0:T(8,128)(2,1)} %bitcast.322, s32[8,1,256]{2,1,0:T(1,128)} %bitcast.352), custom_call_target="tpu_custom_call" | custom-call | tf_op jit(solution)/shard_map/attend_forward/pallas_call | solution.py:119
  146.7 17.1 %all_to_all.49 = bf16[8,256,128]{1,2,0:T(8,128)(2,1)S(1)} all-to-all(bf16[8,256,128]{1,2,0:T(8,128)(2,1)S(1)} %copy.116), channel_id=1, replica_groups=mesh['ep'=4,'rep'=8] {'rep'}, dimensions={0} | all-to-all | bytes 1048576 | tf_op jit(solution)/shard_map/all_to_all | solution.py:474
  168.9 6.2 all_to_all.50
  175.7 14.5 %all-gather.7.cloned.1.call-done.rows_ref = bf16[1024,1024]{1,0:T(8,128)(2,1)} async-done(((bf16[256,1024]{1,0:T(8,128)(2,1)}), bf16[1024,1024]{1,0:T(8,128)(2,1)}) %all-gather.7.cloned.1.call-update) | async-done | bytes 2097168 | tf_op jit(solution)/shard_map/all_gather | solution.py:504
  190.2 49.9 %experts.1 = (bf16[1024,1024]{1,0:T(8,128)(2,1)}, bf16[1024,1024]{1,0:T(8,128)(2,1)}, f32[4,8,256]{2,1,0:T(8,128)}, bf16[4,8,2,192,1024]{4,3,2,1,0:T(8,128)(2,1)}) custom-call(bf16[1024,1024]{1,0:T(8,128)(2,1)} %all-gather.7.cloned.1.call-done.rows_ref, bf16[1024,1024]{1,0:T(8,128)(2,1)} %all-gather.9.cloned.1.call-done.cot_ref, ...), custom_call_target="tpu_custom_call" | custom-call | tf_op jit(solution)/shard_map/experts/pallas_call | solution.py:338
  240.1 6.6 all_to_all.51
  246.7 6.5 all-to-all-start.4
  258.3 19.6 %fusion.102 = (bf16[1,8,2,192,1024]{4,3,2,1,0:T(8,128)(2,1)}, bf16[1,8,2,192,1024]{4,3,2,1,0:T(8,128)(2,1)}, bf16[1,8,2,192,1024]{4,3,2,1,0:T(8,128)(2,1)}, bf16[1,8,2,192,1024]{4,3,2,1,0:T(8,128)(2,1)}) fusion(bf16[4,8,2,192,1024]{4,3,2,1,0:T(8,128)(2,1)} %get-tuple-element.30), kind=kLoop, calls=%fused_computation.243 | loop fusion | bytes 50331648 | tf_op jit(solution)/shard_map/slice | solution.py:518
  278.0 5.6 all-to-all-start.3
  283.7 5.7 constant_dynamic-slice_fusion.7
  297.0 3.9 constant_dynamic-slice_fusion.5
  315.0 6.3 all-to-all-start.6
  321.3 5.6 constant_dynamic-slice_fusion.3
  339.2 37.0 %all-to-all-done.6 = bf16[8,256,128]{2,1,0:T(8,128)(2,1)} async-done(((bf16[8,256,128]{2,1,0:T(8,128)(2,1)}), bf16[8,256,128]{2,1,0:T(8,128)(2,1)}, u32[]{:S(2)}, u32[]{:S(2)}) %all-to-all-start.6) | async-done | bytes 524320 | tf_op jit(solution)/shard_map/all_to_all | solution.py:551
  376.2 26.7 %attend_backward.1 = (f32[2048,128]{1,0:T(8,128)}, f32[2048,64]{1,0:T(8,128)}, f32[2048,64]{1,0:T(8,128)}) custom-call(s32[8]{0:T(128)} %and_select_fusion.low_ref, bf16[2048,256]{1,0:T(8,128)(2,1)} %bitcast.323, bf16[2048,128]{1,0:T(8,128)(2,1)} %bitcast.25.grad_ref, f32[128,2048]{1,0:T(8,128)} %get-tuple-element.25.out_ref, ...), custom_call_target="tpu_custom_call" | custom-call | tf_op jit(solution)/shard_map/attend_backward/pallas_call | solution.py:218
  426.5 4.5 fusion.20
  432.3 6.1 all-to-all-start.7
  457.1 24.6 %collective-permute-done.21 = bf16[2,2,2,192,1024]{4,3,2,0,1:T(8,128)(2,1)} collective-permute-done((bf16[2,2,2,192,1024]{4,3,2,0,1:T(8,128)(2,1)}, bf16[2,2,2,192,1024]{4,3,2,0,1:T(8,128)(2,1)}, u32[]{:S(2)}, u32[]{:S(2)}) %collective-permute-start.21) | collective-permute-done | bytes 3145760 | tf_op jit(solution)/shard_map/ppermute | solution.py:387
  487.0 103.2 %collective-permute-done.12 = bf16[2,2,32,1056]{3,2,1,0:T(8,128)(2,1)S(1)} collective-permute-done((bf16[2,2,32,1056]{3,2,1,0:T(8,128)(2,1)S(1)}, bf16[2,2,32,1056]{3,2,1,0:T(8,128)(2,1)S(1)}, u32[]{:S(2)}, u32[]{:S(2)}) %collective-permute-start.12) | collective-permute-done | bytes 270368 | tf_op jit(solution)/shard_map/ppermute | solution.py:387
  605.2 4.5 fusion.57
  610.5 6.2 all-to-all-start.8
  624.8 10.5 %all-to-all-done.8 = f32[32,1,64]{2,1,0:T(1,128)S(1)} async-done(((f32[32,1,64]{2,1,0:T(1,128)}), f32[32,1,64]{2,1,0:T(1,128)S(1)}, u32[]{:S(2)}, u32[]{:S(2)}) %all-to-all-start.8) | async-done | bytes 8224 | tf_op jit(solution)/shard_map/all_to_all | solution.py:616
  653.7 73.2 %collective-permute-done.26 = bf16[2,192,1024]{2,1,0:T(8,128)(2,1)S(1)} collective-permute-done((bf16[2,192,1024]{2,1,0:T(8,128)(2,1)S(1)}, bf16[2,192,1024]{2,1,0:T(8,128)(2,1)S(1)}, u32[]{:S(2)}, u32[]{:S(2)}) %collective-permute-start.26) | collective-permute-done | bytes 786464 | tf_op jit(solution)/shard_map/ppermute | solution.py:387
  728.2 15.6 %collective-permute-done.20 = bf16[2,192,1024]{2,1,0:T(8,128)(2,1)S(1)} collective-permute-done((bf16[2,192,1024]{2,1,0:T(8,128)(2,1)S(1)}, bf16[2,192,1024]{2,1,0:T(8,128)(2,1)S(1)}, u32[]{:S(2)}, u32[]{:S(2)}) %collective-permute-start.20) | collective-permute-done | bytes 786464 | tf_op jit(solution)/shard_map/ppermute | solution.py:387
  744.0 16.6 %collective-permute-done.23 = bf16[2,192,1024]{2,1,0:T(8,128)(2,1)S(1)} collective-permute-done((bf16[2,192,1024]{2,1,0:T(8,128)(2,1)S(1)}, bf16[2,192,1024]{2,1,0:T(8,128)(2,1)S(1)}, u32[]{:S(2)}, u32[]{:S(2)}) %collective-permute-start.23) | collective-permute-done | bytes 786464 | tf_op jit(solution)/shard_map/ppermute | solution.py:387
  760.9 16.2 %collective-permute-done.17 = bf16[2,192,1024]{2,1,0:T(8,128)(2,1)S(1)} collective-permute-done((bf16[2,192,1024]{2,1,0:T(8,128)(2,1)S(1)}, bf16[2,192,1024]{2,1,0:T(8,128)(2,1)S(1)}, u32[]{:S(2)}, u32[]{:S(2)}) %collective-permute-start.17) | collective-permute-done | bytes 786464 | tf_op jit(solution)/shard_map/ppermute | solution.py:387
  783.7 6.9 collective-permute-done.7
  794.4 4.4 collective-permute-done.8
  (284 shorter events, 186.6 us)
Async XLA Ops:
  8.0 74.4 %all-gather.5.cloned.1.call-start = ((), (), s32[]{:S(2)}) async-start(), calls=%async_computation.9 | async-start | bytes 6758400 | tf_op jit(solution)/shard_map/all_gather | solution.py:447
  92.4 30.3 %all-to-all-start = ((bf16[8,256,256]{2,1,0:T(8,128)(2,1)}), bf16[8,256,256]{2,1,0:T(8,128)(2,1)S(1)}, u32[]{:S(2)}, u32[]{:S(2)}) async-start(bf16[8,256,256]{2,1,0:T(8,128)(2,1)} %maximum_bitcast_fusion.1), calls=%async_computation | async-start | bytes 2097152 | tf_op jit(solution)/shard_map/all_to_all | solution.py:471
  97.9 77.8 %all-gather.9.cloned.1.call-start = ((), (), s32[]{:S(2)}) async-start(), calls=%async_computation.11 | async-start | bytes 2621440 | tf_op jit(solution)/shard_map/all_gather | solution.py:505
  100.0 90.2 %all-gather.7.cloned.1.call-start = ((), (), s32[]{:S(2)}) async-start(), calls=%async_computation.10 | async-start | bytes 2621440 | tf_op jit(solution)/shard_map/all_gather | solution.py:504
  246.7 31.3 %all-to-all-start.4 = ((bf16[4,256,1024]{2,1,0:T(8,128)(2,1)}), bf16[4,256,1024]{2,1,0:T(8,128)(2,1)}, u32[]{:S(2)}, u32[]{:S(2)}) async-start(bf16[4,256,1024]{2,1,0:T(8,128)(2,1)} %bitcast.342), calls=%async_computation.4 | async-start | bytes 4194304 | tf_op jit(solution)/shard_map/all_to_all | solution.py:534
  278.0 29.8 %all-to-all-start.3 = ((bf16[4,256,1024]{2,1,0:T(8,128)(2,1)}), bf16[4,256,1024]{2,1,0:T(8,128)(2,1)}, u32[]{:S(2)}, u32[]{:S(2)}) async-start(bf16[4,256,1024]{2,1,0:T(8,128)(2,1)} %bitcast.341), calls=%async_computation.3 | async-start | bytes 4194304 | tf_op jit(solution)/shard_map/all_to_all | solution.py:531
  296.4 144.4 %collective-permute-start.24 = (bf16[2,2,2,192,1024]{4,3,2,0,1:T(8,128)(2,1)}, bf16[2,2,2,192,1024]{4,3,2,0,1:T(8,128)(2,1)}, u32[]{:S(2)}, u32[]{:S(2)}) collective-permute-start(bf16[2,2,2,192,1024]{4,3,2,0,1:T(8,128)(2,1)} %bitcast.303), channel_id=1, source_target_pairs={{0,2},{1,3},{2,0},{3,1},{4,6},{5,7},{6,4},{7,5},{8,10},{9,11},{10,... | collective-permute-start | bytes 9437192 | tf_op jit(solution)/shard_map/ppermute | solution.py:387
  315.0 61.2 %all-to-all-start.6 = ((bf16[8,256,128]{2,1,0:T(8,128)(2,1)}), bf16[8,256,128]{2,1,0:T(8,128)(2,1)}, u32[]{:S(2)}, u32[]{:S(2)}) async-start(bf16[8,256,128]{2,1,0:T(8,128)(2,1)} %bitcast.310), calls=%async_computation.6 | async-start | bytes 1048576 | tf_op jit(solution)/shard_map/all_to_all | solution.py:551
  331.8 115.4 %collective-permute-start.18 = (bf16[2,2,2,192,1024]{4,3,2,0,1:T(8,128)(2,1)}, bf16[2,2,2,192,1024]{4,3,2,0,1:T(8,128)(2,1)}, u32[]{:S(2)}, u32[]{:S(2)}) collective-permute-start(bf16[2,2,2,192,1024]{4,3,2,0,1:T(8,128)(2,1)} %bitcast.305), channel_id=1, source_target_pairs={{0,1},{1,0},{2,3},{3,2},{4,5},{5,4},{6,7},{7,6},{8,9},{9,8},{10,11... | collective-permute-start | bytes 9437192 | tf_op jit(solution)/shard_map/ppermute | solution.py:387
  333.3 148.5 %collective-permute-start.21 = (bf16[2,2,2,192,1024]{4,3,2,0,1:T(8,128)(2,1)}, bf16[2,2,2,192,1024]{4,3,2,0,1:T(8,128)(2,1)}, u32[]{:S(2)}, u32[]{:S(2)}) collective-permute-start(bf16[2,2,2,192,1024]{4,3,2,0,1:T(8,128)(2,1)} %bitcast.304), channel_id=1, source_target_pairs={{0,1},{1,0},{2,3},{3,2},{4,5},{5,4},{6,7},{7,6},{8,9},{9,8},{10,11... | collective-permute-start | bytes 9437192 | tf_op jit(solution)/shard_map/ppermute | solution.py:387
  333.8 257.2 %collective-permute-start.15 = (bf16[2,2,2,192,1024]{4,3,2,0,1:T(8,128)(2,1)}, bf16[2,2,2,192,1024]{4,3,2,0,1:T(8,128)(2,1)}, u32[]{:S(2)}, u32[]{:S(2)}) collective-permute-start(bf16[2,2,2,192,1024]{4,3,2,0,1:T(8,128)(2,1)} %bitcast.306), channel_id=1, source_target_pairs={{0,1},{1,0},{2,3},{3,2},{4,5},{5,4},{6,7},{7,6},{8,9},{9,8},{10,11... | collective-permute-start | bytes 9437192 | tf_op jit(solution)/shard_map/ppermute | solution.py:387
  339.2 99.3 %collective-permute-start.10 = (bf16[2,2,2,2,32,1056]{5,4,3,2,1,0:T(8,128)(2,1)}, bf16[2,2,2,2,32,1056]{5,4,3,2,1,0:T(8,128)(2,1)}, u32[]{:S(2)}, u32[]{:S(2)}) collective-permute-start(bf16[2,2,2,2,32,1056]{5,4,3,2,1,0:T(8,128)(2,1)} %fusion.37), channel_id=1, source_target_pairs={{0,8},{8,0},{16,24},{24,16},{1,9},{9,1},{17,25},{25,17},{2,10},{10... | collective-permute-start | bytes 3244040 | tf_op jit(solution)/shard_map/ppermute | solution.py:387
  432.3 170.7 %all-to-all-start.7 = ((bf16[8,256,256]{1,2,0:T(8,128)(2,1)}), bf16[8,256,256]{1,2,0:T(8,128)(2,1)}, u32[]{:S(2)}, u32[]{:S(2)}) async-start(bf16[8,256,256]{1,2,0:T(8,128)(2,1)} %copy.125), calls=%async_computation.7 | async-start | bytes 2097152 | tf_op jit(solution)/shard_map/all_to_all | solution.py:566
  440.5 14.8 %collective-permute-start.11 = (bf16[2,2,2,32,1056]{4,3,2,1,0:T(8,128)(2,1)S(1)}, bf16[2,2,2,32,1056]{4,3,2,1,0:T(8,128)(2,1)S(1)}, u32[]{:S(2)}, u32[]{:S(2)}) collective-permute-start(bf16[2,2,2,32,1056]{4,3,2,1,0:T(8,128)(2,1)S(1)} %dynamic-slice_bitcast_fusion.8), channel_id=1, source_target_pairs={{0,16},{8,24},{16,0},{24,8},{1,17},{9,25},{17,1},{25,9},{2,18},{10... | collective-permute-start | bytes 1622024 | tf_op jit(solution)/shard_map/ppermute | solution.py:387
  445.7 190.2 %collective-permute-start.25 = (bf16[2,2,192,1024]{3,2,1,0:T(8,128)(2,1)}, bf16[2,2,192,1024]{3,2,1,0:T(8,128)(2,1)}, u32[]{:S(2)}, u32[]{:S(2)}) collective-permute-start(bf16[2,2,192,1024]{3,2,1,0:T(8,128)(2,1)} %dynamic-slice_bitcast_fusion), channel_id=1, source_target_pairs={{0,1},{1,0},{2,3},{3,2},{4,5},{5,4},{6,7},{7,6},{8,9},{9,8},{10,11... | collective-permute-start | bytes 4718600 | tf_op jit(solution)/shard_map/ppermute | solution.py:387
  452.8 185.4 %collective-permute-start.19 = (bf16[2,2,192,1024]{3,2,1,0:T(8,128)(2,1)}, bf16[2,2,192,1024]{3,2,1,0:T(8,128)(2,1)}, u32[]{:S(2)}, u32[]{:S(2)}) collective-permute-start(bf16[2,2,192,1024]{3,2,1,0:T(8,128)(2,1)} %dynamic-slice_bitcast_fusion.2), channel_id=1, source_target_pairs={{0,2},{1,3},{2,0},{3,1},{4,6},{5,7},{6,4},{7,5},{8,10},{9,11},{10,... | collective-permute-start | bytes 4718600 | tf_op jit(solution)/shard_map/ppermute | solution.py:387
  455.6 134.7 %collective-permute-start.12 = (bf16[2,2,32,1056]{3,2,1,0:T(8,128)(2,1)S(1)}, bf16[2,2,32,1056]{3,2,1,0:T(8,128)(2,1)S(1)}, u32[]{:S(2)}, u32[]{:S(2)}) collective-permute-start(bf16[2,2,32,1056]{3,2,1,0:T(8,128)(2,1)S(1)} %dynamic-slice_bitcast_fusion.11), channel_id=1, source_target_pairs={{0,1},{1,0},{2,3},{3,2},{4,5},{5,4},{6,7},{7,6},{8,9},{9,8},{10,11... | collective-permute-start | bytes 811016 | tf_op jit(solution)/shard_map/ppermute | solution.py:387
  486.5 155.5 %collective-permute-start.22 = (bf16[2,2,192,1024]{3,2,1,0:T(8,128)(2,1)}, bf16[2,2,192,1024]{3,2,1,0:T(8,128)(2,1)}, u32[]{:S(2)}, u32[]{:S(2)}) collective-permute-start(bf16[2,2,192,1024]{3,2,1,0:T(8,128)(2,1)} %dynamic-slice_bitcast_fusion.1), channel_id=1, source_target_pairs={{0,2},{1,3},{2,0},{3,1},{4,6},{5,7},{6,4},{7,5},{8,10},{9,11},{10,... | collective-permute-start | bytes 4718600 | tf_op jit(solution)/shard_map/ppermute | solution.py:387
  597.6 48.1 %collective-permute-start.16 = (bf16[2,2,192,1024]{3,2,1,0:T(8,128)(2,1)}, bf16[2,2,192,1024]{3,2,1,0:T(8,128)(2,1)}, u32[]{:S(2)}, u32[]{:S(2)}) collective-permute-start(bf16[2,2,192,1024]{3,2,1,0:T(8,128)(2,1)} %dynamic-slice_bitcast_fusion.3), channel_id=1, source_target_pairs={{0,2},{1,3},{2,0},{3,1},{4,6},{5,7},{6,4},{7,5},{8,10},{9,11},{10,... | collective-permute-start | bytes 4718600 | tf_op jit(solution)/shard_map/ppermute | solution.py:387
  610.5 24.7 %all-to-all-start.8 = ((f32[32,1,64]{2,1,0:T(1,128)}), f32[32,1,64]{2,1,0:T(1,128)S(1)}, u32[]{:S(2)}, u32[]{:S(2)}) async-start(f32[32,1,64]{2,1,0:T(1,128)} %bitcast.38), calls=%async_computation.8 | async-start | bytes 32768 | tf_op jit(solution)/shard_map/all_to_all | solution.py:616
  619.8 29.6 %collective-permute-start.5 = (bf16[2,2,2,2,32,1024]{5,4,0,1,2,3:T(8,128)(2,1)}, bf16[2,2,2,2,32,1024]{5,4,0,1,2,3:T(8,128)(2,1)}, u32[]{:S(2)}, u32[]{:S(2)}) collective-permute-start(bf16[2,2,2,2,32,1024]{5,4,0,1,2,3:T(8,128)(2,1)} %bitcast.307), channel_id=1, source_target_pairs={{0,8},{8,0},{16,24},{24,16},{1,9},{9,1},{17,25},{25,17},{2,10},{10... | collective-permute-start | bytes 3145736 | tf_op jit(solution)/shard_map/ppermute | solution.py:387
  635.9 16.8 %collective-permute-start = (bf16[2,2,2,2,32,1024]{5,4,1,2,3,0:T(8,128)(2,1)}, bf16[2,2,2,2,32,1024]{5,4,1,2,3,0:T(8,128)(2,1)S(1)}, u32[]{:S(2)}, u32[]{:S(2)}) collective-permute-start(bf16[2,2,2,2,32,1024]{5,4,1,2,3,0:T(8,128)(2,1)} %bitcast.346), channel_id=1, source_target_pairs={{0,8},{8,0},{16,24},{24,16},{1,9},{9,1},{17,25},{25,17},{2,10},{10... | collective-permute-start | bytes 3145736 | tf_op jit(solution)/shard_map/ppermute | solution.py:387
  638.2 88.7 %collective-permute-start.26 = (bf16[2,192,1024]{2,1,0:T(8,128)(2,1)S(1)}, bf16[2,192,1024]{2,1,0:T(8,128)(2,1)S(1)}, u32[]{:S(2)}, u32[]{:S(2)}) collective-permute-start(bf16[2,192,1024]{2,1,0:T(8,128)(2,1)S(1)} %dynamic-slice_bitcast_fusion.4), channel_id=1, source_target_pairs={{0,4},{1,5},{2,6},{3,7},{4,0},{5,1},{6,2},{7,3},{8,12},{9,13},{10,... | collective-permute-start | bytes 2359304 | tf_op jit(solution)/shard_map/ppermute | solution.py:387
  642.0 101.8 %collective-permute-start.20 = (bf16[2,192,1024]{2,1,0:T(8,128)(2,1)S(1)}, bf16[2,192,1024]{2,1,0:T(8,128)(2,1)S(1)}, u32[]{:S(2)}, u32[]{:S(2)}) collective-permute-start(bf16[2,192,1024]{2,1,0:T(8,128)(2,1)S(1)} %dynamic-slice_bitcast_fusion.6), channel_id=1, source_target_pairs={{0,4},{1,5},{2,6},{3,7},{4,0},{5,1},{6,2},{7,3},{8,12},{9,13},{10,... | collective-permute-start | bytes 2359304 | tf_op jit(solution)/shard_map/ppermute | solution.py:387
  645.6 115.0 %collective-permute-start.23 = (bf16[2,192,1024]{2,1,0:T(8,128)(2,1)S(1)}, bf16[2,192,1024]{2,1,0:T(8,128)(2,1)S(1)}, u32[]{:S(2)}, u32[]{:S(2)}) collective-permute-start(bf16[2,192,1024]{2,1,0:T(8,128)(2,1)S(1)} %dynamic-slice_bitcast_fusion.5), channel_id=1, source_target_pairs={{0,4},{1,5},{2,6},{3,7},{4,0},{5,1},{6,2},{7,3},{8,12},{9,13},{10,... | collective-permute-start | bytes 2359304 | tf_op jit(solution)/shard_map/ppermute | solution.py:387
  649.4 127.6 %collective-permute-start.17 = (bf16[2,192,1024]{2,1,0:T(8,128)(2,1)S(1)}, bf16[2,192,1024]{2,1,0:T(8,128)(2,1)S(1)}, u32[]{:S(2)}, u32[]{:S(2)}) collective-permute-start(bf16[2,192,1024]{2,1,0:T(8,128)(2,1)S(1)} %dynamic-slice_bitcast_fusion.7), channel_id=1, source_target_pairs={{0,4},{1,5},{2,6},{3,7},{4,0},{5,1},{6,2},{7,3},{8,12},{9,13},{10,... | collective-permute-start | bytes 2359304 | tf_op jit(solution)/shard_map/ppermute | solution.py:387
  652.7 129.7 %collective-permute-start.6 = (bf16[2,2,2,32,1024]{4,3,0,1,2:T(8,128)(2,1)S(1)}, bf16[2,2,2,32,1024]{4,3,0,1,2:T(8,128)(2,1)S(1)}, u32[]{:S(2)}, u32[]{:S(2)}) collective-permute-start(bf16[2,2,2,32,1024]{4,3,0,1,2:T(8,128)(2,1)S(1)} %dynamic-slice_bitcast_fusion.9), channel_id=1, source_target_pairs={{0,1},{1,0},{2,3},{3,2},{4,5},{5,4},{6,7},{7,6},{8,9},{9,8},{10,11... | collective-permute-start | bytes 1572872 | tf_op jit(solution)/shard_map/ppermute | solution.py:387
  726.9 55.8 %collective-permute-start.1 = (bf16[2,2,2,32,1024]{4,3,0,1,2:T(8,128)(2,1)S(1)}, bf16[2,2,2,32,1024]{4,3,0,1,2:T(8,128)(2,1)S(1)}, u32[]{:S(2)}, u32[]{:S(2)}) collective-permute-start(bf16[2,2,2,32,1024]{4,3,0,1,2:T(8,128)(2,1)S(1)} %dynamic-slice_bitcast_fusion.10), channel_id=1, source_target_pairs={{0,16},{8,24},{16,0},{24,8},{1,17},{9,25},{17,1},{25,9},{2,18},{10... | collective-permute-start | bytes 1572872 | tf_op jit(solution)/shard_map/ppermute | solution.py:387
  782.6 8.0 collective-permute-start.7
  783.0 9.6 %collective-permute-start.2 = (bf16[2,2,32,1024]{3,2,0,1:T(8,128)(2,1)S(1)}, bf16[2,2,32,1024]{3,2,0,1:T(8,128)(2,1)S(1)}, u32[]{:S(2)}, u32[]{:S(2)}) collective-permute-start(bf16[2,2,32,1024]{3,2,0,1:T(8,128)(2,1)S(1)} %dynamic-slice_bitcast_fusion.13), channel_id=1, source_target_pairs={{0,1},{1,0},{2,3},{3,2},{4,5},{5,4},{6,7},{7,6},{8,9},{9,8},{10,11... | collective-permute-start | bytes 786440 | tf_op jit(solution)/shard_map/ppermute | solution.py:387
  790.7 8.1 collective-permute-start.8
  792.6 7.7 collective-permute-start.3
  (42 other events, 507.6 us)
Sparse Core Ops, SparseCore 0:
  12.8 69.5 all-gather.4
Sparse Core Ops, SparseCore 1:
  100.5 22.4 all-gather.8
  167.3 22.9 all-gather.6

commit v3 on v2

--- a/solution.py
+++ b/solution.py
@@ -247,6 +247,7 @@
 
 
 def experts_kernel(
+    place_ref,
     rows_ref,
     cot_ref,
     rank_ref,
@@ -256,16 +257,17 @@
     out_ref,
     grad_ref,
     inner_ref,
-    grad_w_ref,
-    picks_s,
-    out_s,
-    grad_s,
-    *,
+    keep_ref,
+    *others,
     sources,
     rows_dev,
     count,
     copies,
+    per,
+    orders,
 ):
+    send_refs = others[:-3]
+    picks_s, out_s, grad_s = others[-3:]
     step = pl.program_id(0)
     slots = pl.ds(pl.multiple_of(step * CAP, 16), CAP)
     numbers = lax.broadcasted_iota(jnp.int32, (CAP, rows_dev), 0).astype(jnp.float32)
@@ -296,20 +298,35 @@
     sent_out = (weight * produced).astype(jnp.bfloat16)
     grad_out = (weight * grad_mix).astype(jnp.bfloat16)
     grad_active = dot_nt(grad_out, down)
-    grad_down = dot_tn(active, grad_out).astype(grad_w_ref.dtype)
-    share = grad_down.shape[1] // copies
-    tall = hidden_units // copies
-    for r in range(copies):
-        for k in range(copies):
-            grad_w_ref[0, r, 0, share : share + tall, k * share : (k + 1) * share] = grad_down[
-                k * tall : (k + 1) * tall, r * share : (r + 1) * share
-            ]
+    grad_down = dot_tn(active, grad_out).astype(keep_ref.dtype)
     grad_gate = grad_active * up_part * sigmoid_gate * (1.0 + gate_part * (1.0 - sigmoid_gate))
     grad_up = grad_active * gate_part * sigmoid_gate
     grad_both = jnp.concatenate([grad_gate, grad_up], 1).astype(jnp.bfloat16)
-    grad_gate_up = dot_tn(arrived, grad_both).astype(grad_w_ref.dtype)
-    for r in range(copies):
-        grad_w_ref[0, r, 0, :share, :] = grad_gate_up[r * share : (r + 1) * share]
+    grad_gate_up = dot_tn(arrived, grad_both).astype(keep_ref.dtype)
+    share = grad_down.shape[1] // copies
+    tall = hidden_units // copies
+
+    def put(order, mine, send_ref):
+        bit, *later = order
+        for r in range(copies):
+            spot = 0
+            for b in later:
+                spot = 2 * spot + ((r >> b) & 1)
+            ref = keep_ref.at[0] if (r >> bit) & 1 == mine else send_ref
+            ref[spot, 0, :share, :] = grad_gate_up[r * share : (r + 1) * share]
+            for k in range(copies):
+                ref[spot, 0, share : share + tall, k * share : (k + 1) * share] = grad_down[
+                    k * tall : (k + 1) * tall, r * share : (r + 1) * share
+                ]
+
+    place = place_ref[0]
+    for c, send_ref in enumerate(send_refs):
+        for mine in range(2):
+
+            @pl.when((step // per == c) & ((place >> orders[c][0]) & 1 == mine))
+            def _(order=orders[c], mine=mine, send_ref=send_ref):
+                put(order, mine, send_ref)
+
     grad_in = dot_nt(grad_both, gate_up).astype(jnp.bfloat16)
     for s in range(sources):
         part = slice(s * CAP, (s + 1) * CAP)
@@ -326,27 +343,37 @@
             grad_ref[own, :] = dot_tn(table, grad_s[s]).astype(jnp.bfloat16)
 
 
-def experts(rows, cots, ranks, probs, w_gate_up, w_down, copies, chunks):
+def experts(place, rows, cots, ranks, probs, w_gate_up, w_down, copies, orders):
     sources, count, rows_dev = ranks.shape
     total, model_width = rows.shape
     hidden_units = w_down.shape[1]
+    chunks = len(orders)
     per = count // chunks
     tall = model_width // copies + hidden_units // copies
     flat = lambda i: (0, 0)
     cube = lambda i: (0, 0, 0)
+    part = lambda i: (i // per, 0, i % per, 0, 0)
     once = pl.Buffered(1)
     return pl.pallas_call(
         functools.partial(
-            experts_kernel, sources=sources, rows_dev=rows_dev, count=count, copies=copies
+            experts_kernel,
+            sources=sources,
+            rows_dev=rows_dev,
+            count=count,
+            copies=copies,
+            per=per,
+            orders=orders,
         ),
         out_shape=(
             jax.ShapeDtypeStruct((total, model_width), jnp.bfloat16),
             jax.ShapeDtypeStruct((total, model_width), jnp.bfloat16),
             jax.ShapeDtypeStruct((sources, count, rows_dev), jnp.float32),
-            jax.ShapeDtypeStruct((chunks, copies, per, tall, model_width), jnp.bfloat16),
-        ),
+            jax.ShapeDtypeStruct((chunks, copies // 2, per, tall, model_width), jnp.bfloat16),
+        )
+        + (jax.ShapeDtypeStruct((copies // 2, per, tall, model_width), jnp.bfloat16),) * chunks,
         grid=(count,),
         in_specs=[
+            pl.BlockSpec(memory_space=pltpu.SMEM),
             pl.BlockSpec((total, model_width), flat, pipeline_mode=once),
             pl.BlockSpec((total, model_width), flat, pipeline_mode=once),
             pl.BlockSpec((sources, count, rows_dev), cube, pipeline_mode=once),
@@ -355,40 +382,100 @@
             pl.BlockSpec((1, hidden_units, model_width), lambda i: (i, 0, 0)),
         ],
         out_specs=[
-            pl.BlockSpec((total, model_width), flat),
-            pl.BlockSpec((total, model_width), flat),
-            pl.BlockSpec((sources, count, rows_dev), cube),
+            pl.BlockSpec((total, model_width), flat, pipeline_mode=once),
+            pl.BlockSpec((total, model_width), flat, pipeline_mode=once),
+            pl.BlockSpec((sources, count, rows_dev), cube, pipeline_mode=once),
+            pl.BlockSpec((1, copies // 2, 1, tall, model_width), part),
+        ]
+        + [
             pl.BlockSpec(
-                (1, copies, 1, tall, model_width), lambda i: (i // per, 0, i % per, 0, 0)
-            ),
+                (copies // 2, 1, tall, model_width),
+                lambda i, c=c: (0, jnp.clip(i - c * per, 0, per - 1), 0, 0),
+            )
+            for c in range(chunks)
         ],
         scratch_shapes=[
             pltpu.VMEM((sources, count * CAP, rows_dev), jnp.bfloat16),
             pltpu.VMEM((sources, count * CAP, model_width), jnp.bfloat16),
             pltpu.VMEM((sources, count * CAP, model_width), jnp.bfloat16),
         ],
-        compiler_params=pltpu.CompilerParams(vmem_limit_bytes=64 * 1000 * 1000),
+        compiler_params=pltpu.CompilerParams(vmem_limit_bytes=67 * 1000 * 1000),
         name="experts",
-    )(rows, cots, ranks, probs, w_gate_up, w_down)
+    )(place, rows, cots, ranks, probs, w_gate_up, w_down)
 
 
 def bits_of(size):
     return max(size.bit_length() - 1, 0)
 
 
-def halving(block, labels, order, last=jnp.bfloat16):
-    labels = list(labels)
-    for number, (axis, bit) in enumerate(order):
-        dim = labels.index((axis, bit))
-        mine = (lax.axis_index(axis) >> bit) & 1
-        sent = lax.dynamic_index_in_dim(block, 1 - mine, dim, keepdims=False)
-        kept = lax.dynamic_index_in_dim(block, mine, dim, keepdims=False)
-        size = lax.axis_size(axis)
-        came = lax.ppermute(sent, axis, [(i, i ^ (1 << bit)) for i in range(size)])
-        total = kept.astype(jnp.float32) + came.astype(jnp.float32)
-        block = total.astype(last if number == len(order) - 1 else jnp.bfloat16)
-        labels.pop(dim)
-    return block
+def take(block, dim, index):
+    if not isinstance(block, tuple):
+        return lax.dynamic_index_in_dim(block, index, dim, keepdims=False)
+    stack, chunk = block
+    starts = [jnp.int32(0)] * stack.ndim
+    starts[0] = jnp.int32(chunk)
+    starts[dim + 1] = index.astype(jnp.int32)
+    sizes = list(stack.shape)
+    sizes[0] = sizes[dim + 1] = 1
+    sliced = lax.dynamic_slice(stack, starts, sizes)
+    return sliced.reshape(stack.shape[1 : dim + 1] + stack.shape[dim + 2 :])
+
+
+def split(total, labels, axis, bit):
+    dim = labels.index((axis, bit))
+    mine = (lax.axis_index(axis) >> bit) & 1
+    sent = total(lambda block: take(block, dim, 1 - mine))
+    kept = total(lambda block: take(block, dim, mine))
+    return (sent, kept, labels[:dim] + labels[dim + 1 :])
+
+
+def swap(sent, axis, bit):
+    size = lax.axis_size(axis)
+    return lax.ppermute(sent, axis, [(i, i ^ (1 << bit)) for i in range(size)])
+
+
+def after(value, *others):
+    return lax.optimization_barrier((value, *others))[0]
+
+
+class Halving:
+    def __init__(self, order, labels, block=None, halves=None):
+        self.order = list(order)
+        if halves is None:
+            axis, bit = self.order[0]
+            self.sent, self.kept, self.labels = split(
+                lambda slicer: slicer(block), list(labels), axis, bit
+            )
+        else:
+            self.sent, self.kept = halves
+            self.labels = [label for label in labels if label != self.order[0]]
+
+    def send(self, *others):
+        if others:
+            self.sent = after(self.sent, *others)
+        self.came = swap(self.sent, *self.order[0])
+        return self
+
+    def add(self):
+        self.order = self.order[1:]
+        kept, came = self.kept, self.came
+
+        def total(slicer):
+            return slicer(kept).astype(jnp.float32) + slicer(came).astype(jnp.float32)
+
+        if self.order:
+            axis, bit = self.order[0]
+            self.sent, self.kept, self.labels = split(
+                lambda slicer: total(slicer).astype(jnp.bfloat16), self.labels, axis, bit
+            )
+        else:
+            self.result = total(lambda block: block)
+        return self
+
+    def rest(self):
+        while self.order:
+            self.send().add()
+        return self.result
 
 
 def on_device(
@@ -504,30 +591,38 @@
     expert_rows = lax.all_gather(normed_two_b, "ep", axis=0, tiled=True)
     expert_cots = lax.all_gather(grad_output.astype(jnp.bfloat16), "ep", axis=0, tiled=True)
     chunks = 4
-    out_sum, grad_sum, inner, grad_experts = experts(
-        expert_rows, expert_cots, ranks, prob_all, w_gate_up, w_down, n_rep, chunks
-    )
     rep_bits = [("rep", b) for b in reversed(range(bits_of(n_rep)))]
     ep_bits = [("ep", b) for b in reversed(range(bits_of(n_ep)))]
     near_first = rep_bits[::-1]
-    far_first = near_first[-2:-1] + near_first[:-2] + near_first[-1:]
+    far_bit = len(rep_bits) - 2
+    far_first = [("rep", far_bit)] + near_first[:far_bit] + near_first[-1:]
+    chunk_orders = [near_first] * (chunks - 1) + [far_first]
+    out_sum, grad_sum, inner, grad_keep, *grad_send = experts(
+        lax.axis_index("rep").astype(jnp.int32).reshape(1),
+        expert_rows,
+        expert_cots,
+        ranks,
+        prob_all,
+        w_gate_up,
+        w_down,
+        n_rep,
+        [tuple(b for _, b in order) for order in chunk_orders],
+    )
     share = model_width // n_rep
     tall = w_down.shape[1] // n_rep
-    pieces = []
+    lanes = []
+    shape = (2,) * (len(rep_bits) - 1) + grad_keep.shape[2:]
+    grad_keep = grad_keep.reshape((chunks,) + shape)
     for c in range(chunks):
-        block = grad_experts[c].reshape(
-            (2,) * len(rep_bits) + grad_experts.shape[2:]
+        lanes.append(
+            Halving(
+                chunk_orders[c],
+                chunk_orders[c],
+                halves=(grad_send[c].reshape(shape), (grad_keep, c)),
+            )
         )
-        order = far_first if c == chunks - 1 else near_first
-        pieces.append(halving(block, rep_bits, order, jnp.float32))
-    grad_experts = jnp.concatenate(pieces, 0)
-    expert_up = grad_experts[:, :share, :]
-    expert_down = (
-        grad_experts[:, share:, :]
-        .reshape(-1, tall, n_rep, share)
-        .transpose(0, 2, 1, 3)
-        .reshape(-1, tall * n_rep, share)
-    )
+    lanes[0].send()
+    lanes[3].send()
     out_back = lax.all_to_all(
         out_sum.reshape(n_ep, rows_dev, model_width), "ep", split_axis=0, concat_axis=0, tiled=True
     )
@@ -548,6 +643,21 @@
     grad_attn = (branch_scale * grad_hidden).astype(jnp.bfloat16)
     grad_out_w = dot_tn(mixed_rows, grad_attn)
     grad_mixed = dot_nt(grad_attn, full_out).astype(jnp.bfloat16)
+    first = jnp.concatenate([grad_out_w, grad_router], 1).astype(jnp.bfloat16)
+    weight_bits = ep_bits + rep_bits
+    weight_shape = (2,) * len(weight_bits) + (-1,)
+
+    def weight_lane(grad):
+        return Halving(
+            ep_bits[::-1] + near_first,
+            weight_bits,
+            block=grad.reshape(weight_shape + grad.shape[1:]),
+        )
+
+    first = weight_lane(first)
+    for _ in ep_bits[1:]:
+        first.send().add()
+    first.send()
     grad_heads = lax.all_to_all(
         grad_mixed.reshape(rows_dev, n_rep, head_width).transpose(1, 0, 2),
         "rep",
@@ -555,6 +665,10 @@
         concat_axis=0,
         tiled=True,
     ).reshape(length, head_width)
+    lanes[0].add().send()
+    lanes[1].send(lanes[0].sent)
+    lanes[3].add().send()
+    grad_heads = after(grad_heads, lanes[0].sent, lanes[1].sent, lanes[3].sent)
     grad_query, grad_key, grad_value = attend_backward(
         head_rows, grad_heads, mixed_out, totals, starts, lows, heads
     )
@@ -593,20 +707,35 @@
     grad_normed = dot_nt(grad_in_rows, full_in)
     grad_inputs_norm, grad_attn_gain = norm_back(grad_normed, inputs, factor_one, attn_gain)
     grad_inputs = grad_hidden + grad_inputs_norm
-    shape = (2,) * (len(ep_bits) + len(rep_bits)) + (-1,)
-    near = ep_bits[::-1] + near_first
-    other = ep_bits[::-1][:1] + near_first + ep_bits[::-1][1:]
-    first = jnp.concatenate([grad_out_w, grad_router], 1).astype(jnp.bfloat16)
-    first = halving(
-        first.reshape(shape + first.shape[1:]), ep_bits + rep_bits, near, jnp.float32
-    )
-    query_grad = grad_w_query.astype(jnp.bfloat16)
-    query_grad = halving(
-        query_grad.reshape(shape + query_grad.shape[1:]), ep_bits + rep_bits, near, jnp.float32
-    )
-    rest_grad = grad_w_rest.astype(jnp.bfloat16)
-    rest_grad = halving(
-        rest_grad.reshape(shape + rest_grad.shape[1:]), ep_bits + rep_bits, other, jnp.float32
+    query_lane = weight_lane(grad_w_query.astype(jnp.bfloat16))
+    rest_lane = weight_lane(grad_w_rest.astype(jnp.bfloat16))
+    for lane in (query_lane, rest_lane):
+        for _ in ep_bits:
+            lane.send().add()
+    first.add()
+    joint = Halving(
+        near_first,
+        rep_bits,
+        halves=tuple(
+            jnp.concatenate([query, rest, own], -1)
+            for query, rest, own in zip(
+                (query_lane.sent, query_lane.kept),
+                (rest_lane.sent, rest_lane.kept),
+                (first.sent, first.kept),
+            )
+        ),
+    )
+    weights = joint.rest()
+    lanes[0].add().send()
+    lanes[1].add().send()
+    lanes[2].send(lanes[1].sent)
+    grad_experts = jnp.concatenate([lane.add().rest() for lane in lanes], 0)
+    expert_up = grad_experts[:, :share, :]
+    expert_down = (
+        grad_experts[:, share:, :]
+        .reshape(-1, tall, n_rep, share)
+        .transpose(0, 2, 1, 3)
+        .reshape(-1, tall * n_rep, share)
     )
     everything = n_ep * n_rep
     gains = jnp.concatenate(
@@ -620,12 +749,12 @@
         output[None],
         grad_inputs[None],
         gains[:part],
-        query_grad,
-        rest_grad[:, :key_width],
-        rest_grad[:, key_width:],
-        first[:, :model_width],
+        weights[:, :query_width],
+        weights[:, query_width:rotated_width],
+        weights[:, rotated_width:input_width],
+        weights[:, input_width : input_width + model_width],
         gains[part:],
-        first[:, model_width:],
+        weights[:, input_width + model_width :],
         expert_up,
         expert_down,
     )

time: 831 us -> 786 us (0.946)
  local copies, waits for them, and re-layouts: 116 us -> 61.3 us
  blocking collectives: 46.1 us -> 75.5 us
  waiting for transfers between devices: 399 us -> 372 us
  other arithmetic: 56.4 us -> 71.5 us
  starting transfers between devices: 61.7 us -> 50.2 us
    ppermute x27 -> x21, waiting for transfers between devices: 271 us -> 227 us  [swap(): return lax.ppermute(sent, axis, [(i, i ^ 1 << bit) for i in range(size)])]
    all_to_all x1, waiting for transfers between devices: 10.5 us -> 49 us  [on_device(): lax.all_to_all(gains, everyone, split_axis=0, concat_axis=0, tiled=True)]
    all_to_all x1, waiting for transfers between devices: 37 us -> 0.01 us  [on_device(): lax.all_to_all(grad_mixed.reshape(rows_dev, n_rep, head_width).transpose(...]
    all_to_all x0 -> x1, blocking collectives: none -> 29.6 us  [on_device(): lax.all_to_all(grad_sum.reshape(n_ep, rows_dev, model_width), 'ep', split...]
    dynamic_slice x12 -> x2, local copies, waits for them, and re-layouts: 30.9 us -> 1.53 us  [take(): return lax.dynamic_index_in_dim(block, index, dim, keepdims=False)]
    slice x4 -> x3, local copies, waits for them, and re-layouts: 21.6 us -> 1.98 us  [the longest x1 0.72 us: on_device(): weights[:, input_width:input_width + model_width]]
    all_to_all x1, waiting for transfers between devices: 1.96 us -> 17.1 us  [on_device(): lax.all_to_all(out_sum.reshape(n_ep, rows_dev, model_width), 'ep', split_...]
    convert_element_type x20 -> x17, other arithmetic: 27.3 us -> 39.7 us  [add(): total(slicer).astype(jnp.bfloat16)]
  transfers between devices with their start and end apart: 36 -> 29, of which waited for: 19 -> 14; matrix products, arithmetic and copies ran while one was open for 21% -> 16% of each run, Pallas kernels for 6% -> 6%
where the time goes in v3:
time: 786 us; the launch traced here: 770 us
  waiting for transfers between devices  372 us (47%)
  Pallas kernels  105 us (13%)
  blocking collectives  75.5 us (10%)
  other arithmetic  71.5 us (9%)
  local copies, waits for them, and re-layouts  61.3 us (8%)
  starting transfers between devices  50.2 us (6%)
  matrix products  18.1 us (2%)
  between operations  16.6 us (2%)
    ppermute x21, waiting for transfers between devices, swap(): return lax.ppermute(sent, axis, [(i, i ^ 1 << bit) for i in range(size)])  227 us
    pallas_call x1, Pallas kernels, experts(): pl.pallas_call(functools.partial(experts_kernel, sources=sources, rows_de...  56.3 us
    all_to_all x1, waiting for transfers between devices, on_device(): lax.all_to_all(gains, everyone, split_axis=0, concat_axis=0, tiled=True)  49 us
    all_gather x1, waiting for transfers between devices, on_device(): full = lax.all_gather(joined, everyone, axis=0, tiled=True)  41.3 us
    convert_element_type x17, other arithmetic, add(): total(slicer).astype(jnp.bfloat16)  39.7 us
    all_to_all x1, blocking collectives, on_device(): lax.all_to_all(grad_sum.reshape(n_ep, rows_dev, model_width), 'ep', split...  29.6 us
    pallas_call x1, Pallas kernels, attend_backward(): pl.pallas_call(functools.partial(attend_backward_kernel, heads=heads), ou...  26.7 us
    all_to_all x1, waiting for transfers between devices, on_device(): lax.all_to_all(sending, 'rep', split_axis=0, concat_axis=0, tiled=True)  23.3 us
  transfers between devices with their start and end apart: 29, of which 14 were waited for; matrix products, arithmetic and copies ran while one was open for 16% of the time, Pallas kernels for 6%

profile of v3, /device:TPU:26, one launch (start us, length us, event | category | flops | bytes accessed | tf_op | source)
XLA Modules:
  0.0 770.0 jit_solution(16983787876096975153)
XLA Ops:
  12.7 16.3 %all-gather = s32[1,2048]{1,0:T(1,128)S(1)} all-gather(s32[1,256]{1,0:T(1,128)} %param.14), channel_id=2, replica_groups=mesh['ep'=4,'rep'=8] {'rep'}, dimensions={1}, use_global_device_ids=true | all-gather | bytes 9216 | tf_op jit(solution)/shard_map/all_gather | solution.py:512
  41.1 41.3 %all-gather.5.cloned.1.call-done = bf16[1024,3104]{1,0:T(8,128)(2,1)} async-done(((bf16[32,3104]{1,0:T(8,128)(2,1)}), bf16[1024,3104]{1,0:T(8,128)(2,1)}) %all-gather.5.cloned.1.call-update) | async-done | bytes 6357008 | tf_op jit(solution)/shard_map/all_gather | solution.py:534
  82.4 3.5 fusion.2
  90.6 5.6 all-to-all-start
  97.8 23.3 %all-to-all-done = bf16[8,256,256]{2,1,0:T(8,128)(2,1)S(1)} async-done(((bf16[8,256,256]{2,1,0:T(8,128)(2,1)}), bf16[8,256,256]{2,1,0:T(8,128)(2,1)S(1)}, u32[]{:S(2)}, u32[]{:S(2)}) %all-to-all-start) | async-done | bytes 1048608 | tf_op jit(solution)/shard_map/all_to_all | solution.py:558
  122.1 21.7 %attend_forward.1 = (bf16[2048,128]{1,0:T(8,128)(2,1)}, f32[128,2048]{1,0:T(8,128)}, f32[8,2,256]{2,1,0:T(2,128)}) custom-call(s32[8]{0:T(128)} %and_select_fusion.low_ref, bf16[2048,256]{1,0:T(8,128)(2,1)} %bitcast.327, s32[8,1,256]{2,1,0:T(1,128)} %bitcast.361), custom_call_target="tpu_custom_call" | custom-call | tf_op jit(solution)/shard_map/attend_forward/pallas_call | solution.py:119
  145.0 17.1 %all_to_all.49 = bf16[8,256,128]{1,2,0:T(8,128)(2,1)S(1)} all-to-all(bf16[8,256,128]{1,2,0:T(8,128)(2,1)S(1)} %copy.113), channel_id=1, replica_groups=mesh['ep'=4,'rep'=8] {'rep'}, dimensions={0} | all-to-all | bytes 1048576 | tf_op jit(solution)/shard_map/all_to_all | solution.py:561
  168.9 5.8 all_to_all.50
  175.3 14.3 %all-gather.7.cloned.1.call-done.rows_ref = bf16[1024,1024]{1,0:T(8,128)(2,1)} async-done(((bf16[256,1024]{1,0:T(8,128)(2,1)}), bf16[1024,1024]{1,0:T(8,128)(2,1)}) %all-gather.7.cloned.1.call-update) | async-done | bytes 2097168 | tf_op jit(solution)/shard_map/all_gather | solution.py:591
  189.6 56.3 %experts.1 = (bf16[1024,1024]{1,0:T(8,128)(2,1)}, bf16[1024,1024]{1,0:T(8,128)(2,1)}, f32[4,8,256]{2,1,0:T(8,128)}, bf16[4,4,2,192,1024]{4,3,2,1,0:T(8,128)(2,1)...) custom-call(s32[1]{0:T(128)} %bitcast.12.place_ref, ...), custom_call_target="tpu_custom_call" | custom-call | tf_op jit(solution)/shard_map/experts/pallas_call | solution.py:357
  245.9 6.6 all_to_all.51
  252.5 29.6 %all_to_all.52 = bf16[4,256,1024]{2,1,0:T(8,128)(2,1)S(1)} all-to-all(bf16[4,256,1024]{2,1,0:T(8,128)(2,1)} %bitcast.350), channel_id=1, replica_groups=mesh['ep'=4,'rep'=8] {'ep'}, dimensions={0} | all-to-all | bytes 4194304 | tf_op jit(solution)/shard_map/all_to_all | solution.py:629
  282.2 6.6 all-to-all-start.3
  295.8 17.1 %all-to-all-done.3 = bf16[4,256,1024]{2,1,0:T(8,128)(2,1)} async-done(((bf16[4,256,1024]{2,1,0:T(8,128)(2,1)}), bf16[4,256,1024]{2,1,0:T(8,128)(2,1)}, u32[]{:S(2)}, u32[]{:S(2)}) %all-to-all-start.3) | async-done | bytes 2097184 | tf_op jit(solution)/shard_map/all_to_all | solution.py:626
  321.6 6.0 all-to-all-start.6
  331.1 30.3 %collective-permute-done = bf16[2,2,2,192,1024]{4,3,2,1,0:T(8,128)(2,1)} collective-permute-done((bf16[2,2,2,192,1024]{4,3,2,1,0:T(8,128)(2,1)}, bf16[2,2,2,192,1024]{4,3,2,1,0:T(8,128)(2,1)}, u32[]{:S(2)}, u32[]{:S(2)}) %collective-permute-start) | collective-permute-done | bytes 3145760 | tf_op jit(solution)/shard_map/ppermute | solution.py:434
  361.4 5.8 collective-permute-done.1
  367.2 9.9 %fusion.9 = (bf16[2,2,192,1024]{3,2,1,0:T(8,128)(2,1)}, bf16[2,2,192,1024]{3,2,1,0:T(8,128)(2,1)}, bf16[2,2,192,1024]{3,2,1,0:T(8,128)(2,1)}, bf16[2,2,192,1024]{3,2,1,0:T(8,128)(2,1)}) fusion(bf16[2,2,2,192,1024]{4,3,2,1,0:T(8,128)(2,1)} %collective-permute-done, s32[]{:T(128)S(6)} %select_n.172, bf16[4,2,2,2,192,1024]{5,4,3,2,1,0:T(8,128)(2,1)} %bitcast.322, ...), kind=kLoop, calls=%fused_computation.22 | loop fusion | flops 12582912 | bytes 18874384 | tf_op jit(solution)/shard_map/convert_element_type | solution.py:469
  379.2 26.7 %attend_backward.1 = (f32[2048,128]{1,0:T(8,128)}, f32[2048,64]{1,0:T(8,128)}, f32[2048,64]{1,0:T(8,128)}) custom-call(s32[8]{0:T(128)} %and_select_fusion.low_ref, bf16[2048,256]{1,0:T(8,128)(2,1)} %bitcast.328, bf16[2048,128]{1,0:T(8,128)(2,1)} %bitcast.26.grad_ref, f32[128,2048]{1,0:T(8,128)} %get-tuple-element.38.out_ref, ...), custom_call_target="tpu_custom_call" | custom-call | tf_op jit(solution)/shard_map/attend_backward/pallas_call | solution.py:218
  426.5 4.9 fusion.17
  436.7 5.3 all-to-all-start.7
  446.1 9.9 %collective-permute-done.7 = bf16[2,2,2,32,1056]{4,3,2,1,0:T(8,128)(2,1)} collective-permute-done((bf16[2,2,2,32,1056]{4,3,2,1,0:T(8,128)(2,1)}, bf16[2,2,2,32,1056]{4,3,2,1,0:T(8,128)(2,1)}, u32[]{:S(2)}, u32[]{:S(2)}) %collective-permute-start.7) | collective-permute-done | bytes 540704 | tf_op jit(solution)/shard_map/ppermute | solution.py:434
  461.6 45.3 %collective-permute-done.11 = bf16[2,2,192,1024]{3,2,1,0:T(8,128)(2,1)} collective-permute-done((bf16[2,2,192,1024]{3,2,1,0:T(8,128)(2,1)}, bf16[2,2,192,1024]{3,2,1,0:T(8,128)(2,1)}, u32[]{:S(2)}, u32[]{:S(2)}) %collective-permute-start.11) | collective-permute-done | bytes 1572896 | tf_op jit(solution)/shard_map/ppermute | solution.py:434
  517.0 6.3 fusion.8
  537.0 5.7 all-to-all-start.8
  545.2 49.0 %all-to-all-done.8 = f32[32,1,64]{2,1,0:T(1,128)S(1)} async-done(((f32[32,1,64]{2,1,0:T(1,128)}), f32[32,1,64]{2,1,0:T(1,128)S(1)}, u32[]{:S(2)}, u32[]{:S(2)}) %all-to-all-start.8) | async-done | bytes 8224 | tf_op jit(solution)/shard_map/all_to_all | solution.py:745
  601.3 4.4 fusion.6
  605.9 11.3 %collective-permute-done.8 = bf16[2,2,32,3104]{3,2,1,0:T(8,128)(2,1)S(1)} collective-permute-done((bf16[2,2,32,3104]{3,2,1,0:T(8,128)(2,1)S(1)}, bf16[2,2,32,3104]{3,2,1,0:T(8,128)(2,1)S(1)}, u32[]{:S(2)}, u32[]{:S(2)}) %collective-permute-start.8) | collective-permute-done | bytes 794656 | tf_op jit(solution)/shard_map/ppermute | solution.py:434
  623.4 54.7 %collective-permute-done.9 = bf16[2,32,3104]{2,1,0:T(8,128)(2,1)S(1)} collective-permute-done((bf16[2,32,3104]{2,1,0:T(8,128)(2,1)S(1)}, bf16[2,32,3104]{2,1,0:T(8,128)(2,1)S(1)}, u32[]{:S(2)}, u32[]{:S(2)}) %collective-permute-start.9) | collective-permute-done | bytes 397344 | tf_op jit(solution)/shard_map/ppermute | solution.py:434
  684.6 39.8 %collective-permute-done.10 = bf16[32,3104]{1,0:T(8,128)(2,1)S(1)} collective-permute-done((bf16[32,3104]{1,0:T(8,128)(2,1)S(1)}, bf16[32,3104]{1,0:T(8,128)(2,1)S(1)}, u32[]{:S(2)}, u32[]{:S(2)}) %collective-permute-start.10) | collective-permute-done | bytes 198688 | tf_op jit(solution)/shard_map/ppermute | solution.py:434
  726.5 14.8 %collective-permute-done.15 = bf16[2,192,1024]{2,1,0:T(8,128)(2,1)S(1)} collective-permute-done((bf16[2,192,1024]{2,1,0:T(8,128)(2,1)S(1)}, bf16[2,192,1024]{2,1,0:T(8,128)(2,1)S(1)}, u32[]{:S(2)}, u32[]{:S(2)}) %collective-permute-start.15) | collective-permute-done | bytes 786464 | tf_op jit(solution)/shard_map/ppermute | solution.py:434
  741.7 15.3 %collective-permute-done.18 = bf16[2,192,1024]{2,1,0:T(8,128)(2,1)S(1)} collective-permute-done((bf16[2,192,1024]{2,1,0:T(8,128)(2,1)S(1)}, bf16[2,192,1024]{2,1,0:T(8,128)(2,1)S(1)}, u32[]{:S(2)}, u32[]{:S(2)}) %collective-permute-start.18) | collective-permute-done | bytes 786464 | tf_op jit(solution)/shard_map/ppermute | solution.py:434
  (258 shorter events, 142.9 us)
Async XLA Ops:
  8.0 74.4 %all-gather.5.cloned.1.call-start = ((), (), s32[]{:S(2)}) async-start(), calls=%async_computation.9 | async-start | bytes 6758400 | tf_op jit(solution)/shard_map/all_gather | solution.py:534
  30.8 66.4 %copy-start.29 = (s32[2048]{0:T(1024)}, s32[2048]{0:T(1024)S(1)}, u32[]{:S(2)}) copy-start(s32[2048]{0:T(1024)S(1)} %convert_reduce_fusion) | copy-start | bytes 24580
  90.6 30.5 %all-to-all-start = ((bf16[8,256,256]{2,1,0:T(8,128)(2,1)}), bf16[8,256,256]{2,1,0:T(8,128)(2,1)S(1)}, u32[]{:S(2)}, u32[]{:S(2)}) async-start(bf16[8,256,256]{2,1,0:T(8,128)(2,1)} %maximum_bitcast_fusion.1), calls=%async_computation | async-start | bytes 2097152 | tf_op jit(solution)/shard_map/all_to_all | solution.py:558
  96.2 79.1 %all-gather.9.cloned.1.call-start = ((), (), s32[]{:S(2)}) async-start(), calls=%async_computation.11 | async-start | bytes 2621440 | tf_op jit(solution)/shard_map/all_gather | solution.py:592
  97.1 92.5 %all-gather.7.cloned.1.call-start = ((), (), s32[]{:S(2)}) async-start(), calls=%async_computation.10 | async-start | bytes 2621440 | tf_op jit(solution)/shard_map/all_gather | solution.py:591
  282.2 30.7 %all-to-all-start.3 = ((bf16[4,256,1024]{2,1,0:T(8,128)(2,1)}), bf16[4,256,1024]{2,1,0:T(8,128)(2,1)}, u32[]{:S(2)}, u32[]{:S(2)}) async-start(bf16[4,256,1024]{2,1,0:T(8,128)(2,1)} %bitcast.349), calls=%async_computation.3 | async-start | bytes 4194304 | tf_op jit(solution)/shard_map/all_to_all | solution.py:626
  288.8 72.6 %collective-permute-start = (bf16[2,2,2,192,1024]{4,3,2,1,0:T(8,128)(2,1)}, bf16[2,2,2,192,1024]{4,3,2,1,0:T(8,128)(2,1)}, u32[]{:S(2)}, u32[]{:S(2)}) collective-permute-start(bf16[2,2,2,192,1024]{4,3,2,1,0:T(8,128)(2,1)} %bitcast.366), channel_id=1, source_target_pairs={{0,1},{1,0},{2,3},{3,2},{4,5},{5,4},{6,7},{7,6},{8,9},{9,8},{10,11... | collective-permute-start | bytes 9437192 | tf_op jit(solution)/shard_map/ppermute | solution.py:434
  290.3 76.9 %collective-permute-start.1 = (bf16[2,2,2,192,1024]{4,3,2,1,0:T(8,128)(2,1)}, bf16[2,2,2,192,1024]{4,3,2,1,0:T(8,128)(2,1)}, u32[]{:S(2)}, u32[]{:S(2)}) collective-permute-start(bf16[2,2,2,192,1024]{4,3,2,1,0:T(8,128)(2,1)} %bitcast.365), channel_id=1, source_target_pairs={{0,2},{1,3},{2,0},{3,1},{4,6},{5,7},{6,4},{7,5},{8,10},{9,11},{10,... | collective-permute-start | bytes 9437192 | tf_op jit(solution)/shard_map/ppermute | solution.py:434
  321.6 57.5 %all-to-all-start.6 = ((bf16[8,256,128]{2,1,0:T(8,128)(2,1)}), bf16[8,256,128]{2,1,0:T(8,128)(2,1)}, u32[]{:S(2)}, u32[]{:S(2)}) async-start(bf16[8,256,128]{2,1,0:T(8,128)(2,1)} %bitcast.320), calls=%async_computation.6 | async-start | bytes 1048576 | tf_op jit(solution)/shard_map/all_to_all | solution.py:661
  331.1 111.6 %collective-permute-start.6 = (bf16[2,2,2,2,32,1056]{5,4,2,1,3,0:T(8,128)(2,1)}, bf16[2,2,2,2,32,1056]{5,4,2,1,3,0:T(8,128)(2,1)}, u32[]{:S(2)}, u32[]{:S(2)}) collective-permute-start(bf16[2,2,2,2,32,1056]{5,4,2,1,3,0:T(8,128)(2,1)} %copy_bitcast_fusion.1), channel_id=1, source_target_pairs={{0,8},{8,0},{16,24},{24,16},{1,9},{9,1},{17,25},{25,17},{2,10},{10... | collective-permute-start | bytes 3244040 | tf_op jit(solution)/shard_map/ppermute | solution.py:434
  377.1 81.8 %collective-permute-start.19 = (bf16[2,2,192,1024]{3,2,1,0:T(8,128)(2,1)}, bf16[2,2,192,1024]{3,2,1,0:T(8,128)(2,1)}, u32[]{:S(2)}, u32[]{:S(2)}) collective-permute-start(bf16[2,2,192,1024]{3,2,1,0:T(8,128)(2,1)} %get-tuple-element.59), channel_id=1, source_target_pairs={{0,1},{1,0},{2,3},{3,2},{4,5},{5,4},{6,7},{7,6},{8,9},{9,8},{10,11... | collective-permute-start | bytes 4718600 | tf_op jit(solution)/shard_map/ppermute | solution.py:434
  377.7 139.3 %collective-permute-start.13 = (bf16[2,2,2,192,1024]{4,3,2,1,0:T(8,128)(2,1)}, bf16[2,2,2,192,1024]{4,3,2,1,0:T(8,128)(2,1)}, u32[]{:S(2)}, u32[]{:S(2)}) collective-permute-start(bf16[2,2,2,192,1024]{4,3,2,1,0:T(8,128)(2,1)} %bitcast.31), channel_id=1, source_target_pairs={{0,1},{1,0},{2,3},{3,2},{4,5},{5,4},{6,7},{7,6},{8,9},{9,8},{10,11... | collective-permute-start | bytes 9437192 | tf_op jit(solution)/shard_map/ppermute | solution.py:434
  436.7 72.5 %all-to-all-start.7 = ((bf16[8,256,256]{1,2,0:T(8,128)(2,1)}), bf16[8,256,256]{1,2,0:T(8,128)(2,1)}, u32[]{:S(2)}, u32[]{:S(2)}) async-start(bf16[8,256,256]{1,2,0:T(8,128)(2,1)} %copy.122), calls=%async_computation.7 | async-start | bytes 2097152 | tf_op jit(solution)/shard_map/all_to_all | solution.py:680
  442.1 64.8 %collective-permute-start.11 = (bf16[2,2,192,1024]{3,2,1,0:T(8,128)(2,1)}, bf16[2,2,192,1024]{3,2,1,0:T(8,128)(2,1)}, u32[]{:S(2)}, u32[]{:S(2)}) collective-permute-start(bf16[2,2,192,1024]{3,2,1,0:T(8,128)(2,1)} %get-tuple-element.52), channel_id=1, source_target_pairs={{0,2},{1,3},{2,0},{3,1},{4,6},{5,7},{6,4},{7,5},{8,10},{9,11},{10,... | collective-permute-start | bytes 4718600 | tf_op jit(solution)/shard_map/ppermute | solution.py:434
  444.7 11.3 %collective-permute-start.7 = (bf16[2,2,2,32,1056]{4,3,2,1,0:T(8,128)(2,1)}, bf16[2,2,2,32,1056]{4,3,2,1,0:T(8,128)(2,1)}, u32[]{:S(2)}, u32[]{:S(2)}) collective-permute-start(bf16[2,2,2,32,1056]{4,3,2,1,0:T(8,128)(2,1)} %fusion.34), channel_id=1, source_target_pairs={{0,16},{8,24},{16,0},{24,8},{1,17},{9,25},{17,1},{25,9},{2,18},{10... | collective-permute-start | bytes 1622024 | tf_op jit(solution)/shard_map/ppermute | solution.py:434
  457.8 49.1 %copy-start.10 = (bf16[2,2,192,1024]{3,2,1,0:T(8,128)(2,1)S(1)}, bf16[2,2,192,1024]{3,2,1,0:T(8,128)(2,1)}, u32[]{:S(2)}) copy-start(bf16[2,2,192,1024]{3,2,1,0:T(8,128)(2,1)} %get-tuple-element.51) | copy-start | bytes 4718596
  461.3 158.4 %collective-permute-start.20 = (bf16[2,192,1024]{2,1,0:T(8,128)(2,1)}, bf16[2,192,1024]{2,1,0:T(8,128)(2,1)}, u32[]{:S(2)}, u32[]{:S(2)}) collective-permute-start(bf16[2,192,1024]{2,1,0:T(8,128)(2,1)} %fusion.62), channel_id=1, source_target_pairs={{0,4},{1,5},{2,6},{3,7},{4,0},{5,1},{6,2},{7,3},{8,12},{9,13},{10,... | collective-permute-start | bytes 2359304 | tf_op jit(solution)/shard_map/ppermute | solution.py:434
  509.2 112.2 %collective-permute-start.12 = (bf16[2,192,1024]{2,1,0:T(8,128)(2,1)}, bf16[2,192,1024]{2,1,0:T(8,128)(2,1)}, u32[]{:S(2)}, u32[]{:S(2)}) collective-permute-start(bf16[2,192,1024]{2,1,0:T(8,128)(2,1)} %fusion.56), channel_id=1, source_target_pairs={{0,4},{1,5},{2,6},{3,7},{4,0},{5,1},{6,2},{7,3},{8,12},{9,13},{10,... | collective-permute-start | bytes 2359304 | tf_op jit(solution)/shard_map/ppermute | solution.py:434
  512.5 16.9 %collective-permute-start.4 = (bf16[2,2,2,2,32,1024]{5,4,2,1,3,0:T(8,128)(2,1)S(1)}, bf16[2,2,2,2,32,1024]{5,4,2,1,3,0:T(8,128)(2,1)}, u32[]{:S(2)}, u32[]{:S(2)}) collective-permute-start(bf16[2,2,2,2,32,1024]{5,4,2,1,3,0:T(8,128)(2,1)S(1)} %copy_bitcast_fusion.2), channel_id=1, source_target_pairs={{0,8},{8,0},{16,24},{24,16},{1,9},{9,1},{17,25},{25,17},{2,10},{10... | collective-permute-start | bytes 3145736 | tf_op jit(solution)/shard_map/ppermute | solution.py:434
  517.0 16.2 %collective-permute-start.2 = (bf16[2,2,2,2,32,1024]{5,4,2,1,3,0:T(8,128)(2,1)}, bf16[2,2,2,2,32,1024]{5,4,2,1,3,0:T(8,128)(2,1)}, u32[]{:S(2)}, u32[]{:S(2)}) collective-permute-start(bf16[2,2,2,2,32,1024]{5,4,2,1,3,0:T(8,128)(2,1)} %copy_bitcast_fusion.3), channel_id=1, source_target_pairs={{0,8},{8,0},{16,24},{24,16},{1,9},{9,1},{17,25},{25,17},{2,10},{10... | collective-permute-start | bytes 3145736 | tf_op jit(solution)/shard_map/ppermute | solution.py:434
  523.3 78.0 %collective-permute-start.16 = (bf16[2,2,2,192,1024]{4,3,2,1,0:T(8,128)(2,1)}, bf16[2,2,2,192,1024]{4,3,2,1,0:T(8,128)(2,1)}, u32[]{:S(2)}, u32[]{:S(2)}) collective-permute-start(bf16[2,2,2,192,1024]{4,3,2,1,0:T(8,128)(2,1)} %bitcast.95), channel_id=1, source_target_pairs={{0,1},{1,0},{2,3},{3,2},{4,5},{5,4},{6,7},{7,6},{8,9},{9,8},{10,11... | collective-permute-start | bytes 9437192 | tf_op jit(solution)/shard_map/ppermute | solution.py:434
  531.9 62.3 %collective-permute-start.5 = (bf16[2,2,2,32,1024]{4,3,1,0,2:T(8,128)(2,1)}, bf16[2,2,2,32,1024]{4,3,1,0,2:T(8,128)(2,1)}, u32[]{:S(2)}, u32[]{:S(2)}) collective-permute-start(bf16[2,2,2,32,1024]{4,3,1,0,2:T(8,128)(2,1)} %get-tuple-element.80), channel_id=1, source_target_pairs={{0,16},{8,24},{16,0},{24,8},{1,17},{9,25},{17,1},{25,9},{2,18},{10... | collective-permute-start | bytes 1572872 | tf_op jit(solution)/shard_map/ppermute | solution.py:434
  535.5 60.0 %collective-permute-start.3 = (bf16[2,2,2,32,1024]{4,3,1,0,2:T(8,128)(2,1)}, bf16[2,2,2,32,1024]{4,3,1,0,2:T(8,128)(2,1)}, u32[]{:S(2)}, u32[]{:S(2)}) collective-permute-start(bf16[2,2,2,32,1024]{4,3,1,0,2:T(8,128)(2,1)} %get-tuple-element.78), channel_id=1, source_target_pairs={{0,16},{8,24},{16,0},{24,8},{1,17},{9,25},{17,1},{25,9},{2,18},{10... | collective-permute-start | bytes 1572872 | tf_op jit(solution)/shard_map/ppermute | solution.py:434
  537.0 57.2 %all-to-all-start.8 = ((f32[32,1,64]{2,1,0:T(1,128)}), f32[32,1,64]{2,1,0:T(1,128)S(1)}, u32[]{:S(2)}, u32[]{:S(2)}) async-start(f32[32,1,64]{2,1,0:T(1,128)} %bitcast.47), calls=%async_computation.8 | async-start | bytes 32768 | tf_op jit(solution)/shard_map/all_to_all | solution.py:745
  596.9 20.3 %collective-permute-start.8 = (bf16[2,2,32,3104]{3,2,1,0:T(8,128)(2,1)S(1)}, bf16[2,2,32,3104]{3,2,1,0:T(8,128)(2,1)S(1)}, u32[]{:S(2)}, u32[]{:S(2)}) collective-permute-start(bf16[2,2,32,3104]{3,2,1,0:T(8,128)(2,1)S(1)} %pad_maximum_fusion.3), channel_id=1, source_target_pairs={{0,1},{1,0},{2,3},{3,2},{4,5},{5,4},{6,7},{7,6},{8,9},{9,8},{10,11... | collective-permute-start | bytes 2383880 | tf_op jit(solution)/shard_map/ppermute | solution.py:434
  599.3 81.6 %collective-permute-start.14 = (bf16[2,2,192,1024]{3,2,1,0:T(8,128)(2,1)S(1)}, bf16[2,2,192,1024]{3,2,1,0:T(8,128)(2,1)S(1)}, u32[]{:S(2)}, u32[]{:S(2)}) collective-permute-start(bf16[2,2,192,1024]{3,2,1,0:T(8,128)(2,1)S(1)} %copy-done.25), channel_id=1, source_target_pairs={{0,2},{1,3},{2,0},{3,1},{4,6},{5,7},{6,4},{7,5},{8,10},{9,11},{10,... | collective-permute-start | bytes 4718600 | tf_op jit(solution)/shard_map/ppermute | solution.py:434
  605.7 75.8 %collective-permute-start.17 = (bf16[2,2,192,1024]{3,2,1,0:T(8,128)(2,1)S(1)}, bf16[2,2,192,1024]{3,2,1,0:T(8,128)(2,1)S(1)}, u32[]{:S(2)}, u32[]{:S(2)}) collective-permute-start(bf16[2,2,192,1024]{3,2,1,0:T(8,128)(2,1)S(1)} %get-tuple-element.56), channel_id=1, source_target_pairs={{0,2},{1,3},{2,0},{3,1},{4,6},{5,7},{6,4},{7,5},{8,10},{9,11},{10,... | collective-permute-start | bytes 4718600 | tf_op jit(solution)/shard_map/ppermute | solution.py:434
  617.5 60.6 %collective-permute-start.9 = (bf16[2,32,3104]{2,1,0:T(8,128)(2,1)S(1)}, bf16[2,32,3104]{2,1,0:T(8,128)(2,1)S(1)}, u32[]{:S(2)}, u32[]{:S(2)}) collective-permute-start(bf16[2,32,3104]{2,1,0:T(8,128)(2,1)S(1)} %get-tuple-element.72), channel_id=1, source_target_pairs={{0,2},{1,3},{2,0},{3,1},{4,6},{5,7},{6,4},{7,5},{8,10},{9,11},{10,... | collective-permute-start | bytes 1191944 | tf_op jit(solution)/shard_map/ppermute | solution.py:434
  621.5 59.4 %copy-start.14 = (bf16[2,2,192,1024]{3,2,1,0:T(8,128)(2,1)S(1)}, bf16[2,2,192,1024]{3,2,1,0:T(8,128)(2,1)}, u32[]{:S(2)}) copy-start(bf16[2,2,192,1024]{3,2,1,0:T(8,128)(2,1)} %get-tuple-element.53) | copy-start | bytes 4718596
  678.1 46.3 %collective-permute-start.10 = (bf16[32,3104]{1,0:T(8,128)(2,1)S(1)}, bf16[32,3104]{1,0:T(8,128)(2,1)S(1)}, u32[]{:S(2)}, u32[]{:S(2)}) collective-permute-start(bf16[32,3104]{1,0:T(8,128)(2,1)S(1)} %fusion.89), channel_id=1, source_target_pairs={{0,4},{1,5},{2,6},{3,7},{4,0},{5,1},{6,2},{7,3},{8,12},{9,13},{10,... | collective-permute-start | bytes 595976 | tf_op jit(solution)/shard_map/ppermute | solution.py:434
  681.2 60.0 %collective-permute-start.15 = (bf16[2,192,1024]{2,1,0:T(8,128)(2,1)S(1)}, bf16[2,192,1024]{2,1,0:T(8,128)(2,1)S(1)}, u32[]{:S(2)}, u32[]{:S(2)}) collective-permute-start(bf16[2,192,1024]{2,1,0:T(8,128)(2,1)S(1)} %fusion.58), channel_id=1, source_target_pairs={{0,4},{1,5},{2,6},{3,7},{4,0},{5,1},{6,2},{7,3},{8,12},{9,13},{10,... | collective-permute-start | bytes 2359304 | tf_op jit(solution)/shard_map/ppermute | solution.py:434
  681.8 75.1 %collective-permute-start.18 = (bf16[2,192,1024]{2,1,0:T(8,128)(2,1)S(1)}, bf16[2,192,1024]{2,1,0:T(8,128)(2,1)S(1)}, u32[]{:S(2)}, u32[]{:S(2)}) collective-permute-start(bf16[2,192,1024]{2,1,0:T(8,128)(2,1)S(1)} %fusion.60), channel_id=1, source_target_pairs={{0,4},{1,5},{2,6},{3,7},{4,0},{5,1},{6,2},{7,3},{8,12},{9,13},{10,... | collective-permute-start | bytes 2359304 | tf_op jit(solution)/shard_map/ppermute | solution.py:434
  (45 other events, 309.5 us)
Sparse Core Ops, SparseCore 0:
  12.8 69.5 all-gather.4
Sparse Core Ops, SparseCore 1:
  98.8 22.4 all-gather.8
  166.9 22.7 all-gather.6

commit v4 on v1

--- a/solution.py
+++ b/solution.py
@@ -247,6 +247,7 @@
 
 
 def experts_kernel(
+    place_ref,
     rows_ref,
     cot_ref,
     rank_ref,
@@ -256,16 +257,16 @@
     out_ref,
     grad_ref,
     inner_ref,
-    grad_gate_up_ref,
-    grad_down_ref,
-    picks_s,
-    out_s,
-    grad_s,
-    *,
+    keep_ref,
+    *others,
     sources,
     rows_dev,
     count,
+    copies,
+    groups,
 ):
+    send_refs = others[:-3]
+    picks_s, out_s, grad_s = others[-3:]
     step = pl.program_id(0)
     slots = pl.ds(pl.multiple_of(step * CAP, 16), CAP)
     numbers = lax.broadcasted_iota(jnp.int32, (CAP, rows_dev), 0).astype(jnp.float32)
@@ -296,11 +297,39 @@
     sent_out = (weight * produced).astype(jnp.bfloat16)
     grad_out = (weight * grad_mix).astype(jnp.bfloat16)
     grad_active = dot_nt(grad_out, down)
-    grad_down_ref[0] = dot_tn(active, grad_out).astype(grad_down_ref.dtype)
+    grad_down = dot_tn(active, grad_out).astype(keep_ref.dtype)
     grad_gate = grad_active * up_part * sigmoid_gate * (1.0 + gate_part * (1.0 - sigmoid_gate))
     grad_up = grad_active * gate_part * sigmoid_gate
     grad_both = jnp.concatenate([grad_gate, grad_up], 1).astype(jnp.bfloat16)
-    grad_gate_up_ref[0] = dot_tn(arrived, grad_both).astype(grad_gate_up_ref.dtype)
+    grad_gate_up = dot_tn(arrived, grad_both).astype(keep_ref.dtype)
+    share = grad_down.shape[1] // copies
+    tall = hidden_units // copies
+
+    def put(order, mine, send_ref):
+        bit, *later = order
+        for r in range(copies):
+            spot = 0
+            for b in later:
+                spot = 2 * spot + ((r >> b) & 1)
+            ref = keep_ref if (r >> bit) & 1 == mine else send_ref
+            ref[0, spot, :share, :] = grad_gate_up[r * share : (r + 1) * share]
+            for k in range(copies):
+                ref[0, spot, share : share + tall, k * share : (k + 1) * share] = grad_down[
+                    k * tall : (k + 1) * tall, r * share : (r + 1) * share
+                ]
+
+    place = place_ref[0]
+    for (begin, size, order), send_ref in zip(groups, send_refs):
+        for mine in range(2):
+
+            @pl.when(
+                (step >= begin)
+                & (step < begin + size)
+                & ((place >> order[0]) & 1 == mine)
+            )
+            def _(order=order, mine=mine, send_ref=send_ref):
+                put(order, mine, send_ref)
+
     grad_in = dot_nt(grad_both, gate_up).astype(jnp.bfloat16)
     for s in range(sources):
         part = slice(s * CAP, (s + 1) * CAP)
@@ -317,24 +346,36 @@
             grad_ref[own, :] = dot_tn(table, grad_s[s]).astype(jnp.bfloat16)
 
 
-def experts(rows, cots, ranks, probs, w_gate_up, w_down):
+def experts(place, rows, cots, ranks, probs, w_gate_up, w_down, copies, groups):
     sources, count, rows_dev = ranks.shape
     total, model_width = rows.shape
     hidden_units = w_down.shape[1]
+    tall = model_width // copies + hidden_units // copies
     flat = lambda i: (0, 0)
     cube = lambda i: (0, 0, 0)
     once = pl.Buffered(1)
     return pl.pallas_call(
-        functools.partial(experts_kernel, sources=sources, rows_dev=rows_dev, count=count),
+        functools.partial(
+            experts_kernel,
+            sources=sources,
+            rows_dev=rows_dev,
+            count=count,
+            copies=copies,
+            groups=groups,
+        ),
         out_shape=(
             jax.ShapeDtypeStruct((total, model_width), jnp.bfloat16),
             jax.ShapeDtypeStruct((total, model_width), jnp.bfloat16),
             jax.ShapeDtypeStruct((sources, count, rows_dev), jnp.float32),
-            jax.ShapeDtypeStruct(w_gate_up.shape, jnp.bfloat16),
-            jax.ShapeDtypeStruct(w_down.shape, jnp.bfloat16),
+            jax.ShapeDtypeStruct((count, copies // 2, tall, model_width), jnp.bfloat16),
+        )
+        + tuple(
+            jax.ShapeDtypeStruct((size, copies // 2, tall, model_width), jnp.bfloat16)
+            for _, size, _ in groups
         ),
         grid=(count,),
         in_specs=[
+            pl.BlockSpec(memory_space=pltpu.SMEM),
             pl.BlockSpec((total, model_width), flat, pipeline_mode=once),
             pl.BlockSpec((total, model_width), flat, pipeline_mode=once),
             pl.BlockSpec((sources, count, rows_dev), cube, pipeline_mode=once),
@@ -343,20 +384,269 @@
             pl.BlockSpec((1, hidden_units, model_width), lambda i: (i, 0, 0)),
         ],
         out_specs=[
-            pl.BlockSpec((total, model_width), flat),
-            pl.BlockSpec((total, model_width), flat),
-            pl.BlockSpec((sources, count, rows_dev), cube),
-            pl.BlockSpec((1, model_width, 2 * hidden_units), lambda i: (i, 0, 0)),
-            pl.BlockSpec((1, hidden_units, model_width), lambda i: (i, 0, 0)),
+            pl.BlockSpec((total, model_width), flat, pipeline_mode=once),
+            pl.BlockSpec((total, model_width), flat, pipeline_mode=once),
+            pl.BlockSpec((sources, count, rows_dev), cube, pipeline_mode=once),
+            pl.BlockSpec((1, copies // 2, tall, model_width), lambda i: (i, 0, 0, 0)),
+        ]
+        + [
+            pl.BlockSpec(
+                (1, copies // 2, tall, model_width),
+                lambda i, begin=begin, size=size: (jnp.clip(i - begin, 0, size - 1), 0, 0, 0),
+            )
+            for begin, size, _ in groups
         ],
         scratch_shapes=[
             pltpu.VMEM((sources, count * CAP, rows_dev), jnp.bfloat16),
             pltpu.VMEM((sources, count * CAP, model_width), jnp.bfloat16),
             pltpu.VMEM((sources, count * CAP, model_width), jnp.bfloat16),
         ],
-        compiler_params=pltpu.CompilerParams(vmem_limit_bytes=64 * 1000 * 1000),
+        compiler_params=pltpu.CompilerParams(vmem_limit_bytes=67 * 1000 * 1000),
         name="experts",
-    )(rows, cots, ranks, probs, w_gate_up, w_down)
+    )(place, rows, cots, ranks, probs, w_gate_up, w_down)
+
+
+def bits_of(size):
+    return max(size.bit_length() - 1, 0)
+
+
+def swap(sent, axis, bit):
+    size = lax.axis_size(axis)
+    return lax.ppermute(sent, axis, [(i, i ^ (1 << bit)) for i in range(size)])
+
+
+def side(axis, bit):
+    index = lax.axis_index(axis)
+    mine = (index // (1 << bit)) % 2
+    return (mine, index + (1 - 2 * mine) * (1 << bit))
+
+
+def pick(dim, index):
+    return (slice(None),) * dim + (index,)
+
+
+def digits(number, count):
+    return tuple((number // (1 << (count - 1 - k))) % 2 for k in range(count))
+
+
+def reduce_kernel(*refs, groups, labels, weight_order, share):
+    n_groups = len(groups)
+    keep_ref, *refs = refs
+    came_refs, refs = (refs[:n_groups], refs[n_groups:])
+    weight_ref, gain_ref, up_ref, down_ref, weight_out, gain_out, *refs = refs
+    steps = len(groups[0][2]) - 1
+    sends, keeps, gets = ([], [], [])
+    for _ in range(steps):
+        sends.append(refs[0])
+        keeps.append(refs[1])
+        gets.append(refs[2])
+        refs = refs[3:]
+    bits = len(labels)
+    lanes = []
+    for first, out in ((weight_ref, weight_out), (gain_ref, gain_out)):
+        lanes.append((first, refs[: bits - 1], refs[bits - 1 : 2 * bits - 1], out))
+        refs = refs[2 * bits - 1 :]
+    load_keep, load_came, load_sem, unit_send, unit_get, lane_send, lane_get = refs
+    count, spots, tall, width = keep_ref.shape
+    rows = 32 if tall % 32 == 0 else tall
+    blocks = tall // rows
+
+    barrier = pltpu.get_barrier_semaphore()
+    for axis, bit in weight_order:
+        pl.semaphore_signal(
+            barrier,
+            inc=1,
+            device_id={axis: side(axis, bit)[1]},
+            device_id_type=pl.DeviceIdType.MESH,
+        )
+    pl.semaphore_wait(barrier, bits)
+
+    lane_labels = [list(labels)]
+    for label in weight_order:
+        lane_labels.append([other for other in lane_labels[-1] if other != label])
+
+    def lane_copy(number, k):
+        first, sums, got, _ = lanes[number]
+        source = first if k == 0 else sums[k - 1]
+        axis, bit = weight_order[k]
+        mine, partner = side(axis, bit)
+        dim = lane_labels[k].index((axis, bit))
+        return pltpu.make_async_remote_copy(
+            src_ref=source.at[pick(dim, 1 - mine)],
+            dst_ref=got[k],
+            send_sem=lane_send.at[number, k],
+            recv_sem=lane_get.at[number, k],
+            device_id={axis: partner},
+            device_id_type=pl.DeviceIdType.MESH,
+        )
+
+    def lane_start(k):
+        for number in range(2):
+            lane_copy(number, k).start()
+
+    def lane_add(k):
+        axis, bit = weight_order[k]
+        mine, _ = side(axis, bit)
+        dim = lane_labels[k].index((axis, bit))
+        left = bits - 1 - k
+        for number, (first, sums, got, out) in enumerate(lanes):
+            source = first if k == 0 else sums[k - 1]
+            lane_copy(number, k).wait_recv()
+
+            def one(at):
+                here = at[:dim] + (mine,) + at[dim:]
+                return source[here].astype(jnp.float32) + got[k][at].astype(jnp.float32)
+
+            if left == 0:
+                out[...] = one(())
+            else:
+                target = sums[k]
+
+                def body(i, carry):
+                    at = digits(i, left)
+                    target[at] = one(at).astype(target.dtype)
+                    return carry
+
+                lax.fori_loop(0, 1 << left, body, 0)
+
+    lane_start(0)
+
+    units = []
+    for place in range(max(size for _, size, _ in groups)):
+        for g, (begin, size, order) in enumerate(groups):
+            if place < size:
+                units.append((begin + place, g, place, order))
+
+    def loads(n):
+        unit, g, place, _ = units[n]
+        slot = n % 2
+        return (
+            pltpu.make_async_copy(keep_ref.at[unit], load_keep.at[slot], load_sem.at[slot, 0]),
+            pltpu.make_async_copy(
+                came_refs[g].at[place], load_came.at[slot], load_sem.at[slot, 1]
+            ),
+        )
+
+    def unit_copy(unit, order, k):
+        axis, bit = order[k + 1]
+        return pltpu.make_async_remote_copy(
+            src_ref=sends[k].at[unit],
+            dst_ref=gets[k].at[unit],
+            send_sem=unit_send.at[unit, k],
+            recv_sem=unit_get.at[unit, k],
+            device_id={axis: side(axis, bit)[1]},
+            device_id_type=pl.DeviceIdType.MESH,
+        )
+
+    def unit_add(unit, order, k, left, right):
+        mine, _ = side(*order[k + 1])
+        half = spots >> (k + 1)
+
+        def fill(target, which):
+            def body(i, carry):
+                piece = i // blocks
+                own = pl.ds(pl.multiple_of((i % blocks) * rows, rows), rows)
+                total = left[which * half + piece, own, :].astype(jnp.float32) + right[
+                    which * half + piece, own, :
+                ].astype(jnp.float32)
+                target[unit, piece, own, :] = total.astype(jnp.bfloat16)
+                return carry
+
+            lax.fori_loop(0, half * blocks, body, 0)
+
+        fill(sends[k], 1 - mine)
+        unit_copy(unit, order, k).start()
+        fill(keeps[k], mine)
+
+    def begin_unit(n):
+        unit, _, _, order = units[n]
+        for copy in loads(n):
+            copy.wait()
+        unit_add(unit, order, 0, load_keep.at[n % 2], load_came.at[n % 2])
+        if n + 2 < len(units):
+            for copy in loads(n + 2):
+                copy.start()
+
+    def next_unit(n, k):
+        unit, _, _, order = units[n]
+        unit_copy(unit, order, k - 1).wait_recv()
+        unit_add(unit, order, k, keeps[k - 1].at[unit], gets[k - 1].at[unit])
+
+    def end_unit(n):
+        unit, _, _, order = units[n]
+        unit_copy(unit, order, steps - 1).wait_recv()
+        total = keeps[-1][unit, 0].astype(jnp.float32) + gets[-1][unit, 0].astype(jnp.float32)
+        up_ref[unit] = total[:share]
+        pieces = width // share
+        rest = tall - share
+        for p in range(pieces):
+            down_ref[unit, p * rest : (p + 1) * rest, :] = total[
+                share:, p * share : (p + 1) * share
+            ]
+
+    for n in range(min(2, len(units))):
+        for copy in loads(n):
+            copy.start()
+    work = [functools.partial(begin_unit, n) for n in range(len(units))]
+    for k in range(1, steps):
+        work += [functools.partial(next_unit, n, k) for n in range(len(units))]
+    work += [functools.partial(end_unit, n) for n in range(len(units))]
+    marks = [len(units) + (len(work) - len(units)) * k // bits for k in range(bits)]
+    for number, job in enumerate(work):
+        for k, mark in enumerate(marks[:-1]):
+            if number == mark:
+                lane_add(k)
+                lane_start(k + 1)
+        job()
+    lane_add(bits - 1)
+    for unit, _, _, order in units:
+        for k in range(steps):
+            unit_copy(unit, order, k).wait_send()
+    for k in range(bits):
+        for number in range(2):
+            lane_copy(number, k).wait_send()
+
+
+def reduce_rest(keep, came, weights, gains, groups, labels, weight_order, share):
+    count, spots, tall, width = keep.shape
+    bits = len(labels)
+    steps = len(groups[0][2]) - 1
+    anywhere = pl.BlockSpec(memory_space=pl.ANY)
+    vmem = pl.BlockSpec(memory_space=pltpu.VMEM)
+    scratch = []
+    for k in range(steps):
+        scratch += [pltpu.VMEM((count, spots >> (k + 1), tall, width), jnp.bfloat16)] * 3
+    for lane in (weights, gains):
+        tail = lane.shape[bits:]
+        shapes = [pltpu.VMEM((2,) * (bits - 1 - k) + tail, lane.dtype) for k in range(bits)]
+        scratch += shapes[:-1] + shapes
+    scratch += [
+        pltpu.VMEM((2, spots, tall, width), jnp.bfloat16),
+        pltpu.VMEM((2, spots, tall, width), jnp.bfloat16),
+        pltpu.SemaphoreType.DMA((2, 2)),
+        pltpu.SemaphoreType.DMA((count, steps)),
+        pltpu.SemaphoreType.DMA((count, steps)),
+        pltpu.SemaphoreType.DMA((2, bits)),
+        pltpu.SemaphoreType.DMA((2, bits)),
+    ]
+    return pl.pallas_call(
+        functools.partial(
+            reduce_kernel, groups=groups, labels=labels, weight_order=weight_order, share=share
+        ),
+        out_shape=(
+            jax.ShapeDtypeStruct((count, share, width), jnp.float32),
+            jax.ShapeDtypeStruct((count, (tall - share) * (width // share), share), jnp.float32),
+            jax.ShapeDtypeStruct(weights.shape[bits:], jnp.float32),
+            jax.ShapeDtypeStruct(gains.shape[bits:], jnp.float32),
+        ),
+        in_specs=[anywhere] * (1 + len(came)) + [vmem] * 2,
+        out_specs=[vmem] * 4,
+        scratch_shapes=scratch,
+        compiler_params=pltpu.CompilerParams(
+            collective_id=0, has_side_effects=True, vmem_limit_bytes=67 * 1000 * 1000
+        ),
+        name="reduce_rest",
+    )(keep, *came, weights, gains)
 
 
 def on_device(
@@ -463,19 +753,36 @@
     kept = chosen & (rank < CAP)
     rank_sent = jnp.where(kept, rank, -1.0).T
     probs_sent = probs.T
-    ranks = lax.all_to_all(
-        rank_sent.reshape(n_ep, -1, rows_dev), "ep", split_axis=0, concat_axis=0, tiled=True
-    )
-    prob_all = lax.all_to_all(
-        probs_sent.reshape(n_ep, -1, rows_dev), "ep", split_axis=0, concat_axis=0, tiled=True
-    )
+    both_sent = jnp.concatenate(
+        [rank_sent.reshape(n_ep, -1, rows_dev), probs_sent.reshape(n_ep, -1, rows_dev)], 1
+    )
+    both_all = lax.all_to_all(both_sent, "ep", split_axis=0, concat_axis=0, tiled=True)
+    ranks = both_all[:, : experts_all // n_ep]
+    prob_all = both_all[:, experts_all // n_ep :]
     expert_rows = lax.all_gather(normed_two_b, "ep", axis=0, tiled=True)
     expert_cots = lax.all_gather(grad_output.astype(jnp.bfloat16), "ep", axis=0, tiled=True)
-    out_sum, grad_sum, inner, grad_gate_up, grad_down = experts(
-        expert_rows, expert_cots, ranks, prob_all, w_gate_up, w_down
-    )
-    expert_up = lax.psum_scatter(grad_gate_up, "rep", scatter_dimension=1, tiled=True)
-    expert_down = lax.psum_scatter(grad_down, "rep", scatter_dimension=2, tiled=True)
+    rep_bits = [("rep", b) for b in range(bits_of(n_rep))]
+    ep_bits = [("ep", b) for b in range(bits_of(n_ep))]
+    count = experts_all // n_ep
+    sizes = [(count - count // 4) // 2, count - count // 4 - (count - count // 4) // 2, count // 4]
+    groups = []
+    for g, size in enumerate(sizes):
+        lead = [0, len(rep_bits) - 2, len(rep_bits) - 1][g]
+        groups.append(
+            (sum(sizes[:g]), size, [lead] + [b for b in range(len(rep_bits)) if b != lead])
+        )
+    out_sum, grad_sum, inner, grad_keep, *grad_send = experts(
+        lax.axis_index("rep").astype(jnp.int32).reshape(1),
+        expert_rows,
+        expert_cots,
+        ranks,
+        prob_all,
+        w_gate_up,
+        w_down,
+        n_rep,
+        groups,
+    )
+    came = [swap(sent, "rep", order[0]) for sent, (_, _, order) in zip(grad_send, groups)]
     out_back = lax.all_to_all(
         out_sum.reshape(n_ep, rows_dev, model_width), "ep", split_axis=0, concat_axis=0, tiled=True
     )
@@ -540,24 +847,37 @@
     grad_normed = dot_nt(grad_in_rows, full_in)
     grad_inputs_norm, grad_attn_gain = norm_back(grad_normed, inputs, factor_one, attn_gain)
     grad_inputs = grad_hidden + grad_inputs_norm
+    everything = n_ep * n_rep
+    gains = jnp.concatenate(
+        [grad_attn_gain.reshape(everything, -1), grad_mlp_gain.reshape(everything, -1)], 1
+    )
+    labels = ep_bits[::-1] + rep_bits[::-1]
+    shape = (2,) * len(labels)
     weight_grads = jnp.concatenate([grad_w_in, grad_out_w, grad_router], 1).astype(jnp.bfloat16)
-    summed = lax.psum_scatter(weight_grads, everyone, scatter_dimension=0, tiled=True)
-    summed = summed.astype(jnp.float32)
-    gains = lax.psum_scatter(
-        jnp.stack([grad_attn_gain, grad_mlp_gain], 1), everyone, scatter_dimension=0, tiled=True
-    )
+    expert_up, expert_down, weights, gains = reduce_rest(
+        grad_keep,
+        came,
+        weight_grads.reshape(shape + (-1, weight_grads.shape[1])),
+        gains.reshape(shape + (1, -1)),
+        [(begin, size, [("rep", b) for b in order]) for begin, size, order in groups],
+        labels,
+        ep_bits + rep_bits,
+        model_width // n_rep,
+    )
+    gains = gains[0]
+    part = model_width // everything
     return (
         output[None],
         grad_inputs[None],
-        gains[:, 0],
-        summed[:, :query_width],
-        summed[:, query_width:rotated_width],
-        summed[:, rotated_width:input_width],
-        summed[:, input_width : input_width + model_width],
-        gains[:, 1],
-        summed[:, input_width + model_width :],
-        expert_up.astype(jnp.float32),
-        expert_down.astype(jnp.float32),
+        gains[:part],
+        weights[:, :query_width],
+        weights[:, query_width:rotated_width],
+        weights[:, rotated_width:input_width],
+        weights[:, input_width : input_width + model_width],
+        gains[part:],
+        weights[:, input_width + model_width :],
+        expert_up,
+        expert_down,
     )
 
 

time: 1170 us -> 744 us (0.64)
  waiting for transfers between devices: 778 us -> 232 us
  Pallas kernels: 97.8 us -> 267 us
  blocking collectives: 99.8 us -> 72.2 us
  local copies, waits for them, and re-layouts: 79.9 us -> 64.9 us
    reduce_scatter x2 -> x0, waiting for transfers between devices: 429 us -> none  [the longest x1 281 us: on_device(): lax.psum_scatter(grad_gate_up, 'rep', scatter_dimension=1, tiled=True)]
    unnamed x9 -> x3, waiting for transfers between devices: 246 us -> 0.05 us
    pallas_call x0 -> x1, Pallas kernels: none -> 154 us  [reduce_rest(): pl.pallas_call(functools.partial(reduce_kernel, groups=groups, labels=lab...]
    all_to_all x2 -> x1, waiting for transfers between devices: 3.67 us -> 80.1 us  [on_device(): lax.all_to_all(returning.reshape(n_rep, rows_dev, head_width + 2 * HEAD_D...]
    ppermute x0 -> x3, waiting for transfers between devices: none -> 49.1 us  [swap(): return lax.ppermute(sent, axis, [(i, i ^ 1 << bit) for i in range(size)])]
    all_to_all x1, blocking collectives: 29.3 us -> 5.79 us  [on_device(): lax.all_to_all(both_sent, 'ep', split_axis=0, concat_axis=0, tiled=True)]
    unnamed x96 -> x105, local copies, waits for them, and re-layouts: 43.3 us -> 20.1 us
  transfers between devices with their start and end apart: 12 -> 10, of which waited for: 11 -> 7; matrix products, arithmetic and copies ran while one was open for 6% -> 11% of each run, Pallas kernels for 2% -> 8%
where the time goes in v4:
time: 744 us; the launch traced here: 729 us
  Pallas kernels  267 us (36%)
  waiting for transfers between devices  232 us (31%)
  blocking collectives  72.2 us (10%)
  local copies, waits for them, and re-layouts  64.9 us (9%)
  other arithmetic  26.9 us (4%)
  starting transfers between devices  26.3 us (4%)
  matrix products  23.1 us (3%)
  between operations  16.6 us (2%)
    pallas_call x1, Pallas kernels, reduce_rest(): pl.pallas_call(functools.partial(reduce_kernel, groups=groups, labels=lab...  154 us
    all_to_all x1, waiting for transfers between devices, on_device(): lax.all_to_all(returning.reshape(n_rep, rows_dev, head_width + 2 * HEAD_D...  80.1 us
    pallas_call x1, Pallas kernels, experts(): pl.pallas_call(functools.partial(experts_kernel, sources=sources, rows_de...  55.3 us
    ppermute x3, waiting for transfers between devices, swap(): return lax.ppermute(sent, axis, [(i, i ^ 1 << bit) for i in range(size)])  49.1 us
    all_gather x1, waiting for transfers between devices, on_device(): full = lax.all_gather(joined, everyone, axis=0, tiled=True)  41.3 us
    pallas_call x1, Pallas kernels, attend_backward(): pl.pallas_call(functools.partial(attend_backward_kernel, heads=heads), ou...  31.8 us
    all_to_all x1, blocking collectives, on_device(): lax.all_to_all(grad_sum.reshape(n_ep, rows_dev, model_width), 'ep', split...  30.5 us
    pallas_call x1, Pallas kernels, attend_forward(): pl.pallas_call(functools.partial(attend_forward_kernel, heads=heads), out...  26 us
  transfers between devices with their start and end apart: 10, of which 7 were waited for; matrix products, arithmetic and copies ran while one was open for 11% of the time, Pallas kernels for 8%

profile of v4, /device:TPU:26, one launch (start us, length us, event | category | flops | bytes accessed | tf_op | source)
XLA Modules:
  0.0 729.5 jit_solution(15397072491065661011)
XLA Ops:
  12.7 16.3 %all-gather = s32[1,2048]{1,0:T(1,128)S(1)} all-gather(s32[1,256]{1,0:T(1,128)} %param.14), channel_id=2, replica_groups=mesh['ep'=4,'rep'=8] {'rep'}, dimensions={1}, use_global_device_ids=true | all-gather | bytes 9216 | tf_op jit(solution)/shard_map/all_gather | solution.py:683
  37.2 3.0 copy.82
  41.0 41.3 %all-gather.5.cloned.1.call-done = bf16[1024,3104]{1,0:T(8,128)(2,1)} async-done(((bf16[32,3104]{1,0:T(8,128)(2,1)}), bf16[1024,3104]{1,0:T(8,128)(2,1)}) %all-gather.5.cloned.1.call-update) | async-done | bytes 6357008 | tf_op jit(solution)/shard_map/all_gather | solution.py:705
  82.4 3.5 fusion.2
  92.4 5.5 all-to-all-start
  99.4 23.3 %all-to-all-done = bf16[8,256,256]{2,1,0:T(8,128)(2,1)S(1)} async-done(((bf16[8,256,256]{2,1,0:T(8,128)(2,1)}), bf16[8,256,256]{2,1,0:T(8,128)(2,1)S(1)}, u32[]{:S(2)}, u32[]{:S(2)}) %all-to-all-start) | async-done | bytes 1048608 | tf_op jit(solution)/shard_map/all_to_all | solution.py:729
  123.7 26.0 %attend_forward.1 = (bf16[2048,128]{1,0:T(8,128)(2,1)}, f32[128,2048]{1,0:T(8,128)}, f32[8,2,256]{2,1,0:T(2,128)}) custom-call(s32[8]{0:T(128)} %and_select_fusion.low_ref, bf16[2048,256]{1,0:T(8,128)(2,1)} %bitcast.155, s32[8,1,256]{2,1,0:T(1,128)} %bitcast.180), custom_call_target="tpu_custom_call" | custom-call | tf_op jit(solution)/shard_map/attend_forward/pallas_call | solution.py:119
  150.9 12.9 %all_to_all.40 = bf16[8,256,128]{1,2,0:T(8,128)(2,1)S(1)} all-to-all(bf16[8,256,128]{1,2,0:T(8,128)(2,1)S(1)} %copy.88), channel_id=1, replica_groups=mesh['ep'=4,'rep'=8] {'rep'}, dimensions={0} | all-to-all | bytes 1048576 | tf_op jit(solution)/shard_map/all_to_all | solution.py:732
  163.8 2.6 multiply_reduce_fusion.2
  170.6 5.8 all_to_all.41
  177.1 14.1 %all-gather.7.cloned.1.call-done.rows_ref = bf16[1024,1024]{1,0:T(8,128)(2,1)} async-done(((bf16[256,1024]{1,0:T(8,128)(2,1)}), bf16[1024,1024]{1,0:T(8,128)(2,1)}) %all-gather.7.cloned.1.call-update) | async-done | bytes 2097168 | tf_op jit(solution)/shard_map/all_gather | solution.py:762
  191.2 55.3 %experts.1 = (bf16[1024,1024]{1,0:T(8,128)(2,1)}, bf16[1024,1024]{1,0:T(8,128)(2,1)}, f32[4,8,256]{2,1,0:T(8,128)}, bf16[8,4,192,1024]{3,2,1,0:T(8,128)(2,1)}, b...) custom-call(s32[1]{0:T(128)} %bitcast.12.place_ref, ...), custom_call_target="tpu_custom_call" | custom-call | tf_op jit(solution)/shard_map/experts/pallas_call | solution.py:357
  246.5 6.6 all_to_all.42
  253.1 30.5 %all_to_all.43 = bf16[4,256,1024]{2,1,0:T(8,128)(2,1)} all-to-all(bf16[4,256,1024]{2,1,0:T(8,128)(2,1)} %bitcast.171), channel_id=1, replica_groups=mesh['ep'=4,'rep'=8] {'ep'}, dimensions={0} | all-to-all | bytes 4194304 | tf_op jit(solution)/shard_map/all_to_all | solution.py:789
  283.6 5.6 all-to-all-start.3
  291.5 3.4 multiply_reduce_fusion
  294.9 18.3 %all-to-all-done.3 = bf16[4,256,1024]{2,1,0:T(8,128)(2,1)S(1)} async-done(((bf16[4,256,1024]{2,1,0:T(8,128)(2,1)}), bf16[4,256,1024]{2,1,0:T(8,128)(2,1)S(1)}, u32[]{:S(2)}, u32[]{:S(2)}) %all-to-all-start.3) | async-done | bytes 2097184 | tf_op jit(solution)/shard_map/all_to_all | solution.py:786
  319.4 6.0 all-to-all-start.6
  331.5 6.0 all-to-all-done.6
  337.5 31.8 %attend_backward.1 = (f32[2048,128]{1,0:T(8,128)}, f32[2048,64]{1,0:T(8,128)}, f32[2048,64]{1,0:T(8,128)}) custom-call(s32[8]{0:T(128)} %and_select_fusion.low_ref, bf16[2048,256]{1,0:T(8,128)(2,1)} %bitcast.156, bf16[2048,128]{1,0:T(8,128)(2,1)} %bitcast.26.grad_ref, f32[128,2048]{1,0:T(8,128)} %get-tuple-element.32.out_ref, ...), custom_call_target="tpu_custom_call" | custom-call | tf_op jit(solution)/shard_map/attend_backward/pallas_call | solution.py:218
  372.2 2.7 fusion.67
  374.9 2.8 copy.92
  377.7 2.9 copy.95
  389.9 4.1 fusion.9
  395.4 6.6 all-to-all-start.7
  405.9 80.1 %all-to-all-done.7 = bf16[8,256,256]{1,2,0:T(8,128)(2,1)S(1)} async-done(((bf16[8,256,256]{1,2,0:T(8,128)(2,1)}), bf16[8,256,256]{1,2,0:T(8,128)(2,1)S(1)}, u32[]{:S(2)}, u32[]{:S(2)}) %all-to-all-start.7) | async-done | bytes 1048608 | tf_op jit(solution)/shard_map/all_to_all | solution.py:821
  492.1 4.8 fusion.35
  497.0 2.6 fusion.65
  503.0 3.2 pad_maximum_fusion.refs_4_
  506.2 49.1 %collective-permute-done.2.refs_3_ = bf16[2,4,192,1024]{3,2,1,0:T(8,128)(2,1)} collective-permute-done((bf16[2,4,192,1024]{3,2,1,0:T(8,128)(2,1)}, bf16[2,4,192,1024]{3,2,1,0:T(8,128)(2,1)}, u32[]{:S(2)}, u32[]{:S(2)}) %collective-permute-start.2) | collective-permute-done | bytes 3145760 | tf_op jit(solution)/shard_map/ppermute | solution.py:415
  555.3 154.2 %reduce_rest.1 = (f32[8,128,1024]{2,1,0:T(8,128)}, f32[8,512,128]{2,1,0:T(8,128)}, f32[32,3104]{1,0:T(8,128)}, f32[1,64]{1,0:T(1,128)}) custom-call(bf16[8,4,192,1024]{3,2,1,0:T(8,128)(2,1)} %get-tuple-element.37.refs_0_, bf16[3,4,192,1024]{3,2,1,0:T(8,128)(2,1)} %collective-permute-done.refs_1_, bf16[3,4,192,1024]{3,2,1,0:T(8,128)(2,1)} %collective-permute-done.1.refs_2_, ...), custom_call_target="tpu_custom_call" | custom-call | tf_op jit(solution)/shard_map/reduce_rest/pallas_call | solution.py:632
  715.4 4.9 copy.127
  (193 shorter events, 77.1 us)
Async XLA Ops:
  8.0 74.4 %all-gather.5.cloned.1.call-start = ((), (), s32[]{:S(2)}) async-start(), calls=%async_computation.8 | async-start | bytes 6758400 | tf_op jit(solution)/shard_map/all_gather | solution.py:705
  30.8 68.0 %copy-start.29 = (s32[2048]{0:T(1024)}, s32[2048]{0:T(1024)S(1)}, u32[]{:S(2)}) copy-start(s32[2048]{0:T(1024)S(1)} %convert_reduce_fusion) | copy-start | bytes 24580
  37.2 45.2 %copy-start.42 = (f32[1024]{0:T(1024)S(1)}, f32[1024]{0:T(1024)}, u32[]{:S(2)}) copy-start(f32[1024]{0:T(1024)} %param.16) | copy-start | bytes 12292
  41.0 44.9 %copy-start.45 = (f32[256]{0:T(256)}, f32[256]{0:T(256)S(1)}, u32[]{:S(2)}) copy-start(f32[256]{0:T(256)S(1)} %get-tuple-element.73) | copy-start | bytes 3076
  89.9 7.9 %copy-start.14 = (f32[1,256,1024]{2,1,0:T(8,128)S(1)}, f32[1,256,1024]{2,1,0:T(8,128)}, u32[]{:S(2)}) copy-start(f32[1,256,1024]{2,1,0:T(8,128)} %param.25) | copy-start | bytes 3145732
  92.4 30.3 %all-to-all-start = ((bf16[8,256,256]{2,1,0:T(8,128)(2,1)}), bf16[8,256,256]{2,1,0:T(8,128)(2,1)S(1)}, u32[]{:S(2)}, u32[]{:S(2)}) async-start(bf16[8,256,256]{2,1,0:T(8,128)(2,1)} %maximum_bitcast_fusion), calls=%async_computation | async-start | bytes 2097152 | tf_op jit(solution)/shard_map/all_to_all | solution.py:729
  97.9 79.2 %all-gather.9.cloned.1.call-start = ((), (), s32[]{:S(2)}) async-start(), calls=%async_computation.10 | async-start | bytes 2621440 | tf_op jit(solution)/shard_map/all_gather | solution.py:763
  98.8 92.4 %all-gather.7.cloned.1.call-start = ((), (), s32[]{:S(2)}) async-start(), calls=%async_computation.9 | async-start | bytes 2621440 | tf_op jit(solution)/shard_map/all_gather | solution.py:762
  170.0 6.5 copy-start.30
  283.6 5.6 copy-start.31
  283.6 5.6 copy-start.35
  283.6 29.6 %all-to-all-start.3 = ((bf16[4,256,1024]{2,1,0:T(8,128)(2,1)}), bf16[4,256,1024]{2,1,0:T(8,128)(2,1)S(1)}, u32[]{:S(2)}, u32[]{:S(2)}) async-start(bf16[4,256,1024]{2,1,0:T(8,128)(2,1)} %bitcast.170), calls=%async_computation.3 | async-start | bytes 4194304 | tf_op jit(solution)/shard_map/all_to_all | solution.py:786
  289.3 5.6 copy-start.39
  294.9 18.7 %copy-start.47 = (f32[256]{0:T(256)S(1)}, f32[256]{0:T(256)}, u32[]{:S(2)}) copy-start(f32[256]{0:T(256)} %get-tuple-element.74) | copy-start | bytes 3076
  316.1 9.3 %copy-start.17 = (f32[2048,32]{0,1:T(8,128)S(1)}, f32[2048,32]{0,1:T(8,128)}, u32[]{:S(2)}) copy-start(f32[2048,32]{0,1:T(8,128)} %copy-done.16) | copy-start | bytes 786436
  316.1 9.3 %copy-start.19 = (f32[2048,32]{0,1:T(8,128)S(1)}, f32[2048,32]{0,1:T(8,128)}, u32[]{:S(2)}) copy-start(f32[2048,32]{0,1:T(8,128)} %copy-done.18) | copy-start | bytes 786436
  316.1 9.3 %copy-start.21 = (f32[2048,32]{0,1:T(8,128)S(1)}, f32[2048,32]{0,1:T(8,128)}, u32[]{:S(2)}) copy-start(f32[2048,32]{0,1:T(8,128)} %copy-done.20) | copy-start | bytes 786436
  319.4 18.1 %all-to-all-start.6 = ((bf16[8,256,128]{2,1,0:T(8,128)(2,1)}), bf16[8,256,128]{2,1,0:T(8,128)(2,1)}, u32[]{:S(2)}, u32[]{:S(2)}) async-start(bf16[8,256,128]{2,1,0:T(8,128)(2,1)} %bitcast.151), calls=%async_computation.6 | async-start | bytes 1048576 | tf_op jit(solution)/shard_map/all_to_all | solution.py:806
  329.5 225.8 %collective-permute-start = (bf16[3,4,192,1024]{3,2,1,0:T(8,128)(2,1)}, bf16[3,4,192,1024]{3,2,1,0:T(8,128)(2,1)}, u32[]{:S(2)}, u32[]{:S(2)}) collective-permute-start(bf16[3,4,192,1024]{3,2,1,0:T(8,128)(2,1)} %get-tuple-element.38), channel_id=1, source_target_pairs={{0,1},{1,0},{2,3},{3,2},{4,5},{5,4},{6,7},{7,6},{8,9},{9,8},{10,11... | collective-permute-start | bytes 14155784 | tf_op jit(solution)/shard_map/ppermute | solution.py:415
  330.9 224.3 %collective-permute-start.1 = (bf16[3,4,192,1024]{3,2,1,0:T(8,128)(2,1)}, bf16[3,4,192,1024]{3,2,1,0:T(8,128)(2,1)}, u32[]{:S(2)}, u32[]{:S(2)}) collective-permute-start(bf16[3,4,192,1024]{3,2,1,0:T(8,128)(2,1)} %get-tuple-element.39), channel_id=1, source_target_pairs={{0,2},{1,3},{2,0},{3,1},{4,6},{5,7},{6,4},{7,5},{8,10},{9,11},{10,... | collective-permute-start | bytes 14155784 | tf_op jit(solution)/shard_map/ppermute | solution.py:415
  384.7 5.2 copy-start.22
  394.1 8.4 %copy-start.8 = (bf16[256,1024]{1,0:T(8,128)(2,1)S(1)}, bf16[256,1024]{1,0:T(8,128)(2,1)}, u32[]{:S(2)}) copy-start(bf16[256,1024]{1,0:T(8,128)(2,1)} %multiply_convert_fusion.1) | copy-start | bytes 1572868
  394.2 8.4 %copy-start.36 = (f32[256]{0:T(256)S(1)}, f32[256]{0:T(256)}, u32[]{:S(2)}) copy-start(f32[256]{0:T(256)} %copy-done.34) | copy-start | bytes 3076
  394.2 8.4 %copy-start.40 = (f32[256]{0:T(256)S(1)}, f32[256]{0:T(256)}, u32[]{:S(2)}) copy-start(f32[256]{0:T(256)} %copy-done.39) | copy-start | bytes 3076
  394.2 9.7 %copy-start.12 = (bf16[8,256,128]{1,2,0:T(8,128)(2,1)S(1)}, bf16[8,256,128]{1,2,0:T(8,128)(2,1)}, u32[]{:S(2)}) copy-start(bf16[8,256,128]{1,2,0:T(8,128)(2,1)} %copy-done.11) | copy-start | bytes 1572868
  395.4 90.7 %all-to-all-start.7 = ((bf16[8,256,256]{1,2,0:T(8,128)(2,1)}), bf16[8,256,256]{1,2,0:T(8,128)(2,1)S(1)}, u32[]{:S(2)}, u32[]{:S(2)}) async-start(bf16[8,256,256]{1,2,0:T(8,128)(2,1)} %copy.97), calls=%async_computation.7 | async-start | bytes 2097152 | tf_op jit(solution)/shard_map/all_to_all | solution.py:821
  401.9 153.4 %collective-permute-start.2 = (bf16[2,4,192,1024]{3,2,1,0:T(8,128)(2,1)}, bf16[2,4,192,1024]{3,2,1,0:T(8,128)(2,1)}, u32[]{:S(2)}, u32[]{:S(2)}) collective-permute-start(bf16[2,4,192,1024]{3,2,1,0:T(8,128)(2,1)} %get-tuple-element.40), channel_id=1, source_target_pairs={{0,4},{1,5},{2,6},{3,7},{4,0},{5,1},{6,2},{7,3},{8,12},{9,13},{10,... | collective-permute-start | bytes 9437192 | tf_op jit(solution)/shard_map/ppermute | solution.py:415
  486.0 6.0 copy-start.4
  486.0 6.0 copy-start.43
  486.0 6.0 copy-start.46
  490.9 6.0 copy-start.27
  715.4 4.9 copy-start.23
  (26 other events, 60.0 us)
Sparse Core Ops, SparseCore 0:
  12.8 69.5 all-gather.4
Sparse Core Ops, SparseCore 1:
  100.5 22.4 all-gather.8
  168.6 22.5 all-gather.6

commit v5 on v1

--- a/solution.py
+++ b/solution.py
@@ -246,40 +246,366 @@
     )(lows, rows, grads, outs, totals, starts)
 
 
+def bits_of(size):
+    return max(size.bit_length() - 1, 0)
+
+
+def swap(sent, axis, bit):
+    size = lax.axis_size(axis)
+    return lax.ppermute(sent, axis, [(i, i ^ (1 << bit)) for i in range(size)])
+
+
+def side(axis, bit):
+    index = lax.axis_index(axis)
+    mine = (index // (1 << bit)) % 2
+    return (mine, index + (1 - 2 * mine) * (1 << bit))
+
+
+def pick(dim, index):
+    return (slice(None),) * dim + (index,)
+
+
+def digits(number, count):
+    return tuple((number // (1 << (count - 1 - k))) % 2 for k in range(count))
+
+
+def mesh_copy(source, target, sends, gets, axis, partner):
+    return pltpu.make_async_remote_copy(
+        src_ref=source,
+        dst_ref=target,
+        send_sem=sends,
+        recv_sem=gets,
+        device_id={axis: partner},
+        device_id_type=pl.DeviceIdType.MESH,
+    )
+
+
+def greet(partners):
+    barrier = pltpu.get_barrier_semaphore()
+    for axis, partner in partners:
+        pl.semaphore_signal(
+            barrier, inc=1, device_id={axis: partner}, device_id_type=pl.DeviceIdType.MESH
+        )
+    pl.semaphore_wait(barrier, len(partners))
+
+
+class Lane:
+    def __init__(self, labels, order, first, refs, sends, gets, rows=None):
+        bits = len(labels)
+        self.order, self.first, self.sends, self.gets = (order, first, sends, gets)
+        self.sums, self.got = (refs[: bits - 1], refs[bits - 1 : 2 * bits - 1])
+        self.labels = [list(labels)]
+        for label in order:
+            self.labels.append([other for other in self.labels[-1] if other != label])
+        self.rows = rows
+
+    @staticmethod
+    def scratch(bits, tail, dtype):
+        shapes = [pltpu.VMEM((2,) * (bits - 1 - k) + tail, dtype) for k in range(bits)]
+        return shapes[:-1] + shapes
+
+    def source(self, k):
+        return self.first if k == 0 else self.sums[k - 1]
+
+    def copy(self, k):
+        axis, bit = self.order[k]
+        mine, partner = side(axis, bit)
+        dim = self.labels[k].index((axis, bit))
+        return mesh_copy(
+            self.source(k).at[pick(dim, 1 - mine)],
+            self.got[k],
+            self.sends.at[k],
+            self.gets.at[k],
+            axis,
+            partner,
+        )
+
+    def start(self, k):
+        self.copy(k).start()
+
+    def add(self, k, out=None):
+        axis, bit = self.order[k]
+        mine, _ = side(axis, bit)
+        dim = self.labels[k].index((axis, bit))
+        left = len(self.order) - 1 - k
+        self.copy(k).wait_recv()
+        source, got = (self.source(k), self.got[k])
+        target = out if left == 0 else self.sums[k]
+        height = got.shape[left]
+        rows = self.rows or height
+        blocks = height // rows
+
+        def body(i, carry):
+            at = digits(i // blocks, left)
+            own = pl.ds(pl.multiple_of((i % blocks) * rows, rows), rows)
+            if blocks == 1:
+                own = slice(None)
+            here = at[:dim] + (mine,) + at[dim:]
+            total = source[here + (own,)].astype(jnp.float32) + got[at + (own,)].astype(
+                jnp.float32
+            )
+            target[at + (own,)] = total.astype(target.dtype)
+            return carry
+
+        lax.fori_loop(0, blocks << left, body, 0)
+
+    def finish(self):
+        for k in range(len(self.order)):
+            self.copy(k).wait_send()
+
+
+def reduce_kernel(*refs, units, n_came, labels, weight_order, share):
+    keep_ref, *refs = refs
+    came_refs, refs = (refs[:n_came], refs[n_came:])
+    weight_ref, gain_ref, up_ref, down_ref, weight_out, gain_out, *refs = refs
+    steps = len(units[0][3]) - 1
+    sends, keeps, gets = ([], [], [])
+    for _ in range(steps):
+        sends.append(refs[0])
+        keeps.append(refs[1])
+        gets.append(refs[2])
+        refs = refs[3:]
+    bits = len(labels)
+    lane_refs, refs = (refs[: 2 * (2 * bits - 1)], refs[2 * (2 * bits - 1) :])
+    load_keep, load_came, load_sem, unit_send, unit_get, lane_send, lane_get = refs
+    lanes = [
+        Lane(
+            labels,
+            weight_order,
+            first,
+            lane_refs[number * (2 * bits - 1) : (number + 1) * (2 * bits - 1)],
+            lane_send.at[number],
+            lane_get.at[number],
+        )
+        for number, first in enumerate((weight_ref, gain_ref))
+    ]
+    count, spots, tall, width = keep_ref.shape
+    rows = 32 if tall % 32 == 0 else tall
+    blocks = tall // rows
+
+    greet([(axis, side(axis, bit)[1]) for axis, bit in weight_order])
+
+    def lane_start(k):
+        for lane in lanes:
+            lane.start(k)
+
+    def lane_add(k):
+        for lane, out in zip(lanes, (weight_out, gain_out)):
+            lane.add(k, out)
+
+    lane_start(0)
+
+    def loads(n):
+        unit, g, place, _ = units[n]
+        slot = n % 2
+        return (
+            pltpu.make_async_copy(keep_ref.at[unit], load_keep.at[slot], load_sem.at[slot, 0]),
+            pltpu.make_async_copy(
+                came_refs[g].at[place], load_came.at[slot], load_sem.at[slot, 1]
+            ),
+        )
+
+    def unit_copy(unit, order, k):
+        axis, bit = order[k + 1]
+        return mesh_copy(
+            sends[k].at[unit],
+            gets[k].at[unit],
+            unit_send.at[unit, k],
+            unit_get.at[unit, k],
+            axis,
+            side(axis, bit)[1],
+        )
+
+    def unit_add(unit, order, k, left, right):
+        mine, _ = side(*order[k + 1])
+        half = spots >> (k + 1)
+
+        def fill(target, which):
+            def body(i, carry):
+                piece = i // blocks
+                own = pl.ds(pl.multiple_of((i % blocks) * rows, rows), rows)
+                total = left[which * half + piece, own, :].astype(jnp.float32) + right[
+                    which * half + piece, own, :
+                ].astype(jnp.float32)
+                target[unit, piece, own, :] = total.astype(jnp.bfloat16)
+                return carry
+
+            lax.fori_loop(0, half * blocks, body, 0)
+
+        fill(sends[k], 1 - mine)
+        unit_copy(unit, order, k).start()
+        fill(keeps[k], mine)
+
+    def begin_unit(n):
+        unit, _, _, order = units[n]
+        for copy in loads(n):
+            copy.wait()
+        unit_add(unit, order, 0, load_keep.at[n % 2], load_came.at[n % 2])
+        if n + 2 < len(units):
+            for copy in loads(n + 2):
+                copy.start()
+
+    def next_unit(n, k):
+        unit, _, _, order = units[n]
+        unit_copy(unit, order, k - 1).wait_recv()
+        unit_add(unit, order, k, keeps[k - 1].at[unit], gets[k - 1].at[unit])
+
+    def end_unit(n):
+        unit, _, _, order = units[n]
+        unit_copy(unit, order, steps - 1).wait_recv()
+        total = keeps[-1][unit, 0].astype(jnp.float32) + gets[-1][unit, 0].astype(jnp.float32)
+        up_ref[unit] = total[:share]
+        pieces = width // share
+        rest = tall - share
+        for p in range(pieces):
+            down_ref[unit, p * rest : (p + 1) * rest, :] = total[
+                share:, p * share : (p + 1) * share
+            ]
+
+    for n in range(min(2, len(units))):
+        for copy in loads(n):
+            copy.start()
+    work = [functools.partial(begin_unit, n) for n in range(len(units))]
+    for k in range(1, steps):
+        work += [functools.partial(next_unit, n, k) for n in range(len(units))]
+    work += [functools.partial(end_unit, n) for n in range(len(units))]
+    marks = [len(units) + (len(work) - len(units)) * k // bits for k in range(bits)]
+    for number, job in enumerate(work):
+        for k, mark in enumerate(marks[:-1]):
+            if number == mark:
+                lane_add(k)
+                lane_start(k + 1)
+        job()
+    lane_add(bits - 1)
+    for unit, _, _, order in units:
+        for k in range(steps):
+            unit_copy(unit, order, k).wait_send()
+    for lane in lanes:
+        lane.finish()
+
+
+def reduce_rest(keep, came, weights, gains, units, labels, weight_order, share):
+    count, spots, tall, width = keep.shape
+    bits = len(labels)
+    steps = len(units[0][3]) - 1
+    anywhere = pl.BlockSpec(memory_space=pl.ANY)
+    vmem = pl.BlockSpec(memory_space=pltpu.VMEM)
+    scratch = []
+    for k in range(steps):
+        scratch += [pltpu.VMEM((count, spots >> (k + 1), tall, width), jnp.bfloat16)] * 3
+    for lane in (weights, gains):
+        scratch += Lane.scratch(bits, lane.shape[bits:], lane.dtype)
+    scratch += [
+        pltpu.VMEM((2, spots, tall, width), jnp.bfloat16),
+        pltpu.VMEM((2, spots, tall, width), jnp.bfloat16),
+        pltpu.SemaphoreType.DMA((2, 2)),
+        pltpu.SemaphoreType.DMA((count, steps)),
+        pltpu.SemaphoreType.DMA((count, steps)),
+        pltpu.SemaphoreType.DMA((2, bits)),
+        pltpu.SemaphoreType.DMA((2, bits)),
+    ]
+    return pl.pallas_call(
+        functools.partial(
+            reduce_kernel,
+            units=units,
+            n_came=len(came),
+            labels=labels,
+            weight_order=weight_order,
+            share=share,
+        ),
+        out_shape=(
+            jax.ShapeDtypeStruct((count, share, width), jnp.float32),
+            jax.ShapeDtypeStruct((count, (tall - share) * (width // share), share), jnp.float32),
+            jax.ShapeDtypeStruct(weights.shape[bits:], jnp.float32),
+            jax.ShapeDtypeStruct(gains.shape[bits:], jnp.float32),
+        ),
+        in_specs=[anywhere] * (1 + len(came)) + [vmem] * 2,
+        out_specs=[vmem] * 4,
+        scratch_shapes=scratch,
+        compiler_params=pltpu.CompilerParams(
+            collective_id=0, has_side_effects=True, vmem_limit_bytes=67 * 1000 * 1000
+        ),
+        name="reduce_rest",
+    )(keep, *came, weights, gains)
+
+
 def experts_kernel(
-    rows_ref,
-    cot_ref,
-    rank_ref,
-    prob_ref,
-    gate_up_ref,
-    down_ref,
-    out_ref,
-    grad_ref,
-    inner_ref,
-    grad_gate_up_ref,
-    grad_down_ref,
-    picks_s,
-    out_s,
-    grad_s,
-    *,
-    sources,
-    rows_dev,
-    count,
+    *refs, sources, rows_dev, count, copies, orders, near, labels, ep_order
 ):
+    rows_hbm, cot_hbm, rank_ref, prob_ref, gate_up_ref, down_ref, *refs = refs
+    out_ref, grad_ref, inner_ref, keep_ref, came_ref, *refs = refs
+    far = count - near
+    sent_refs, refs = (refs[:far], refs[far:])
+    rows_s, cot_s, picks_s, out_s, grad_s, send_s, inner_s, inner_got, *refs = refs
+    bits = len(labels)
+    lane_refs, refs = (refs[: 2 * (2 * bits - 1)], refs[2 * (2 * bits - 1) :])
+    load_sem, unit_send, unit_get, lane_send, lane_get, inner_send, inner_take = refs
+    me = lax.axis_index("ep")
     step = pl.program_id(0)
+    grad_lane, out_lane = [
+        Lane(
+            labels,
+            ep_order,
+            first,
+            lane_refs[number * (2 * bits - 1) : (number + 1) * (2 * bits - 1)],
+            lane_send.at[number],
+            lane_get.at[number],
+            rows=32,
+        )
+        for number, first in enumerate((cot_s, rows_s))
+    ]
+
+    def unit_copy(e):
+        bit = orders[e][0]
+        if e < near:
+            return mesh_copy(
+                send_s.at[e],
+                came_ref.at[e],
+                unit_send.at[e],
+                unit_get.at[e],
+                "rep",
+                side("rep", bit)[1],
+            )
+        return pltpu.make_async_copy(send_s.at[e], sent_refs[e - near], unit_send.at[e])
+
+    def inner_copy(d):
+        peer = (me + d) % sources
+        return mesh_copy(
+            inner_s.at[peer],
+            inner_got.at[me],
+            inner_send.at[d - 1],
+            inner_take.at[d - 1],
+            "ep",
+            peer,
+        )
+
+    @pl.when(step == 0)
+    def _():
+        loads = [
+            pltpu.make_async_copy(rows_hbm, rows_s, load_sem.at[0]),
+            pltpu.make_async_copy(cot_hbm, cot_s, load_sem.at[1]),
+        ]
+        for copy in loads:
+            copy.start()
+        partners = [("ep", (me + d) % sources) for d in range(1, sources)]
+        for bit in sorted({order[0] for order in orders[:near]}):
+            partners.append(("rep", side("rep", bit)[1]))
+        greet(partners)
+        for copy in loads:
+            copy.wait()
+
     slots = pl.ds(pl.multiple_of(step * CAP, 16), CAP)
     numbers = lax.broadcasted_iota(jnp.int32, (CAP, rows_dev), 0).astype(jnp.float32)
     rows_in, cots, weights, picks = [], [], [], []
     for s in range(sources):
         rank = rank_ref[s, pl.ds(step, 1), :]
-        pick = jnp.where(rank == numbers, 1.0, 0.0)
-        weights.append(jnp.sum(pick * prob_ref[s, pl.ds(step, 1), :], 1, keepdims=True))
-        pick_b = pick.astype(jnp.bfloat16)
-        picks.append(pick)
+        pick_table = jnp.where(rank == numbers, 1.0, 0.0)
+        weights.append(jnp.sum(pick_table * prob_ref[s, pl.ds(step, 1), :], 1, keepdims=True))
+        pick_b = pick_table.astype(jnp.bfloat16)
+        picks.append(pick_table)
         picks_s[s, slots, :] = pick_b
-        own = slice(s * rows_dev, (s + 1) * rows_dev)
-        rows_in.append(product(pick_b, rows_ref[own, :]).astype(jnp.bfloat16))
-        cots.append(product(pick_b, cot_ref[own, :]))
+        rows_in.append(product(pick_b, rows_s[digits(s, bits)]).astype(jnp.bfloat16))
+        cots.append(product(pick_b, cot_s[digits(s, bits)]))
     arrived = jnp.concatenate(rows_in, 0)
     weight = jnp.concatenate(weights, 0)
     grad_mix = branch_scale * jnp.concatenate(cots, 0)
@@ -296,67 +622,149 @@
     sent_out = (weight * produced).astype(jnp.bfloat16)
     grad_out = (weight * grad_mix).astype(jnp.bfloat16)
     grad_active = dot_nt(grad_out, down)
-    grad_down_ref[0] = dot_tn(active, grad_out).astype(grad_down_ref.dtype)
+    grad_down = dot_tn(active, grad_out).astype(jnp.bfloat16)
     grad_gate = grad_active * up_part * sigmoid_gate * (1.0 + gate_part * (1.0 - sigmoid_gate))
     grad_up = grad_active * gate_part * sigmoid_gate
     grad_both = jnp.concatenate([grad_gate, grad_up], 1).astype(jnp.bfloat16)
-    grad_gate_up_ref[0] = dot_tn(arrived, grad_both).astype(grad_gate_up_ref.dtype)
+    grad_gate_up = dot_tn(arrived, grad_both).astype(jnp.bfloat16)
+    share = grad_down.shape[1] // copies
+    tall = hidden_units // copies
+
+    def put(order, mine):
+        bit, *later = order
+        for r in range(copies):
+            spot = 0
+            for b in later:
+                spot = 2 * spot + ((r >> b) & 1)
+            ref = keep_ref.at[0] if (r >> bit) & 1 == mine else send_s.at[step]
+            ref[spot, :share, :] = grad_gate_up[r * share : (r + 1) * share]
+            for k in range(copies):
+                ref[spot, share : share + tall, k * share : (k + 1) * share] = grad_down[
+                    k * tall : (k + 1) * tall, r * share : (r + 1) * share
+                ]
+
+    for order in {tuple(order): order for order in orders}.values():
+        members = [e for e in range(count) if orders[e] == order]
+        here = functools.reduce(jnp.logical_or, [step == e for e in members])
+        side_mine, _ = side("rep", order[0])
+        for mine in range(2):
+
+            @pl.when(here & (side_mine == mine))
+            def _(order=order, mine=mine):
+                put(order, mine)
+
     grad_in = dot_nt(grad_both, gate_up).astype(jnp.bfloat16)
     for s in range(sources):
         part = slice(s * CAP, (s + 1) * CAP)
         out_s[s, slots, :] = sent_out[part]
         grad_s[s, slots, :] = grad_in[part]
-        inner_ref[s, pl.ds(step, 1), :] = jnp.sum(picks[s] * inner[part], 0, keepdims=True)
+        inner_s[s, pl.ds(step, 1), :] = jnp.sum(picks[s] * inner[part], 0, keepdims=True)
+    for e in range(count):
+
+        @pl.when(step == e)
+        def _(e=e):
+            unit_copy(e).start()
 
     @pl.when(step == count - 1)
     def _():
-        for s in range(sources):
-            own = slice(s * rows_dev, (s + 1) * rows_dev)
-            table = picks_s[s]
-            out_ref[own, :] = dot_tn(table, out_s[s]).astype(jnp.bfloat16)
-            grad_ref[own, :] = dot_tn(table, grad_s[s]).astype(jnp.bfloat16)
-
-
-def experts(rows, cots, ranks, probs, w_gate_up, w_down):
+        for table_of, target, lane in ((grad_s, cot_s, grad_lane), (out_s, rows_s, out_lane)):
+            for s in range(sources):
+                target[digits(s, bits)] = dot_tn(picks_s[s], table_of[s]).astype(jnp.bfloat16)
+            lane.start(0)
+        for d in range(1, sources):
+            inner_copy(d).start()
+        for k in range(bits):
+            for lane, total in ((grad_lane, grad_ref), (out_lane, out_ref)):
+                lane.add(k, total)
+                if k + 1 < bits:
+                    lane.start(k + 1)
+        inner_got[me] = inner_s[me]
+        for d in range(1, sources):
+            inner_copy(d).wait_recv()
+        inner_ref[...] = inner_got[...]
+        for d in range(1, sources):
+            inner_copy(d).wait_send()
+        grad_lane.finish()
+        out_lane.finish()
+        for e in range(count):
+            unit_copy(e).wait()
+
+
+def experts(rows, cots, ranks, probs, w_gate_up, w_down, copies, orders, near, labels, ep_order):
     sources, count, rows_dev = ranks.shape
     total, model_width = rows.shape
     hidden_units = w_down.shape[1]
+    bits = len(labels)
+    tall = model_width // copies + hidden_units // copies
     flat = lambda i: (0, 0)
     cube = lambda i: (0, 0, 0)
     once = pl.Buffered(1)
+    anywhere = pl.BlockSpec(memory_space=pl.ANY)
+    far = count - near
+    shape = (2,) * bits + (rows_dev, model_width)
+    piece = (copies // 2, tall, model_width)
     return pl.pallas_call(
-        functools.partial(experts_kernel, sources=sources, rows_dev=rows_dev, count=count),
+        functools.partial(
+            experts_kernel,
+            sources=sources,
+            rows_dev=rows_dev,
+            count=count,
+            copies=copies,
+            orders=orders,
+            near=near,
+            labels=labels,
+            ep_order=ep_order,
+        ),
         out_shape=(
-            jax.ShapeDtypeStruct((total, model_width), jnp.bfloat16),
-            jax.ShapeDtypeStruct((total, model_width), jnp.bfloat16),
+            jax.ShapeDtypeStruct((rows_dev, model_width), jnp.float32),
+            jax.ShapeDtypeStruct((rows_dev, model_width), jnp.float32),
             jax.ShapeDtypeStruct((sources, count, rows_dev), jnp.float32),
-            jax.ShapeDtypeStruct(w_gate_up.shape, jnp.bfloat16),
-            jax.ShapeDtypeStruct(w_down.shape, jnp.bfloat16),
-        ),
+            jax.ShapeDtypeStruct((count,) + piece, jnp.bfloat16),
+            jax.ShapeDtypeStruct((near,) + piece, jnp.bfloat16),
+        )
+        + (jax.ShapeDtypeStruct(piece, jnp.bfloat16),) * far,
         grid=(count,),
         in_specs=[
-            pl.BlockSpec((total, model_width), flat, pipeline_mode=once),
-            pl.BlockSpec((total, model_width), flat, pipeline_mode=once),
+            anywhere,
+            anywhere,
             pl.BlockSpec((sources, count, rows_dev), cube, pipeline_mode=once),
             pl.BlockSpec((sources, count, rows_dev), cube, pipeline_mode=once),
             pl.BlockSpec((1, model_width, 2 * hidden_units), lambda i: (i, 0, 0)),
             pl.BlockSpec((1, hidden_units, model_width), lambda i: (i, 0, 0)),
         ],
         out_specs=[
-            pl.BlockSpec((total, model_width), flat),
-            pl.BlockSpec((total, model_width), flat),
-            pl.BlockSpec((sources, count, rows_dev), cube),
-            pl.BlockSpec((1, model_width, 2 * hidden_units), lambda i: (i, 0, 0)),
-            pl.BlockSpec((1, hidden_units, model_width), lambda i: (i, 0, 0)),
-        ],
+            pl.BlockSpec((rows_dev, model_width), flat, pipeline_mode=once),
+            pl.BlockSpec((rows_dev, model_width), flat, pipeline_mode=once),
+            pl.BlockSpec((sources, count, rows_dev), cube, pipeline_mode=once),
+            pl.BlockSpec((1,) + piece, lambda i: (i, 0, 0, 0)),
+            anywhere,
+        ]
+        + [anywhere] * far,
         scratch_shapes=[
+            pltpu.VMEM(shape, jnp.bfloat16),
+            pltpu.VMEM(shape, jnp.bfloat16),
             pltpu.VMEM((sources, count * CAP, rows_dev), jnp.bfloat16),
             pltpu.VMEM((sources, count * CAP, model_width), jnp.bfloat16),
             pltpu.VMEM((sources, count * CAP, model_width), jnp.bfloat16),
+            pltpu.VMEM((count,) + piece, jnp.bfloat16),
+            pltpu.VMEM((sources, count, rows_dev), jnp.float32),
+            pltpu.VMEM((sources, count, rows_dev), jnp.float32),
+        ]
+        + Lane.scratch(bits, (rows_dev, model_width), jnp.bfloat16) * 2
+        + [
+            pltpu.SemaphoreType.DMA((2,)),
+            pltpu.SemaphoreType.DMA((count,)),
+            pltpu.SemaphoreType.DMA((near,)),
+            pltpu.SemaphoreType.DMA((2, bits)),
+            pltpu.SemaphoreType.DMA((2, bits)),
+            pltpu.SemaphoreType.DMA((sources - 1,)),
+            pltpu.SemaphoreType.DMA((sources - 1,)),
         ],
-        compiler_params=pltpu.CompilerParams(vmem_limit_bytes=64 * 1000 * 1000),
+        compiler_params=pltpu.CompilerParams(
+            collective_id=1, has_side_effects=True, vmem_limit_bytes=67 * 1000 * 1000
+        ),
         name="experts",
-    )(rows, cots, ranks, probs, w_gate_up, w_down)
+    )(rows.reshape(shape), cots.reshape(shape), ranks, probs, w_gate_up, w_down)
 
 
 def on_device(
@@ -463,32 +871,50 @@
     kept = chosen & (rank < CAP)
     rank_sent = jnp.where(kept, rank, -1.0).T
     probs_sent = probs.T
-    ranks = lax.all_to_all(
-        rank_sent.reshape(n_ep, -1, rows_dev), "ep", split_axis=0, concat_axis=0, tiled=True
-    )
-    prob_all = lax.all_to_all(
-        probs_sent.reshape(n_ep, -1, rows_dev), "ep", split_axis=0, concat_axis=0, tiled=True
-    )
+    both_sent = jnp.concatenate(
+        [rank_sent.reshape(n_ep, -1, rows_dev), probs_sent.reshape(n_ep, -1, rows_dev)], 1
+    )
+    both_all = lax.all_to_all(both_sent, "ep", split_axis=0, concat_axis=0, tiled=True)
+    ranks = both_all[:, : experts_all // n_ep]
+    prob_all = both_all[:, experts_all // n_ep :]
     expert_rows = lax.all_gather(normed_two_b, "ep", axis=0, tiled=True)
     expert_cots = lax.all_gather(grad_output.astype(jnp.bfloat16), "ep", axis=0, tiled=True)
-    out_sum, grad_sum, inner, grad_gate_up, grad_down = experts(
-        expert_rows, expert_cots, ranks, prob_all, w_gate_up, w_down
-    )
-    expert_up = lax.psum_scatter(grad_gate_up, "rep", scatter_dimension=1, tiled=True)
-    expert_down = lax.psum_scatter(grad_down, "rep", scatter_dimension=2, tiled=True)
-    out_back = lax.all_to_all(
-        out_sum.reshape(n_ep, rows_dev, model_width), "ep", split_axis=0, concat_axis=0, tiled=True
-    )
-    grad_back = lax.all_to_all(
-        grad_sum.reshape(n_ep, rows_dev, model_width), "ep", split_axis=0, concat_axis=0, tiled=True
-    )
-    inner_back = lax.all_to_all(inner, "ep", split_axis=0, concat_axis=0, tiled=True)
-    output = hidden + branch_scale * jnp.sum(out_back.astype(jnp.float32), 0)
+    rep_bits = [("rep", b) for b in range(bits_of(n_rep))]
+    ep_bits = [("ep", b) for b in range(bits_of(n_ep))]
+    count = experts_all // n_ep
+    near = count * 5 // 8
+    kinds = [2, 0, 1, 0, 1][:near] + [0, 1, 2][near - count :]
+    leads = [0, len(rep_bits) - 2, len(rep_bits) - 1]
+    orders = [
+        [leads[kind]] + [b for b in range(len(rep_bits)) if b != leads[kind]] for kind in kinds
+    ]
+    out_sum, grad_sum, inner_back, grad_keep, came_near, *sent = experts(
+        expert_rows,
+        expert_cots,
+        ranks,
+        prob_all,
+        w_gate_up,
+        w_down,
+        n_rep,
+        orders,
+        near,
+        ep_bits[::-1],
+        ep_bits,
+    )
+    came = [came_near] + [
+        swap(half, "rep", order[0])[None] for half, order in zip(sent, orders[near:])
+    ]
+    units = [(e, 0, e, [("rep", b) for b in orders[e]]) for e in range(near)]
+    units += [
+        (e, 1 + e - near, 0, [("rep", b) for b in orders[e]]) for e in range(near, count)
+    ]
+    units = units[1:3] + units[:1] + units[3:]
+    output = hidden + branch_scale * out_sum
     grad_probs = inner_back.reshape(experts_all, rows_dev).T
     grad_logits = probs * (grad_probs - jnp.sum(grad_probs * probs, -1, keepdims=True))
     normed_two_f = normed_two_b.astype(jnp.float32)
     grad_router = jnp.dot(normed_two_f.T, grad_logits, precision=lax.Precision.HIGHEST)
-    grad_normed_two = jnp.sum(grad_back.astype(jnp.float32), 0) + jnp.dot(
+    grad_normed_two = grad_sum + jnp.dot(
         grad_logits, router_f.T, precision=lax.Precision.HIGHEST
     )
     grad_hidden_norm, grad_mlp_gain = norm_back(grad_normed_two, hidden, factor_two, mlp_gain)
@@ -540,24 +966,37 @@
     grad_normed = dot_nt(grad_in_rows, full_in)
     grad_inputs_norm, grad_attn_gain = norm_back(grad_normed, inputs, factor_one, attn_gain)
     grad_inputs = grad_hidden + grad_inputs_norm
+    everything = n_ep * n_rep
+    gains = jnp.concatenate(
+        [grad_attn_gain.reshape(everything, -1), grad_mlp_gain.reshape(everything, -1)], 1
+    )
+    labels = ep_bits[::-1] + rep_bits[::-1]
+    shape = (2,) * len(labels)
     weight_grads = jnp.concatenate([grad_w_in, grad_out_w, grad_router], 1).astype(jnp.bfloat16)
-    summed = lax.psum_scatter(weight_grads, everyone, scatter_dimension=0, tiled=True)
-    summed = summed.astype(jnp.float32)
-    gains = lax.psum_scatter(
-        jnp.stack([grad_attn_gain, grad_mlp_gain], 1), everyone, scatter_dimension=0, tiled=True
-    )
+    expert_up, expert_down, weights, gains = reduce_rest(
+        grad_keep,
+        came,
+        weight_grads.reshape(shape + (-1, weight_grads.shape[1])),
+        gains.reshape(shape + (1, -1)),
+        units,
+        labels,
+        ep_bits + rep_bits,
+        model_width // n_rep,
+    )
+    gains = gains[0]
+    part = model_width // everything
     return (
         output[None],
         grad_inputs[None],
-        gains[:, 0],
-        summed[:, :query_width],
-        summed[:, query_width:rotated_width],
-        summed[:, rotated_width:input_width],
-        summed[:, input_width : input_width + model_width],
-        gains[:, 1],
-        summed[:, input_width + model_width :],
-        expert_up.astype(jnp.float32),
-        expert_down.astype(jnp.float32),
+        gains[:part],
+        weights[:, :query_width],
+        weights[:, query_width:rotated_width],
+        weights[:, rotated_width:input_width],
+        weights[:, input_width : input_width + model_width],
+        gains[part:],
+        weights[:, input_width + model_width :],
+        expert_up,
+        expert_down,
     )
 
 

time: 1170 us -> 687 us (0.59)
  waiting for transfers between devices: 778 us -> 153 us
  Pallas kernels: 97.8 us -> 339 us
  blocking collectives: 99.8 us -> 38.9 us
  local copies, waits for them, and re-layouts: 79.9 us -> 62.1 us
    reduce_scatter x2 -> x0, waiting for transfers between devices: 429 us -> none  [the longest x1 281 us: on_device(): lax.psum_scatter(grad_gate_up, 'rep', scatter_dimension=1, tiled=True)]
    unnamed x9 -> x3, waiting for transfers between devices: 246 us -> 0.05 us
    pallas_call x0 -> x1, Pallas kernels: none -> 156 us  [reduce_rest(): pl.pallas_call(functools.partial(reduce_kernel, units=units, n_came=len(c...]
    pallas_call x1, Pallas kernels: 49.4 us -> 126 us  [experts(): pl.pallas_call(functools.partial(experts_kernel, sources=sources, rows_de...]
    all_to_all x3 -> x1, blocking collectives: 66.5 us -> 5.52 us  [on_device(): lax.all_to_all(both_sent, 'ep', split_axis=0, concat_axis=0, tiled=True)]
    ppermute x0 -> x3, waiting for transfers between devices: none -> 48.2 us  [swap(): return lax.ppermute(sent, axis, [(i, i ^ 1 << bit) for i in range(size)])]
    unnamed x96 -> x99, local copies, waits for them, and re-layouts: 43.3 us -> 18.8 us
  transfers between devices with their start and end apart: 12 -> 9, of which waited for: 11 -> 8; matrix products, arithmetic and copies ran while one was open for 6% -> 7% of each run, Pallas kernels for 2% -> 4%
where the time goes in v5:
time: 687 us; the launch traced here: 679 us
  Pallas kernels  339 us (49%)
  waiting for transfers between devices  153 us (22%)
  local copies, waits for them, and re-layouts  62.1 us (9%)
  blocking collectives  38.9 us (6%)
  other arithmetic  25.1 us (4%)
  matrix products  22.1 us (3%)
  starting transfers between devices  21.1 us (3%)
  between operations  16.7 us (2%)
    pallas_call x1, Pallas kernels, reduce_rest(): pl.pallas_call(functools.partial(reduce_kernel, units=units, n_came=len(c...  156 us
    pallas_call x1, Pallas kernels, experts(): pl.pallas_call(functools.partial(experts_kernel, sources=sources, rows_de...  126 us
    ppermute x3, waiting for transfers between devices, swap(): return lax.ppermute(sent, axis, [(i, i ^ 1 << bit) for i in range(size)])  48.2 us
    all_gather x1, waiting for transfers between devices, on_device(): full = lax.all_gather(joined, everyone, axis=0, tiled=True)  41.4 us
    pallas_call x1, Pallas kernels, attend_backward(): pl.pallas_call(functools.partial(attend_backward_kernel, heads=heads), ou...  31.8 us
    pallas_call x1, Pallas kernels, attend_forward(): pl.pallas_call(functools.partial(attend_forward_kernel, heads=heads), out...  26 us
    all_to_all x1, waiting for transfers between devices, on_device(): lax.all_to_all(sending, 'rep', split_axis=0, concat_axis=0, tiled=True)  23.3 us
    unnamed x99, local copies, waits for them, and re-layouts  18.8 us
  transfers between devices with their start and end apart: 9, of which 8 were waited for; matrix products, arithmetic and copies ran while one was open for 7% of the time, Pallas kernels for 4%

profile of v5, /device:TPU:26, one launch (start us, length us, event | category | flops | bytes accessed | tf_op | source)
XLA Modules:
  0.0 678.6 jit_solution(2542561149661628375)
XLA Ops:
  12.7 16.3 %all-gather = s32[1,2048]{1,0:T(1,128)S(1)} all-gather(s32[1,256]{1,0:T(1,128)} %param.14), channel_id=2, replica_groups=mesh['ep'=4,'rep'=8] {'rep'}, dimensions={1}, use_global_device_ids=true | all-gather | bytes 9216 | tf_op jit(solution)/shard_map/all_gather | solution.py:801
  37.2 3.0 copy.82
  41.0 41.4 %all-gather.5.cloned.1.call-done = bf16[1024,3104]{1,0:T(8,128)(2,1)} async-done(((bf16[32,3104]{1,0:T(8,128)(2,1)}), bf16[1024,3104]{1,0:T(8,128)(2,1)}) %all-gather.5.cloned.1.call-update) | async-done | bytes 6357008 | tf_op jit(solution)/shard_map/all_gather | solution.py:823
  82.4 3.5 fusion.2
  89.9 2.4 maximum_bitcast_fusion
  92.3 5.5 all-to-all-start
  99.4 23.3 %all-to-all-done = bf16[8,256,256]{2,1,0:T(8,128)(2,1)S(1)} async-done(((bf16[8,256,256]{2,1,0:T(8,128)(2,1)}), bf16[8,256,256]{2,1,0:T(8,128)(2,1)S(1)}, u32[]{:S(2)}, u32[]{:S(2)}) %all-to-all-start) | async-done | bytes 1048608 | tf_op jit(solution)/shard_map/all_to_all | solution.py:847
  123.7 26.0 %attend_forward.1 = (bf16[2048,128]{1,0:T(8,128)(2,1)}, f32[128,2048]{1,0:T(8,128)}, f32[8,2,256]{2,1,0:T(2,128)}) custom-call(s32[8]{0:T(128)} %and_select_fusion.low_ref, bf16[2048,256]{1,0:T(8,128)(2,1)} %bitcast.157, s32[8,1,256]{2,1,0:T(1,128)} %bitcast.182), custom_call_target="tpu_custom_call" | custom-call | tf_op jit(solution)/shard_map/attend_forward/pallas_call | solution.py:119
  150.9 17.1 %all_to_all.25 = bf16[8,256,128]{1,2,0:T(8,128)(2,1)S(1)} all-to-all(bf16[8,256,128]{1,2,0:T(8,128)(2,1)S(1)} %copy.88), channel_id=1, replica_groups=mesh['ep'=4,'rep'=8] {'rep'}, dimensions={0} | all-to-all | bytes 1048576 | tf_op jit(solution)/shard_map/all_to_all | solution.py:850
  168.0 2.6 multiply_reduce_fusion.2
  174.7 5.5 all_to_all.26
  180.9 14.6 %all-gather.7.cloned.1.call-done = bf16[1024,1024]{1,0:T(8,128)(2,1)} async-done(((bf16[256,1024]{1,0:T(8,128)(2,1)}), bf16[1024,1024]{1,0:T(8,128)(2,1)}) %all-gather.7.cloned.1.call-update) | async-done | bytes 2097168 | tf_op jit(solution)/shard_map/all_gather | solution.py:880
  195.5 125.8 %experts.1 = (f32[256,1024]{1,0:T(8,128)}, f32[256,1024]{1,0:T(8,128)}, f32[4,8,256]{2,1,0:T(8,128)}, bf16[8,4,192,1024]{3,2,1,0:T(8,128)(2,1)}, bf16[5,4,192,10...) custom-call(bf16[2,2,256,1024]{3,2,1,0:T(8,128)(2,1)} %bitcast.172, ...), custom_call_target="tpu_custom_call" | custom-call | tf_op jit(solution)/shard_map/experts/pallas_call | solution.py:706
  322.3 2.6 multiply_reduce_fusion
  329.6 6.3 all-to-all-start.3
  339.9 7.7 %all-to-all-done.3 = bf16[8,256,128]{2,1,0:T(8,128)(2,1)} async-done(((bf16[8,256,128]{2,1,0:T(8,128)(2,1)}), bf16[8,256,128]{2,1,0:T(8,128)(2,1)}, u32[]{:S(2)}, u32[]{:S(2)}) %all-to-all-start.3) | async-done | bytes 524320 | tf_op jit(solution)/shard_map/all_to_all | solution.py:925
  347.6 31.8 %attend_backward.1 = (f32[2048,128]{1,0:T(8,128)}, f32[2048,64]{1,0:T(8,128)}, f32[2048,64]{1,0:T(8,128)}) custom-call(s32[8]{0:T(128)} %and_select_fusion.low_ref, bf16[2048,256]{1,0:T(8,128)(2,1)} %bitcast.158, bf16[2048,128]{1,0:T(8,128)(2,1)} %bitcast.25.grad_ref, f32[128,2048]{1,0:T(8,128)} %get-tuple-element.33.out_ref, ...), custom_call_target="tpu_custom_call" | custom-call | tf_op jit(solution)/shard_map/attend_backward/pallas_call | solution.py:218
  382.3 2.7 fusion.67
  385.0 2.8 copy.92
  387.9 2.8 copy.95
  400.0 4.1 fusion.9
  405.5 6.6 all-to-all-start.4
  417.4 18.1 %all-to-all-done.4 = bf16[8,256,256]{1,2,0:T(8,128)(2,1)S(1)} async-done(((bf16[8,256,256]{1,2,0:T(8,128)(2,1)}), bf16[8,256,256]{1,2,0:T(8,128)(2,1)S(1)}, u32[]{:S(2)}, u32[]{:S(2)}) %all-to-all-start.4) | async-done | bytes 1048608 | tf_op jit(solution)/shard_map/all_to_all | solution.py:940
  440.8 4.6 fusion.35
  445.6 2.6 fusion.65
  449.1 2.4 convolution_convert_fusion
  451.5 3.2 pad_maximum_fusion.refs_5_
  454.7 4.2 collective-permute-done
  458.9 32.7 %collective-permute-done.1 = bf16[4,192,1024]{2,1,0:T(8,128)(2,1)} collective-permute-done((bf16[4,192,1024]{2,1,0:T(8,128)(2,1)}, bf16[4,192,1024]{2,1,0:T(8,128)(2,1)}, u32[]{:S(2)}, u32[]{:S(2)}) %collective-permute-start.1) | collective-permute-done | bytes 1572896 | tf_op jit(solution)/shard_map/ppermute | solution.py:255
  491.6 11.3 %collective-permute-done.2 = bf16[4,192,1024]{2,1,0:T(8,128)(2,1)} collective-permute-done((bf16[4,192,1024]{2,1,0:T(8,128)(2,1)}, bf16[4,192,1024]{2,1,0:T(8,128)(2,1)}, u32[]{:S(2)}, u32[]{:S(2)}) %collective-permute-start.2) | collective-permute-done | bytes 1572896 | tf_op jit(solution)/shard_map/ppermute | solution.py:255
  502.9 155.7 %reduce_rest.1 = (f32[8,128,1024]{2,1,0:T(8,128)}, f32[8,512,128]{2,1,0:T(8,128)}, f32[32,3104]{1,0:T(8,128)}, f32[1,64]{1,0:T(1,128)}) custom-call(bf16[8,4,192,1024]{3,2,1,0:T(8,128)(2,1)} %get-tuple-element.38.refs_0_, bf16[5,4,192,1024]{3,2,1,0:T(8,128)(2,1)} %get-tuple-element.39.refs_1_, bf16[1,4,192,1024]{3,2,1,0:T(8,128)(2,1)} %bitcast.38.refs_2_, ...), custom_call_target="tpu_custom_call" | custom-call | tf_op jit(solution)/shard_map/reduce_rest/pallas_call | solution.py:507
  664.5 4.9 copy.127
  (181 shorter events, 67.7 us)
Async XLA Ops:
  8.0 74.4 %all-gather.5.cloned.1.call-start = ((), (), s32[]{:S(2)}) async-start(), calls=%async_computation.5 | async-start | bytes 6758400 | tf_op jit(solution)/shard_map/all_gather | solution.py:823
  30.8 68.0 %copy-start.29 = (s32[2048]{0:T(1024)}, s32[2048]{0:T(1024)S(1)}, u32[]{:S(2)}) copy-start(s32[2048]{0:T(1024)S(1)} %convert_reduce_fusion) | copy-start | bytes 24580
  35.9 4.4 copy-start.3
  37.2 45.2 %copy-start.39 = (f32[1024]{0:T(1024)S(1)}, f32[1024]{0:T(1024)}, u32[]{:S(2)}) copy-start(f32[1024]{0:T(1024)} %param.16) | copy-start | bytes 12292
  41.0 44.9 %copy-start.42 = (f32[256]{0:T(256)}, f32[256]{0:T(256)S(1)}, u32[]{:S(2)}) copy-start(f32[256]{0:T(256)S(1)} %get-tuple-element.75) | copy-start | bytes 3076
  89.9 7.9 %copy-start.13 = (f32[1,256,1024]{2,1,0:T(8,128)S(1)}, f32[1,256,1024]{2,1,0:T(8,128)}, u32[]{:S(2)}) copy-start(f32[1,256,1024]{2,1,0:T(8,128)} %param.25) | copy-start | bytes 3145732
  92.3 30.4 %all-to-all-start = ((bf16[8,256,256]{2,1,0:T(8,128)(2,1)}), bf16[8,256,256]{2,1,0:T(8,128)(2,1)S(1)}, u32[]{:S(2)}, u32[]{:S(2)}) async-start(bf16[8,256,256]{2,1,0:T(8,128)(2,1)} %maximum_bitcast_fusion), calls=%async_computation | async-start | bytes 2097152 | tf_op jit(solution)/shard_map/all_to_all | solution.py:847
  97.9 83.0 %all-gather.9.cloned.1.call-start = ((), (), s32[]{:S(2)}) async-start(), calls=%async_computation.7 | async-start | bytes 2621440 | tf_op jit(solution)/shard_map/all_gather | solution.py:881
  98.8 96.7 %all-gather.7.cloned.1.call-start = ((), (), s32[]{:S(2)}) async-start(), calls=%async_computation.6 | async-start | bytes 2621440 | tf_op jit(solution)/shard_map/all_gather | solution.py:880
  174.1 6.1 copy-start.30
  326.3 9.6 %copy-start.16 = (f32[2048,32]{0,1:T(8,128)S(1)}, f32[2048,32]{0,1:T(8,128)}, u32[]{:S(2)}) copy-start(f32[2048,32]{0,1:T(8,128)} %copy-done.15) | copy-start | bytes 786436
  326.3 9.6 %copy-start.18 = (f32[2048,32]{0,1:T(8,128)S(1)}, f32[2048,32]{0,1:T(8,128)}, u32[]{:S(2)}) copy-start(f32[2048,32]{0,1:T(8,128)} %copy-done.17) | copy-start | bytes 786436
  326.3 9.6 %copy-start.20 = (f32[2048,32]{0,1:T(8,128)S(1)}, f32[2048,32]{0,1:T(8,128)}, u32[]{:S(2)}) copy-start(f32[2048,32]{0,1:T(8,128)} %copy-done.19) | copy-start | bytes 786436
  329.6 18.0 %all-to-all-start.3 = ((bf16[8,256,128]{2,1,0:T(8,128)(2,1)}), bf16[8,256,128]{2,1,0:T(8,128)(2,1)}, u32[]{:S(2)}, u32[]{:S(2)}) async-start(bf16[8,256,128]{2,1,0:T(8,128)(2,1)} %bitcast.153), calls=%async_computation.3 | async-start | bytes 1048576 | tf_op jit(solution)/shard_map/all_to_all | solution.py:925
  387.8 4.4 copy-start.2
  394.8 5.2 copy-start.21
  404.3 7.9 %copy-start.8 = (bf16[256,1024]{1,0:T(8,128)(2,1)S(1)}, bf16[256,1024]{1,0:T(8,128)(2,1)}, u32[]{:S(2)}) copy-start(bf16[256,1024]{1,0:T(8,128)(2,1)} %multiply_convert_fusion.1) | copy-start | bytes 1572868
  404.3 7.9 %copy-start.26 = (f32[4,8,256]{2,1,0:T(8,128)S(1)}, f32[4,8,256]{2,1,0:T(8,128)}, u32[]{:S(2)}) copy-start(f32[4,8,256]{2,1,0:T(8,128)} %get-tuple-element.32) | copy-start | bytes 98308
  404.3 7.9 %copy-start.31 = (f32[256]{0:T(256)S(1)}, f32[256]{0:T(256)}, u32[]{:S(2)}) copy-start(f32[256]{0:T(256)} %copy-done.30) | copy-start | bytes 3076
  404.3 7.9 %copy-start.35 = (f32[256]{0:T(256)S(1)}, f32[256]{0:T(256)}, u32[]{:S(2)}) copy-start(f32[256]{0:T(256)} %copy-done.34) | copy-start | bytes 3076
  404.3 11.1 %copy-start.12 = (bf16[8,256,128]{1,2,0:T(8,128)(2,1)S(1)}, bf16[8,256,128]{1,2,0:T(8,128)(2,1)}, u32[]{:S(2)}) copy-start(bf16[8,256,128]{1,2,0:T(8,128)(2,1)} %copy-done.11) | copy-start | bytes 1572868
  405.5 30.1 %all-to-all-start.4 = ((bf16[8,256,256]{1,2,0:T(8,128)(2,1)}), bf16[8,256,256]{1,2,0:T(8,128)(2,1)S(1)}, u32[]{:S(2)}, u32[]{:S(2)}) async-start(bf16[8,256,256]{1,2,0:T(8,128)(2,1)} %copy.97), calls=%async_computation.4 | async-start | bytes 2097152 | tf_op jit(solution)/shard_map/all_to_all | solution.py:940
  412.7 46.2 %collective-permute-start = (bf16[4,192,1024]{2,1,0:T(8,128)(2,1)}, bf16[4,192,1024]{2,1,0:T(8,128)(2,1)}, u32[]{:S(2)}, u32[]{:S(2)}) collective-permute-start(bf16[4,192,1024]{2,1,0:T(8,128)(2,1)} %get-tuple-element.40), channel_id=1, source_target_pairs={{0,1},{1,0},{2,3},{3,2},{4,5},{5,4},{6,7},{7,6},{8,9},{9,8},{10,11... | collective-permute-start | bytes 4718600 | tf_op jit(solution)/shard_map/ppermute | solution.py:255
  414.3 77.4 %collective-permute-start.1 = (bf16[4,192,1024]{2,1,0:T(8,128)(2,1)}, bf16[4,192,1024]{2,1,0:T(8,128)(2,1)}, u32[]{:S(2)}, u32[]{:S(2)}) collective-permute-start(bf16[4,192,1024]{2,1,0:T(8,128)(2,1)} %get-tuple-element.41), channel_id=1, source_target_pairs={{0,2},{1,3},{2,0},{3,1},{4,6},{5,7},{6,4},{7,5},{8,10},{9,11},{10,... | collective-permute-start | bytes 4718600 | tf_op jit(solution)/shard_map/ppermute | solution.py:255
  414.8 88.1 %collective-permute-start.2 = (bf16[4,192,1024]{2,1,0:T(8,128)(2,1)}, bf16[4,192,1024]{2,1,0:T(8,128)(2,1)}, u32[]{:S(2)}, u32[]{:S(2)}) collective-permute-start(bf16[4,192,1024]{2,1,0:T(8,128)(2,1)} %get-tuple-element.42), channel_id=1, source_target_pairs={{0,4},{1,5},{2,6},{3,7},{4,0},{5,1},{6,2},{7,3},{8,12},{9,13},{10,... | collective-permute-start | bytes 4718600 | tf_op jit(solution)/shard_map/ppermute | solution.py:255
  435.6 5.2 copy-start.4
  435.6 5.2 copy-start.40
  435.6 5.2 copy-start.43
  439.6 5.9 copy-start.27
  440.8 4.7 copy-start.28
  440.8 4.7 copy-start.41
  664.5 4.9 copy-start.22
  (22 other events, 50.1 us)
Sparse Core Ops, SparseCore 0:
  12.8 69.5 all-gather.4
Sparse Core Ops, SparseCore 1:
  100.5 22.4 all-gather.8
  172.7 22.7 all-gather.6

commit v6 on v5

--- a/solution.py
+++ b/solution.py
@@ -151,13 +151,17 @@
     out_ref,
     total_ref,
     start_ref,
-    grad_query_ref,
-    grad_key_ref,
-    grad_value_ref,
+    cosine_ref,
+    sine_ref,
+    back_ref,
     key_s,
     value_s,
+    grad_query_s,
+    grad_key_s,
+    grad_value_s,
     *,
     heads,
+    blocks,
 ):
     step = pl.program_id(0)
     width = heads * HEAD_DIM
@@ -166,8 +170,8 @@
     def _():
         key_s[...] = rows_ref[:, width : width + HEAD_DIM]
         value_s[...] = rows_ref[:, width + HEAD_DIM : width + 2 * HEAD_DIM]
-        grad_key_ref[...] = jnp.zeros_like(grad_key_ref)
-        grad_value_ref[...] = jnp.zeros_like(grad_value_ref)
+        grad_key_s[...] = jnp.zeros_like(grad_key_s)
+        grad_value_s[...] = jnp.zeros_like(grad_value_s)
 
     own = pl.ds(pl.multiple_of(step * BLOCK, BLOCK), BLOCK)
     block_rows = rows_ref[own, :]
@@ -191,8 +195,8 @@
         place = j * BLOCK + lax.broadcasted_iota(jnp.int32, (BLOCK, BLOCK), 0)
         allowed = (place >= starts) & (place <= at)
         result = []
-        key_sum = grad_key_ref[rows, :]
-        value_sum = grad_value_ref[rows, :]
+        key_sum = grad_key_s[rows, :]
+        value_sum = grad_value_s[rows, :]
         for h in range(heads):
             scores = jnp.where(allowed, dot_nt(key_block, scaled[h]), far_below)
             prob = jnp.exp(scores - totals[h])
@@ -201,27 +205,45 @@
             value_sum = value_sum + product(prob.astype(jnp.bfloat16), grads[h])
             key_sum = key_sum + product(grad_scores, queries[h])
             result.append(carry[h] + dot_tn(grad_scores, key_block))
-        grad_key_ref[rows, :] = key_sum
-        grad_value_ref[rows, :] = value_sum
+        grad_key_s[rows, :] = key_sum
+        grad_value_s[rows, :] = value_sum
         return tuple(result)
 
     first = tuple(jnp.zeros((BLOCK, HEAD_DIM), jnp.float32) for _ in range(heads))
     done = lax.fori_loop(low_ref[step], step + 1, one, first)
     for h in range(heads):
-        grad_query_ref[:, h * HEAD_DIM : (h + 1) * HEAD_DIM] = done[h]
-
-
-def attend_backward(rows, grads, outs, totals, starts, lows, heads):
+        grad_query_s[own, h * HEAD_DIM : (h + 1) * HEAD_DIM] = done[h]
+
+    @pl.when(step == blocks - 1)
+    def _():
+        def turn(j, carry):
+            rows = pl.ds(pl.multiple_of(j * BLOCK, BLOCK), BLOCK)
+            cosine = cosine_ref[rows, :]
+            sine = sine_ref[rows, :]
+            parts = [
+                grad_query_s[rows, h * HEAD_DIM : (h + 1) * HEAD_DIM] for h in range(heads)
+            ]
+            parts.append(grad_key_s[rows, :])
+            half = HEAD_DIM // 2
+            turned = [
+                part * cosine - jnp.concatenate([part[:, half:], part[:, :half]], 1) * sine
+                for part in parts
+            ]
+            turned.append(grad_value_s[rows, :])
+            back_ref[rows, :] = jnp.concatenate(turned, 1).astype(jnp.bfloat16)
+            return carry
+
+        lax.fori_loop(0, blocks, turn, 0)
+
+
+def attend_backward(rows, grads, outs, totals, starts, lows, cosine, sine, heads):
     length, width = rows.shape
     blocks = length // BLOCK
     whole = lambda i, low: (0, 0)
+    once = pl.Buffered(1)
     return pl.pallas_call(
-        functools.partial(attend_backward_kernel, heads=heads),
-        out_shape=(
-            jax.ShapeDtypeStruct((length, heads * HEAD_DIM), jnp.float32),
-            jax.ShapeDtypeStruct((length, HEAD_DIM), jnp.float32),
-            jax.ShapeDtypeStruct((length, HEAD_DIM), jnp.float32),
-        ),
+        functools.partial(attend_backward_kernel, heads=heads, blocks=blocks),
+        out_shape=jax.ShapeDtypeStruct((length, width), jnp.bfloat16),
         grid_spec=pltpu.PrefetchScalarGridSpec(
             num_scalar_prefetch=1,
             grid=(blocks,),
@@ -231,19 +253,24 @@
                 pl.BlockSpec((heads * HEAD_DIM, BLOCK), lambda i, low: (0, i)),
                 pl.BlockSpec((1, heads, BLOCK), lambda i, low: (i, 0, 0)),
                 pl.BlockSpec((1, 1, BLOCK), lambda i, low: (i, 0, 0)),
+                pl.BlockSpec((length, HEAD_DIM), whole, pipeline_mode=once),
+                pl.BlockSpec((length, HEAD_DIM), whole, pipeline_mode=once),
             ],
-            out_specs=[
-                pl.BlockSpec((BLOCK, heads * HEAD_DIM), lambda i, low: (i, 0)),
-                pl.BlockSpec((length, HEAD_DIM), whole),
-                pl.BlockSpec((length, HEAD_DIM), whole),
-            ],
+            out_specs=pl.BlockSpec((length, width), whole),
             scratch_shapes=[
                 pltpu.VMEM((length, HEAD_DIM), jnp.bfloat16),
                 pltpu.VMEM((length, HEAD_DIM), jnp.bfloat16),
+                pltpu.VMEM((length, heads * HEAD_DIM), jnp.float32),
+                pltpu.VMEM((length, HEAD_DIM), jnp.float32),
+                pltpu.VMEM((length, HEAD_DIM), jnp.float32),
             ],
         ),
         name="attend_backward",
-    )(lows, rows, grads, outs, totals, starts)
+    )(lows, rows, grads, outs, totals, starts, cosine, sine)
+
+
+def after(value, *others):
+    return lax.optimization_barrier((value, *others))[0]
 
 
 def bits_of(size):
@@ -883,8 +910,8 @@
     ep_bits = [("ep", b) for b in range(bits_of(n_ep))]
     count = experts_all // n_ep
     near = count * 5 // 8
-    kinds = [2, 0, 1, 0, 1][:near] + [0, 1, 2][near - count :]
-    leads = [0, len(rep_bits) - 2, len(rep_bits) - 1]
+    kinds = [0, 1, 0, 1, 0][:near] + [0, 1, 0][near - count :]
+    leads = [0, len(rep_bits) - 2]
     orders = [
         [leads[kind]] + [b for b in range(len(rep_bits)) if b != leads[kind]] for kind in kinds
     ]
@@ -901,14 +928,10 @@
         ep_bits[::-1],
         ep_bits,
     )
-    came = [came_near] + [
-        swap(half, "rep", order[0])[None] for half, order in zip(sent, orders[near:])
-    ]
     units = [(e, 0, e, [("rep", b) for b in orders[e]]) for e in range(near)]
     units += [
         (e, 1 + e - near, 0, [("rep", b) for b in orders[e]]) for e in range(near, count)
     ]
-    units = units[1:3] + units[:1] + units[3:]
     output = hidden + branch_scale * out_sum
     grad_probs = inner_back.reshape(experts_all, rows_dev).T
     grad_logits = probs * (grad_probs - jnp.sum(grad_probs * probs, -1, keepdims=True))
@@ -929,14 +952,14 @@
         concat_axis=0,
         tiled=True,
     ).reshape(length, head_width)
-    grad_query, grad_key, grad_value = attend_backward(
-        head_rows, grad_heads, mixed_out, totals, starts, lows, heads
-    )
-    turn_back = jnp.concatenate([grad_query, grad_key], 1)
-    turn_back = turn_back * jnp.tile(cosine, (1, heads + 1)) - swap_halves(turn_back) * jnp.tile(
-        sine, (1, heads + 1)
-    )
-    returning = jnp.concatenate([turn_back, grad_value], 1).astype(jnp.bfloat16)
+    beside = [
+        swap(after(sent[k], grad_heads), "rep", orders[near + k][0])[None]
+        for k in range(len(sent) - 1)
+    ]
+    returning = attend_backward(
+        head_rows, grad_heads, mixed_out, totals, starts, lows, cosine, sine, heads
+    )
+    returning = after(returning, *beside)
     returned = lax.all_to_all(
         returning.reshape(n_rep, rows_dev, head_width + 2 * HEAD_DIM),
         "rep",
@@ -944,6 +967,8 @@
         concat_axis=0,
         tiled=True,
     ).transpose(1, 0, 2)
+    last = swap(after(sent[-1], returned), "rep", orders[-1][0])[None]
+    came = [came_near] + beside + [last]
     grad_query_rows = returned[:, :, :head_width].reshape(rows_dev, query_width)
     key_back = returned[:, :, head_width : head_width + HEAD_DIM]
     value_back = returned[:, :, head_width + HEAD_DIM :]

time: 687 us -> 651 us (0.948)
  waiting for transfers between devices: 153 us -> 122 us
  local copies, waits for them, and re-layouts: 62.1 us -> 41.4 us
  blocking collectives: 38.9 us -> 55.7 us
  Pallas kernels: 339 us -> 349 us
    pallas_call x1, Pallas kernels: 156 us -> 182 us  [reduce_rest(): pl.pallas_call(functools.partial(reduce_kernel, units=units, n_came=len(c...]
    ppermute x3, waiting for transfers between devices: 48.2 us -> 27.3 us  [swap(): return lax.ppermute(sent, axis, [(i, i ^ 1 << bit) for i in range(size)])]
    all_to_all x0 -> x1, blocking collectives: none -> 16.7 us  [on_device(): lax.all_to_all(grad_mixed.reshape(rows_dev, n_rep, head_width).transpose(...]
    concatenate x9 -> x0, local copies, waits for them, and re-layouts: 14 us -> none  [the longest x2 4.39 us: swap_halves(): jnp.roll(values, half_dim, 1)]
    pallas_call x1, Pallas kernels: 126 us -> 116 us  [experts(): pl.pallas_call(functools.partial(experts_kernel, sources=sources, rows_de...]
    all_to_all x1 -> x0, waiting for transfers between devices: 7.69 us -> none  [on_device(): lax.all_to_all(grad_mixed.reshape(rows_dev, n_rep, head_width).transpose(...]
    unnamed x99 -> x88, local copies, waits for them, and re-layouts: 18.8 us -> 14.6 us
  transfers between devices with their start and end apart: 9 -> 8, of which waited for: 8 -> 7; matrix products, arithmetic and copies ran while one was open for 7% -> 6% of each run, Pallas kernels for 4% -> 8%
where the time goes in v6:
time: 651 us; the launch traced here: 643 us
  Pallas kernels  349 us (54%)
  waiting for transfers between devices  122 us (19%)
  blocking collectives  55.7 us (9%)
  local copies, waits for them, and re-layouts  41.4 us (6%)
  other arithmetic  22.4 us (3%)
  matrix products  21.3 us (3%)
  between operations  16.1 us (2%)
  starting transfers between devices  15.2 us (2%)
    pallas_call x1, Pallas kernels, reduce_rest(): pl.pallas_call(functools.partial(reduce_kernel, units=units, n_came=len(c...  182 us
    pallas_call x1, Pallas kernels, experts(): pl.pallas_call(functools.partial(experts_kernel, sources=sources, rows_de...  116 us
    all_gather x1, waiting for transfers between devices, on_device(): full = lax.all_gather(joined, everyone, axis=0, tiled=True)  37.7 us
    pallas_call x1, Pallas kernels, attend_backward(): pl.pallas_call(functools.partial(attend_backward_kernel, heads=heads, blo...  29.6 us
    ppermute x3, waiting for transfers between devices, swap(): return lax.ppermute(sent, axis, [(i, i ^ 1 << bit) for i in range(size)])  27.3 us
    all_to_all x1, waiting for transfers between devices, on_device(): lax.all_to_all(sending, 'rep', split_axis=0, concat_axis=0, tiled=True)  23.1 us
    pallas_call x1, Pallas kernels, attend_forward(): pl.pallas_call(functools.partial(attend_forward_kernel, heads=heads), out...  21.7 us
    all_to_all x1, waiting for transfers between devices, on_device(): lax.all_to_all(returning.reshape(n_rep, rows_dev, head_width + 2 * HEAD_D...  19.3 us
  transfers between devices with their start and end apart: 8, of which 7 were waited for; matrix products, arithmetic and copies ran while one was open for 6% of the time, Pallas kernels for 8%

profile of v6, /device:TPU:26, one launch (start us, length us, event | category | flops | bytes accessed | tf_op | source)
XLA Modules:
  0.0 643.0 jit_solution(16196080896346456522)
XLA Ops:
  12.7 16.3 %all-gather = s32[1,2048]{1,0:T(1,128)S(1)} all-gather(s32[1,256]{1,0:T(1,128)} %param.14), channel_id=2, replica_groups=mesh['ep'=4,'rep'=8] {'rep'}, dimensions={1}, use_global_device_ids=true | all-gather | bytes 9216 | tf_op jit(solution)/shard_map/all_gather | solution.py:828
  30.8 3.7 multiply_sine_fusion
  37.7 1.9 copy.71
  40.9 3.0 copy.73
  44.7 37.7 %all-gather.5.cloned.1.call-done = bf16[1024,3104]{1,0:T(8,128)(2,1)} async-done(((bf16[32,3104]{1,0:T(8,128)(2,1)}), bf16[1024,3104]{1,0:T(8,128)(2,1)}) %all-gather.5.cloned.1.call-update) | async-done | bytes 6357008 | tf_op jit(solution)/shard_map/all_gather | solution.py:850
  82.4 3.5 fusion.2
  90.0 2.4 maximum_bitcast_fusion
  92.4 5.5 all-to-all-start
  99.7 23.1 %all-to-all-done = bf16[8,256,256]{2,1,0:T(8,128)(2,1)S(1)} async-done(((bf16[8,256,256]{2,1,0:T(8,128)(2,1)}), bf16[8,256,256]{2,1,0:T(8,128)(2,1)S(1)}, u32[]{:S(2)}, u32[]{:S(2)}) %all-to-all-start) | async-done | bytes 1048608 | tf_op jit(solution)/shard_map/all_to_all | solution.py:874
  123.8 21.7 %attend_forward.1 = (bf16[2048,128]{1,0:T(8,128)(2,1)}, f32[128,2048]{1,0:T(8,128)}, f32[8,2,256]{2,1,0:T(2,128)}) custom-call(s32[8]{0:T(128)} %and_select_fusion.low_ref, bf16[2048,256]{1,0:T(8,128)(2,1)} %bitcast.130, s32[8,1,256]{2,1,0:T(1,128)} %bitcast.152), custom_call_target="tpu_custom_call" | custom-call | tf_op jit(solution)/shard_map/attend_forward/pallas_call | solution.py:119
  146.7 17.1 %all_to_all.25 = bf16[8,256,128]{1,2,0:T(8,128)(2,1)S(1)} all-to-all(bf16[8,256,128]{1,2,0:T(8,128)(2,1)S(1)} %copy.79), channel_id=1, replica_groups=mesh['ep'=4,'rep'=8] {'rep'}, dimensions={0} | all-to-all | bytes 1048576 | tf_op jit(solution)/shard_map/all_to_all | solution.py:877
  163.8 2.6 multiply_reduce_fusion.2
  170.7 5.7 all_to_all.26
  177.0 14.6 %all-gather.7.cloned.1.call-done = bf16[1024,1024]{1,0:T(8,128)(2,1)} async-done(((bf16[256,1024]{1,0:T(8,128)(2,1)}), bf16[1024,1024]{1,0:T(8,128)(2,1)}) %all-gather.7.cloned.1.call-update) | async-done | bytes 2097168 | tf_op jit(solution)/shard_map/all_gather | solution.py:907
  191.6 115.8 %experts.1 = (f32[256,1024]{1,0:T(8,128)}, f32[256,1024]{1,0:T(8,128)}, f32[4,8,256]{2,1,0:T(8,128)}, bf16[8,4,192,1024]{3,2,1,0:T(8,128)(2,1)}, bf16[5,4,192,10...) custom-call(bf16[2,2,256,1024]{3,2,1,0:T(8,128)(2,1)} %bitcast.140, ...), custom_call_target="tpu_custom_call" | custom-call | tf_op jit(solution)/shard_map/experts/pallas_call | solution.py:733
  308.4 2.6 multiply_reduce_fusion
  312.4 2.5 fusion.20
  315.0 16.7 %all_to_all.27 = bf16[8,256,128]{2,1,0:T(8,128)(2,1)} all-to-all(bf16[8,256,128]{2,1,0:T(8,128)(2,1)S(1)} %bitcast.143), channel_id=1, replica_groups=mesh['ep'=4,'rep'=8] {'rep'}, dimensions={0} | all-to-all | bytes 1048576 | tf_op jit(solution)/shard_map/all_to_all | solution.py:948
  333.5 2.0 pad_maximum_fusion.2
  335.4 29.6 %attend_backward.1 = bf16[2048,256]{1,0:T(8,128)(2,1)} custom-call(s32[8]{0:T(128)} %and_select_fusion.low_ref, bf16[2048,256]{1,0:T(8,128)(2,1)} %bitcast.131, bf16[2048,128]{1,0:T(8,128)(2,1)} %bitcast.141, f32[128,2048]{1,0:T(8,128)} %get-tuple-element.34.out_ref, f32[8,2,256]{2,1,0:T(2,128)} %get-tuple-element.35.total_ref, s32[8,1,256]{2,1,0:T(1,128)} %bitcast.153, ...), custom_call_target="tpu_custom_call" | custom-call | tf_op jit(solution)/shard_map/attend_backward/pallas_call | solution.py:244
  365.0 2.7 collective-permute-done
  369.3 2.3 copy.81
  371.6 5.8 all-to-all-start.4
  378.2 2.0 convolution_convert_fusion.1
  380.2 19.3 %all-to-all-done.4 = bf16[8,256,256]{1,2,0:T(8,128)(2,1)S(1)} async-done(((bf16[8,256,256]{1,2,0:T(8,128)(2,1)}), bf16[8,256,256]{1,2,0:T(8,128)(2,1)S(1)}, u32[]{:S(2)}, u32[]{:S(2)}) %all-to-all-start.4) | async-done | bytes 1048608 | tf_op jit(solution)/shard_map/all_to_all | solution.py:963
  404.8 1.9 collective-permute-start.2
  406.7 3.7 fusion.33
  412.7 2.4 convolution_convert_fusion
  415.2 3.3 pad_maximum_fusion.refs_5_
  418.5 23.1 %collective-permute-done.2 = bf16[4,192,1024]{2,1,0:T(8,128)(2,1)} collective-permute-done((bf16[4,192,1024]{2,1,0:T(8,128)(2,1)}, bf16[4,192,1024]{2,1,0:T(8,128)(2,1)}, u32[]{:S(2)}, u32[]{:S(2)}) %collective-permute-start.2) | collective-permute-done | bytes 1572896 | tf_op jit(solution)/shard_map/ppermute | solution.py:282
  441.5 181.9 %reduce_rest.1 = (f32[8,128,1024]{2,1,0:T(8,128)}, f32[8,512,128]{2,1,0:T(8,128)}, f32[32,3104]{1,0:T(8,128)}, f32[1,64]{1,0:T(1,128)}) custom-call(bf16[8,4,192,1024]{3,2,1,0:T(8,128)(2,1)} %get-tuple-element.41.refs_0_, bf16[5,4,192,1024]{3,2,1,0:T(8,128)(2,1)} %get-tuple-element.42.refs_1_, bf16[1,4,192,1024]{3,2,1,0:T(8,128)(2,1)} %bitcast.144, ...), custom_call_target="tpu_custom_call" | custom-call | tf_op jit(solution)/shard_map/reduce_rest/pallas_call | solution.py:534
  629.3 4.9 copy.108
  (154 shorter events, 45.7 us)
Async XLA Ops:
  8.0 74.4 %all-gather.5.cloned.1.call-start = ((), (), s32[]{:S(2)}) async-start(), calls=%async_computation.5 | async-start | bytes 6758400 | tf_op jit(solution)/shard_map/all_gather | solution.py:850
  30.8 68.3 %copy-start.25 = (s32[2048]{0:T(1024)}, s32[2048]{0:T(1024)S(1)}, u32[]{:S(2)}) copy-start(s32[2048]{0:T(1024)S(1)} %convert_reduce_fusion) | copy-start | bytes 24580
  39.5 4.4 copy-start.8
  40.9 41.5 %copy-start.35 = (f32[1024]{0:T(1024)S(1)}, f32[1024]{0:T(1024)}, u32[]{:S(2)}) copy-start(f32[1024]{0:T(1024)} %param.16) | copy-start | bytes 12292
  44.7 41.2 %copy-start.38 = (f32[256]{0:T(256)}, f32[256]{0:T(256)S(1)}, u32[]{:S(2)}) copy-start(f32[256]{0:T(256)S(1)} %get-tuple-element.75) | copy-start | bytes 3076
  90.0 7.9 %copy-start.16 = (f32[1,256,1024]{2,1,0:T(8,128)S(1)}, f32[1,256,1024]{2,1,0:T(8,128)}, u32[]{:S(2)}) copy-start(f32[1,256,1024]{2,1,0:T(8,128)} %param.25) | copy-start | bytes 3145732
  92.4 30.3 %all-to-all-start = ((bf16[8,256,256]{2,1,0:T(8,128)(2,1)}), bf16[8,256,256]{2,1,0:T(8,128)(2,1)S(1)}, u32[]{:S(2)}, u32[]{:S(2)}) async-start(bf16[8,256,256]{2,1,0:T(8,128)(2,1)} %maximum_bitcast_fusion), calls=%async_computation | async-start | bytes 2097152 | tf_op jit(solution)/shard_map/all_to_all | solution.py:874
  97.9 79.0 %all-gather.9.cloned.1.call-start = ((), (), s32[]{:S(2)}) async-start(), calls=%async_computation.7 | async-start | bytes 2621440 | tf_op jit(solution)/shard_map/all_gather | solution.py:908
  98.8 92.7 %all-gather.7.cloned.1.call-start = ((), (), s32[]{:S(2)}) async-start(), calls=%async_computation.6 | async-start | bytes 2621440 | tf_op jit(solution)/shard_map/all_gather | solution.py:907
  163.8 3.8 copy-start.28
  170.0 6.3 copy-start.26
  307.4 3.7 copy-start.1
  307.4 3.7 copy-start.17
  312.4 21.0 %copy-start.3 = (f32[2048,32]{1,0:T(8,128)S(1)}, f32[2048,32]{1,0:T(8,128)}, u32[]{:S(2)}) copy-start(f32[2048,32]{1,0:T(8,128)} %copy-done.2) | copy-start | bytes 786436
  312.4 21.0 %copy-start.5 = (f32[2048,32]{1,0:T(8,128)S(1)}, f32[2048,32]{1,0:T(8,128)}, u32[]{:S(2)}) copy-start(f32[2048,32]{1,0:T(8,128)} %copy-done.4) | copy-start | bytes 786436
  312.4 21.0 %copy-start.7 = (f32[2048,32]{1,0:T(8,128)S(1)}, f32[2048,32]{1,0:T(8,128)}, u32[]{:S(2)}) copy-start(f32[2048,32]{1,0:T(8,128)} %copy-done.6) | copy-start | bytes 786436
  331.7 36.0 %collective-permute-start = (bf16[4,192,1024]{2,1,0:T(8,128)(2,1)}, bf16[4,192,1024]{2,1,0:T(8,128)(2,1)S(1)}, u32[]{:S(2)}, u32[]{:S(2)}) collective-permute-start(bf16[4,192,1024]{2,1,0:T(8,128)(2,1)} %get-tuple-element.37), channel_id=1, source_target_pairs={{0,1},{1,0},{2,3},{3,2},{4,5},{5,4},{6,7},{7,6},{8,9},{9,8},{10,11... | collective-permute-start | bytes 4718600 | tf_op jit(solution)/shard_map/ppermute | solution.py:282
  333.4 35.8 %collective-permute-start.1 = (bf16[4,192,1024]{2,1,0:T(8,128)(2,1)}, bf16[4,192,1024]{2,1,0:T(8,128)(2,1)}, u32[]{:S(2)}, u32[]{:S(2)}) collective-permute-start(bf16[4,192,1024]{2,1,0:T(8,128)(2,1)} %get-tuple-element.39), channel_id=1, source_target_pairs={{0,2},{1,3},{2,0},{3,1},{4,6},{5,7},{6,4},{7,5},{8,10},{9,11},{10,... | collective-permute-start | bytes 4718600 | tf_op jit(solution)/shard_map/ppermute | solution.py:282
  369.3 8.3 %copy-start.12 = (bf16[256,1024]{1,0:T(8,128)(2,1)S(1)}, bf16[256,1024]{1,0:T(8,128)(2,1)}, u32[]{:S(2)}) copy-start(bf16[256,1024]{1,0:T(8,128)(2,1)} %multiply_convert_fusion.1) | copy-start | bytes 1572868
  369.3 8.3 %copy-start.22 = (f32[4,8,256]{2,1,0:T(8,128)S(1)}, f32[4,8,256]{2,1,0:T(8,128)}, u32[]{:S(2)}) copy-start(f32[4,8,256]{2,1,0:T(8,128)} %get-tuple-element.33) | copy-start | bytes 98308
  369.3 8.3 %copy-start.27 = (f32[256]{0:T(256)S(1)}, f32[256]{0:T(256)}, u32[]{:S(2)}) copy-start(f32[256]{0:T(256)} %copy-done.26) | copy-start | bytes 3076
  369.3 8.3 %copy-start.31 = (f32[256]{0:T(256)S(1)}, f32[256]{0:T(256)}, u32[]{:S(2)}) copy-start(f32[256]{0:T(256)} %copy-done.30) | copy-start | bytes 3076
  369.3 8.9 %copy-start.15 = (bf16[8,256,128]{1,2,0:T(8,128)(2,1)S(1)}, bf16[8,256,128]{1,2,0:T(8,128)(2,1)}, u32[]{:S(2)}) copy-start(bf16[8,256,128]{1,2,0:T(8,128)(2,1)} %copy-done.14) | copy-start | bytes 1572868
  371.6 27.8 %all-to-all-start.4 = ((bf16[8,256,256]{1,2,0:T(8,128)(2,1)}), bf16[8,256,256]{1,2,0:T(8,128)(2,1)S(1)}, u32[]{:S(2)}, u32[]{:S(2)}) async-start(bf16[8,256,256]{1,2,0:T(8,128)(2,1)} %copy.81), calls=%async_computation.4 | async-start | bytes 2097152 | tf_op jit(solution)/shard_map/all_to_all | solution.py:963
  399.5 7.2 %copy-start.9 = (f32[1,256,1024]{2,1,0:T(8,128)S(1)}, f32[1,256,1024]{2,1,0:T(8,128)}, u32[]{:S(2)}) copy-start(f32[1,256,1024]{2,1,0:T(8,128)} %param.13) | copy-start | bytes 3145732
  399.5 7.2 %copy-start.36 = (f32[1024]{0:T(1024)S(1)}, f32[1024]{0:T(1024)}, u32[]{:S(2)}) copy-start(f32[1024]{0:T(1024)} %param.16) | copy-start | bytes 12292
  399.5 7.2 %copy-start.39 = (f32[256]{0:T(256)S(1)}, f32[256]{0:T(256)}, u32[]{:S(2)}) copy-start(f32[256]{0:T(256)} %copy-done.38) | copy-start | bytes 3076
  402.2 8.1 %copy-start.23 = (bf16[256,512]{1,0:T(8,128)(2,1)}, bf16[256,512]{1,0:T(8,128)(2,1)S(1)}, u32[]{:S(2)}) copy-start(bf16[256,512]{1,0:T(8,128)(2,1)S(1)} %copy.83) | copy-start | bytes 786436
  403.4 6.9 %copy-start.24 = (bf16[256,512]{1,0:T(8,128)(2,1)}, bf16[256,512]{1,0:T(8,128)(2,1)S(1)}, u32[]{:S(2)}) copy-start(bf16[256,512]{1,0:T(8,128)(2,1)S(1)} %copy.84) | copy-start | bytes 786436
  404.8 5.6 copy-start.37
  404.8 36.7 %collective-permute-start.2 = (bf16[4,192,1024]{2,1,0:T(8,128)(2,1)}, bf16[4,192,1024]{2,1,0:T(8,128)(2,1)}, u32[]{:S(2)}, u32[]{:S(2)}) collective-permute-start(bf16[4,192,1024]{2,1,0:T(8,128)(2,1)} %get-tuple-element.44), channel_id=1, source_target_pairs={{0,1},{1,0},{2,3},{3,2},{4,5},{5,4},{6,7},{7,6},{8,9},{9,8},{10,11... | collective-permute-start | bytes 4718600 | tf_op jit(solution)/shard_map/ppermute | solution.py:282
  629.3 4.9 copy-start.18
  (17 other events, 32.5 us)
Sparse Core Ops, SparseCore 0:
  12.8 69.5 all-gather.4
Sparse Core Ops, SparseCore 1:
  100.5 22.4 all-gather.8
  168.7 22.9 all-gather.6

commit v7 on v6

--- a/solution.py
+++ b/solution.py
@@ -381,11 +381,10 @@
             self.copy(k).wait_send()
 
 
-def reduce_kernel(*refs, units, n_came, labels, weight_order, share):
-    keep_ref, *refs = refs
-    came_refs, refs = (refs[:n_came], refs[n_came:])
+def reduce_kernel(*refs, units, n_parts, labels, weight_order, share):
+    part_refs, refs = (refs[:n_parts], refs[n_parts:])
     weight_ref, gain_ref, up_ref, down_ref, weight_out, gain_out, *refs = refs
-    steps = len(units[0][3]) - 1
+    steps = len(units[0][2]) - 1
     sends, keeps, gets = ([], [], [])
     for _ in range(steps):
         sends.append(refs[0])
@@ -406,7 +405,7 @@
         )
         for number, first in enumerate((weight_ref, gain_ref))
     ]
-    count, spots, tall, width = keep_ref.shape
+    _, spots, tall, width = load_keep.shape
     rows = 32 if tall % 32 == 0 else tall
     blocks = tall // rows
 
@@ -422,15 +421,24 @@
 
     lane_start(0)
 
-    def loads(n):
-        unit, g, place, _ = units[n]
-        slot = n % 2
-        return (
-            pltpu.make_async_copy(keep_ref.at[unit], load_keep.at[slot], load_sem.at[slot, 0]),
+    sequence = [
+        n for k in range(steps + 1) for n, unit in enumerate(units) if unit[3] == k
+    ]
+
+    def loads(turn):
+        _, parts, _, skip = units[sequence[turn]]
+        slot = turn % 2
+        size = spots >> skip
+        return [
             pltpu.make_async_copy(
-                came_refs[g].at[place], load_came.at[slot], load_sem.at[slot, 1]
-            ),
-        )
+                part_refs[which].at[place],
+                buffer.at[slot, pl.ds(0, size)],
+                load_sem.at[slot, number],
+            )
+            for number, ((which, place), buffer) in enumerate(
+                zip(parts, (load_keep, load_came))
+            )
+        ]
 
     def unit_copy(unit, order, k):
         axis, bit = order[k + 1]
@@ -464,23 +472,30 @@
         fill(keeps[k], mine)
 
     def begin_unit(n):
-        unit, _, _, order = units[n]
-        for copy in loads(n):
+        unit, _, order, skip = units[n]
+        turn = sequence.index(n)
+        for copy in loads(turn):
             copy.wait()
-        unit_add(unit, order, 0, load_keep.at[n % 2], load_came.at[n % 2])
-        if n + 2 < len(units):
-            for copy in loads(n + 2):
+        left, right = (load_keep.at[turn % 2], load_came.at[turn % 2])
+        if skip < steps:
+            unit_add(unit, order, skip, left, right)
+        else:
+            give(unit, left[0].astype(jnp.float32) + right[0].astype(jnp.float32))
+        if turn + 2 < len(units):
+            for copy in loads(turn + 2):
                 copy.start()
 
     def next_unit(n, k):
-        unit, _, _, order = units[n]
+        unit, _, order, _ = units[n]
         unit_copy(unit, order, k - 1).wait_recv()
         unit_add(unit, order, k, keeps[k - 1].at[unit], gets[k - 1].at[unit])
 
     def end_unit(n):
-        unit, _, _, order = units[n]
+        unit, _, order, _ = units[n]
         unit_copy(unit, order, steps - 1).wait_recv()
-        total = keeps[-1][unit, 0].astype(jnp.float32) + gets[-1][unit, 0].astype(jnp.float32)
+        give(unit, keeps[-1][unit, 0].astype(jnp.float32) + gets[-1][unit, 0].astype(jnp.float32))
+
+    def give(unit, total):
         up_ref[unit] = total[:share]
         pieces = width // share
         rest = tall - share
@@ -489,14 +504,23 @@
                 share:, p * share : (p + 1) * share
             ]
 
-    for n in range(min(2, len(units))):
-        for copy in loads(n):
+    for turn in range(min(2, len(units))):
+        for copy in loads(turn):
             copy.start()
-    work = [functools.partial(begin_unit, n) for n in range(len(units))]
-    for k in range(1, steps):
-        work += [functools.partial(next_unit, n, k) for n in range(len(units))]
-    work += [functools.partial(end_unit, n) for n in range(len(units))]
-    marks = [len(units) + (len(work) - len(units)) * k // bits for k in range(bits)]
+    work = []
+    first_jobs = 0
+    for k in range(steps):
+        for n, unit in enumerate(units):
+            if unit[3] == k:
+                work.append(functools.partial(begin_unit, n))
+            elif unit[3] < k:
+                work.append(functools.partial(next_unit, n, k))
+        first_jobs = first_jobs or len(work)
+    for last in (True, False):
+        for n, unit in enumerate(units):
+            if (unit[3] == steps) == last:
+                work.append(functools.partial(begin_unit if last else end_unit, n))
+    marks = [first_jobs + (len(work) - first_jobs) * k // bits for k in range(bits)]
     for number, job in enumerate(work):
         for k, mark in enumerate(marks[:-1]):
             if number == mark:
@@ -504,17 +528,18 @@
                 lane_start(k + 1)
         job()
     lane_add(bits - 1)
-    for unit, _, _, order in units:
-        for k in range(steps):
+    for unit, _, order, skip in units:
+        for k in range(skip, steps):
             unit_copy(unit, order, k).wait_send()
     for lane in lanes:
         lane.finish()
 
 
-def reduce_rest(keep, came, weights, gains, units, labels, weight_order, share):
-    count, spots, tall, width = keep.shape
+def reduce_rest(parts, weights, gains, units, labels, weight_order, share):
+    _, spots, tall, width = parts[0].shape
+    count = len(units)
     bits = len(labels)
-    steps = len(units[0][3]) - 1
+    steps = len(units[0][2]) - 1
     anywhere = pl.BlockSpec(memory_space=pl.ANY)
     vmem = pl.BlockSpec(memory_space=pltpu.VMEM)
     scratch = []
@@ -535,7 +560,7 @@
         functools.partial(
             reduce_kernel,
             units=units,
-            n_came=len(came),
+            n_parts=len(parts),
             labels=labels,
             weight_order=weight_order,
             share=share,
@@ -546,14 +571,14 @@
             jax.ShapeDtypeStruct(weights.shape[bits:], jnp.float32),
             jax.ShapeDtypeStruct(gains.shape[bits:], jnp.float32),
         ),
-        in_specs=[anywhere] * (1 + len(came)) + [vmem] * 2,
+        in_specs=[anywhere] * len(parts) + [vmem] * 2,
         out_specs=[vmem] * 4,
         scratch_shapes=scratch,
         compiler_params=pltpu.CompilerParams(
             collective_id=0, has_side_effects=True, vmem_limit_bytes=67 * 1000 * 1000
         ),
         name="reduce_rest",
-    )(keep, *came, weights, gains)
+    )(*parts, weights, gains)
 
 
 def experts_kernel(
@@ -909,8 +934,8 @@
     rep_bits = [("rep", b) for b in range(bits_of(n_rep))]
     ep_bits = [("ep", b) for b in range(bits_of(n_ep))]
     count = experts_all // n_ep
-    near = count * 5 // 8
-    kinds = [0, 1, 0, 1, 0][:near] + [0, 1, 0][near - count :]
+    near = count * 3 // 4
+    kinds = [k % 2 for k in range(near)] + [0] * (count - near)
     leads = [0, len(rep_bits) - 2]
     orders = [
         [leads[kind]] + [b for b in range(len(rep_bits)) if b != leads[kind]] for kind in kinds
@@ -928,10 +953,31 @@
         ep_bits[::-1],
         ep_bits,
     )
-    units = [(e, 0, e, [("rep", b) for b in orders[e]]) for e in range(near)]
-    units += [
-        (e, 1 + e - near, 0, [("rep", b) for b in orders[e]]) for e in range(near, count)
-    ]
+    rep_orders = [[("rep", b) for b in order] for order in orders]
+    early = list(range(0, near, 2))
+    late = early[2:]
+    early = early[:2]
+
+    def halves(left, right, label, e=None):
+        mine, _ = side(*label)
+        half = left.shape[-3] // 2
+
+        def total(which):
+            parts = []
+            for stack in (left, right):
+                start = [jnp.int32(0)] * stack.ndim
+                start[-3] = (which * half).astype(jnp.int32)
+                size = stack.shape[-3:]
+                if e is not None:
+                    start[0] = jnp.int32(e)
+                part = lax.dynamic_slice(
+                    stack, start, (1,) * (stack.ndim - 3) + (half,) + size[1:]
+                )
+                parts.append(part.reshape((half,) + size[1:]).astype(jnp.float32))
+            return (parts[0] + parts[1]).astype(jnp.bfloat16)
+
+        return (total(1 - mine), total(mine))
+
     output = hidden + branch_scale * out_sum
     grad_probs = inner_back.reshape(experts_all, rows_dev).T
     grad_logits = probs * (grad_probs - jnp.sum(grad_probs * probs, -1, keepdims=True))
@@ -952,10 +998,12 @@
         concat_axis=0,
         tiled=True,
     ).reshape(length, head_width)
-    beside = [
-        swap(after(sent[k], grad_heads), "rep", orders[near + k][0])[None]
-        for k in range(len(sent) - 1)
-    ]
+    beside = [swap(after(sent[0], grad_heads), *rep_orders[near][0])]
+    second = {}
+    for e in early:
+        give, own = halves(grad_keep, came_near, rep_orders[e][1], e)
+        second[e] = (own, swap(after(give, grad_heads), *rep_orders[e][1]))
+        beside.append(second[e][1])
     returning = attend_backward(
         head_rows, grad_heads, mixed_out, totals, starts, lows, cosine, sine, heads
     )
@@ -967,8 +1015,27 @@
         concat_axis=0,
         tiled=True,
     ).transpose(1, 0, 2)
-    last = swap(after(sent[-1], returned), "rep", orders[-1][0])[None]
-    came = [came_near] + beside + [last]
+    parts = [grad_keep, came_near]
+    steps_of = {e: ((0, e), (1, e), 0) for e in range(near)}
+
+    def put_by(e, own, got, skip):
+        steps_of[e] = ((len(parts), 0), (len(parts) + 1, 0), skip)
+        parts.extend([own[None], got[None]])
+
+    for k, half in enumerate(sent):
+        got = beside[0] if k == 0 else swap(after(half, returned), *rep_orders[near + k][0])
+        steps_of[near + k] = ((0, near + k), (len(parts), 0), 0)
+        parts.append(got[None])
+    for e in late:
+        give, own = halves(grad_keep, came_near, rep_orders[e][1], e)
+        put_by(e, own, swap(after(give, returned), *rep_orders[e][1]), 1)
+    for e in early:
+        give, own = halves(*second[e], rep_orders[e][2])
+        put_by(e, own, swap(after(give, returned), *rep_orders[e][2]), 2)
+    units = [
+        (e, steps_of[e][:2], rep_orders[e], steps_of[e][2])
+        for e in sorted(range(count), key=lambda e: (e < near, e))
+    ]
     grad_query_rows = returned[:, :, :head_width].reshape(rows_dev, query_width)
     key_back = returned[:, :, head_width : head_width + HEAD_DIM]
     value_back = returned[:, :, head_width + HEAD_DIM :]
@@ -999,8 +1066,7 @@
     shape = (2,) * len(labels)
     weight_grads = jnp.concatenate([grad_w_in, grad_out_w, grad_router], 1).astype(jnp.bfloat16)
     expert_up, expert_down, weights, gains = reduce_rest(
-        grad_keep,
-        came,
+        parts,
         weight_grads.reshape(shape + (-1, weight_grads.shape[1])),
         gains.reshape(shape + (1, -1)),
         units,

time: 651 us -> 648 us (level)
  Pallas kernels: 349 us -> 326 us
  other arithmetic: 22.4 us -> 36.7 us
  waiting for transfers between devices: 122 us -> 108 us
    pallas_call x1, Pallas kernels: 182 us -> 145 us  [reduce_rest(): pl.pallas_call(functools.partial(reduce_kernel, units=units, n_parts=len(...]
    convert_element_type x0 -> x3, other arithmetic: none -> 12.2 us  [total(): return (parts[0] + parts[1]).astype(jnp.bfloat16)]
    all_to_all x1, blocking collectives: 16.7 us -> 27.1 us  [on_device(): lax.all_to_all(grad_mixed.reshape(rows_dev, n_rep, head_width).transpose(...]
    all_to_all x1, waiting for transfers between devices: 19.3 us -> 10.8 us  [on_device(): lax.all_to_all(returning.reshape(n_rep, rows_dev, head_width + 2 * HEAD_D...]
    ppermute x3 -> x7, waiting for transfers between devices: 27.3 us -> 22.5 us  [swap(): return lax.ppermute(sent, axis, [(i, i ^ 1 << bit) for i in range(size)])]
    unnamed x88 -> x92, local copies, waits for them, and re-layouts: 14.6 us -> 15.7 us
  transfers between devices with their start and end apart: 8 -> 12, of which waited for: 7 -> 7; matrix products, arithmetic and copies ran while one was open for 6% -> 10% of each run, Pallas kernels for 8% -> 10%
where the time goes in v7:
time: 648 us; the launch traced here: 636 us
  Pallas kernels  326 us (50%)
  waiting for transfers between devices  108 us (17%)
  blocking collectives  61.8 us (10%)
  local copies, waits for them, and re-layouts  43.3 us (7%)
  other arithmetic  36.7 us (6%)
  matrix products  23.3 us (4%)
  starting transfers between devices  20 us (3%)
  between operations  16.3 us (3%)
    pallas_call x1, Pallas kernels, reduce_rest(): pl.pallas_call(functools.partial(reduce_kernel, units=units, n_parts=len(...  145 us
    pallas_call x1, Pallas kernels, experts(): pl.pallas_call(functools.partial(experts_kernel, sources=sources, rows_de...  120 us
    all_gather x1, waiting for transfers between devices, on_device(): full = lax.all_gather(joined, everyone, axis=0, tiled=True)  37.7 us
    pallas_call x1, Pallas kernels, attend_backward(): pl.pallas_call(functools.partial(attend_backward_kernel, heads=heads, blo...  34.7 us
    all_to_all x1, blocking collectives, on_device(): lax.all_to_all(grad_mixed.reshape(rows_dev, n_rep, head_width).transpose(...  27.1 us
    pallas_call x1, Pallas kernels, attend_forward(): pl.pallas_call(functools.partial(attend_forward_kernel, heads=heads), out...  26 us
    all_to_all x1, waiting for transfers between devices, on_device(): lax.all_to_all(sending, 'rep', split_axis=0, concat_axis=0, tiled=True)  23 us
    ppermute x7, waiting for transfers between devices, swap(): return lax.ppermute(sent, axis, [(i, i ^ 1 << bit) for i in range(size)])  22.5 us
  transfers between devices with their start and end apart: 12, of which 7 were waited for; matrix products, arithmetic and copies ran while one was open for 10% of the time, Pallas kernels for 10%

profile of v7, /device:TPU:26, one launch (start us, length us, event | category | flops | bytes accessed | tf_op | source)
XLA Modules:
  0.0 635.6 jit_solution(2988636696136597166)
XLA Ops:
  12.7 16.3 %all-gather = s32[1,2048]{1,0:T(1,128)S(1)} all-gather(s32[1,256]{1,0:T(1,128)} %param.14), channel_id=2, replica_groups=mesh['ep'=4,'rep'=8] {'rep'}, dimensions={1}, use_global_device_ids=true | all-gather | bytes 9216 | tf_op jit(solution)/shard_map/all_gather | solution.py:853
  30.8 3.7 multiply_sine_fusion
  40.9 3.0 copy.73
  44.7 37.7 %all-gather.5.cloned.1.call-done = bf16[1024,3104]{1,0:T(8,128)(2,1)} async-done(((bf16[32,3104]{1,0:T(8,128)(2,1)}), bf16[1024,3104]{1,0:T(8,128)(2,1)}) %all-gather.5.cloned.1.call-update) | async-done | bytes 6357008 | tf_op jit(solution)/shard_map/all_gather | solution.py:875
  82.4 3.5 fusion.2
  90.0 2.4 maximum_bitcast_fusion
  92.4 5.5 all-to-all-start
  99.8 23.0 %all-to-all-done = bf16[8,256,256]{2,1,0:T(8,128)(2,1)S(1)} async-done(((bf16[8,256,256]{2,1,0:T(8,128)(2,1)}), bf16[8,256,256]{2,1,0:T(8,128)(2,1)S(1)}, u32[]{:S(2)}, u32[]{:S(2)}) %all-to-all-start) | async-done | bytes 1048608 | tf_op jit(solution)/shard_map/all_to_all | solution.py:899
  123.8 26.0 %attend_forward.1 = (bf16[2048,128]{1,0:T(8,128)(2,1)}, f32[128,2048]{1,0:T(8,128)}, f32[8,2,256]{2,1,0:T(2,128)}) custom-call(s32[8]{0:T(128)} %and_select_fusion.low_ref, bf16[2048,256]{1,0:T(8,128)(2,1)} %bitcast.154, s32[8,1,256]{2,1,0:T(1,128)} %bitcast.176), custom_call_target="tpu_custom_call" | custom-call | tf_op jit(solution)/shard_map/attend_forward/pallas_call | solution.py:119
  151.0 12.9 %all_to_all.25 = bf16[8,256,128]{1,2,0:T(8,128)(2,1)S(1)} all-to-all(bf16[8,256,128]{1,2,0:T(8,128)(2,1)S(1)} %copy.79), channel_id=1, replica_groups=mesh['ep'=4,'rep'=8] {'rep'}, dimensions={0} | all-to-all | bytes 1048576 | tf_op jit(solution)/shard_map/all_to_all | solution.py:902
  163.9 2.6 multiply_reduce_fusion.2
  170.8 5.5 all_to_all.26
  176.9 14.4 %all-gather.7.cloned.1.call-done = bf16[1024,1024]{1,0:T(8,128)(2,1)} async-done(((bf16[256,1024]{1,0:T(8,128)(2,1)}), bf16[1024,1024]{1,0:T(8,128)(2,1)}) %all-gather.7.cloned.1.call-update) | async-done | bytes 2097168 | tf_op jit(solution)/shard_map/all_gather | solution.py:932
  191.3 120.5 %experts.1 = (f32[256,1024]{1,0:T(8,128)}, f32[256,1024]{1,0:T(8,128)}, f32[4,8,256]{2,1,0:T(8,128)}, bf16[8,4,192,1024]{3,2,1,0:T(8,128)(2,1)}, bf16[6,4,192,10...) custom-call(bf16[2,2,256,1024]{3,2,1,0:T(8,128)(2,1)} %bitcast.164, ...), custom_call_target="tpu_custom_call" | custom-call | tf_op jit(solution)/shard_map/experts/pallas_call | solution.py:758
  312.8 2.6 multiply_reduce_fusion
  316.9 2.3 fusion.20
  319.3 27.1 %all_to_all.27 = bf16[8,256,128]{2,1,0:T(8,128)(2,1)} all-to-all(bf16[8,256,128]{2,1,0:T(8,128)(2,1)S(1)} %bitcast.167), channel_id=1, replica_groups=mesh['ep'=4,'rep'=8] {'rep'}, dimensions={0} | all-to-all | bytes 1048576 | tf_op jit(solution)/shard_map/all_to_all | solution.py:994
  348.1 7.5 %add_convert_fusion = (bf16[1,2,192,1024]{3,2,1,0:T(8,128)(2,1)}, bf16[1,2,192,1024]{3,2,1,0:T(8,128)(2,1)}, bf16[2,192,1024]{2,1,0:T(8,128)(2,1)}, bf16[1,2,192...) fusion(bf16[6,4,192,1024]{3,2,1,0:T(8,128)(2,1)} %get-tuple-element.42.refs_1_, ...), kind=kLoop, calls=%fused_computation.17 | loop fusion | flops 9437184 | bytes 14155784 | tf_op jit(solution)/shard_map/convert_element_type | solution.py:977
  359.6 34.7 %attend_backward.1 = bf16[2048,256]{1,0:T(8,128)(2,1)} custom-call(s32[8]{0:T(128)} %and_select_fusion.low_ref, bf16[2048,256]{1,0:T(8,128)(2,1)} %bitcast.155, bf16[2048,128]{1,0:T(8,128)(2,1)} %bitcast.165, f32[128,2048]{1,0:T(8,128)} %get-tuple-element.37.out_ref, f32[8,2,256]{2,1,0:T(2,128)} %get-tuple-element.38.total_ref, s32[8,1,256]{2,1,0:T(1,128)} %bitcast.177, ...), custom_call_target="tpu_custom_call" | custom-call | tf_op jit(solution)/shard_map/attend_backward/pallas_call | solution.py:244
  395.5 2.3 copy.81
  397.9 6.0 all-to-all-start.4
  406.6 2.4 fusion.39
  409.0 2.3 fusion.37
  411.3 10.8 %all-to-all-done.4 = bf16[8,256,256]{1,2,0:T(8,128)(2,1)S(1)} async-done(((bf16[8,256,256]{1,2,0:T(8,128)(2,1)}), bf16[8,256,256]{1,2,0:T(8,128)(2,1)S(1)}, u32[]{:S(2)}, u32[]{:S(2)}) %all-to-all-start.4) | async-done | bytes 1048608 | tf_op jit(solution)/shard_map/all_to_all | solution.py:1011
  424.7 2.1 collective-permute-start.5
  431.9 3.7 fusion.33
  437.9 4.6 convolution_convert_fusion
  443.3 5.5 pad_maximum_fusion.refs_10_
  449.0 8.3 %collective-permute-done.5 = bf16[1,192,1024]{2,1,0:T(8,128)(2,1)} collective-permute-done((bf16[1,192,1024]{2,1,0:T(8,128)(2,1)}, bf16[1,192,1024]{2,1,0:T(8,128)(2,1)}, u32[]{:S(2)}, u32[]{:S(2)}) %collective-permute-start.5) | collective-permute-done | bytes 393248 | tf_op jit(solution)/shard_map/ppermute | solution.py:282
  457.3 13.9 %collective-permute-done.4 = bf16[2,192,1024]{2,1,0:T(8,128)(2,1)} collective-permute-done((bf16[2,192,1024]{2,1,0:T(8,128)(2,1)}, bf16[2,192,1024]{2,1,0:T(8,128)(2,1)}, u32[]{:S(2)}, u32[]{:S(2)}) %collective-permute-start.4) | collective-permute-done | bytes 786464 | tf_op jit(solution)/shard_map/ppermute | solution.py:282
  471.3 144.6 %reduce_rest.1 = (f32[8,128,1024]{2,1,0:T(8,128)}, f32[8,512,128]{2,1,0:T(8,128)}, f32[32,3104]{1,0:T(8,128)}, f32[1,64]{1,0:T(1,128)}) custom-call(bf16[8,4,192,1024]{3,2,1,0:T(8,128)(2,1)} %get-tuple-element.41.refs_0_, bf16[6,4,192,1024]{3,2,1,0:T(8,128)(2,1)} %get-tuple-element.42.refs_1_, bf16[1,4,192,1024]{3,2,1,0:T(8,128)(2,1)} %bitcast.168, ...), custom_call_target="tpu_custom_call" | custom-call | tf_op jit(solution)/shard_map/reduce_rest/pallas_call | solution.py:559
  621.7 4.9 copy.108
  (169 shorter events, 56.5 us)
Async XLA Ops:
  8.0 74.4 %all-gather.5.cloned.1.call-start = ((), (), s32[]{:S(2)}) async-start(), calls=%async_computation.5 | async-start | bytes 6758400 | tf_op jit(solution)/shard_map/all_gather | solution.py:875
  30.8 68.4 %copy-start.27 = (s32[2048]{0:T(1024)}, s32[2048]{0:T(1024)S(1)}, u32[]{:S(2)}) copy-start(s32[2048]{0:T(1024)S(1)} %convert_reduce_fusion) | copy-start | bytes 24580
  40.9 41.5 %copy-start.37 = (f32[1024]{0:T(1024)S(1)}, f32[1024]{0:T(1024)}, u32[]{:S(2)}) copy-start(f32[1024]{0:T(1024)} %param.16) | copy-start | bytes 12292
  44.7 41.2 %copy-start.40 = (f32[256]{0:T(256)}, f32[256]{0:T(256)S(1)}, u32[]{:S(2)}) copy-start(f32[256]{0:T(256)S(1)} %get-tuple-element.91) | copy-start | bytes 3076
  90.0 7.9 %copy-start.16 = (f32[1,256,1024]{2,1,0:T(8,128)S(1)}, f32[1,256,1024]{2,1,0:T(8,128)}, u32[]{:S(2)}) copy-start(f32[1,256,1024]{2,1,0:T(8,128)} %param.25) | copy-start | bytes 3145732
  92.4 30.4 %all-to-all-start = ((bf16[8,256,256]{2,1,0:T(8,128)(2,1)}), bf16[8,256,256]{2,1,0:T(8,128)(2,1)S(1)}, u32[]{:S(2)}, u32[]{:S(2)}) async-start(bf16[8,256,256]{2,1,0:T(8,128)(2,1)} %maximum_bitcast_fusion), calls=%async_computation | async-start | bytes 2097152 | tf_op jit(solution)/shard_map/all_to_all | solution.py:899
  97.9 79.0 %all-gather.9.cloned.1.call-start = ((), (), s32[]{:S(2)}) async-start(), calls=%async_computation.7 | async-start | bytes 2621440 | tf_op jit(solution)/shard_map/all_gather | solution.py:933
  98.8 92.5 %all-gather.7.cloned.1.call-start = ((), (), s32[]{:S(2)}) async-start(), calls=%async_computation.6 | async-start | bytes 2621440 | tf_op jit(solution)/shard_map/all_gather | solution.py:932
  170.1 6.2 copy-start.28
  346.4 48.0 %collective-permute-start = (bf16[4,192,1024]{2,1,0:T(8,128)(2,1)}, bf16[4,192,1024]{2,1,0:T(8,128)(2,1)S(1)}, u32[]{:S(2)}, u32[]{:S(2)}) collective-permute-start(bf16[4,192,1024]{2,1,0:T(8,128)(2,1)} %get-tuple-element.40), channel_id=1, source_target_pairs={{0,1},{1,0},{2,3},{3,2},{4,5},{5,4},{6,7},{7,6},{8,9},{9,8},{10,11... | collective-permute-start | bytes 4718600 | tf_op jit(solution)/shard_map/ppermute | solution.py:282
  348.1 9.6 %copy-start.3 = (f32[2048,32]{1,0:T(8,128)S(1)}, f32[2048,32]{1,0:T(8,128)}, u32[]{:S(2)}) copy-start(f32[2048,32]{1,0:T(8,128)} %copy-done.2) | copy-start | bytes 786436
  348.1 9.6 %copy-start.5 = (f32[2048,32]{1,0:T(8,128)S(1)}, f32[2048,32]{1,0:T(8,128)}, u32[]{:S(2)}) copy-start(f32[2048,32]{1,0:T(8,128)} %copy-done.4) | copy-start | bytes 786436
  348.1 9.6 %copy-start.7 = (f32[2048,32]{1,0:T(8,128)S(1)}, f32[2048,32]{1,0:T(8,128)}, u32[]{:S(2)}) copy-start(f32[2048,32]{1,0:T(8,128)} %copy-done.6) | copy-start | bytes 786436
  355.7 38.7 %collective-permute-start.1 = (bf16[2,192,1024]{2,1,0:T(8,128)(2,1)}, bf16[2,192,1024]{2,1,0:T(8,128)(2,1)}, u32[]{:S(2)}, u32[]{:S(2)}) collective-permute-start(bf16[2,192,1024]{2,1,0:T(8,128)(2,1)} %get-tuple-element.43), channel_id=1, source_target_pairs={{0,2},{1,3},{2,0},{3,1},{4,6},{5,7},{6,4},{7,5},{8,10},{9,11},{10,... | collective-permute-start | bytes 2359304 | tf_op jit(solution)/shard_map/ppermute | solution.py:282
  355.7 38.7 %collective-permute-start.2 = (bf16[2,192,1024]{2,1,0:T(8,128)(2,1)S(1)}, bf16[2,192,1024]{2,1,0:T(8,128)(2,1)}, u32[]{:S(2)}, u32[]{:S(2)}) collective-permute-start(bf16[2,192,1024]{2,1,0:T(8,128)(2,1)S(1)} %get-tuple-element.44), channel_id=1, source_target_pairs={{0,2},{1,3},{2,0},{3,1},{4,6},{5,7},{6,4},{7,5},{8,10},{9,11},{10,... | collective-permute-start | bytes 2359304 | tf_op jit(solution)/shard_map/ppermute | solution.py:282
  395.5 8.5 %copy-start.12 = (bf16[256,1024]{1,0:T(8,128)(2,1)S(1)}, bf16[256,1024]{1,0:T(8,128)(2,1)}, u32[]{:S(2)}) copy-start(bf16[256,1024]{1,0:T(8,128)(2,1)} %multiply_convert_fusion.1) | copy-start | bytes 1572868
  395.5 8.5 %copy-start.24 = (f32[4,8,256]{2,1,0:T(8,128)S(1)}, f32[4,8,256]{2,1,0:T(8,128)}, u32[]{:S(2)}) copy-start(f32[4,8,256]{2,1,0:T(8,128)} %get-tuple-element.36) | copy-start | bytes 98308
  395.5 8.5 %copy-start.29 = (f32[256]{0:T(256)S(1)}, f32[256]{0:T(256)}, u32[]{:S(2)}) copy-start(f32[256]{0:T(256)} %copy-done.28) | copy-start | bytes 3076
  395.5 8.5 %copy-start.33 = (f32[256]{0:T(256)S(1)}, f32[256]{0:T(256)}, u32[]{:S(2)}) copy-start(f32[256]{0:T(256)} %copy-done.32) | copy-start | bytes 3076
  397.9 6.7 %copy-start.15 = (bf16[8,256,128]{1,2,0:T(8,128)(2,1)S(1)}, bf16[8,256,128]{1,2,0:T(8,128)(2,1)}, u32[]{:S(2)}) copy-start(bf16[8,256,128]{1,2,0:T(8,128)(2,1)} %copy-done.14) | copy-start | bytes 1572868
  397.9 24.3 %all-to-all-start.4 = ((bf16[8,256,256]{1,2,0:T(8,128)(2,1)}), bf16[8,256,256]{1,2,0:T(8,128)(2,1)S(1)}, u32[]{:S(2)}, u32[]{:S(2)}) async-start(bf16[8,256,256]{1,2,0:T(8,128)(2,1)} %copy.81), calls=%async_computation.4 | async-start | bytes 2097152 | tf_op jit(solution)/shard_map/all_to_all | solution.py:1011
  422.2 9.7 %copy-start.9 = (f32[1,256,1024]{2,1,0:T(8,128)S(1)}, f32[1,256,1024]{2,1,0:T(8,128)}, u32[]{:S(2)}) copy-start(f32[1,256,1024]{2,1,0:T(8,128)} %param.13) | copy-start | bytes 3145732
  422.2 9.7 %copy-start.38 = (f32[1024]{0:T(1024)S(1)}, f32[1024]{0:T(1024)}, u32[]{:S(2)}) copy-start(f32[1024]{0:T(1024)} %param.16) | copy-start | bytes 12292
  422.2 9.7 %copy-start.41 = (f32[256]{0:T(256)S(1)}, f32[256]{0:T(256)}, u32[]{:S(2)}) copy-start(f32[256]{0:T(256)} %copy-done.40) | copy-start | bytes 3076
  423.8 25.2 %collective-permute-start.6 = (bf16[1,192,1024]{2,1,0:T(8,128)(2,1)}, bf16[1,192,1024]{2,1,0:T(8,128)(2,1)}, u32[]{:S(2)}, u32[]{:S(2)}) collective-permute-start(bf16[1,192,1024]{2,1,0:T(8,128)(2,1)} %get-tuple-element.50), channel_id=1, source_target_pairs={{0,4},{1,5},{2,6},{3,7},{4,0},{5,1},{6,2},{7,3},{8,12},{9,13},{10,... | collective-permute-start | bytes 1179656 | tf_op jit(solution)/shard_map/ppermute | solution.py:282
  424.7 32.7 %collective-permute-start.5 = (bf16[1,192,1024]{2,1,0:T(8,128)(2,1)}, bf16[1,192,1024]{2,1,0:T(8,128)(2,1)}, u32[]{:S(2)}, u32[]{:S(2)}) collective-permute-start(bf16[1,192,1024]{2,1,0:T(8,128)(2,1)} %get-tuple-element.49), channel_id=1, source_target_pairs={{0,4},{1,5},{2,6},{3,7},{4,0},{5,1},{6,2},{7,3},{8,12},{9,13},{10,... | collective-permute-start | bytes 1179656 | tf_op jit(solution)/shard_map/ppermute | solution.py:282
  427.8 7.7 %copy-start.25 = (bf16[256,512]{1,0:T(8,128)(2,1)}, bf16[256,512]{1,0:T(8,128)(2,1)S(1)}, u32[]{:S(2)}) copy-start(bf16[256,512]{1,0:T(8,128)(2,1)S(1)} %copy.83) | copy-start | bytes 786436
  429.0 6.5 %copy-start.26 = (bf16[256,512]{1,0:T(8,128)(2,1)}, bf16[256,512]{1,0:T(8,128)(2,1)S(1)}, u32[]{:S(2)}) copy-start(bf16[256,512]{1,0:T(8,128)(2,1)S(1)} %copy.84) | copy-start | bytes 786436
  430.4 5.2 copy-start.39
  430.4 40.9 %collective-permute-start.3 = (bf16[4,192,1024]{2,1,0:T(8,128)(2,1)}, bf16[4,192,1024]{2,1,0:T(8,128)(2,1)}, u32[]{:S(2)}, u32[]{:S(2)}) collective-permute-start(bf16[4,192,1024]{2,1,0:T(8,128)(2,1)} %get-tuple-element.47), channel_id=1, source_target_pairs={{0,1},{1,0},{2,3},{3,2},{4,5},{5,4},{6,7},{7,6},{8,9},{9,8},{10,11... | collective-permute-start | bytes 4718600 | tf_op jit(solution)/shard_map/ppermute | solution.py:282
  437.9 33.4 %collective-permute-start.4 = (bf16[2,192,1024]{2,1,0:T(8,128)(2,1)}, bf16[2,192,1024]{2,1,0:T(8,128)(2,1)}, u32[]{:S(2)}, u32[]{:S(2)}) collective-permute-start(bf16[2,192,1024]{2,1,0:T(8,128)(2,1)} %get-tuple-element.48), channel_id=1, source_target_pairs={{0,2},{1,3},{2,0},{3,1},{4,6},{5,7},{6,4},{7,5},{8,10},{9,11},{10,... | collective-permute-start | bytes 2359304 | tf_op jit(solution)/shard_map/ppermute | solution.py:282
  437.9 5.4 copy-start.11
  (23 other events, 54.5 us)
Sparse Core Ops, SparseCore 0:
  12.8 69.5 all-gather.4
Sparse Core Ops, SparseCore 1:
  100.5 22.4 all-gather.8
  168.8 22.5 all-gather.6

commit v8 on v7

--- a/solution.py
+++ b/solution.py
@@ -383,7 +383,7 @@
 
 def reduce_kernel(*refs, units, n_parts, labels, weight_order, share):
     part_refs, refs = (refs[:n_parts], refs[n_parts:])
-    weight_ref, gain_ref, up_ref, down_ref, weight_out, gain_out, *refs = refs
+    weight_ref, gain_ref, up_ref, down_ref, weight_out, gain_out, late_ref, *refs = refs
     steps = len(units[0][2]) - 1
     sends, keeps, gets = ([], [], [])
     for _ in range(steps):
@@ -393,7 +393,7 @@
         refs = refs[3:]
     bits = len(labels)
     lane_refs, refs = (refs[: 2 * (2 * bits - 1)], refs[2 * (2 * bits - 1) :])
-    load_keep, load_came, load_sem, unit_send, unit_get, lane_send, lane_get = refs
+    load_keep, load_came, load_sem, unit_send, unit_get, lane_send, lane_get, late_sem = refs
     lanes = [
         Lane(
             labels,
@@ -421,24 +421,43 @@
 
     lane_start(0)
 
-    sequence = [
-        n for k in range(steps + 1) for n, unit in enumerate(units) if unit[3] == k
-    ]
+    late = [n for n, unit in enumerate(units) if unit[3] < 0]
+    half_way = [n for n, unit in enumerate(units) if 0 < unit[3] < steps]
+    fresh = [n for n, unit in enumerate(units) if unit[3] == 0]
+    done = [n for n, unit in enumerate(units) if unit[3] == steps]
+    sequence = half_way + fresh + late + done
+
+    def late_copy(n):
+        _, ((_, _), (which, place)), order, _ = units[n]
+        axis, bit = order[0]
+        return mesh_copy(
+            part_refs[which].at[place],
+            late_ref.at[late.index(n)],
+            late_sem.at[0, late.index(n)],
+            late_sem.at[1, late.index(n)],
+            axis,
+            side(axis, bit)[1],
+        )
 
     def loads(turn):
-        _, parts, _, skip = units[sequence[turn]]
+        n = sequence[turn]
+        _, parts, _, skip = units[n]
         slot = turn % 2
-        size = spots >> skip
+        size = spots >> max(skip, 0)
+        sources = [part_refs[which].at[place] for which, place in parts]
+        if skip < 0:
+            sources[1] = late_ref.at[late.index(n)]
         return [
             pltpu.make_async_copy(
-                part_refs[which].at[place],
-                buffer.at[slot, pl.ds(0, size)],
-                load_sem.at[slot, number],
+                source, buffer.at[slot, pl.ds(0, size)], load_sem.at[slot, number]
             )
-            for number, ((which, place), buffer) in enumerate(
-                zip(parts, (load_keep, load_came))
-            )
+            for number, (source, buffer) in enumerate(zip(sources, (load_keep, load_came)))
         ]
+
+    def load(turn):
+        if turn < len(units) and units[sequence[turn]][3] >= 0:
+            for copy in loads(turn):
+                copy.start()
 
     def unit_copy(unit, order, k):
         axis, bit = order[k + 1]
@@ -474,16 +493,18 @@
     def begin_unit(n):
         unit, _, order, skip = units[n]
         turn = sequence.index(n)
+        if skip < 0:
+            late_copy(n).wait_recv()
+            for copy in loads(turn):
+                copy.start()
         for copy in loads(turn):
             copy.wait()
         left, right = (load_keep.at[turn % 2], load_came.at[turn % 2])
         if skip < steps:
-            unit_add(unit, order, skip, left, right)
+            unit_add(unit, order, max(skip, 0), left, right)
         else:
             give(unit, left[0].astype(jnp.float32) + right[0].astype(jnp.float32))
-        if turn + 2 < len(units):
-            for copy in loads(turn + 2):
-                copy.start()
+        load(turn + 2)
 
     def next_unit(n, k):
         unit, _, order, _ = units[n]
@@ -504,33 +525,40 @@
                 share:, p * share : (p + 1) * share
             ]
 
-    for turn in range(min(2, len(units))):
-        for copy in loads(turn):
-            copy.start()
-    work = []
-    first_jobs = 0
-    for k in range(steps):
-        for n, unit in enumerate(units):
-            if unit[3] == k:
-                work.append(functools.partial(begin_unit, n))
-            elif unit[3] < k:
-                work.append(functools.partial(next_unit, n, k))
-        first_jobs = first_jobs or len(work)
-    for last in (True, False):
-        for n, unit in enumerate(units):
-            if (unit[3] == steps) == last:
-                work.append(functools.partial(begin_unit if last else end_unit, n))
-    marks = [first_jobs + (len(work) - first_jobs) * k // bits for k in range(bits)]
-    for number, job in enumerate(work):
-        for k, mark in enumerate(marks[:-1]):
-            if number == mark:
-                lane_add(k)
-                lane_start(k + 1)
-        job()
-    lane_add(bits - 1)
+    load(0)
+    load(1)
+    def late_start():
+        for n in late:
+            late_copy(n).start()
+
+    def lane_turn(k):
+        lane_add(k)
+        if k + 1 < bits:
+            lane_start(k + 1)
+
+    work = [(begin_unit, n) for n in half_way + fresh[:1]] + [(lane_turn, 0)]
+    work += [(begin_unit, n) for n in fresh[1:2]] + [(late_start,)]
+    work += [(begin_unit, n) for n in fresh[2:]]
+    for k in range(1, steps):
+        onward = [n for n in half_way if units[n][3] < k] + fresh
+        work += [(next_unit, n, k) for n in onward[:2]]
+        if k == 1:
+            work += [(lane_turn, 1)] + [(begin_unit, n) for n in late]
+        work += [(next_unit, n, k) for n in onward[2:3]]
+        work += [(next_unit, n, k) for n in late]
+        work += [(next_unit, n, k) for n in onward[3:]]
+    work += [(begin_unit, n) for n in done]
+    work += [(end_unit, n) for n in half_way + fresh[:2] + late] + [(lane_turn, 2)]
+    work += [(end_unit, n) for n in fresh[2:3]] + [(lane_turn, 3)]
+    work += [(end_unit, n) for n in fresh[3:]]
+    work += [(lane_turn, k) for k in range(4, bits)]
+    for job, *arguments in work:
+        job(*arguments)
     for unit, _, order, skip in units:
-        for k in range(skip, steps):
+        for k in range(max(skip, 0), steps):
             unit_copy(unit, order, k).wait_send()
+    for n in late:
+        late_copy(n).wait_send()
     for lane in lanes:
         lane.finish()
 
@@ -540,6 +568,7 @@
     count = len(units)
     bits = len(labels)
     steps = len(units[0][2]) - 1
+    late = max(1, len([unit for unit in units if unit[3] < 0]))
     anywhere = pl.BlockSpec(memory_space=pl.ANY)
     vmem = pl.BlockSpec(memory_space=pltpu.VMEM)
     scratch = []
@@ -555,6 +584,7 @@
         pltpu.SemaphoreType.DMA((count, steps)),
         pltpu.SemaphoreType.DMA((2, bits)),
         pltpu.SemaphoreType.DMA((2, bits)),
+        pltpu.SemaphoreType.DMA((2, late)),
     ]
     return pl.pallas_call(
         functools.partial(
@@ -570,9 +600,10 @@
             jax.ShapeDtypeStruct((count, (tall - share) * (width // share), share), jnp.float32),
             jax.ShapeDtypeStruct(weights.shape[bits:], jnp.float32),
             jax.ShapeDtypeStruct(gains.shape[bits:], jnp.float32),
+            jax.ShapeDtypeStruct((late, spots, tall, width), jnp.bfloat16),
         ),
         in_specs=[anywhere] * len(parts) + [vmem] * 2,
-        out_specs=[vmem] * 4,
+        out_specs=[vmem] * 4 + [anywhere],
         scratch_shapes=scratch,
         compiler_params=pltpu.CompilerParams(
             collective_id=0, has_side_effects=True, vmem_limit_bytes=67 * 1000 * 1000
@@ -871,13 +902,14 @@
     starts = doc_start.reshape(blocks, 1, BLOCK)
     lows = doc_start[::BLOCK] // BLOCK
 
-    joined = jnp.concatenate([w_query, w_key, w_value, w_out, w_router], 1)
-    full = lax.all_gather(joined, everyone, axis=0, tiled=True)
     rotated_width = query_width + key_width
     input_width = rotated_width + key_width
-    full_in = full[:, :input_width]
-    full_out = full[:, input_width : input_width + model_width]
-    full_router = full[:, input_width + model_width :]
+    full_in = lax.all_gather(
+        jnp.concatenate([w_query, w_key, w_value], 1), everyone, axis=0, tiled=True
+    )
+    full = lax.all_gather(jnp.concatenate([w_out, w_router], 1), everyone, axis=0, tiled=True)
+    full_out = full[:, :model_width]
+    full_router = full[:, model_width:]
 
     normed, factor_one = rms_norm(inputs, attn_gain)
     normed_b = normed.astype(jnp.bfloat16)
@@ -1023,9 +1055,8 @@
         parts.extend([own[None], got[None]])
 
     for k, half in enumerate(sent):
-        got = beside[0] if k == 0 else swap(after(half, returned), *rep_orders[near + k][0])
-        steps_of[near + k] = ((0, near + k), (len(parts), 0), 0)
-        parts.append(got[None])
+        steps_of[near + k] = ((0, near + k), (len(parts), 0), 0 if k == 0 else -1)
+        parts.append((beside[0] if k == 0 else half)[None])
     for e in late:
         give, own = halves(grad_keep, came_near, rep_orders[e][1], e)
         put_by(e, own, swap(after(give, returned), *rep_orders[e][1]), 1)
@@ -1065,7 +1096,7 @@
     labels = ep_bits[::-1] + rep_bits[::-1]
     shape = (2,) * len(labels)
     weight_grads = jnp.concatenate([grad_w_in, grad_out_w, grad_router], 1).astype(jnp.bfloat16)
-    expert_up, expert_down, weights, gains = reduce_rest(
+    expert_up, expert_down, weights, gains, _ = reduce_rest(
         parts,
         weight_grads.reshape(shape + (-1, weight_grads.shape[1])),
         gains.reshape(shape + (1, -1)),

time: 648 us -> 656 us (1.012)
  waiting for transfers between devices: 108 us -> 132 us
  blocking collectives: 61.8 us -> 49.8 us
    all_to_all x1 -> x0, blocking collectives: 12.9 us -> none  [on_device(): lax.all_to_all(mixed.reshape(n_rep, rows_dev, head_width), 'rep', split_a...]
    all_to_all x0 -> x1, waiting for transfers between devices: none -> 11.5 us  [on_device(): lax.all_to_all(mixed.reshape(n_rep, rows_dev, head_width), 'rep', split_a...]
    pallas_call x1, Pallas kernels: 145 us -> 154 us  [reduce_rest(): pl.pallas_call(functools.partial(reduce_kernel, units=units, n_parts=len(...]
    ppermute x7 -> x6, waiting for transfers between devices: 22.5 us -> 27.2 us  [swap(): return lax.ppermute(sent, axis, [(i, i ^ 1 << bit) for i in range(size)])]
    all_gather x1 -> x2, waiting for transfers between devices: 37.7 us -> 34.7 us  [the longest x1 34.7 us: on_device(): lax.all_gather(jnp.concatenate([w_query, w_key, w_value], 1), everyone, a...]
  transfers between devices with their start and end apart: 12 -> 13, of which waited for: 7 -> 9; matrix products, arithmetic and copies ran while one was open for 10% -> 11% of each run, Pallas kernels for 10% -> 8%
where the time goes in v8:
time: 656 us; the launch traced here: 645 us
  Pallas kernels  326 us (50%)
  waiting for transfers between devices  132 us (20%)
  blocking collectives  49.8 us (8%)
  local copies, waits for them, and re-layouts  39.1 us (6%)
  other arithmetic  38.8 us (6%)
  starting transfers between devices  23.2 us (4%)
  matrix products  21.7 us (3%)
  between operations  14.6 us (2%)
    pallas_call x1, Pallas kernels, reduce_rest(): pl.pallas_call(functools.partial(reduce_kernel, units=units, n_parts=len(...  154 us
    pallas_call x1, Pallas kernels, experts(): pl.pallas_call(functools.partial(experts_kernel, sources=sources, rows_de...  120 us
    all_gather x1, waiting for transfers between devices, on_device(): lax.all_gather(jnp.concatenate([w_query, w_key, w_value], 1), everyone, a...  34.7 us
    pallas_call x1, Pallas kernels, attend_backward(): pl.pallas_call(functools.partial(attend_backward_kernel, heads=heads, blo...  29.6 us
    ppermute x6, waiting for transfers between devices, swap(): return lax.ppermute(sent, axis, [(i, i ^ 1 << bit) for i in range(size)])  27.2 us
    all_to_all x1, blocking collectives, on_device(): lax.all_to_all(grad_mixed.reshape(rows_dev, n_rep, head_width).transpose(...  27.1 us
    all_to_all x1, waiting for transfers between devices, on_device(): lax.all_to_all(sending, 'rep', split_axis=0, concat_axis=0, tiled=True)  26 us
    pallas_call x1, Pallas kernels, attend_forward(): pl.pallas_call(functools.partial(attend_forward_kernel, heads=heads), out...  21.7 us
  transfers between devices with their start and end apart: 13, of which 9 were waited for; matrix products, arithmetic and copies ran while one was open for 11% of the time, Pallas kernels for 8%

profile of v8, /device:TPU:26, one launch (start us, length us, event | category | flops | bytes accessed | tf_op | source)
XLA Modules:
  0.0 645.3 jit_solution(3565972601196081908)
XLA Ops:
  10.4 16.3 %all-gather = s32[1,2048]{1,0:T(1,128)S(1)} all-gather(s32[1,256]{1,0:T(1,128)} %param.14), channel_id=2, replica_groups=mesh['ep'=4,'rep'=8] {'rep'}, dimensions={1}, use_global_device_ids=true | all-gather | bytes 9216 | tf_op jit(solution)/shard_map/all_gather | solution.py:884
  28.5 3.7 multiply_sine_fusion
  38.4 34.7 %all-gather.6.cloned.1.call-done = bf16[1024,2048]{1,0:T(8,128)(2,1)} async-done(((bf16[32,2048]{1,0:T(8,128)(2,1)}), bf16[1024,2048]{1,0:T(8,128)(2,1)}) %all-gather.6.cloned.1.call-update) | async-done | bytes 4194320 | tf_op jit(solution)/shard_map/all_gather | solution.py:907
  73.0 3.5 fusion.69
  86.0 5.3 all-to-all-start
  93.2 26.0 %all-to-all-done = bf16[8,256,256]{2,1,0:T(8,128)(2,1)S(1)} async-done(((bf16[8,256,256]{2,1,0:T(8,128)(2,1)}), bf16[8,256,256]{2,1,0:T(8,128)(2,1)S(1)}, u32[]{:S(2)}, u32[]{:S(2)}) %all-to-all-start) | async-done | bytes 1048608 | tf_op jit(solution)/shard_map/all_to_all | solution.py:931
  120.1 21.7 %attend_forward.1 = (bf16[2048,128]{1,0:T(8,128)(2,1)}, f32[128,2048]{1,0:T(8,128)}, f32[8,2,256]{2,1,0:T(2,128)}) custom-call(s32[8]{0:T(128)} %and_select_fusion.low_ref, bf16[2048,256]{1,0:T(8,128)(2,1)} %bitcast.156, s32[8,1,256]{2,1,0:T(1,128)} %bitcast.178), custom_call_target="tpu_custom_call" | custom-call | tf_op jit(solution)/shard_map/attend_forward/pallas_call | solution.py:119
  143.9 5.6 all-to-all-start.1
  149.5 11.5 %all-to-all-done.1 = bf16[8,256,128]{1,2,0:T(8,128)(2,1)S(1)} async-done(((bf16[8,256,128]{1,2,0:T(8,128)(2,1)}), bf16[8,256,128]{1,2,0:T(8,128)(2,1)S(1)}, u32[]{:S(2)}, u32[]{:S(2)}) %all-to-all-start.1) | async-done | bytes 524320 | tf_op jit(solution)/shard_map/all_to_all | solution.py:934
  161.0 2.6 multiply_reduce_fusion.2
  167.9 6.4 all_to_all.25
  174.9 15.2 %all-gather.10.cloned.1.call-done = bf16[1024,1024]{1,0:T(8,128)(2,1)} async-done(((bf16[256,1024]{1,0:T(8,128)(2,1)}), bf16[1024,1024]{1,0:T(8,128)(2,1)}) %all-gather.10.cloned.1.call-update) | async-done | bytes 2097168 | tf_op jit(solution)/shard_map/all_gather | solution.py:964
  190.1 120.4 %experts.1 = (f32[256,1024]{1,0:T(8,128)}, f32[256,1024]{1,0:T(8,128)}, f32[4,8,256]{2,1,0:T(8,128)}, bf16[8,4,192,1024]{3,2,1,0:T(8,128)(2,1)}, bf16[6,4,192,10...) custom-call(bf16[2,2,256,1024]{3,2,1,0:T(8,128)(2,1)} %bitcast.166, ...), custom_call_target="tpu_custom_call" | custom-call | tf_op jit(solution)/shard_map/experts/pallas_call | solution.py:789
  311.5 2.6 multiply_reduce_fusion
  317.2 27.1 %all_to_all.26 = bf16[8,256,128]{2,1,0:T(8,128)(2,1)} all-to-all(bf16[8,256,128]{2,1,0:T(8,128)(2,1)S(1)} %bitcast.169), channel_id=1, replica_groups=mesh['ep'=4,'rep'=8] {'rep'}, dimensions={0} | all-to-all | bytes 1048576 | tf_op jit(solution)/shard_map/all_to_all | solution.py:1026
  346.1 7.6 %add_convert_fusion = (bf16[1,2,192,1024]{3,2,1,0:T(8,128)(2,1)}, bf16[1,2,192,1024]{3,2,1,0:T(8,128)(2,1)}, bf16[2,192,1024]{2,1,0:T(8,128)(2,1)}, bf16[1,2,192...) fusion(bf16[6,4,192,1024]{3,2,1,0:T(8,128)(2,1)} %get-tuple-element.41.refs_1_, ...), kind=kLoop, calls=%fused_computation.13 | loop fusion | flops 9437184 | bytes 14155784 | tf_op jit(solution)/shard_map/convert_element_type | solution.py:1009
  357.7 29.6 %attend_backward.1 = bf16[2048,256]{1,0:T(8,128)(2,1)} custom-call(s32[8]{0:T(128)} %and_select_fusion.low_ref, bf16[2048,256]{1,0:T(8,128)(2,1)} %bitcast.157, bf16[2048,128]{1,0:T(8,128)(2,1)} %bitcast.167, f32[128,2048]{1,0:T(8,128)} %get-tuple-element.36.out_ref, f32[8,2,256]{2,1,0:T(2,128)} %get-tuple-element.37.total_ref, s32[8,1,256]{2,1,0:T(1,128)} %bitcast.179, ...), custom_call_target="tpu_custom_call" | custom-call | tf_op jit(solution)/shard_map/attend_backward/pallas_call | solution.py:244
  387.3 2.0 collective-permute-done.2
  389.3 2.3 copy.81
  391.6 5.2 all-to-all-start.4
  399.6 2.4 fusion.35
  402.0 2.3 fusion.33
  404.3 17.3 %all-to-all-done.4 = bf16[8,256,256]{1,2,0:T(8,128)(2,1)S(1)} async-done(((bf16[8,256,256]{1,2,0:T(8,128)(2,1)}), bf16[8,256,256]{1,2,0:T(8,128)(2,1)S(1)}, u32[]{:S(2)}, u32[]{:S(2)}) %all-to-all-start.4) | async-done | bytes 1048608 | tf_op jit(solution)/shard_map/all_to_all | solution.py:1043
  423.3 2.9 collective-permute-start.4
  429.9 3.7 fusion.29
  436.0 4.6 convolution_convert_fusion
  441.4 5.5 pad_maximum_fusion.refs_10_
  446.9 5.7 collective-permute-done.5
  452.6 8.3 %collective-permute-done.4 = bf16[1,192,1024]{2,1,0:T(8,128)(2,1)} collective-permute-done((bf16[1,192,1024]{2,1,0:T(8,128)(2,1)}, bf16[1,192,1024]{2,1,0:T(8,128)(2,1)}, u32[]{:S(2)}, u32[]{:S(2)}) %collective-permute-start.4) | collective-permute-done | bytes 393248 | tf_op jit(solution)/shard_map/ppermute | solution.py:282
  460.9 11.1 %collective-permute-done.3 = bf16[2,192,1024]{2,1,0:T(8,128)(2,1)} collective-permute-done((bf16[2,192,1024]{2,1,0:T(8,128)(2,1)}, bf16[2,192,1024]{2,1,0:T(8,128)(2,1)}, u32[]{:S(2)}, u32[]{:S(2)}) %collective-permute-start.3) | collective-permute-done | bytes 786464 | tf_op jit(solution)/shard_map/ppermute | solution.py:282
  472.0 154.4 %reduce_rest.1 = (f32[8,128,1024]{2,1,0:T(8,128)}, f32[8,512,128]{2,1,0:T(8,128)}, f32[32,3104]{1,0:T(8,128)}, f32[1,64]{1,0:T(1,128)}, bf16[1,4,192,1024]{3,2,1,0:T(8,128)(2,1)}) custom-call(bf16[8,4,192,1024]{3,2,1,0:T(8,128)(2,1)} %get-tuple-element.40.refs_0_, bf16[6,4,192,1024]{3,2,1,0:T(8,128)(2,1)} %get-tuple-element.41.refs_1_, ...), custom_call_target="tpu_custom_call" | custom-call | tf_op jit(solution)/shard_map/reduce_rest/pallas_call | solution.py:589
  632.4 4.9 copy.104
  (172 shorter events, 58.0 us)
Async XLA Ops:
  7.2 65.9 %all-gather.6.cloned.1.call-start = ((), (), s32[]{:S(2)}) async-start(), calls=%async_computation.5 | async-start | bytes 4325376 | tf_op jit(solution)/shard_map/all_gather | solution.py:907
  8.8 140.7 %all-gather.8.cloned.1.call-start = ((), (), s32[]{:S(2)}) async-start(), calls=%async_computation.6 | async-start | bytes 2433024 | tf_op jit(solution)/shard_map/all_gather | solution.py:910
  28.4 64.1 %copy-start.29 = (s32[2048]{0:T(1024)}, s32[2048]{0:T(1024)S(1)}, u32[]{:S(2)}) copy-start(s32[2048]{0:T(1024)S(1)} %convert_reduce_fusion) | copy-start | bytes 24580
  36.0 37.1 %copy-start.36 = (f32[1024]{0:T(1024)S(1)}, f32[1024]{0:T(1024)}, u32[]{:S(2)}) copy-start(f32[1024]{0:T(1024)} %param.16) | copy-start | bytes 12292
  38.3 38.2 %copy-start.40 = (f32[256]{0:T(256)}, f32[256]{0:T(256)S(1)}, u32[]{:S(2)}) copy-start(f32[256]{0:T(256)S(1)} %get-tuple-element.89) | copy-start | bytes 3076
  84.7 6.9 %copy-start.17 = (f32[1,256,1024]{2,1,0:T(8,128)S(1)}, f32[1,256,1024]{2,1,0:T(8,128)}, u32[]{:S(2)}) copy-start(f32[1,256,1024]{2,1,0:T(8,128)} %param.25) | copy-start | bytes 3145732
  86.0 33.1 %all-to-all-start = ((bf16[8,256,256]{2,1,0:T(8,128)(2,1)}), bf16[8,256,256]{2,1,0:T(8,128)(2,1)S(1)}, u32[]{:S(2)}, u32[]{:S(2)}) async-start(bf16[8,256,256]{2,1,0:T(8,128)(2,1)} %maximum_bitcast_fusion), calls=%async_computation | async-start | bytes 2097152 | tf_op jit(solution)/shard_map/all_to_all | solution.py:931
  91.4 83.5 %all-gather.12.cloned.1.call-start = ((), (), s32[]{:S(2)}) async-start(), calls=%async_computation.8 | async-start | bytes 2621440 | tf_op jit(solution)/shard_map/all_gather | solution.py:965
  143.9 17.1 %all-to-all-start.1 = ((bf16[8,256,128]{1,2,0:T(8,128)(2,1)}), bf16[8,256,128]{1,2,0:T(8,128)(2,1)S(1)}, u32[]{:S(2)}, u32[]{:S(2)}) async-start(bf16[8,256,128]{1,2,0:T(8,128)(2,1)} %copy.79), calls=%async_computation.1 | async-start | bytes 1048576 | tf_op jit(solution)/shard_map/all_to_all | solution.py:934
  149.5 40.6 %all-gather.10.cloned.1.call-start = ((), (), s32[]{:S(2)}) async-start(), calls=%async_computation.7 | async-start | bytes 2621440 | tf_op jit(solution)/shard_map/all_gather | solution.py:964
  167.2 7.0 %copy-start.30 = (f32[256]{0:T(256)}, f32[256]{0:T(256)S(1)}, u32[]{:S(2)}) copy-start(f32[256]{0:T(256)S(1)} %get-tuple-element.57) | copy-start | bytes 3076
  344.3 45.0 %collective-permute-start = (bf16[4,192,1024]{2,1,0:T(8,128)(2,1)}, bf16[4,192,1024]{2,1,0:T(8,128)(2,1)}, u32[]{:S(2)}, u32[]{:S(2)}) collective-permute-start(bf16[4,192,1024]{2,1,0:T(8,128)(2,1)} %get-tuple-element.39), channel_id=1, source_target_pairs={{0,1},{1,0},{2,3},{3,2},{4,5},{5,4},{6,7},{7,6},{8,9},{9,8},{10,11... | collective-permute-start | bytes 4718600 | tf_op jit(solution)/shard_map/ppermute | solution.py:282
  346.0 9.7 %copy-start.5 = (f32[2048,32]{1,0:T(8,128)S(1)}, f32[2048,32]{1,0:T(8,128)}, u32[]{:S(2)}) copy-start(f32[2048,32]{1,0:T(8,128)} %copy-done.4) | copy-start | bytes 786436
  346.0 9.7 %copy-start.7 = (f32[2048,32]{1,0:T(8,128)S(1)}, f32[2048,32]{1,0:T(8,128)}, u32[]{:S(2)}) copy-start(f32[2048,32]{1,0:T(8,128)} %copy-done.6) | copy-start | bytes 786436
  346.1 9.7 %copy-start.9 = (f32[2048,32]{1,0:T(8,128)S(1)}, f32[2048,32]{1,0:T(8,128)}, u32[]{:S(2)}) copy-start(f32[2048,32]{1,0:T(8,128)} %copy-done.8) | copy-start | bytes 786436
  353.7 33.6 %collective-permute-start.1 = (bf16[2,192,1024]{2,1,0:T(8,128)(2,1)S(1)}, bf16[2,192,1024]{2,1,0:T(8,128)(2,1)}, u32[]{:S(2)}, u32[]{:S(2)}) collective-permute-start(bf16[2,192,1024]{2,1,0:T(8,128)(2,1)S(1)} %get-tuple-element.42), channel_id=1, source_target_pairs={{0,2},{1,3},{2,0},{3,1},{4,6},{5,7},{6,4},{7,5},{8,10},{9,11},{10,... | collective-permute-start | bytes 2359304 | tf_op jit(solution)/shard_map/ppermute | solution.py:282
  353.7 35.6 %collective-permute-start.2 = (bf16[2,192,1024]{2,1,0:T(8,128)(2,1)S(1)}, bf16[2,192,1024]{2,1,0:T(8,128)(2,1)}, u32[]{:S(2)}, u32[]{:S(2)}) collective-permute-start(bf16[2,192,1024]{2,1,0:T(8,128)(2,1)S(1)} %get-tuple-element.43), channel_id=1, source_target_pairs={{0,2},{1,3},{2,0},{3,1},{4,6},{5,7},{6,4},{7,5},{8,10},{9,11},{10,... | collective-permute-start | bytes 2359304 | tf_op jit(solution)/shard_map/ppermute | solution.py:282
  389.3 7.7 %copy-start.12 = (bf16[256,1024]{1,0:T(8,128)(2,1)S(1)}, bf16[256,1024]{1,0:T(8,128)(2,1)}, u32[]{:S(2)}) copy-start(bf16[256,1024]{1,0:T(8,128)(2,1)} %multiply_convert_fusion.1) | copy-start | bytes 1572868
  389.3 7.7 %copy-start.26 = (f32[4,8,256]{2,1,0:T(8,128)S(1)}, f32[4,8,256]{2,1,0:T(8,128)}, u32[]{:S(2)}) copy-start(f32[4,8,256]{2,1,0:T(8,128)} %get-tuple-element.35) | copy-start | bytes 98308
  389.3 7.7 %copy-start.31 = (f32[256]{0:T(256)S(1)}, f32[256]{0:T(256)}, u32[]{:S(2)}) copy-start(f32[256]{0:T(256)} %copy-done.30) | copy-start | bytes 3076
  389.3 7.7 %copy-start.35 = (f32[256]{0:T(256)S(1)}, f32[256]{0:T(256)}, u32[]{:S(2)}) copy-start(f32[256]{0:T(256)} %copy-done.34) | copy-start | bytes 3076
  391.6 5.9 copy-start.16
  391.6 30.0 %all-to-all-start.4 = ((bf16[8,256,256]{1,2,0:T(8,128)(2,1)}), bf16[8,256,256]{1,2,0:T(8,128)(2,1)S(1)}, u32[]{:S(2)}, u32[]{:S(2)}) async-start(bf16[8,256,256]{1,2,0:T(8,128)(2,1)} %copy.81), calls=%async_computation.4 | async-start | bytes 2097152 | tf_op jit(solution)/shard_map/all_to_all | solution.py:1043
  421.6 8.2 %copy-start.1 = (f32[1,256,1024]{2,1,0:T(8,128)S(1)}, f32[1,256,1024]{2,1,0:T(8,128)}, u32[]{:S(2)}) copy-start(f32[1,256,1024]{2,1,0:T(8,128)} %param.13) | copy-start | bytes 3145732
  421.6 8.2 %copy-start.37 = (f32[1024]{0:T(1024)S(1)}, f32[1024]{0:T(1024)}, u32[]{:S(2)}) copy-start(f32[1024]{0:T(1024)} %param.16) | copy-start | bytes 12292
  421.6 8.2 %copy-start.41 = (f32[256]{0:T(256)S(1)}, f32[256]{0:T(256)}, u32[]{:S(2)}) copy-start(f32[256]{0:T(256)} %copy-done.40) | copy-start | bytes 3076
  423.3 29.3 %collective-permute-start.5 = (bf16[1,192,1024]{2,1,0:T(8,128)(2,1)}, bf16[1,192,1024]{2,1,0:T(8,128)(2,1)}, u32[]{:S(2)}, u32[]{:S(2)}) collective-permute-start(bf16[1,192,1024]{2,1,0:T(8,128)(2,1)} %get-tuple-element.48), channel_id=1, source_target_pairs={{0,4},{1,5},{2,6},{3,7},{4,0},{5,1},{6,2},{7,3},{8,12},{9,13},{10,... | collective-permute-start | bytes 1179656 | tf_op jit(solution)/shard_map/ppermute | solution.py:282
  423.3 37.6 %collective-permute-start.4 = (bf16[1,192,1024]{2,1,0:T(8,128)(2,1)}, bf16[1,192,1024]{2,1,0:T(8,128)(2,1)}, u32[]{:S(2)}, u32[]{:S(2)}) collective-permute-start(bf16[1,192,1024]{2,1,0:T(8,128)(2,1)} %get-tuple-element.47), channel_id=1, source_target_pairs={{0,4},{1,5},{2,6},{3,7},{4,0},{5,1},{6,2},{7,3},{8,12},{9,13},{10,... | collective-permute-start | bytes 1179656 | tf_op jit(solution)/shard_map/ppermute | solution.py:282
  427.3 6.3 copy-start.27
  428.5 5.1 copy-start.28
  436.0 36.1 %collective-permute-start.3 = (bf16[2,192,1024]{2,1,0:T(8,128)(2,1)}, bf16[2,192,1024]{2,1,0:T(8,128)(2,1)}, u32[]{:S(2)}, u32[]{:S(2)}) collective-permute-start(bf16[2,192,1024]{2,1,0:T(8,128)(2,1)} %get-tuple-element.46), channel_id=1, source_target_pairs={{0,2},{1,3},{2,0},{3,1},{4,6},{5,7},{6,4},{7,5},{8,10},{9,11},{10,... | collective-permute-start | bytes 2359304 | tf_op jit(solution)/shard_map/ppermute | solution.py:282
  436.0 5.4 copy-start.11
  (26 other events, 60.3 us)
Sparse Core Ops, SparseCore 0:
  11.6 61.3 all-gather.5
  76.5 64.4 all-gather.7
  142.6 21.7 all-gather.11
  165.9 24.1 all-gather.9

commit v9 on v8

--- a/solution.py
+++ b/solution.py
@@ -381,9 +381,10 @@
             self.copy(k).wait_send()
 
 
-def reduce_kernel(*refs, units, n_parts, labels, weight_order, share):
+def reduce_kernel(*refs, units, n_parts, n_lanes, labels, weight_order, share):
     part_refs, refs = (refs[:n_parts], refs[n_parts:])
-    weight_ref, gain_ref, up_ref, down_ref, weight_out, gain_out, late_ref, *refs = refs
+    lane_ins, (up_ref, down_ref, *refs) = (refs[:n_lanes], refs[n_lanes:])
+    lane_outs, (late_ref, *refs) = (refs[:n_lanes], refs[n_lanes:])
     steps = len(units[0][2]) - 1
     sends, keeps, gets = ([], [], [])
     for _ in range(steps):
@@ -392,18 +393,19 @@
         gets.append(refs[2])
         refs = refs[3:]
     bits = len(labels)
-    lane_refs, refs = (refs[: 2 * (2 * bits - 1)], refs[2 * (2 * bits - 1) :])
+    each = 2 * bits - 1
+    lane_refs, refs = (refs[: n_lanes * each], refs[n_lanes * each :])
     load_keep, load_came, load_sem, unit_send, unit_get, lane_send, lane_get, late_sem = refs
     lanes = [
         Lane(
             labels,
             weight_order,
             first,
-            lane_refs[number * (2 * bits - 1) : (number + 1) * (2 * bits - 1)],
+            lane_refs[number * each : (number + 1) * each],
             lane_send.at[number],
             lane_get.at[number],
         )
-        for number, first in enumerate((weight_ref, gain_ref))
+        for number, first in enumerate(lane_ins)
     ]
     _, spots, tall, width = load_keep.shape
     rows = 32 if tall % 32 == 0 else tall
@@ -416,7 +418,7 @@
             lane.start(k)
 
     def lane_add(k):
-        for lane, out in zip(lanes, (weight_out, gain_out)):
+        for lane, out in zip(lanes, lane_outs):
             lane.add(k, out)
 
     lane_start(0)
@@ -541,16 +543,16 @@
     work += [(begin_unit, n) for n in fresh[2:]]
     for k in range(1, steps):
         onward = [n for n in half_way if units[n][3] < k] + fresh
-        work += [(next_unit, n, k) for n in onward[:2]]
+        work += [(next_unit, n, k) for n in onward[:3]]
         if k == 1:
             work += [(lane_turn, 1)] + [(begin_unit, n) for n in late]
-        work += [(next_unit, n, k) for n in onward[2:3]]
+        work += [(next_unit, n, k) for n in onward[3:4]]
         work += [(next_unit, n, k) for n in late]
-        work += [(next_unit, n, k) for n in onward[3:]]
+        work += [(next_unit, n, k) for n in onward[4:]]
     work += [(begin_unit, n) for n in done]
-    work += [(end_unit, n) for n in half_way + fresh[:2] + late] + [(lane_turn, 2)]
-    work += [(end_unit, n) for n in fresh[2:3]] + [(lane_turn, 3)]
-    work += [(end_unit, n) for n in fresh[3:]]
+    work += [(end_unit, n) for n in half_way + fresh[:3] + late] + [(lane_turn, 2)]
+    work += [(end_unit, n) for n in fresh[3:4]] + [(lane_turn, 3)]
+    work += [(end_unit, n) for n in fresh[4:]]
     work += [(lane_turn, k) for k in range(4, bits)]
     for job, *arguments in work:
         job(*arguments)
@@ -563,7 +565,7 @@
         lane.finish()
 
 
-def reduce_rest(parts, weights, gains, units, labels, weight_order, share):
+def reduce_rest(parts, lanes, units, labels, weight_order, share):
     _, spots, tall, width = parts[0].shape
     count = len(units)
     bits = len(labels)
@@ -574,7 +576,7 @@
     scratch = []
     for k in range(steps):
         scratch += [pltpu.VMEM((count, spots >> (k + 1), tall, width), jnp.bfloat16)] * 3
-    for lane in (weights, gains):
+    for lane in lanes:
         scratch += Lane.scratch(bits, lane.shape[bits:], lane.dtype)
     scratch += [
         pltpu.VMEM((2, spots, tall, width), jnp.bfloat16),
@@ -582,8 +584,8 @@
         pltpu.SemaphoreType.DMA((2, 2)),
         pltpu.SemaphoreType.DMA((count, steps)),
         pltpu.SemaphoreType.DMA((count, steps)),
-        pltpu.SemaphoreType.DMA((2, bits)),
-        pltpu.SemaphoreType.DMA((2, bits)),
+        pltpu.SemaphoreType.DMA((len(lanes), bits)),
+        pltpu.SemaphoreType.DMA((len(lanes), bits)),
         pltpu.SemaphoreType.DMA((2, late)),
     ]
     return pl.pallas_call(
@@ -591,6 +593,7 @@
             reduce_kernel,
             units=units,
             n_parts=len(parts),
+            n_lanes=len(lanes),
             labels=labels,
             weight_order=weight_order,
             share=share,
@@ -598,18 +601,17 @@
         out_shape=(
             jax.ShapeDtypeStruct((count, share, width), jnp.float32),
             jax.ShapeDtypeStruct((count, (tall - share) * (width // share), share), jnp.float32),
-            jax.ShapeDtypeStruct(weights.shape[bits:], jnp.float32),
-            jax.ShapeDtypeStruct(gains.shape[bits:], jnp.float32),
-            jax.ShapeDtypeStruct((late, spots, tall, width), jnp.bfloat16),
-        ),
-        in_specs=[anywhere] * len(parts) + [vmem] * 2,
-        out_specs=[vmem] * 4 + [anywhere],
+        )
+        + tuple(jax.ShapeDtypeStruct(lane.shape[bits:], jnp.float32) for lane in lanes)
+        + (jax.ShapeDtypeStruct((late, spots, tall, width), jnp.bfloat16),),
+        in_specs=[anywhere] * len(parts) + [vmem] * len(lanes),
+        out_specs=[vmem] * (2 + len(lanes)) + [anywhere],
         scratch_shapes=scratch,
         compiler_params=pltpu.CompilerParams(
             collective_id=0, has_side_effects=True, vmem_limit_bytes=67 * 1000 * 1000
         ),
         name="reduce_rest",
-    )(*parts, weights, gains)
+    )(*parts, *lanes)
 
 
 def experts_kernel(
@@ -904,12 +906,11 @@
 
     rotated_width = query_width + key_width
     input_width = rotated_width + key_width
-    full_in = lax.all_gather(
-        jnp.concatenate([w_query, w_key, w_value], 1), everyone, axis=0, tiled=True
-    )
-    full = lax.all_gather(jnp.concatenate([w_out, w_router], 1), everyone, axis=0, tiled=True)
-    full_out = full[:, :model_width]
-    full_router = full[:, model_width:]
+    joined = jnp.concatenate([w_query, w_key, w_value, w_out, w_router], 1)
+    full = lax.all_gather(joined, everyone, axis=0, tiled=True)
+    full_in = full[:, :input_width]
+    full_out = full[:, input_width : input_width + model_width]
+    full_router = full[:, input_width + model_width :]
 
     normed, factor_one = rms_norm(inputs, attn_gain)
     normed_b = normed.astype(jnp.bfloat16)
@@ -987,7 +988,6 @@
     )
     rep_orders = [[("rep", b) for b in order] for order in orders]
     early = list(range(0, near, 2))
-    late = early[2:]
     early = early[:2]
 
     def halves(left, right, label, e=None):
@@ -1057,15 +1057,14 @@
     for k, half in enumerate(sent):
         steps_of[near + k] = ((0, near + k), (len(parts), 0), 0 if k == 0 else -1)
         parts.append((beside[0] if k == 0 else half)[None])
-    for e in late:
-        give, own = halves(grad_keep, came_near, rep_orders[e][1], e)
-        put_by(e, own, swap(after(give, returned), *rep_orders[e][1]), 1)
-    for e in early:
+    for e in early[1:]:
+        put_by(e, *second[e], 1)
+    for e in early[:1]:
         give, own = halves(*second[e], rep_orders[e][2])
         put_by(e, own, swap(after(give, returned), *rep_orders[e][2]), 2)
     units = [
         (e, steps_of[e][:2], rep_orders[e], steps_of[e][2])
-        for e in sorted(range(count), key=lambda e: (e < near, e))
+        for e in sorted(range(count), key=lambda e: (e < near, e > 1 and e % 2, e))
     ]
     grad_query_rows = returned[:, :, :head_width].reshape(rows_dev, query_width)
     key_back = returned[:, :, head_width : head_width + HEAD_DIM]
@@ -1095,11 +1094,12 @@
     )
     labels = ep_bits[::-1] + rep_bits[::-1]
     shape = (2,) * len(labels)
-    weight_grads = jnp.concatenate([grad_w_in, grad_out_w, grad_router], 1).astype(jnp.bfloat16)
-    expert_up, expert_down, weights, gains, _ = reduce_rest(
+    grads = [grad.astype(jnp.bfloat16) for grad in (grad_w_in, grad_out_w, grad_router)]
+    lanes = [grad.reshape(shape + (-1, grad.shape[1])) for grad in grads]
+    lanes.append(gains.reshape(shape + (1, -1)))
+    expert_up, expert_down, weights, weights_out, weights_router, gains, _ = reduce_rest(
         parts,
-        weight_grads.reshape(shape + (-1, weight_grads.shape[1])),
-        gains.reshape(shape + (1, -1)),
+        lanes,
         units,
         labels,
         ep_bits + rep_bits,
@@ -1114,9 +1114,9 @@
         weights[:, :query_width],
         weights[:, query_width:rotated_width],
         weights[:, rotated_width:input_width],
-        weights[:, input_width : input_width + model_width],
+        weights_out,
         gains[part:],
-        weights[:, input_width + model_width :],
+        weights_router,
         expert_up,
         expert_down,
     )

time: 656 us -> 625 us (0.953)
  waiting for transfers between devices: 132 us -> 108 us
  blocking collectives: 49.8 us -> 65.7 us
  other arithmetic: 38.8 us -> 27.1 us
  starting transfers between devices: 23.2 us -> 14.9 us
    all_to_all x0 -> x1, blocking collectives: none -> 17 us  [on_device(): lax.all_to_all(mixed.reshape(n_rep, rows_dev, head_width), 'rep', split_a...]
    ppermute x6 -> x4, waiting for transfers between devices: 27.2 us -> 13.4 us  [swap(): return lax.ppermute(sent, axis, [(i, i ^ 1 << bit) for i in range(size)])]
    all_to_all x1 -> x0, waiting for transfers between devices: 11.5 us -> none  [on_device(): lax.all_to_all(mixed.reshape(n_rep, rows_dev, head_width), 'rep', split_a...]
    concatenate x3 -> x0, other arithmetic: 8.53 us -> none  [the longest x1 5.49 us: on_device(): jnp.concatenate([grad_w_in, grad_out_w, grad_router], 1)]
    all_gather x2 -> x1, waiting for transfers between devices: 34.7 us -> 37.7 us  [on_device(): full = lax.all_gather(joined, everyone, axis=0, tiled=True)]
  transfers between devices with their start and end apart: 13 -> 9, of which waited for: 9 -> 6; matrix products, arithmetic and copies ran while one was open for 11% -> 7% of each run, Pallas kernels for 8% -> 8%
where the time goes in v9:
time: 625 us; the launch traced here: 616 us
  Pallas kernels  324 us (52%)
  waiting for transfers between devices  108 us (17%)
  blocking collectives  65.7 us (11%)
  local copies, waits for them, and re-layouts  38 us (6%)
  other arithmetic  27.1 us (4%)
  matrix products  22.2 us (4%)
  between operations  16.3 us (3%)
  starting transfers between devices  14.9 us (2%)
    pallas_call x1, Pallas kernels, reduce_rest(): pl.pallas_call(functools.partial(reduce_kernel, units=units, n_parts=len(...  152 us
    pallas_call x1, Pallas kernels, experts(): pl.pallas_call(functools.partial(experts_kernel, sources=sources, rows_de...  120 us
    all_gather x1, waiting for transfers between devices, on_device(): full = lax.all_gather(joined, everyone, axis=0, tiled=True)  37.7 us
    pallas_call x1, Pallas kernels, attend_backward(): pl.pallas_call(functools.partial(attend_backward_kernel, heads=heads, blo...  29.6 us
    all_to_all x1, blocking collectives, on_device(): lax.all_to_all(grad_mixed.reshape(rows_dev, n_rep, head_width).transpose(...  26.2 us
    all_to_all x1, waiting for transfers between devices, on_device(): lax.all_to_all(sending, 'rep', split_axis=0, concat_axis=0, tiled=True)  23 us
    pallas_call x1, Pallas kernels, attend_forward(): pl.pallas_call(functools.partial(attend_forward_kernel, heads=heads), out...  21.7 us
    all_to_all x1, waiting for transfers between devices, on_device(): lax.all_to_all(returning.reshape(n_rep, rows_dev, head_width + 2 * HEAD_D...  18.9 us
  transfers between devices with their start and end apart: 9, of which 6 were waited for; matrix products, arithmetic and copies ran while one was open for 7% of the time, Pallas kernels for 8%

profile of v9, /device:TPU:26, one launch (start us, length us, event | category | flops | bytes accessed | tf_op | source)
XLA Modules:
  0.0 615.6 jit_solution(15396592742953060961)
XLA Ops:
  12.7 16.3 %all-gather = s32[1,2048]{1,0:T(1,128)S(1)} all-gather(s32[1,256]{1,0:T(1,128)} %param.14), channel_id=2, replica_groups=mesh['ep'=4,'rep'=8] {'rep'}, dimensions={1}, use_global_device_ids=true | all-gather | bytes 9216 | tf_op jit(solution)/shard_map/all_gather | solution.py:886
  30.8 3.7 multiply_sine_fusion
  40.9 3.0 copy.61
  44.6 37.7 %all-gather.5.cloned.1.call-done = bf16[1024,3104]{1,0:T(8,128)(2,1)} async-done(((bf16[32,3104]{1,0:T(8,128)(2,1)}), bf16[1024,3104]{1,0:T(8,128)(2,1)}) %all-gather.5.cloned.1.call-update) | async-done | bytes 6357008 | tf_op jit(solution)/shard_map/all_gather | solution.py:910
  82.4 3.5 fusion.2
  90.0 2.4 maximum_bitcast_fusion
  92.4 5.5 all-to-all-start
  99.8 23.0 %all-to-all-done = bf16[8,256,256]{2,1,0:T(8,128)(2,1)S(1)} async-done(((bf16[8,256,256]{2,1,0:T(8,128)(2,1)}), bf16[8,256,256]{2,1,0:T(8,128)(2,1)S(1)}, u32[]{:S(2)}, u32[]{:S(2)}) %all-to-all-start) | async-done | bytes 1048608 | tf_op jit(solution)/shard_map/all_to_all | solution.py:932
  123.8 21.7 %attend_forward.1 = (bf16[2048,128]{1,0:T(8,128)(2,1)}, f32[128,2048]{1,0:T(8,128)}, f32[8,2,256]{2,1,0:T(2,128)}) custom-call(s32[8]{0:T(128)} %and_select_fusion.low_ref, bf16[2048,256]{1,0:T(8,128)(2,1)} %bitcast.127, s32[8,1,256]{2,1,0:T(1,128)} %bitcast.152), custom_call_target="tpu_custom_call" | custom-call | tf_op jit(solution)/shard_map/attend_forward/pallas_call | solution.py:119
  146.7 17.0 %all_to_all.25 = bf16[8,256,128]{1,2,0:T(8,128)(2,1)S(1)} all-to-all(bf16[8,256,128]{1,2,0:T(8,128)(2,1)S(1)} %copy.67), channel_id=1, replica_groups=mesh['ep'=4,'rep'=8] {'rep'}, dimensions={0} | all-to-all | bytes 1048576 | tf_op jit(solution)/shard_map/all_to_all | solution.py:935
  163.7 2.6 multiply_reduce_fusion.2
  170.6 6.1 all_to_all.26
  177.3 14.7 %all-gather.7.cloned.1.call-done = bf16[1024,1024]{1,0:T(8,128)(2,1)} async-done(((bf16[256,1024]{1,0:T(8,128)(2,1)}), bf16[1024,1024]{1,0:T(8,128)(2,1)}) %all-gather.7.cloned.1.call-update) | async-done | bytes 2097168 | tf_op jit(solution)/shard_map/all_gather | solution.py:965
  192.0 120.4 %experts.1 = (f32[256,1024]{1,0:T(8,128)}, f32[256,1024]{1,0:T(8,128)}, f32[4,8,256]{2,1,0:T(8,128)}, bf16[8,4,192,1024]{3,2,1,0:T(8,128)(2,1)}, bf16[6,4,192,10...) custom-call(bf16[2,2,256,1024]{3,2,1,0:T(8,128)(2,1)} %bitcast.138, ...), custom_call_target="tpu_custom_call" | custom-call | tf_op jit(solution)/shard_map/experts/pallas_call | solution.py:791
  313.5 2.6 multiply_reduce_fusion
  317.5 2.3 fusion.20
  319.9 26.2 %all_to_all.27 = bf16[8,256,128]{2,1,0:T(8,128)(2,1)} all-to-all(bf16[8,256,128]{2,1,0:T(8,128)(2,1)S(1)} %bitcast.142), channel_id=1, replica_groups=mesh['ep'=4,'rep'=8] {'rep'}, dimensions={0} | all-to-all | bytes 1048576 | tf_op jit(solution)/shard_map/all_to_all | solution.py:1026
  348.0 5.7 add_convert_fusion
  353.7 2.0 collective-permute-start.2
  355.7 2.0 pad_maximum_fusion.1
  357.7 29.6 %attend_backward.1 = bf16[2048,256]{1,0:T(8,128)(2,1)} custom-call(s32[8]{0:T(128)} %and_select_fusion.low_ref, bf16[2048,256]{1,0:T(8,128)(2,1)} %bitcast.128, bf16[2048,128]{1,0:T(8,128)(2,1)} %bitcast.139, f32[128,2048]{1,0:T(8,128)} %get-tuple-element.36.out_ref, f32[8,2,256]{2,1,0:T(2,128)} %get-tuple-element.37.total_ref, s32[8,1,256]{2,1,0:T(1,128)} %bitcast.153, ...), custom_call_target="tpu_custom_call" | custom-call | tf_op jit(solution)/shard_map/attend_backward/pallas_call | solution.py:244
  387.3 2.0 collective-permute-done.2
  389.3 2.3 copy.69
  391.6 5.2 all-to-all-start.4
  398.2 2.0 convolution_convert_fusion.1
  400.2 2.4 fusion.35
  402.7 18.9 %all-to-all-done.4 = bf16[8,256,256]{1,2,0:T(8,128)(2,1)S(1)} async-done(((bf16[8,256,256]{1,2,0:T(8,128)(2,1)}), bf16[8,256,256]{1,2,0:T(8,128)(2,1)S(1)}, u32[]{:S(2)}, u32[]{:S(2)}) %all-to-all-start.4) | async-done | bytes 1048608 | tf_op jit(solution)/shard_map/all_to_all | solution.py:1043
  421.8 3.8 fusion.32
  427.6 3.4 convolution_convert_fusion
  431.1 11.4 %collective-permute-done.3 = bf16[1,192,1024]{2,1,0:T(8,128)(2,1)} collective-permute-done((bf16[1,192,1024]{2,1,0:T(8,128)(2,1)}, bf16[1,192,1024]{2,1,0:T(8,128)(2,1)}, u32[]{:S(2)}, u32[]{:S(2)}) %collective-permute-start.3) | collective-permute-done | bytes 393248 | tf_op jit(solution)/shard_map/ppermute | solution.py:282
  442.5 151.9 %reduce_rest.1 = (f32[8,128,1024]{2,1,0:T(8,128)}, f32[8,512,128]{2,1,0:T(8,128)}, f32[32,2048]{1,0:T(8,128)}, f32[32,1024]{1,0:T(8,128)}, f32[32,32]{1,0:T(8,12...) custom-call(bf16[8,4,192,1024]{3,2,1,0:T(8,128)(2,1)} %get-tuple-element.40.refs_0_, ...), custom_call_target="tpu_custom_call" | custom-call | tf_op jit(solution)/shard_map/reduce_rest/pallas_call | solution.py:591
  601.7 4.9 copy.93
  (156 shorter events, 42.8 us)
Async XLA Ops:
  8.0 74.4 %all-gather.5.cloned.1.call-start = ((), (), s32[]{:S(2)}) async-start(), calls=%async_computation.5 | async-start | bytes 6758400 | tf_op jit(solution)/shard_map/all_gather | solution.py:910
  30.8 68.4 %copy-start.28 = (s32[2048]{0:T(1024)}, s32[2048]{0:T(1024)S(1)}, u32[]{:S(2)}) copy-start(s32[2048]{0:T(1024)S(1)} %convert_reduce_fusion) | copy-start | bytes 24580
  39.5 4.4 copy-start
  40.9 41.5 %copy-start.26 = (f32[1024]{0:T(1024)S(1)}, f32[1024]{0:T(1024)}, u32[]{:S(2)}) copy-start(f32[1024]{0:T(1024)} %param.16) | copy-start | bytes 12292
  44.6 41.2 %copy-start.35 = (f32[256]{0:T(256)}, f32[256]{0:T(256)S(1)}, u32[]{:S(2)}) copy-start(f32[256]{0:T(256)S(1)} %get-tuple-element.81) | copy-start | bytes 3076
  90.0 7.9 %copy-start.15 = (f32[1,256,1024]{2,1,0:T(8,128)S(1)}, f32[1,256,1024]{2,1,0:T(8,128)}, u32[]{:S(2)}) copy-start(f32[1,256,1024]{2,1,0:T(8,128)} %param.25) | copy-start | bytes 3145732
  92.4 30.3 %all-to-all-start = ((bf16[8,256,256]{2,1,0:T(8,128)(2,1)}), bf16[8,256,256]{2,1,0:T(8,128)(2,1)S(1)}, u32[]{:S(2)}, u32[]{:S(2)}) async-start(bf16[8,256,256]{2,1,0:T(8,128)(2,1)} %maximum_bitcast_fusion), calls=%async_computation | async-start | bytes 2097152 | tf_op jit(solution)/shard_map/all_to_all | solution.py:932
  97.9 79.4 %all-gather.9.cloned.1.call-start = ((), (), s32[]{:S(2)}) async-start(), calls=%async_computation.7 | async-start | bytes 2621440 | tf_op jit(solution)/shard_map/all_gather | solution.py:966
  98.9 93.1 %all-gather.7.cloned.1.call-start = ((), (), s32[]{:S(2)}) async-start(), calls=%async_computation.6 | async-start | bytes 2621440 | tf_op jit(solution)/shard_map/all_gather | solution.py:965
  163.7 3.8 copy-start.31
  170.0 6.7 %copy-start.29 = (f32[256]{0:T(256)}, f32[256]{0:T(256)S(1)}, u32[]{:S(2)}) copy-start(f32[256]{0:T(256)S(1)} %get-tuple-element.57) | copy-start | bytes 3076
  312.4 3.7 copy-start.3
  346.2 43.1 %collective-permute-start = (bf16[4,192,1024]{2,1,0:T(8,128)(2,1)}, bf16[4,192,1024]{2,1,0:T(8,128)(2,1)}, u32[]{:S(2)}, u32[]{:S(2)}) collective-permute-start(bf16[4,192,1024]{2,1,0:T(8,128)(2,1)} %get-tuple-element.39), channel_id=1, source_target_pairs={{0,1},{1,0},{2,3},{3,2},{4,5},{5,4},{6,7},{7,6},{8,9},{9,8},{10,11... | collective-permute-start | bytes 4718600 | tf_op jit(solution)/shard_map/ppermute | solution.py:282
  348.0 7.8 %copy-start.5 = (f32[2048,32]{1,0:T(8,128)S(1)}, f32[2048,32]{1,0:T(8,128)}, u32[]{:S(2)}) copy-start(f32[2048,32]{1,0:T(8,128)} %copy-done.4) | copy-start | bytes 786436
  348.0 7.8 %copy-start.7 = (f32[2048,32]{1,0:T(8,128)S(1)}, f32[2048,32]{1,0:T(8,128)}, u32[]{:S(2)}) copy-start(f32[2048,32]{1,0:T(8,128)} %copy-done.6) | copy-start | bytes 786436
  348.0 7.8 %copy-start.9 = (f32[2048,32]{1,0:T(8,128)S(1)}, f32[2048,32]{1,0:T(8,128)}, u32[]{:S(2)}) copy-start(f32[2048,32]{1,0:T(8,128)} %copy-done.8) | copy-start | bytes 786436
  353.7 33.6 %collective-permute-start.1 = (bf16[2,192,1024]{2,1,0:T(8,128)(2,1)S(1)}, bf16[2,192,1024]{2,1,0:T(8,128)(2,1)}, u32[]{:S(2)}, u32[]{:S(2)}) collective-permute-start(bf16[2,192,1024]{2,1,0:T(8,128)(2,1)S(1)} %get-tuple-element.42), channel_id=1, source_target_pairs={{0,2},{1,3},{2,0},{3,1},{4,6},{5,7},{6,4},{7,5},{8,10},{9,11},{10,... | collective-permute-start | bytes 2359304 | tf_op jit(solution)/shard_map/ppermute | solution.py:282
  353.7 35.6 %collective-permute-start.2 = (bf16[2,192,1024]{2,1,0:T(8,128)(2,1)S(1)}, bf16[2,192,1024]{2,1,0:T(8,128)(2,1)}, u32[]{:S(2)}, u32[]{:S(2)}) collective-permute-start(bf16[2,192,1024]{2,1,0:T(8,128)(2,1)S(1)} %get-tuple-element.43), channel_id=1, source_target_pairs={{0,2},{1,3},{2,0},{3,1},{4,6},{5,7},{6,4},{7,5},{8,10},{9,11},{10,... | collective-permute-start | bytes 2359304 | tf_op jit(solution)/shard_map/ppermute | solution.py:282
  389.3 7.7 %copy-start.11 = (bf16[256,1024]{1,0:T(8,128)(2,1)S(1)}, bf16[256,1024]{1,0:T(8,128)(2,1)}, u32[]{:S(2)}) copy-start(bf16[256,1024]{1,0:T(8,128)(2,1)} %multiply_convert_fusion.1) | copy-start | bytes 1572868
  389.3 7.7 %copy-start.25 = (f32[4,8,256]{2,1,0:T(8,128)S(1)}, f32[4,8,256]{2,1,0:T(8,128)}, u32[]{:S(2)}) copy-start(f32[4,8,256]{2,1,0:T(8,128)} %get-tuple-element.35) | copy-start | bytes 98308
  389.3 7.7 %copy-start.30 = (f32[256]{0:T(256)S(1)}, f32[256]{0:T(256)}, u32[]{:S(2)}) copy-start(f32[256]{0:T(256)} %copy-done.29) | copy-start | bytes 3076
  389.3 7.7 %copy-start.34 = (f32[256]{0:T(256)S(1)}, f32[256]{0:T(256)}, u32[]{:S(2)}) copy-start(f32[256]{0:T(256)} %copy-done.33) | copy-start | bytes 3076
  391.6 6.6 %copy-start.14 = (bf16[8,256,128]{1,2,0:T(8,128)(2,1)S(1)}, bf16[8,256,128]{1,2,0:T(8,128)(2,1)}, u32[]{:S(2)}) copy-start(bf16[8,256,128]{1,2,0:T(8,128)(2,1)} %copy-done.13) | copy-start | bytes 1572868
  391.6 29.9 %all-to-all-start.4 = ((bf16[8,256,256]{1,2,0:T(8,128)(2,1)}), bf16[8,256,256]{1,2,0:T(8,128)(2,1)S(1)}, u32[]{:S(2)}, u32[]{:S(2)}) async-start(bf16[8,256,256]{1,2,0:T(8,128)(2,1)} %copy.69), calls=%async_computation.4 | async-start | bytes 2097152 | tf_op jit(solution)/shard_map/all_to_all | solution.py:1043
  400.2 21.5 %copy-start.1 = (f32[1,256,1024]{2,1,0:T(8,128)S(1)}, f32[1,256,1024]{2,1,0:T(8,128)}, u32[]{:S(2)}) copy-start(f32[1,256,1024]{2,1,0:T(8,128)} %param.13) | copy-start | bytes 3145732
  400.2 21.5 %copy-start.27 = (f32[1024]{0:T(1024)S(1)}, f32[1024]{0:T(1024)}, u32[]{:S(2)}) copy-start(f32[1024]{0:T(1024)} %param.16) | copy-start | bytes 12292
  400.2 21.5 %copy-start.36 = (f32[256]{0:T(256)S(1)}, f32[256]{0:T(256)}, u32[]{:S(2)}) copy-start(f32[256]{0:T(256)} %copy-done.35) | copy-start | bytes 3076
  421.6 3.9 copy-start.18
  421.6 3.9 copy-start.21
  421.6 20.8 %collective-permute-start.3 = (bf16[1,192,1024]{2,1,0:T(8,128)(2,1)}, bf16[1,192,1024]{2,1,0:T(8,128)(2,1)}, u32[]{:S(2)}, u32[]{:S(2)}) collective-permute-start(bf16[1,192,1024]{2,1,0:T(8,128)(2,1)} %get-tuple-element.46), channel_id=1, source_target_pairs={{0,4},{1,5},{2,6},{3,7},{4,0},{5,1},{6,2},{7,3},{8,12},{9,13},{10,... | collective-permute-start | bytes 1179656 | tf_op jit(solution)/shard_map/ppermute | solution.py:282
  421.8 3.9 copy-start.40
  601.7 4.9 copy-start.20
  (19 other events, 38.1 us)
Sparse Core Ops, SparseCore 0:
  12.8 69.5 all-gather.4
Sparse Core Ops, SparseCore 1:
  100.5 22.4 all-gather.8
  168.6 23.3 all-gather.6

commit v10 on v9

--- a/solution.py
+++ b/solution.py
@@ -379,6 +379,62 @@
     def finish(self):
         for k in range(len(self.order)):
             self.copy(k).wait_send()
+
+
+def gather_kernel(*refs, lanes, partners):
+    count = len(lanes)
+    ins, outs = (refs[:count], refs[count : 2 * count])
+    sends, gets = refs[2 * count :]
+    greet([(axis, side(axis, bit)[1]) for axis, bit in partners])
+
+    def copy(number, k):
+        labels, order = lanes[number]
+        region = tuple(
+            slice(None) if label in order[:k] else side(*label)[0] for label in labels
+        )
+        target = outs[number].at[region]
+        axis, bit = order[k]
+        return mesh_copy(
+            ins[number] if k == 0 else target,
+            target,
+            sends.at[number, k],
+            gets.at[number, k],
+            axis,
+            side(axis, bit)[1],
+        )
+
+    most = max(len(order) for _, order in lanes)
+    for k in range(most + 1):
+        for number, (labels, order) in enumerate(lanes):
+            if 0 < k <= len(order):
+                copy(number, k - 1).wait_recv()
+            if k < len(order):
+                copy(number, k).start()
+            if k == 0:
+                outs[number][tuple(side(*label)[0] for label in labels)] = ins[number][...]
+    for number, (_, order) in enumerate(lanes):
+        for k in range(len(order)):
+            copy(number, k).wait_send()
+
+
+def gather(arrays, lanes, partners):
+    vmem = pl.BlockSpec(memory_space=pltpu.VMEM)
+    most = max(len(order) for _, order in lanes)
+    return pl.pallas_call(
+        functools.partial(gather_kernel, lanes=lanes, partners=partners),
+        out_shape=[
+            jax.ShapeDtypeStruct((2,) * len(order) + array.shape, array.dtype)
+            for array, (_, order) in zip(arrays, lanes)
+        ],
+        in_specs=[vmem] * len(arrays),
+        out_specs=[vmem] * len(arrays),
+        scratch_shapes=[
+            pltpu.SemaphoreType.DMA((len(arrays), most)),
+            pltpu.SemaphoreType.DMA((len(arrays), most)),
+        ],
+        compiler_params=pltpu.CompilerParams(collective_id=2, has_side_effects=True),
+        name="gather",
+    )(*arrays)
 
 
 def reduce_kernel(*refs, units, n_parts, n_lanes, labels, weight_order, share):
@@ -883,38 +939,50 @@
     experts_all = w_router.shape[1]
     half_dim = HEAD_DIM // 2
 
-    pack_ids = lax.all_gather(segments[0], "rep", axis=0, tiled=True)
+    rep_bits = [("rep", b) for b in range(bits_of(n_rep))]
+    ep_bits = [("ep", b) for b in range(bits_of(n_ep))]
+    labels = ep_bits[::-1] + rep_bits[::-1]
+    rep_down, ep_down = (rep_bits[::-1], ep_bits[::-1])
+    full_query, full_rest, pack_ids = gather(
+        [w_query, jnp.concatenate([w_key, w_value], 1), segments],
+        [
+            (labels, rep_down + ep_down),
+            (labels, rep_down[:-1] + ep_down[:-1] + rep_bits[:1] + ep_bits[:1]),
+            (rep_down, rep_down),
+        ],
+        labels,
+    )
+    full_query = full_query.reshape(model_width, -1)
+    full_rest = full_rest.reshape(model_width, -1)
+    pack_ids = pack_ids.reshape(-1)
+    rotated_width = query_width + key_width
+    input_width = rotated_width + key_width
+    joined = after(jnp.concatenate([w_out, w_router], 1), full_query)
+    full = lax.all_gather(joined, everyone, axis=0, tiled=True)
+    full_out = full[:, :model_width]
+    full_router = full[:, model_width:]
+
     length = pack_ids.shape[0]
     blocks = length // BLOCK
     offset = lax.axis_index("rep") * rows_dev
     doc_start = jnp.sum((pack_ids[None, :] < pack_ids[:, None]).astype(jnp.int32), 1)
-    position = (jnp.arange(length, dtype=jnp.int32) - doc_start).astype(jnp.float32)
-    angles = (
-        position[:, None]
-        * jnp.exp(jnp.arange(half_dim, dtype=jnp.float32) * (-math.log(10000.0) / half_dim))[
-            None, :
-        ]
-    )
-    cosine = jnp.cos(angles)
-    sine = jnp.sin(angles)
-    cosine = jnp.concatenate([cosine, cosine], 1)
-    sine = jnp.concatenate([-sine, sine], 1)
-    own_cosine = lax.dynamic_slice_in_dim(cosine, offset, rows_dev, 0)
-    own_sine = lax.dynamic_slice_in_dim(sine, offset, rows_dev, 0)
     starts = doc_start.reshape(blocks, 1, BLOCK)
     lows = doc_start[::BLOCK] // BLOCK
-
-    rotated_width = query_width + key_width
-    input_width = rotated_width + key_width
-    joined = jnp.concatenate([w_query, w_key, w_value, w_out, w_router], 1)
-    full = lax.all_gather(joined, everyone, axis=0, tiled=True)
-    full_in = full[:, :input_width]
-    full_out = full[:, input_width : input_width + model_width]
-    full_router = full[:, input_width + model_width :]
+    pace = jnp.exp(jnp.arange(half_dim, dtype=jnp.float32) * (-math.log(10000.0) / half_dim))
+
+    def rope_tables(first, begins):
+        places = first + jnp.arange(begins.shape[0], dtype=jnp.int32)
+        angles = (places - begins).astype(jnp.float32)[:, None] * pace[None, :]
+        cosine = jnp.cos(angles)
+        sine = jnp.sin(angles)
+        return (jnp.concatenate([cosine, cosine], 1), jnp.concatenate([-sine, sine], 1))
+
+    own_starts = jnp.sum((pack_ids[None, :] < segments[0][:, None]).astype(jnp.int32), 1)
+    own_cosine, own_sine = rope_tables(offset, own_starts)
 
     normed, factor_one = rms_norm(inputs, attn_gain)
     normed_b = normed.astype(jnp.bfloat16)
-    mixed_in = product(normed_b, full_in)
+    mixed_in = jnp.concatenate([product(normed_b, full_query), product(normed_b, full_rest)], 1)
     turn = mixed_in[:, :rotated_width]
     times = rotated_width // HEAD_DIM
     turned = turn * jnp.tile(own_cosine, (1, times)) + swap_halves(turn) * jnp.tile(
@@ -932,6 +1000,7 @@
     head_rows = lax.all_to_all(sending, "rep", split_axis=0, concat_axis=0, tiled=True)
     head_rows = head_rows.reshape(length, head_width + 2 * HEAD_DIM)
     mixed, mixed_out, totals = attend_forward(head_rows, starts, lows, heads)
+    cosine, sine = rope_tables(0, after(doc_start, mixed))
     mixed_rows = lax.all_to_all(
         mixed.reshape(n_rep, rows_dev, head_width), "rep", split_axis=0, concat_axis=0, tiled=True
     )
@@ -964,8 +1033,6 @@
     prob_all = both_all[:, experts_all // n_ep :]
     expert_rows = lax.all_gather(normed_two_b, "ep", axis=0, tiled=True)
     expert_cots = lax.all_gather(grad_output.astype(jnp.bfloat16), "ep", axis=0, tiled=True)
-    rep_bits = [("rep", b) for b in range(bits_of(n_rep))]
-    ep_bits = [("ep", b) for b in range(bits_of(n_ep))]
     count = experts_all // n_ep
     near = count * 3 // 4
     kinds = [k % 2 for k in range(near)] + [0] * (count - near)
@@ -1085,14 +1152,15 @@
         1,
     )
     grad_w_in = dot_tn(normed_b, grad_in_rows)
-    grad_normed = dot_nt(grad_in_rows, full_in)
+    grad_normed = dot_nt(grad_in_rows[:, :query_width], full_query) + dot_nt(
+        grad_in_rows[:, query_width:], full_rest
+    )
     grad_inputs_norm, grad_attn_gain = norm_back(grad_normed, inputs, factor_one, attn_gain)
     grad_inputs = grad_hidden + grad_inputs_norm
     everything = n_ep * n_rep
     gains = jnp.concatenate(
         [grad_attn_gain.reshape(everything, -1), grad_mlp_gain.reshape(everything, -1)], 1
     )
-    labels = ep_bits[::-1] + rep_bits[::-1]
     shape = (2,) * len(labels)
     grads = [grad.astype(jnp.bfloat16) for grad in (grad_w_in, grad_out_w, grad_router)]
     lanes = [grad.reshape(shape + (-1, grad.shape[1])) for grad in grads]

time: 625 us -> 618 us (0.989)
  Pallas kernels: 324 us -> 376 us
  waiting for transfers between devices: 108 us -> 58.3 us
  blocking collectives: 65.7 us -> 44.1 us
    pallas_call x0 -> x1, Pallas kernels: none -> 37.8 us  [gather(): pl.pallas_call(functools.partial(gather_kernel, lanes=lanes, partners=par...]
    all_gather x1, waiting for transfers between devices: 37.7 us -> 0.01 us  [on_device(): full = lax.all_gather(joined, everyone, axis=0, tiled=True)]
    all_gather x1 -> x0, blocking collectives: 16.3 us -> none  [on_device(): pack_ids = lax.all_gather(segments[0], 'rep', axis=0, tiled=True)]
    all_to_all x1, waiting for transfers between devices: 18.9 us -> 10.1 us  [on_device(): lax.all_to_all(returning.reshape(n_rep, rows_dev, head_width + 2 * HEAD_D...]
    all_to_all x1, blocking collectives: 26.2 us -> 17.8 us  [on_device(): lax.all_to_all(grad_mixed.reshape(rows_dev, n_rep, head_width).transpose(...]
    unnamed x92 -> x88, local copies, waits for them, and re-layouts: 17.4 us -> 15.7 us
  transfers between devices with their start and end apart: 9 -> 9, of which waited for: 6 -> 4; matrix products, arithmetic and copies ran while one was open for 7% -> 9% of each run, Pallas kernels for 8% -> 10%
where the time goes in v10:
time: 618 us; the launch traced here: 607 us
  Pallas kernels  376 us (61%)
  waiting for transfers between devices  58.3 us (9%)
  blocking collectives  44.1 us (7%)
  local copies, waits for them, and re-layouts  39.3 us (6%)
  other arithmetic  33.3 us (5%)
  matrix products  22.5 us (4%)
  starting transfers between devices  18.2 us (3%)
  between operations  14.8 us (2%)
    pallas_call x1, Pallas kernels, reduce_rest(): pl.pallas_call(functools.partial(reduce_kernel, units=units, n_parts=len(...  157 us
    pallas_call x1, Pallas kernels, experts(): pl.pallas_call(functools.partial(experts_kernel, sources=sources, rows_de...  120 us
    pallas_call x1, Pallas kernels, gather(): pl.pallas_call(functools.partial(gather_kernel, lanes=lanes, partners=par...  37.8 us
    pallas_call x1, Pallas kernels, attend_backward(): pl.pallas_call(functools.partial(attend_backward_kernel, heads=heads, blo...  34.7 us
    all_to_all x1, waiting for transfers between devices, on_device(): lax.all_to_all(sending, 'rep', split_axis=0, concat_axis=0, tiled=True)  26 us
    pallas_call x1, Pallas kernels, attend_forward(): pl.pallas_call(functools.partial(attend_forward_kernel, heads=heads), out...  26 us
    all_to_all x1, blocking collectives, on_device(): lax.all_to_all(grad_mixed.reshape(rows_dev, n_rep, head_width).transpose(...  17.8 us
    unnamed x88, local copies, waits for them, and re-layouts  15.7 us
  transfers between devices with their start and end apart: 9, of which 4 were waited for; matrix products, arithmetic and copies ran while one was open for 9% of the time, Pallas kernels for 10%

profile of v10, /device:TPU:26, one launch (start us, length us, event | category | flops | bytes accessed | tf_op | source)
XLA Modules:
  0.0 606.9 jit_solution(16523048208832184079)
XLA Ops:
  10.2 37.8 %gather.1 = (bf16[2,2,2,2,2,32,1024]{6,5,4,3,2,1,0:T(8,128)(2,1)}, bf16[2,2,2,2,2,32,1024]{6,5,4,3,2,1,0:T(8,128)(2,1)}, s32[2,2,2,1,256]{4,3,2,1,0:T(1,128)}) custom-call(bf16[32,1024]{1,0:T(8,128)(2,1)} %refs_0_.1, bf16[32,1024]{1,0:T(8,128)(2,1)} %pad_maximum_fusion.4.refs_1_, s32[1,256]{1,0:T(1,128)} %refs_2_.1), custom_call_target="tpu_custom_call" | custom-call | tf_op jit(solution)/shard_map/gather/pallas_call | solution.py:423
  50.1 2.4 fusion.77
  55.7 3.0 copy.53
  60.0 3.1 copy.54
  63.1 2.4 fusion.79
  70.6 7.3 %all-to-all-start = ((bf16[8,256,256]{2,1,0:T(8,128)(2,1)}), bf16[8,256,256]{2,1,0:T(8,128)(2,1)S(1)}, u32[]{:S(2)}, u32[]{:S(2)}) async-start(bf16[8,256,256]{2,1,0:T(8,128)(2,1)} %maximum_bitcast_fusion), calls=%async_computation | async-start | bytes 2097152 | tf_op jit(solution)/shard_map/all_to_all | solution.py:1000
  78.8 1.8 convert_reduce_fusion
  81.2 26.0 %all-to-all-done = bf16[8,256,256]{2,1,0:T(8,128)(2,1)S(1)} async-done(((bf16[8,256,256]{2,1,0:T(8,128)(2,1)}), bf16[8,256,256]{2,1,0:T(8,128)(2,1)S(1)}, u32[]{:S(2)}, u32[]{:S(2)}) %all-to-all-start) | async-done | bytes 1048608 | tf_op jit(solution)/shard_map/all_to_all | solution.py:1000
  108.2 26.0 %attend_forward.1 = (bf16[2048,128]{1,0:T(8,128)(2,1)}, f32[128,2048]{1,0:T(8,128)}, f32[8,2,256]{2,1,0:T(2,128)}) custom-call(s32[8]{0:T(128)} %and_select_fusion.low_ref, bf16[2048,256]{1,0:T(8,128)(2,1)} %bitcast.138, s32[8,1,256]{2,1,0:T(1,128)} %bitcast.168), custom_call_target="tpu_custom_call" | custom-call | tf_op jit(solution)/shard_map/attend_forward/pallas_call | solution.py:119
  135.4 15.6 %all_to_all.25 = bf16[8,256,128]{1,2,0:T(8,128)(2,1)S(1)} all-to-all(bf16[8,256,128]{1,2,0:T(8,128)(2,1)S(1)} %copy.60), channel_id=1, replica_groups=mesh['ep'=4,'rep'=8] {'rep'}, dimensions={0} | all-to-all | bytes 1048576 | tf_op jit(solution)/shard_map/all_to_all | solution.py:1004
  151.0 2.6 multiply_reduce_fusion.2
  157.7 10.7 %all_to_all.26 = f32[4,16,256]{2,1,0:T(8,128)S(1)} all-to-all(f32[4,16,256]{2,1,0:T(8,128)S(1)} %pad_maximum_fusion.7), channel_id=1, replica_groups=mesh['ep'=4,'rep'=8] {'ep'}, dimensions={0} | all-to-all | bytes 131072 | tf_op jit(solution)/shard_map/all_to_all | solution.py:1031
  169.0 14.0 %all-gather.6.cloned.1.call-done = bf16[1024,1024]{1,0:T(8,128)(2,1)} async-done(((bf16[256,1024]{1,0:T(8,128)(2,1)}), bf16[1024,1024]{1,0:T(8,128)(2,1)}) %all-gather.6.cloned.1.call-update) | async-done | bytes 2097168 | tf_op jit(solution)/shard_map/all_gather | solution.py:1034
  183.0 120.4 %experts.1 = (f32[256,1024]{1,0:T(8,128)}, f32[256,1024]{1,0:T(8,128)}, f32[4,8,256]{2,1,0:T(8,128)}, bf16[8,4,192,1024]{3,2,1,0:T(8,128)(2,1)}, bf16[6,4,192,10...) custom-call(bf16[2,2,256,1024]{3,2,1,0:T(8,128)(2,1)} %bitcast.159, ...), custom_call_target="tpu_custom_call" | custom-call | tf_op jit(solution)/shard_map/experts/pallas_call | solution.py:847
  304.4 2.6 multiply_reduce_fusion
  310.0 17.8 %all_to_all.27 = bf16[8,256,128]{2,1,0:T(8,128)(2,1)} all-to-all(bf16[8,256,128]{2,1,0:T(8,128)(2,1)S(1)} %bitcast.161), channel_id=1, replica_groups=mesh['ep'=4,'rep'=8] {'rep'}, dimensions={0} | all-to-all | bytes 1048576 | tf_op jit(solution)/shard_map/all_to_all | solution.py:1093
  329.6 5.4 add_convert_fusion
  335.0 2.0 collective-permute-start.2
  337.1 3.7 fusion.51
  343.4 34.7 %attend_backward.1 = bf16[2048,256]{1,0:T(8,128)(2,1)} custom-call(s32[8]{0:T(128)} %and_select_fusion.low_ref, bf16[2048,256]{1,0:T(8,128)(2,1)} %bitcast.139, bf16[2048,128]{1,0:T(8,128)(2,1)} %bitcast.160, f32[128,2048]{1,0:T(8,128)} %get-tuple-element.45.out_ref, f32[8,2,256]{2,1,0:T(2,128)} %get-tuple-element.46.total_ref, s32[8,1,256]{2,1,0:T(1,128)} %bitcast.169, ...), custom_call_target="tpu_custom_call" | custom-call | tf_op jit(solution)/shard_map/attend_backward/pallas_call | solution.py:244
  379.4 2.3 copy.63
  381.7 6.3 %all-to-all-start.4 = ((bf16[8,256,256]{1,2,0:T(8,128)(2,1)}), bf16[8,256,256]{1,2,0:T(8,128)(2,1)S(1)}, u32[]{:S(2)}, u32[]{:S(2)}) async-start(bf16[8,256,256]{1,2,0:T(8,128)(2,1)} %copy.63), calls=%async_computation.4 | async-start | bytes 2097152 | tf_op jit(solution)/shard_map/all_to_all | solution.py:1110
  390.0 2.0 convolution_convert_fusion.1
  392.0 2.4 fusion.41
  394.5 10.1 %all-to-all-done.4 = bf16[8,256,256]{1,2,0:T(8,128)(2,1)S(1)} async-done(((bf16[8,256,256]{1,2,0:T(8,128)(2,1)}), bf16[8,256,256]{1,2,0:T(8,128)(2,1)S(1)}, u32[]{:S(2)}, u32[]{:S(2)}) %all-to-all-start.4) | async-done | bytes 1048608 | tf_op jit(solution)/shard_map/all_to_all | solution.py:1110
  407.7 2.5 fusion.84
  410.3 1.9 fusion.38
  414.2 2.5 fusion.33
  417.4 3.4 convolution_convert_fusion
  420.9 8.1 %collective-permute-done.3 = bf16[1,192,1024]{2,1,0:T(8,128)(2,1)} collective-permute-done((bf16[1,192,1024]{2,1,0:T(8,128)(2,1)S(1)}, bf16[1,192,1024]{2,1,0:T(8,128)(2,1)}, u32[]{:S(2)}, u32[]{:S(2)}) %collective-permute-start.3) | collective-permute-done | bytes 393248 | tf_op jit(solution)/shard_map/ppermute | solution.py:282
  429.0 157.4 %reduce_rest.1 = (f32[8,128,1024]{2,1,0:T(8,128)}, f32[8,512,128]{2,1,0:T(8,128)}, f32[32,2048]{1,0:T(8,128)}, f32[32,1024]{1,0:T(8,128)}, f32[32,32]{1,0:T(8,12...) custom-call(bf16[8,4,192,1024]{3,2,1,0:T(8,128)(2,1)} %get-tuple-element.50.refs_0_, ...), custom_call_target="tpu_custom_call" | custom-call | tf_op jit(solution)/shard_map/reduce_rest/pallas_call | solution.py:647
  593.6 4.9 copy.83
  (158 shorter events, 48.8 us)
Async XLA Ops:
  7.2 42.9 %copy-start = (f32[1,256,1024]{2,1,0:T(8,128)S(1)}, f32[1,256,1024]{2,1,0:T(8,128)}, u32[]{:S(2)}) copy-start(f32[1,256,1024]{2,1,0:T(8,128)} %param.13) | copy-start | bytes 3145732
  7.2 143.8 %all-gather.4.cloned.1.call-start = ((), (), s32[]{:S(2)}) async-start(), calls=%async_computation.5 | async-start | bytes 2433024 | tf_op jit(solution)/shard_map/all_gather | solution.py:961
  58.7 4.4 copy-start.19
  69.3 8.6 %copy-start.12 = (f32[1,256,1024]{2,1,0:T(8,128)S(1)}, f32[1,256,1024]{2,1,0:T(8,128)}, u32[]{:S(2)}) copy-start(f32[1,256,1024]{2,1,0:T(8,128)} %param.25) | copy-start | bytes 3145732
  70.6 36.7 %all-to-all-start = ((bf16[8,256,256]{2,1,0:T(8,128)(2,1)}), bf16[8,256,256]{2,1,0:T(8,128)(2,1)S(1)}, u32[]{:S(2)}, u32[]{:S(2)}) async-start(bf16[8,256,256]{2,1,0:T(8,128)(2,1)} %maximum_bitcast_fusion), calls=%async_computation | async-start | bytes 2097152 | tf_op jit(solution)/shard_map/all_to_all | solution.py:1000
  77.8 91.2 %all-gather.8.cloned.1.call-start = ((), (), s32[]{:S(2)}) async-start(), calls=%async_computation.7 | async-start | bytes 2621440 | tf_op jit(solution)/shard_map/all_gather | solution.py:1035
  78.7 104.3 %all-gather.6.cloned.1.call-start = ((), (), s32[]{:S(2)}) async-start(), calls=%async_computation.6 | async-start | bytes 2621440 | tf_op jit(solution)/shard_map/all_gather | solution.py:1034
  80.6 26.7 %copy-start.23 = (s32[2048]{0:T(1024)}, s32[2048]{0:T(1024)S(1)}, u32[]{:S(2)}) copy-start(s32[2048]{0:T(1024)S(1)} %convert_reduce_fusion) | copy-start | bytes 24580
  151.0 3.6 copy-start.29
  154.3 14.8 %copy-start.33 = (f32[256]{0:T(256)}, f32[256]{0:T(256)S(1)}, u32[]{:S(2)}) copy-start(f32[256]{0:T(256)S(1)} %get-tuple-element.92) | copy-start | bytes 3076
  157.1 11.3 %copy-start.27 = (f32[256]{0:T(256)}, f32[256]{0:T(256)S(1)}, u32[]{:S(2)}) copy-start(f32[256]{0:T(256)S(1)} %get-tuple-element.67) | copy-start | bytes 3076
  303.4 3.7 copy-start.3
  303.4 3.7 copy-start.13
  303.4 3.7 copy-start.18
  303.4 3.7 copy-start.30
  303.5 3.6 copy-start.34
  303.5 3.6 copy-start.39
  309.9 19.7 %copy-start.24 = (s32[2048]{0:T(1024)S(1)}, s32[2048]{0:T(1024)}, u32[]{:S(2)}) copy-start(s32[2048]{0:T(1024)} %copy-done.23) | copy-start | bytes 24580
  327.8 50.3 %collective-permute-start = (bf16[4,192,1024]{2,1,0:T(8,128)(2,1)}, bf16[4,192,1024]{2,1,0:T(8,128)(2,1)S(1)}, u32[]{:S(2)}, u32[]{:S(2)}) collective-permute-start(bf16[4,192,1024]{2,1,0:T(8,128)(2,1)} %get-tuple-element.49), channel_id=1, source_target_pairs={{0,1},{1,0},{2,3},{3,2},{4,5},{5,4},{6,7},{7,6},{8,9},{9,8},{10,11... | collective-permute-start | bytes 4718600 | tf_op jit(solution)/shard_map/ppermute | solution.py:282
  329.6 7.5 %copy-start.41 = (f32[32]{0:T(128)S(1)}, f32[32]{0:T(128)}, u32[]{:S(2)}) copy-start(f32[32]{0:T(128)} %copy-done.40) | copy-start | bytes 388
  335.0 43.1 %collective-permute-start.1 = (bf16[2,192,1024]{2,1,0:T(8,128)(2,1)}, bf16[2,192,1024]{2,1,0:T(8,128)(2,1)}, u32[]{:S(2)}, u32[]{:S(2)}) collective-permute-start(bf16[2,192,1024]{2,1,0:T(8,128)(2,1)} %get-tuple-element.52), channel_id=1, source_target_pairs={{0,2},{1,3},{2,0},{3,1},{4,6},{5,7},{6,4},{7,5},{8,10},{9,11},{10,... | collective-permute-start | bytes 2359304 | tf_op jit(solution)/shard_map/ppermute | solution.py:282
  335.0 43.1 %collective-permute-start.2 = (bf16[2,192,1024]{2,1,0:T(8,128)(2,1)S(1)}, bf16[2,192,1024]{2,1,0:T(8,128)(2,1)}, u32[]{:S(2)}, u32[]{:S(2)}) collective-permute-start(bf16[2,192,1024]{2,1,0:T(8,128)(2,1)S(1)} %get-tuple-element.53), channel_id=1, source_target_pairs={{0,2},{1,3},{2,0},{3,1},{4,6},{5,7},{6,4},{7,5},{8,10},{9,11},{10,... | collective-permute-start | bytes 2359304 | tf_op jit(solution)/shard_map/ppermute | solution.py:282
  379.4 8.7 %copy-start.6 = (bf16[256,1024]{1,0:T(8,128)(2,1)S(1)}, bf16[256,1024]{1,0:T(8,128)(2,1)}, u32[]{:S(2)}) copy-start(bf16[256,1024]{1,0:T(8,128)(2,1)} %multiply_convert_fusion.1) | copy-start | bytes 1572868
  379.4 8.7 %copy-start.20 = (f32[4,8,256]{2,1,0:T(8,128)S(1)}, f32[4,8,256]{2,1,0:T(8,128)}, u32[]{:S(2)}) copy-start(f32[4,8,256]{2,1,0:T(8,128)} %get-tuple-element.44) | copy-start | bytes 98308
  379.4 8.7 %copy-start.22 = (pred[256,32]{0,1:T(32,128)(4,1)S(1)}, pred[256,32]{0,1:T(32,128)(4,1)}, u32[]{:S(2)}) copy-start(pred[256,32]{0,1:T(32,128)(4,1)} %copy-done.21) | copy-start | bytes 24580
  379.4 8.7 %copy-start.28 = (f32[256]{0:T(256)S(1)}, f32[256]{0:T(256)}, u32[]{:S(2)}) copy-start(f32[256]{0:T(256)} %copy-done.27) | copy-start | bytes 3076
  379.4 8.7 %copy-start.32 = (f32[256]{0:T(256)S(1)}, f32[256]{0:T(256)}, u32[]{:S(2)}) copy-start(f32[256]{0:T(256)} %copy-done.31) | copy-start | bytes 3076
  381.7 8.3 %copy-start.10 = (bf16[8,256,128]{1,2,0:T(8,128)(2,1)S(1)}, bf16[8,256,128]{1,2,0:T(8,128)(2,1)}, u32[]{:S(2)}) copy-start(bf16[8,256,128]{1,2,0:T(8,128)(2,1)} %copy-done.9) | copy-start | bytes 1572868
  381.7 22.9 %all-to-all-start.4 = ((bf16[8,256,256]{1,2,0:T(8,128)(2,1)}), bf16[8,256,256]{1,2,0:T(8,128)(2,1)S(1)}, u32[]{:S(2)}, u32[]{:S(2)}) async-start(bf16[8,256,256]{1,2,0:T(8,128)(2,1)} %copy.63), calls=%async_computation.4 | async-start | bytes 2097152 | tf_op jit(solution)/shard_map/all_to_all | solution.py:1110
  410.3 4.0 copy-start.38
  412.7 16.2 %collective-permute-start.3 = (bf16[1,192,1024]{2,1,0:T(8,128)(2,1)S(1)}, bf16[1,192,1024]{2,1,0:T(8,128)(2,1)}, u32[]{:S(2)}, u32[]{:S(2)}) collective-permute-start(bf16[1,192,1024]{2,1,0:T(8,128)(2,1)S(1)} %get-tuple-element.56), channel_id=1, source_target_pairs={{0,4},{1,5},{2,6},{3,7},{4,0},{5,1},{6,2},{7,3},{8,12},{9,13},{10,... | collective-permute-start | bytes 1179656 | tf_op jit(solution)/shard_map/ppermute | solution.py:282
  593.6 4.9 copy-start.16
  (19 other events, 29.6 us)
Sparse Core Ops, SparseCore 0:
  48.2 65.7 all-gather.3
  116.1 21.7 all-gather.7
  155.7 27.2 all-gather.5

commit v11 on v10

--- a/solution.py
+++ b/solution.py
@@ -999,8 +999,9 @@
     sending = jnp.concatenate([query_part, key_part, value_part], 2).transpose(1, 0, 2)
     head_rows = lax.all_to_all(sending, "rep", split_axis=0, concat_axis=0, tiled=True)
     head_rows = head_rows.reshape(length, head_width + 2 * HEAD_DIM)
+    cosine, sine = rope_tables(0, after(doc_start, sending))
+    head_rows = after(head_rows, cosine, sine)
     mixed, mixed_out, totals = attend_forward(head_rows, starts, lows, heads)
-    cosine, sine = rope_tables(0, after(doc_start, mixed))
     mixed_rows = lax.all_to_all(
         mixed.reshape(n_rep, rows_dev, head_width), "rep", split_axis=0, concat_axis=0, tiled=True
     )

time: 618 us -> 610 us (0.987); the launches traced: 607 us -> 607 us
  waiting for transfers between devices: 58.3 us -> 65.4 us
    ppermute x4, waiting for transfers between devices: 8.1 us -> 14.8 us  [swap(): return lax.ppermute(sent, axis, [(i, i ^ 1 << bit) for i in range(size)])]
    all_to_all x1, waiting for transfers between devices: 26 us -> 19.5 us  [on_device(): lax.all_to_all(sending, 'rep', split_axis=0, concat_axis=0, tiled=True)]
    all_to_all x1, waiting for transfers between devices: 10.1 us -> 16.6 us  [on_device(): lax.all_to_all(returning.reshape(n_rep, rows_dev, head_width + 2 * HEAD_D...]
    unnamed x88 -> x82, local copies, waits for them, and re-layouts: 15.7 us -> 15.7 us
  transfers between devices with their start and end apart: 9 -> 9, of which waited for: 4 -> 5; matrix products, arithmetic and copies ran while one was open for 9% -> 9% of each run, Pallas kernels for 10% -> 8%
where the time goes in v11:
time: 610 us; the launch traced here: 607 us
  Pallas kernels  370 us (61%)
  waiting for transfers between devices  65.4 us (11%)
  blocking collectives  44.1 us (7%)
  local copies, waits for them, and re-layouts  39.4 us (6%)
  other arithmetic  33.3 us (5%)
  matrix products  22.5 us (4%)
  starting transfers between devices  17.3 us (3%)
  between operations  14.7 us (2%)
    pallas_call x1, Pallas kernels, reduce_rest(): pl.pallas_call(functools.partial(reduce_kernel, units=units, n_parts=len(...  161 us
    pallas_call x1, Pallas kernels, experts(): pl.pallas_call(functools.partial(experts_kernel, sources=sources, rows_de...  120 us
    pallas_call x1, Pallas kernels, gather(): pl.pallas_call(functools.partial(gather_kernel, lanes=lanes, partners=par...  37.8 us
    pallas_call x1, Pallas kernels, attend_backward(): pl.pallas_call(functools.partial(attend_backward_kernel, heads=heads, blo...  29.6 us
    pallas_call x1, Pallas kernels, attend_forward(): pl.pallas_call(functools.partial(attend_forward_kernel, heads=heads), out...  21.7 us
    all_to_all x1, blocking collectives, on_device(): lax.all_to_all(mixed.reshape(n_rep, rows_dev, head_width), 'rep', split_a...  19.8 us
    all_to_all x1, waiting for transfers between devices, on_device(): lax.all_to_all(sending, 'rep', split_axis=0, concat_axis=0, tiled=True)  19.5 us
    all_to_all x1, blocking collectives, on_device(): lax.all_to_all(grad_mixed.reshape(rows_dev, n_rep, head_width).transpose(...  17.8 us
  transfers between devices with their start and end apart: 9, of which 5 were waited for; matrix products, arithmetic and copies ran while one was open for 9% of the time, Pallas kernels for 8%

profile of v11, /device:TPU:26, one launch (start us, length us, event | category | flops | bytes accessed | tf_op | source)
XLA Modules:
  0.0 607.2 jit_solution(17305149674348768003)
XLA Ops:
  10.2 37.8 %gather.1 = (bf16[2,2,2,2,2,32,1024]{6,5,4,3,2,1,0:T(8,128)(2,1)}, bf16[2,2,2,2,2,32,1024]{6,5,4,3,2,1,0:T(8,128)(2,1)}, s32[2,2,2,1,256]{4,3,2,1,0:T(1,128)}) custom-call(bf16[32,1024]{1,0:T(8,128)(2,1)} %refs_0_.1, bf16[32,1024]{1,0:T(8,128)(2,1)} %pad_maximum_fusion.4.refs_1_, s32[1,256]{1,0:T(1,128)} %refs_2_.1), custom_call_target="tpu_custom_call" | custom-call | tf_op jit(solution)/shard_map/gather/pallas_call | solution.py:423
  50.0 2.4 fusion.77
  55.6 3.0 copy.53
  60.0 3.1 copy.54
  63.0 2.4 fusion.79
  70.5 7.3 %all-to-all-start = ((bf16[8,256,256]{2,1,0:T(8,128)(2,1)}), bf16[8,256,256]{2,1,0:T(8,128)(2,1)S(1)}, u32[]{:S(2)}, u32[]{:S(2)}) async-start(bf16[8,256,256]{2,1,0:T(8,128)(2,1)} %maximum_bitcast_fusion), calls=%async_computation | async-start | bytes 2097152 | tf_op jit(solution)/shard_map/all_to_all | solution.py:1000
  81.3 3.7 fusion.51
  87.7 19.5 %all-to-all-done = bf16[8,256,256]{2,1,0:T(8,128)(2,1)S(1)} async-done(((bf16[8,256,256]{2,1,0:T(8,128)(2,1)}), bf16[8,256,256]{2,1,0:T(8,128)(2,1)S(1)}, u32[]{:S(2)}, u32[]{:S(2)}) %all-to-all-start) | async-done | bytes 1048608 | tf_op jit(solution)/shard_map/all_to_all | solution.py:1000
  108.2 21.7 %attend_forward.1 = (bf16[2048,128]{1,0:T(8,128)(2,1)}, f32[128,2048]{1,0:T(8,128)}, f32[8,2,256]{2,1,0:T(2,128)}) custom-call(s32[8]{0:T(128)} %and_select_fusion.low_ref, bf16[2048,256]{1,0:T(8,128)(2,1)} %bitcast.138, s32[8,1,256]{2,1,0:T(1,128)} %bitcast.168), custom_call_target="tpu_custom_call" | custom-call | tf_op jit(solution)/shard_map/attend_forward/pallas_call | solution.py:119
  131.1 19.8 %all_to_all.25 = bf16[8,256,128]{1,2,0:T(8,128)(2,1)S(1)} all-to-all(bf16[8,256,128]{1,2,0:T(8,128)(2,1)S(1)} %copy.61), channel_id=1, replica_groups=mesh['ep'=4,'rep'=8] {'rep'}, dimensions={0} | all-to-all | bytes 1048576 | tf_op jit(solution)/shard_map/all_to_all | solution.py:1005
  150.9 2.6 multiply_reduce_fusion.2
  157.7 6.4 %all_to_all.26 = f32[4,16,256]{2,1,0:T(8,128)S(1)} all-to-all(f32[4,16,256]{2,1,0:T(8,128)S(1)} %pad_maximum_fusion.7), channel_id=1, replica_groups=mesh['ep'=4,'rep'=8] {'ep'}, dimensions={0} | all-to-all | bytes 131072 | tf_op jit(solution)/shard_map/all_to_all | solution.py:1032
  164.7 14.4 %all-gather.6.cloned.1.call-done = bf16[1024,1024]{1,0:T(8,128)(2,1)} async-done(((bf16[256,1024]{1,0:T(8,128)(2,1)}), bf16[1024,1024]{1,0:T(8,128)(2,1)}) %all-gather.6.cloned.1.call-update) | async-done | bytes 2097168 | tf_op jit(solution)/shard_map/all_gather | solution.py:1035
  179.2 120.4 %experts.1 = (f32[256,1024]{1,0:T(8,128)}, f32[256,1024]{1,0:T(8,128)}, f32[4,8,256]{2,1,0:T(8,128)}, bf16[8,4,192,1024]{3,2,1,0:T(8,128)(2,1)}, bf16[6,4,192,10...) custom-call(bf16[2,2,256,1024]{3,2,1,0:T(8,128)(2,1)} %bitcast.159, ...), custom_call_target="tpu_custom_call" | custom-call | tf_op jit(solution)/shard_map/experts/pallas_call | solution.py:847
  300.6 2.6 multiply_reduce_fusion
  306.2 17.8 %all_to_all.27 = bf16[8,256,128]{2,1,0:T(8,128)(2,1)} all-to-all(bf16[8,256,128]{2,1,0:T(8,128)(2,1)S(1)} %bitcast.161), channel_id=1, replica_groups=mesh['ep'=4,'rep'=8] {'rep'}, dimensions={0} | all-to-all | bytes 1048576 | tf_op jit(solution)/shard_map/all_to_all | solution.py:1094
  325.7 5.4 add_convert_fusion
  331.2 2.0 collective-permute-start.2
  333.2 29.6 %attend_backward.1 = bf16[2048,256]{1,0:T(8,128)(2,1)} custom-call(s32[8]{0:T(128)} %and_select_fusion.low_ref, bf16[2048,256]{1,0:T(8,128)(2,1)} %bitcast.139, bf16[2048,128]{1,0:T(8,128)(2,1)} %bitcast.160, f32[128,2048]{1,0:T(8,128)} %get-tuple-element.48.out_ref, f32[8,2,256]{2,1,0:T(2,128)} %get-tuple-element.49.total_ref, s32[8,1,256]{2,1,0:T(1,128)} %bitcast.169, ...), custom_call_target="tpu_custom_call" | custom-call | tf_op jit(solution)/shard_map/attend_backward/pallas_call | solution.py:244
  362.8 4.2 collective-permute-done.2
  368.2 2.3 copy.63
  370.5 5.2 all-to-all-start.4
  377.7 2.0 convolution_convert_fusion.1
  379.7 2.4 fusion.41
  382.1 16.6 %all-to-all-done.4 = bf16[8,256,256]{1,2,0:T(8,128)(2,1)S(1)} async-done(((bf16[8,256,256]{1,2,0:T(8,128)(2,1)}), bf16[8,256,256]{1,2,0:T(8,128)(2,1)S(1)}, u32[]{:S(2)}, u32[]{:S(2)}) %all-to-all-start.4) | async-done | bytes 1048608 | tf_op jit(solution)/shard_map/all_to_all | solution.py:1111
  401.9 2.5 fusion.84
  404.4 1.9 fusion.38
  408.4 2.5 fusion.33
  411.6 3.4 convolution_convert_fusion
  415.1 10.6 %collective-permute-done.3 = bf16[1,192,1024]{2,1,0:T(8,128)(2,1)} collective-permute-done((bf16[1,192,1024]{2,1,0:T(8,128)(2,1)S(1)}, bf16[1,192,1024]{2,1,0:T(8,128)(2,1)}, u32[]{:S(2)}, u32[]{:S(2)}) %collective-permute-start.3) | collective-permute-done | bytes 393248 | tf_op jit(solution)/shard_map/ppermute | solution.py:282
  425.7 161.0 %reduce_rest.1 = (f32[8,128,1024]{2,1,0:T(8,128)}, f32[8,512,128]{2,1,0:T(8,128)}, f32[32,2048]{1,0:T(8,128)}, f32[32,1024]{1,0:T(8,128)}, f32[32,32]{1,0:T(8,12...) custom-call(bf16[8,4,192,1024]{3,2,1,0:T(8,128)(2,1)} %get-tuple-element.52.refs_0_, ...), custom_call_target="tpu_custom_call" | custom-call | tf_op jit(solution)/shard_map/reduce_rest/pallas_call | solution.py:647
  594.0 4.9 copy.83
  (152 shorter events, 50.9 us)
Async XLA Ops:
  7.2 42.9 %copy-start = (f32[1,256,1024]{2,1,0:T(8,128)S(1)}, f32[1,256,1024]{2,1,0:T(8,128)}, u32[]{:S(2)}) copy-start(f32[1,256,1024]{2,1,0:T(8,128)} %param.13) | copy-start | bytes 3145732
  7.2 143.8 %all-gather.4.cloned.1.call-start = ((), (), s32[]{:S(2)}) async-start(), calls=%async_computation.5 | async-start | bytes 2433024 | tf_op jit(solution)/shard_map/all_gather | solution.py:961
  58.7 4.4 copy-start.19
  69.2 8.6 %copy-start.12 = (f32[1,256,1024]{2,1,0:T(8,128)S(1)}, f32[1,256,1024]{2,1,0:T(8,128)}, u32[]{:S(2)}) copy-start(f32[1,256,1024]{2,1,0:T(8,128)} %param.25) | copy-start | bytes 3145732
  70.5 36.7 %all-to-all-start = ((bf16[8,256,256]{2,1,0:T(8,128)(2,1)}), bf16[8,256,256]{2,1,0:T(8,128)(2,1)S(1)}, u32[]{:S(2)}, u32[]{:S(2)}) async-start(bf16[8,256,256]{2,1,0:T(8,128)(2,1)} %maximum_bitcast_fusion), calls=%async_computation | async-start | bytes 2097152 | tf_op jit(solution)/shard_map/all_to_all | solution.py:1000
  77.8 87.0 %all-gather.8.cloned.1.call-start = ((), (), s32[]{:S(2)}) async-start(), calls=%async_computation.7 | async-start | bytes 2621440 | tf_op jit(solution)/shard_map/all_gather | solution.py:1036
  78.7 100.5 %all-gather.6.cloned.1.call-start = ((), (), s32[]{:S(2)}) async-start(), calls=%async_computation.6 | async-start | bytes 2621440 | tf_op jit(solution)/shard_map/all_gather | solution.py:1035
  80.7 5.7 copy-start.23
  150.9 2.6 copy-start.9
  150.9 3.6 copy-start.28
  154.2 10.5 %copy-start.32 = (f32[256]{0:T(256)}, f32[256]{0:T(256)S(1)}, u32[]{:S(2)}) copy-start(f32[256]{0:T(256)S(1)} %get-tuple-element.94) | copy-start | bytes 3076
  157.0 7.1 %copy-start.26 = (f32[256]{0:T(256)}, f32[256]{0:T(256)S(1)}, u32[]{:S(2)}) copy-start(f32[256]{0:T(256)S(1)} %get-tuple-element.69) | copy-start | bytes 3076
  299.5 3.7 copy-start.3
  299.5 3.7 copy-start.13
  299.6 3.7 copy-start.18
  299.6 3.7 copy-start.29
  299.6 3.6 copy-start.33
  299.6 3.6 copy-start.38
  324.0 43.0 %collective-permute-start = (bf16[4,192,1024]{2,1,0:T(8,128)(2,1)}, bf16[4,192,1024]{2,1,0:T(8,128)(2,1)S(1)}, u32[]{:S(2)}, u32[]{:S(2)}) collective-permute-start(bf16[4,192,1024]{2,1,0:T(8,128)(2,1)} %get-tuple-element.51), channel_id=1, source_target_pairs={{0,1},{1,0},{2,3},{3,2},{4,5},{5,4},{6,7},{7,6},{8,9},{9,8},{10,11... | collective-permute-start | bytes 4718600 | tf_op jit(solution)/shard_map/ppermute | solution.py:282
  331.2 31.6 %collective-permute-start.1 = (bf16[2,192,1024]{2,1,0:T(8,128)(2,1)}, bf16[2,192,1024]{2,1,0:T(8,128)(2,1)}, u32[]{:S(2)}, u32[]{:S(2)}) collective-permute-start(bf16[2,192,1024]{2,1,0:T(8,128)(2,1)} %get-tuple-element.54), channel_id=1, source_target_pairs={{0,2},{1,3},{2,0},{3,1},{4,6},{5,7},{6,4},{7,5},{8,10},{9,11},{10,... | collective-permute-start | bytes 2359304 | tf_op jit(solution)/shard_map/ppermute | solution.py:282
  331.2 35.8 %collective-permute-start.2 = (bf16[2,192,1024]{2,1,0:T(8,128)(2,1)S(1)}, bf16[2,192,1024]{2,1,0:T(8,128)(2,1)}, u32[]{:S(2)}, u32[]{:S(2)}) collective-permute-start(bf16[2,192,1024]{2,1,0:T(8,128)(2,1)S(1)} %get-tuple-element.55), channel_id=1, source_target_pairs={{0,2},{1,3},{2,0},{3,1},{4,6},{5,7},{6,4},{7,5},{8,10},{9,11},{10,... | collective-permute-start | bytes 2359304 | tf_op jit(solution)/shard_map/ppermute | solution.py:282
  368.2 7.6 %copy-start.6 = (bf16[256,1024]{1,0:T(8,128)(2,1)S(1)}, bf16[256,1024]{1,0:T(8,128)(2,1)}, u32[]{:S(2)}) copy-start(bf16[256,1024]{1,0:T(8,128)(2,1)} %multiply_convert_fusion.1) | copy-start | bytes 1572868
  368.2 7.6 %copy-start.20 = (f32[4,8,256]{2,1,0:T(8,128)S(1)}, f32[4,8,256]{2,1,0:T(8,128)}, u32[]{:S(2)}) copy-start(f32[4,8,256]{2,1,0:T(8,128)} %get-tuple-element.47) | copy-start | bytes 98308
  368.2 7.6 %copy-start.22 = (pred[256,32]{0,1:T(32,128)(4,1)S(1)}, pred[256,32]{0,1:T(32,128)(4,1)}, u32[]{:S(2)}) copy-start(pred[256,32]{0,1:T(32,128)(4,1)} %copy-done.21) | copy-start | bytes 24580
  368.2 7.6 %copy-start.27 = (f32[256]{0:T(256)S(1)}, f32[256]{0:T(256)}, u32[]{:S(2)}) copy-start(f32[256]{0:T(256)} %copy-done.26) | copy-start | bytes 3076
  368.2 7.6 %copy-start.31 = (f32[256]{0:T(256)S(1)}, f32[256]{0:T(256)}, u32[]{:S(2)}) copy-start(f32[256]{0:T(256)} %copy-done.30) | copy-start | bytes 3076
  370.5 7.2 %copy-start.10 = (bf16[8,256,128]{1,2,0:T(8,128)(2,1)S(1)}, bf16[8,256,128]{1,2,0:T(8,128)(2,1)}, u32[]{:S(2)}) copy-start(bf16[8,256,128]{1,2,0:T(8,128)(2,1)} %copy-done.9) | copy-start | bytes 1572868
  370.5 28.2 %all-to-all-start.4 = ((bf16[8,256,256]{1,2,0:T(8,128)(2,1)}), bf16[8,256,256]{1,2,0:T(8,128)(2,1)S(1)}, u32[]{:S(2)}, u32[]{:S(2)}) async-start(bf16[8,256,256]{1,2,0:T(8,128)(2,1)} %copy.63), calls=%async_computation.4 | async-start | bytes 2097152 | tf_op jit(solution)/shard_map/all_to_all | solution.py:1111
  401.9 2.5 copy-start.5
  404.4 4.0 copy-start.37
  406.9 18.8 %collective-permute-start.3 = (bf16[1,192,1024]{2,1,0:T(8,128)(2,1)S(1)}, bf16[1,192,1024]{2,1,0:T(8,128)(2,1)}, u32[]{:S(2)}, u32[]{:S(2)}) collective-permute-start(bf16[1,192,1024]{2,1,0:T(8,128)(2,1)S(1)} %get-tuple-element.58), channel_id=1, source_target_pairs={{0,4},{1,5},{2,6},{3,7},{4,0},{5,1},{6,2},{7,3},{8,12},{9,13},{10,... | collective-permute-start | bytes 1179656 | tf_op jit(solution)/shard_map/ppermute | solution.py:282
  594.0 4.9 copy-start.16
  (16 other events, 23.8 us)
Sparse Core Ops, SparseCore 0:
  48.2 65.7 all-gather.3
  115.5 21.7 all-gather.7
  155.7 23.4 all-gather.5

commit v12 on v11

--- a/solution.py
+++ b/solution.py
@@ -1108,6 +1108,10 @@
         head_rows, grad_heads, mixed_out, totals, starts, lows, cosine, sine, heads
     )
     returning = after(returning, *beside)
+    onward, third = ({}, {})
+    for e in early[:1]:
+        give, third[e] = halves(*second[e], rep_orders[e][2])
+        onward[e] = swap(after(give, returning), *rep_orders[e][2])
     returned = lax.all_to_all(
         returning.reshape(n_rep, rows_dev, head_width + 2 * HEAD_DIM),
         "rep",
@@ -1128,8 +1132,8 @@
     for e in early[1:]:
         put_by(e, *second[e], 1)
     for e in early[:1]:
-        give, own = halves(*second[e], rep_orders[e][2])
-        put_by(e, own, swap(after(give, returned), *rep_orders[e][2]), 2)
+        own = third[e]
+        put_by(e, own, onward[e], 2)
     units = [
         (e, steps_of[e][:2], rep_orders[e], steps_of[e][2])
         for e in sorted(range(count), key=lambda e: (e < near, e > 1 and e % 2, e))

time: 610 us -> 605 us (level)
  the two profiles are of different devices: /device:TPU:26 before, /device:TPU:5 now
where the time goes in v12:
time: 605 us; the launch traced here: 602 us
  Pallas kernels  376 us (62%)
  waiting for transfers between devices  60.6 us (10%)
  blocking collectives  44.7 us (7%)
  local copies, waits for them, and re-layouts  35.2 us (6%)
  other arithmetic  33.9 us (6%)
  matrix products  21.7 us (4%)
  starting transfers between devices  15 us (2%)
  between operations  14.8 us (2%)
    pallas_call x1, Pallas kernels, reduce_rest(): pl.pallas_call(functools.partial(reduce_kernel, units=units, n_parts=len(...  164 us
    pallas_call x1, Pallas kernels, experts(): pl.pallas_call(functools.partial(experts_kernel, sources=sources, rows_de...  120 us
    pallas_call x1, Pallas kernels, gather(): pl.pallas_call(functools.partial(gather_kernel, lanes=lanes, partners=par...  40.8 us
    pallas_call x1, Pallas kernels, attend_backward(): pl.pallas_call(functools.partial(attend_backward_kernel, heads=heads, blo...  29.6 us
    all_to_all x1, waiting for transfers between devices, on_device(): lax.all_to_all(returning.reshape(n_rep, rows_dev, head_width + 2 * HEAD_D...  23.6 us
    all_to_all x1, waiting for transfers between devices, on_device(): lax.all_to_all(sending, 'rep', split_axis=0, concat_axis=0, tiled=True)  22 us
    pallas_call x1, Pallas kernels, attend_forward(): pl.pallas_call(functools.partial(attend_forward_kernel, heads=heads), out...  21.7 us
    all_to_all x1, blocking collectives, on_device(): lax.all_to_all(grad_mixed.reshape(rows_dev, n_rep, head_width).transpose(...  18 us
  transfers between devices with their start and end apart: 9, of which 4 were waited for; matrix products, arithmetic and copies ran while one was open for 10% of the time, Pallas kernels for 9%

profile of v12, /device:TPU:5, one launch (start us, length us, event | category | flops | bytes accessed | tf_op | source)
XLA Modules:
  0.0 602.2 jit_solution(9662941843398688700)
XLA Ops:
  10.2 40.8 %gather.1 = (bf16[2,2,2,2,2,32,1024]{6,5,4,3,2,1,0:T(8,128)(2,1)}, bf16[2,2,2,2,2,32,1024]{6,5,4,3,2,1,0:T(8,128)(2,1)}, s32[2,2,2,1,256]{4,3,2,1,0:T(1,128)}) custom-call(bf16[32,1024]{1,0:T(8,128)(2,1)} %refs_0_.1, bf16[32,1024]{1,0:T(8,128)(2,1)} %pad_maximum_fusion.4.refs_1_, s32[1,256]{1,0:T(1,128)} %refs_2_.1), custom_call_target="tpu_custom_call" | custom-call | tf_op jit(solution)/shard_map/gather/pallas_call | solution.py:423
  53.0 2.4 fusion.77
  58.6 3.0 copy.53
  63.0 3.1 copy.54
  66.1 2.4 fusion.79
  73.5 5.5 all-to-all-start
  80.2 1.8 convert_reduce_fusion
  82.6 3.7 fusion.51
  89.0 22.0 %all-to-all-done = bf16[8,256,256]{2,1,0:T(8,128)(2,1)S(1)} async-done(((bf16[8,256,256]{2,1,0:T(8,128)(2,1)}), bf16[8,256,256]{2,1,0:T(8,128)(2,1)S(1)}, u32[]{:S(2)}, u32[]{:S(2)}) %all-to-all-start) | async-done | bytes 1048608 | tf_op jit(solution)/shard_map/all_to_all | solution.py:1000
  112.0 21.7 %attend_forward.1 = (bf16[2048,128]{1,0:T(8,128)(2,1)}, f32[128,2048]{1,0:T(8,128)}, f32[8,2,256]{2,1,0:T(2,128)}) custom-call(s32[8]{0:T(128)} %and_select_fusion.low_ref, bf16[2048,256]{1,0:T(8,128)(2,1)} %bitcast.138, s32[8,1,256]{2,1,0:T(1,128)} %bitcast.166), custom_call_target="tpu_custom_call" | custom-call | tf_op jit(solution)/shard_map/attend_forward/pallas_call | solution.py:119
  135.0 14.4 %all_to_all.25 = bf16[8,256,128]{1,2,0:T(8,128)(2,1)S(1)} all-to-all(bf16[8,256,128]{1,2,0:T(8,128)(2,1)S(1)} %copy.61), channel_id=1, replica_groups=mesh['ep'=4,'rep'=8] {'rep'}, dimensions={0} | all-to-all | bytes 1048576 | tf_op jit(solution)/shard_map/all_to_all | solution.py:1005
  149.4 2.6 multiply_reduce_fusion.2
  156.1 12.3 %all_to_all.26 = f32[4,16,256]{2,1,0:T(8,128)S(1)} all-to-all(f32[4,16,256]{2,1,0:T(8,128)S(1)} %pad_maximum_fusion.7), channel_id=1, replica_groups=mesh['ep'=4,'rep'=8] {'ep'}, dimensions={0} | all-to-all | bytes 131072 | tf_op jit(solution)/shard_map/all_to_all | solution.py:1032
  169.0 11.8 %all-gather.6.cloned.1.call-done = bf16[1024,1024]{1,0:T(8,128)(2,1)} async-done(((bf16[256,1024]{1,0:T(8,128)(2,1)}), bf16[1024,1024]{1,0:T(8,128)(2,1)}) %all-gather.6.cloned.1.call-update) | async-done | bytes 2097168 | tf_op jit(solution)/shard_map/all_gather | solution.py:1035
  180.8 120.3 %experts.1 = (f32[256,1024]{1,0:T(8,128)}, f32[256,1024]{1,0:T(8,128)}, f32[4,8,256]{2,1,0:T(8,128)}, bf16[8,4,192,1024]{3,2,1,0:T(8,128)(2,1)}, bf16[6,4,192,10...) custom-call(bf16[2,2,256,1024]{3,2,1,0:T(8,128)(2,1)} %bitcast.157, ...), custom_call_target="tpu_custom_call" | custom-call | tf_op jit(solution)/shard_map/experts/pallas_call | solution.py:847
  302.1 2.6 multiply_reduce_fusion
  307.7 18.0 %all_to_all.27 = bf16[8,256,128]{2,1,0:T(8,128)(2,1)} all-to-all(bf16[8,256,128]{2,1,0:T(8,128)(2,1)S(1)} %bitcast.159), channel_id=1, replica_groups=mesh['ep'=4,'rep'=8] {'rep'}, dimensions={0} | all-to-all | bytes 1048576 | tf_op jit(solution)/shard_map/all_to_all | solution.py:1094
  326.2 5.4 add_convert_fusion
  333.1 29.6 %attend_backward.1 = bf16[2048,256]{1,0:T(8,128)(2,1)} custom-call(s32[8]{0:T(128)} %and_select_fusion.low_ref, bf16[2048,256]{1,0:T(8,128)(2,1)} %bitcast.139, bf16[2048,128]{1,0:T(8,128)(2,1)} %bitcast.158, f32[128,2048]{1,0:T(8,128)} %get-tuple-element.48.out_ref, f32[8,2,256]{2,1,0:T(2,128)} %get-tuple-element.49.total_ref, s32[8,1,256]{2,1,0:T(1,128)} %bitcast.167, ...), custom_call_target="tpu_custom_call" | custom-call | tf_op jit(solution)/shard_map/attend_backward/pallas_call | solution.py:244
  362.7 3.1 collective-permute-done.2
  367.0 2.3 copy.63
  369.4 5.2 all-to-all-start.4
  375.9 2.0 convolution_convert_fusion.1
  378.0 2.7 fusion.41
  380.7 2.1 collective-permute-start.3
  382.8 23.6 %all-to-all-done.4 = bf16[8,256,256]{1,2,0:T(8,128)(2,1)} async-done(((bf16[8,256,256]{1,2,0:T(8,128)(2,1)}), bf16[8,256,256]{1,2,0:T(8,128)(2,1)}, u32[]{:S(2)}, u32[]{:S(2)}) %all-to-all-start.4) | async-done | bytes 1048608 | tf_op jit(solution)/shard_map/all_to_all | solution.py:1115
  410.7 1.9 fusion.38
  413.4 4.4 convolution_convert_fusion
  417.8 164.0 %reduce_rest.1 = (f32[8,128,1024]{2,1,0:T(8,128)}, f32[8,512,128]{2,1,0:T(8,128)}, f32[32,2048]{1,0:T(8,128)}, f32[32,1024]{1,0:T(8,128)}, f32[32,32]{1,0:T(8,12...) custom-call(bf16[8,4,192,1024]{3,2,1,0:T(8,128)(2,1)} %get-tuple-element.52.refs_0_, ...), custom_call_target="tpu_custom_call" | custom-call | tf_op jit(solution)/shard_map/reduce_rest/pallas_call | solution.py:647
  581.8 1.6 slice.100
  586.3 3.3 fusion.33
  590.8 2.1 copy.83
  (162 shorter events, 45.7 us)
Async XLA Ops:
  7.2 45.9 %copy-start = (f32[1,256,1024]{2,1,0:T(8,128)S(1)}, f32[1,256,1024]{2,1,0:T(8,128)}, u32[]{:S(2)}) copy-start(f32[1,256,1024]{2,1,0:T(8,128)} %param.13) | copy-start | bytes 3145732
  7.2 142.2 %all-gather.4.cloned.1.call-start = ((), (), s32[]{:S(2)}) async-start(), calls=%async_computation.5 | async-start | bytes 2433024 | tf_op jit(solution)/shard_map/all_gather | solution.py:961
  61.7 4.4 copy-start.24
  72.2 6.8 %copy-start.16 = (f32[1,256,1024]{2,1,0:T(8,128)S(1)}, f32[1,256,1024]{2,1,0:T(8,128)}, u32[]{:S(2)}) copy-start(f32[1,256,1024]{2,1,0:T(8,128)} %param.25) | copy-start | bytes 3145732
  73.5 37.5 %all-to-all-start = ((bf16[8,256,256]{2,1,0:T(8,128)(2,1)}), bf16[8,256,256]{2,1,0:T(8,128)(2,1)S(1)}, u32[]{:S(2)}, u32[]{:S(2)}) async-start(bf16[8,256,256]{2,1,0:T(8,128)(2,1)} %maximum_bitcast_fusion), calls=%async_computation | async-start | bytes 2097152 | tf_op jit(solution)/shard_map/all_to_all | solution.py:1000
  79.1 89.9 %all-gather.8.cloned.1.call-start = ((), (), s32[]{:S(2)}) async-start(), calls=%async_computation.7 | async-start | bytes 2621440 | tf_op jit(solution)/shard_map/all_gather | solution.py:1036
  80.0 100.8 %all-gather.6.cloned.1.call-start = ((), (), s32[]{:S(2)}) async-start(), calls=%async_computation.6 | async-start | bytes 2621440 | tf_op jit(solution)/shard_map/all_gather | solution.py:1035
  82.0 5.7 copy-start.29
  152.6 16.4 %copy-start.37 = (f32[256]{0:T(256)}, f32[256]{0:T(256)S(1)}, u32[]{:S(2)}) copy-start(f32[256]{0:T(256)S(1)} %get-tuple-element.94) | copy-start | bytes 3076
  155.4 12.9 %copy-start.30 = (f32[256]{0:T(256)}, f32[256]{0:T(256)S(1)}, u32[]{:S(2)}) copy-start(f32[256]{0:T(256)S(1)} %get-tuple-element.69) | copy-start | bytes 3076
  301.1 3.7 copy-start.3
  301.1 3.7 copy-start.17
  301.1 3.7 copy-start.23
  301.1 3.7 copy-start.33
  306.2 69.7 %copy-start.4 = (f32[256,1024]{1,0:T(8,128)}, f32[256,1024]{1,0:T(8,128)S(1)}, u32[]{:S(2)}) copy-start(f32[256,1024]{1,0:T(8,128)S(1)} %get-tuple-element.79) | copy-start | bytes 3145732
  325.8 40.1 %collective-permute-start = (bf16[4,192,1024]{2,1,0:T(8,128)(2,1)}, bf16[4,192,1024]{2,1,0:T(8,128)(2,1)S(1)}, u32[]{:S(2)}, u32[]{:S(2)}) collective-permute-start(bf16[4,192,1024]{2,1,0:T(8,128)(2,1)} %get-tuple-element.51), channel_id=1, source_target_pairs={{0,1},{1,0},{2,3},{3,2},{4,5},{5,4},{6,7},{7,6},{8,9},{9,8},{10,11... | collective-permute-start | bytes 4718600 | tf_op jit(solution)/shard_map/ppermute | solution.py:282
  331.6 31.1 %collective-permute-start.1 = (bf16[2,192,1024]{2,1,0:T(8,128)(2,1)}, bf16[2,192,1024]{2,1,0:T(8,128)(2,1)}, u32[]{:S(2)}, u32[]{:S(2)}) collective-permute-start(bf16[2,192,1024]{2,1,0:T(8,128)(2,1)} %get-tuple-element.54), channel_id=1, source_target_pairs={{0,2},{1,3},{2,0},{3,1},{4,6},{5,7},{6,4},{7,5},{8,10},{9,11},{10,... | collective-permute-start | bytes 2359304 | tf_op jit(solution)/shard_map/ppermute | solution.py:282
  331.6 34.2 %collective-permute-start.2 = (bf16[2,192,1024]{2,1,0:T(8,128)(2,1)S(1)}, bf16[2,192,1024]{2,1,0:T(8,128)(2,1)}, u32[]{:S(2)}, u32[]{:S(2)}) collective-permute-start(bf16[2,192,1024]{2,1,0:T(8,128)(2,1)S(1)} %get-tuple-element.55), channel_id=1, source_target_pairs={{0,2},{1,3},{2,0},{3,1},{4,6},{5,7},{6,4},{7,5},{8,10},{9,11},{10,... | collective-permute-start | bytes 2359304 | tf_op jit(solution)/shard_map/ppermute | solution.py:282
  367.0 7.6 %copy-start.8 = (bf16[256,1024]{1,0:T(8,128)(2,1)S(1)}, bf16[256,1024]{1,0:T(8,128)(2,1)}, u32[]{:S(2)}) copy-start(bf16[256,1024]{1,0:T(8,128)(2,1)} %multiply_convert_fusion.1) | copy-start | bytes 1572868
  367.0 7.6 %copy-start.25 = (f32[4,8,256]{2,1,0:T(8,128)S(1)}, f32[4,8,256]{2,1,0:T(8,128)}, u32[]{:S(2)}) copy-start(f32[4,8,256]{2,1,0:T(8,128)} %get-tuple-element.47) | copy-start | bytes 98308
  367.0 7.6 %copy-start.27 = (pred[256,32]{0,1:T(32,128)(4,1)S(1)}, pred[256,32]{0,1:T(32,128)(4,1)}, u32[]{:S(2)}) copy-start(pred[256,32]{0,1:T(32,128)(4,1)} %copy-done.26) | copy-start | bytes 24580
  367.0 7.6 %copy-start.31 = (f32[256]{0:T(256)S(1)}, f32[256]{0:T(256)}, u32[]{:S(2)}) copy-start(f32[256]{0:T(256)} %copy-done.30) | copy-start | bytes 3076
  367.0 7.6 %copy-start.35 = (f32[256]{0:T(256)S(1)}, f32[256]{0:T(256)}, u32[]{:S(2)}) copy-start(f32[256]{0:T(256)} %copy-done.34) | copy-start | bytes 3076
  369.4 6.6 %copy-start.12 = (bf16[8,256,128]{1,2,0:T(8,128)(2,1)S(1)}, bf16[8,256,128]{1,2,0:T(8,128)(2,1)}, u32[]{:S(2)}) copy-start(bf16[8,256,128]{1,2,0:T(8,128)(2,1)} %copy-done.11) | copy-start | bytes 1572868
  369.4 37.0 %all-to-all-start.4 = ((bf16[8,256,256]{1,2,0:T(8,128)(2,1)}), bf16[8,256,256]{1,2,0:T(8,128)(2,1)}, u32[]{:S(2)}, u32[]{:S(2)}) async-start(bf16[8,256,256]{1,2,0:T(8,128)(2,1)} %copy.63), calls=%async_computation.4 | async-start | bytes 2097152 | tf_op jit(solution)/shard_map/all_to_all | solution.py:1115
  378.0 30.8 %copy-start.6 = (bf16[2,2,2,2,2,32,1024]{6,5,4,3,2,1,0:T(8,128)(2,1)S(1)}, bf16[2,2,2,2,2,32,1024]{6,5,4,3,2,1,0:T(8,128)(2,1)}, u32[]{:S(2)}) copy-start(bf16[2,2,2,2,2,32,1024]{6,5,4,3,2,1,0:T(8,128)(2,1)} %get-tuple-element.39) | copy-start | bytes 6291460
  380.7 37.1 %collective-permute-start.3 = (bf16[1,192,1024]{2,1,0:T(8,128)(2,1)}, bf16[1,192,1024]{2,1,0:T(8,128)(2,1)}, u32[]{:S(2)}, u32[]{:S(2)}) collective-permute-start(bf16[1,192,1024]{2,1,0:T(8,128)(2,1)} %get-tuple-element.58), channel_id=1, source_target_pairs={{0,4},{1,5},{2,6},{3,7},{4,0},{5,1},{6,2},{7,3},{8,12},{9,13},{10,... | collective-permute-start | bytes 1179656 | tf_op jit(solution)/shard_map/ppermute | solution.py:282
  408.7 3.9 copy-start.19
  417.8 168.5 %copy-start.42 = (f32[256]{0:T(256)S(1)}, f32[256]{0:T(256)}, u32[]{:S(2)}) copy-start(f32[256]{0:T(256)} %get-tuple-element.91) | copy-start | bytes 3076
  583.4 6.2 %copy-start.28 = (f32[32,1024]{1,0:T(8,128)S(1)}, f32[32,1024]{1,0:T(8,128)}, u32[]{:S(2)}) copy-start(f32[32,1024]{1,0:T(8,128)} %get-tuple-element.123) | copy-start | bytes 393220
  586.3 3.9 copy-start.36
  586.3 4.5 copy-start.15
  (21 other events, 40.1 us)
Sparse Core Ops, SparseCore 0:
  51.2 64.6 all-gather.3
  117.4 21.4 all-gather.7
  154.1 26.6 all-gather.5
